TPU v7x, 32 devices: a whole 2x2x4 slice. The times are simulated.
32 devices in a mesh: row: 4 (over y, x), ctx: 8 (over z, core).
Axes of the slice: x: 2, y: 2, z: 4, core: 2. Of those that a mesh axis runs over, the one named last changes fastest.
Arguments:
- inputs: bfloat16 [4, 1024, 1024], P('row', 'ctx'), may hold values from -6 to 6
- lengths: int32 [4], P('row'), may hold values from 1 to 1024, 3328 in all
- gain_attn: float32 [1024], replicated, may hold values from 0.25 to 1.75
- w_fact: bfloat16 [1024, 800], replicated, may hold values from -0.25 to 0.25
- w_out: bfloat16 [1024, 1024], replicated, may hold values from -1.5 to 1.5
- gain_ffn: float32 [1024], replicated, may hold values from 0.25 to 1.75
- w_gate: bfloat16 [1024, 2816], replicated, may hold values from -0.1875 to 0.1875
- w_up: bfloat16 [1024, 2816], replicated, may hold values from -0.1875 to 0.1875
- w_down: bfloat16 [2816, 1024], replicated, may hold values from -0.109375 to 0.109375
- cotangent: bfloat16 [4, 1024, 1024], P('row', 'ctx'), may hold values from -6 to 6
Outputs:
- block_out: bfloat16 [4, 1024, 1024], P('row', 'ctx')
- grad_inputs: float32 [4, 1024, 1024], P('row', 'ctx')
- grad_gain_attn: float32 [1024], replicated
- grad_w_fact: float32 [1024, 800], P('ctx', 'row')
- grad_w_out: float32 [1024, 1024], P('ctx', 'row')
- grad_gain_ffn: float32 [1024], replicated
- grad_w_gate: float32 [1024, 2816], P('ctx', 'row')
- grad_w_up: float32 [1024, 2816], P('ctx', 'row')
- grad_w_down: float32 [2816, 1024], P('ctx', 'row')
Inputs may be any that keep to these rules, and one draw needn't show every extreme that they name: `lengths`: the longest row is full.
All inputs are finite; a program needn't handle non-finite values. No bound on the sum of `lengths` on one device may be relied on, other than what follows from the above.
Results may differ from a plain program's by a relative error of at most 0.015.
The roundings to bfloat16 on the way count: a program that leaves them out, or rounds other values in their place, can miss the bound.
Values may be sent and summed in bfloat16 or wider, within the bound.
No kernel may reach another device: no remote copies, remote signals or barrier semaphores. Data moves between devices by JAX's collectives and lax.ppermute only.
A program may use at most 384 MiB of HBM per device.

v0:
```python
import jax
import jax.numpy as jnp
from jax import lax
from jax.sharding import PartitionSpec as P

H = 16
DH = 64
RQ = 6
RK = 2


def slot_position(index, block_len, slots_all):
    block_id = index // (2 * block_len)
    within = index % (2 * block_len)
    return jnp.where(
        within < block_len,
        block_id * block_len + within,
        (slots_all // block_len - 1 - block_id) * block_len + within - block_len,
    )


def rope_angles(positions, head_dim):
    half_dim = head_dim // 2
    frequency = jnp.exp(
        -jnp.log(10000.0) * (2.0 * jnp.arange(half_dim, dtype=jnp.float32)) / head_dim
    )
    angles = positions.astype(jnp.float32)[:, None] * frequency[None, :]
    return (jnp.cos(angles)[:, None, :], jnp.sin(angles)[:, None, :])


def rotate(vectors, cosine, sine):
    half_dim = vectors.shape[-1] // 2
    upper_half = vectors[..., :half_dim]
    lower_half = vectors[..., half_dim:]
    return jnp.concatenate(
        [upper_half * cosine - lower_half * sine, lower_half * cosine + upper_half * sine], axis=-1
    )


def rotate_back(vectors, cosine, sine):
    half_dim = vectors.shape[-1] // 2
    upper_half = vectors[..., :half_dim]
    lower_half = vectors[..., half_dim:]
    return jnp.concatenate(
        [upper_half * cosine + lower_half * sine, lower_half * cosine - upper_half * sine], axis=-1
    )


def inv_rms(values):
    return lax.rsqrt(jnp.mean(values * values, axis=-1, keepdims=True) + 1e-06)


def expand(flat_a, flat_b):
    factor_a = flat_a.reshape(-1, 2 * RK, H)
    factor_b = flat_b.reshape(-1, 2 * RK, DH)
    key_rows = (
        jnp.einsum(
            "tsh,tsd->thd", factor_a[:, :RK], factor_b[:, :RK], preferred_element_type=jnp.float32
        )
        / RK
    )
    value_rows = (
        jnp.einsum(
            "tsh,tsd->thd", factor_a[:, RK:], factor_b[:, RK:], preferred_element_type=jnp.float32
        )
        / RK
    )
    return (key_rows.astype(jnp.bfloat16), value_rows.astype(jnp.bfloat16), factor_a, factor_b)


def body(inputs, lengths, gain_attn, w_fact, w_out, gain_ffn, w_gate, w_up, w_down, cotangent):
    highest = lax.Precision.HIGHEST
    seqs_here, local_len, model_width = inputs.shape
    block_len = local_len // 2
    group_size = lax.axis_size("ctx")
    slots_all = local_len * group_size
    score_scale = DH ** (-0.5)
    local_pos = slot_position(
        lax.axis_index("ctx") * local_len + jnp.arange(local_len, dtype=jnp.int32),
        block_len,
        slots_all,
    )
    key_pos = slot_position(jnp.arange(slots_all, dtype=jnp.int32), block_len, slots_all)
    cosine, sine = rope_angles(local_pos, DH)
    tokens = seqs_here * local_len
    rows_dims = (((0,), (0,)), ((), ()))
    cols_dims = (((1,), (1,)), ((), ()))
    x_flat = inputs.astype(jnp.float32).reshape(tokens, model_width)
    scale_one = inv_rms(x_flat)
    normed_one = x_flat * scale_one
    h_one = (normed_one * gain_attn).astype(jnp.bfloat16)
    factors = jnp.dot(h_one, w_fact, preferred_element_type=jnp.float32)
    query_cols = RQ * H
    start_k = RQ * (H + DH)
    start_b = start_k + 2 * RK * H
    query_a = factors[:, :query_cols].reshape(seqs_here, local_len, RQ, H)
    query_b = rotate(
        factors[:, query_cols:start_k].reshape(seqs_here, local_len, RQ, DH), cosine, sine
    )
    kv_a = (
        factors[:, start_k:start_b].astype(jnp.bfloat16).reshape(seqs_here, local_len * 2 * RK * H)
    )
    raw_b = factors[:, start_b:].reshape(seqs_here, local_len, 2 * RK, DH)
    kv_b = jnp.concatenate([rotate(raw_b[:, :, :RK], cosine, sine), raw_b[:, :, RK:]], axis=2)
    kv_b = kv_b.astype(jnp.bfloat16).reshape(seqs_here, local_len * 2 * RK * DH)
    queries = (jnp.einsum("slrh,slrd->slhd", query_a, query_b, precision=highest) / RQ).astype(
        jnp.bfloat16
    )
    all_a, all_b = (
        lax.all_gather(kv_a, "ctx", axis=1, tiled=True),
        lax.all_gather(kv_b, "ctx", axis=1, tiled=True),
    )

    def allowed_for(seq_len):
        return (key_pos[None, :] <= local_pos[:, None]) & (key_pos[None, :] < seq_len)

    def attend_forward(row_item):
        query_seq, flat_a, flat_b, seq_len = row_item
        key_rows, value_rows, factor_a, factor_b = expand(flat_a, flat_b)
        scores = (
            jnp.einsum("qhd,khd->hqk", query_seq, key_rows, preferred_element_type=jnp.float32)
            * score_scale
        )
        scores = jnp.where(allowed_for(seq_len)[None], scores, -1e30)
        row_max = jnp.max(scores, axis=-1, keepdims=True)
        exponent = jnp.exp(scores - row_max)
        row_total = jnp.sum(exponent, axis=-1, keepdims=True)
        probability = (exponent / row_total).astype(jnp.bfloat16)
        mixed_seq = jnp.einsum(
            "hqk,khd->qhd", probability, value_rows, preferred_element_type=jnp.float32
        )
        return (mixed_seq, row_max + jnp.log(row_total))

    mixed, log_total = lax.map(attend_forward, (queries, all_a, all_b, lengths))
    mixed_low = mixed.astype(jnp.bfloat16).reshape(tokens, H * DH)
    attn_out = jnp.dot(mixed_low, w_out, preferred_element_type=jnp.float32)
    residual = x_flat + attn_out
    scale_two = inv_rms(residual)
    normed_two = residual * scale_two
    h_two = (normed_two * gain_ffn).astype(jnp.bfloat16)
    gate_pre = jnp.dot(h_two, w_gate, preferred_element_type=jnp.float32)
    upward = jnp.dot(h_two, w_up, preferred_element_type=jnp.float32)
    gate_sigmoid = jax.nn.sigmoid(gate_pre)
    silu_gate = gate_pre * gate_sigmoid
    hidden = (silu_gate * upward).astype(jnp.bfloat16)
    branch = jnp.dot(hidden, w_down, preferred_element_type=jnp.float32)
    block_out = (residual + branch).astype(jnp.bfloat16).reshape(inputs.shape)
    valid_mask = (local_pos[None, :] < lengths[:, None]).astype(jnp.bfloat16)
    grad_out = (cotangent * valid_mask[:, :, None]).reshape(tokens, model_width)
    grad_w_down = lax.dot_general(hidden, grad_out, rows_dims, preferred_element_type=jnp.float32)
    grad_hidden = lax.dot_general(grad_out, w_down, cols_dims, preferred_element_type=jnp.float32)
    grad_gate = (
        grad_hidden * upward * gate_sigmoid * (1.0 + gate_pre * (1.0 - gate_sigmoid))
    ).astype(jnp.bfloat16)
    grad_up = (grad_hidden * silu_gate).astype(jnp.bfloat16)
    grad_w_gate = lax.dot_general(h_two, grad_gate, rows_dims, preferred_element_type=jnp.float32)
    grad_w_up = lax.dot_general(h_two, grad_up, rows_dims, preferred_element_type=jnp.float32)
    grad_h_two = lax.dot_general(
        grad_gate, w_gate, cols_dims, preferred_element_type=jnp.float32
    ) + lax.dot_general(grad_up, w_up, cols_dims, preferred_element_type=jnp.float32)
    grad_gain_ffn = jnp.sum(grad_h_two * normed_two, axis=0)
    grad_normed_two = grad_h_two * gain_ffn
    grad_resid = grad_out.astype(jnp.float32) + scale_two * (
        grad_normed_two
        - normed_two * jnp.mean(grad_normed_two * normed_two, axis=-1, keepdims=True)
    )
    grad_branch = grad_resid.astype(jnp.bfloat16)
    grad_w_out = lax.dot_general(
        mixed_low, grad_branch, rows_dims, preferred_element_type=jnp.float32
    )
    grad_mixed = lax.dot_general(grad_branch, w_out, cols_dims, preferred_element_type=jnp.float32)
    grad_mixed = grad_mixed.astype(jnp.bfloat16).reshape(seqs_here, local_len, H, DH)
    back_a, back_b = (
        lax.all_gather(kv_a, "ctx", axis=1, tiled=True),
        lax.all_gather(kv_b, "ctx", axis=1, tiled=True),
    )

    def attend_backward(row_item):
        query_seq, grad_seq, log_seq, flat_a, flat_b, seq_len = row_item
        key_rows, value_rows, factor_a, factor_b = expand(flat_a, flat_b)
        scores = (
            jnp.einsum("qhd,khd->hqk", query_seq, key_rows, preferred_element_type=jnp.float32)
            * score_scale
        )
        scores = jnp.where(allowed_for(seq_len)[None], scores, -1e30)
        probability = jnp.exp(scores - log_seq)
        grad_probs = jnp.einsum(
            "qhd,khd->hqk", grad_seq, value_rows, preferred_element_type=jnp.float32
        )
        inner_sum = jnp.sum(probability * grad_probs, axis=-1, keepdims=True)
        grad_scores = (probability * (grad_probs - inner_sum)).astype(jnp.bfloat16)
        grad_query = (
            jnp.einsum("hqk,khd->qhd", grad_scores, key_rows, preferred_element_type=jnp.float32)
            * score_scale
        )
        grad_keys = (
            jnp.einsum("hqk,qhd->khd", grad_scores, query_seq, preferred_element_type=jnp.float32)
            * score_scale
        )
        grad_values = jnp.einsum(
            "hqk,qhd->khd",
            probability.astype(jnp.bfloat16),
            grad_seq,
            preferred_element_type=jnp.float32,
        )
        wide_a = factor_a.astype(jnp.float32)
        wide_b = factor_b.astype(jnp.float32)
        grad_key_a = jnp.einsum("thd,tsd->tsh", grad_keys, wide_b[:, :RK], precision=highest) / RK
        grad_key_b = jnp.einsum("thd,tsh->tsd", grad_keys, wide_a[:, :RK], precision=highest) / RK
        grad_value_a = (
            jnp.einsum("thd,tsd->tsh", grad_values, wide_b[:, RK:], precision=highest) / RK
        )
        grad_value_b = (
            jnp.einsum("thd,tsh->tsd", grad_values, wide_a[:, RK:], precision=highest) / RK
        )
        grad_flat_a = jnp.concatenate([grad_key_a, grad_value_a], axis=1).reshape(-1)
        grad_flat_b = jnp.concatenate([grad_key_b, grad_value_b], axis=1).reshape(-1)
        return (grad_query, grad_flat_a, grad_flat_b)

    grad_queries, grad_all_a, grad_all_b = lax.map(
        attend_backward, (queries, grad_mixed, log_total, back_a, back_b, lengths)
    )
    owned_a, owned_b = (
        lax.psum_scatter(grad_all_a, "ctx", scatter_dimension=1, tiled=True),
        lax.psum_scatter(grad_all_b, "ctx", scatter_dimension=1, tiled=True),
    )
    owned_b = owned_b.reshape(seqs_here, local_len, 2 * RK, DH)
    grad_kv_b = jnp.concatenate(
        [rotate_back(owned_b[:, :, :RK], cosine, sine), owned_b[:, :, RK:]], axis=2
    )
    grad_query_a = jnp.einsum("slhd,slrd->slrh", grad_queries, query_b, precision=highest) / RQ
    grad_query_b = rotate_back(
        jnp.einsum("slhd,slrh->slrd", grad_queries, query_a, precision=highest) / RQ, cosine, sine
    )
    grad_factors = jnp.concatenate(
        [
            grad_query_a.reshape(tokens, RQ * H),
            grad_query_b.reshape(tokens, RQ * DH),
            owned_a.reshape(tokens, 2 * RK * H),
            grad_kv_b.reshape(tokens, 2 * RK * DH),
        ],
        axis=1,
    ).astype(jnp.bfloat16)
    grad_w_fact = lax.dot_general(
        h_one, grad_factors, rows_dims, preferred_element_type=jnp.float32
    )
    grad_h_one = lax.dot_general(
        grad_factors, w_fact, cols_dims, preferred_element_type=jnp.float32
    )
    grad_gain_attn = jnp.sum(grad_h_one * normed_one, axis=0)
    grad_normed_one = grad_h_one * gain_attn
    grad_inputs = grad_resid + scale_one * (
        grad_normed_one
        - normed_one * jnp.mean(grad_normed_one * normed_one, axis=-1, keepdims=True)
    )
    gain_sums = lax.psum((grad_gain_attn, grad_gain_ffn), ("row", "ctx"))
    section_one = (
        lax.psum_scatter(grad_w_fact, "ctx", scatter_dimension=0, tiled=True),
        lax.psum_scatter(grad_w_out, "ctx", scatter_dimension=0, tiled=True),
        lax.psum_scatter(grad_w_gate, "ctx", scatter_dimension=0, tiled=True),
        lax.psum_scatter(grad_w_up, "ctx", scatter_dimension=0, tiled=True),
        lax.psum_scatter(grad_w_down, "ctx", scatter_dimension=0, tiled=True),
    )
    section_two = (
        lax.psum_scatter(
            section_one[0].astype(jnp.bfloat16), "row", scatter_dimension=1, tiled=True
        ).astype(jnp.float32),
        lax.psum_scatter(
            section_one[1].astype(jnp.bfloat16), "row", scatter_dimension=1, tiled=True
        ).astype(jnp.float32),
        lax.psum_scatter(
            section_one[2].astype(jnp.bfloat16), "row", scatter_dimension=1, tiled=True
        ).astype(jnp.float32),
        lax.psum_scatter(
            section_one[3].astype(jnp.bfloat16), "row", scatter_dimension=1, tiled=True
        ).astype(jnp.float32),
        lax.psum_scatter(
            section_one[4].astype(jnp.bfloat16), "row", scatter_dimension=1, tiled=True
        ).astype(jnp.float32),
    )
    return (
        block_out,
        grad_inputs.reshape(inputs.shape),
        gain_sums[0],
        section_two[0],
        section_two[1],
        gain_sums[1],
        section_two[2],
        section_two[3],
        section_two[4],
    )


def solution(mesh):
    placed = (
        P("row", "ctx", None),
        P("row"),
        P(),
        P(),
        P(),
        P(),
        P(),
        P(),
        P(),
        P("row", "ctx", None),
    )
    return jax.shard_map(
        body,
        mesh=mesh,
        in_specs=placed,
        out_specs=(
            P("row", "ctx", None),
            P("row", "ctx", None),
            P(),
            P("ctx", "row"),
            P("ctx", "row"),
            P(),
            P("ctx", "row"),
            P("ctx", "row"),
            P("ctx", "row"),
        ),
        check_vma=False,
    )
```

profile of v0, /device:TPU:3, one launch (start us, length us, event | category | flops | bytes accessed | tf_op | source)
XLA Modules:
  0.0 2407.9 jit_solution(1714052851788649499)
XLA Ops:
  12.5 14.9 all_gather.8
  31.4 18.2 all_gather.9
  49.6 12.7 reduce.1
  89.7 7.3 copy.140
  134.5 7.2 fusion.6
  153.4 8.2 copy.148
  161.7 9.8 convolution_multiply_fusion.3
  171.4 8.0 copy.149
  179.5 9.2 convolution_multiply_fusion.2
  189.9 21.0 broadcast_in_dim.82
  217.7 7.7 convolution_multiply_fusion
  226.5 135.8 %broadcast_in_dim.83 = f32[1,262144]{0,1:T(8,128)} reshape(f32[1024,4,64]{2,1,0:T(4,128)S(1)} %pad_maximum_fusion.1) | data formatting | bytes 2097152 | tf_op jit(solution)/shard_map/while/body/jit(dynamic_update_index_in_dim)/broadcast_in_dim | solution.py:220
  379.5 155.9 %reduce-scatter.37.cloned.1.call-done = f32[8192,1]{1,0:T(8,128)} async-done(((f32[65536,1]{1,0:T(8,128)}), f32[8192,1]{1,0:T(8,128)}) %reduce-scatter.37.cloned.1.call-update) | async-done | bytes 32784
  538.6 1267.0 %reduce-scatter.39.cloned.1.call-done = f32[32768,1]{1,0:T(8,128)} async-done(((f32[262144,1]{1,0:T(8,128)}), f32[32768,1]{1,0:T(8,128)}) %reduce-scatter.39.cloned.1.call-update) | async-done | bytes 131088
  1805.7 8.2 bitcast_reduce_fusion
  1837.3 19.0 reduce-scatter.25.cloned.1.call-done
  1858.2 39.9 %reduce-scatter.23.cloned.1.call-done = f32[128,800]{0,1:T(8,128)} async-done(((f32[1024,800]{0,1:T(8,128)}), f32[128,800]{0,1:T(8,128)}) %reduce-scatter.23.cloned.1.call-update) | async-done | bytes 409616 | tf_op jit(solution)/shard_map/reduce_scatter | solution.py:258
  1899.8 118.7 %reduce-scatter.31.cloned.1.call-done = f32[128,2816]{1,0:T(8,128)} async-done(((f32[1024,2816]{1,0:T(8,128)}), f32[128,2816]{1,0:T(8,128)}) %reduce-scatter.31.cloned.1.call-update) | async-done | bytes 1441808 | tf_op jit(solution)/shard_map/reduce_scatter | solution.py:261
  2021.1 117.3 %reduce-scatter.29.cloned.1.call-done = f32[128,2816]{1,0:T(8,128)} async-done(((f32[1024,2816]{1,0:T(8,128)}), f32[128,2816]{1,0:T(8,128)}) %reduce-scatter.29.cloned.1.call-update) | async-done | bytes 1441808 | tf_op jit(solution)/shard_map/reduce_scatter | solution.py:260
  2141.1 117.5 %reduce-scatter.33.cloned.1.call-done = f32[352,1024]{1,0:T(8,128)} async-done(((f32[2816,1024]{1,0:T(8,128)}), f32[352,1024]{1,0:T(8,128)}) %reduce-scatter.33.cloned.1.call-update) | async-done | bytes 1441808 | tf_op jit(solution)/shard_map/reduce_scatter | solution.py:262
  2268.2 39.7 %all-reduce.1 = (f32[1024]{0:T(1024)}, f32[1024]{0:T(1024)}) all-reduce(f32[1024]{0:T(1024)} %get-tuple-element.119, f32[1024]{0:T(1024)S(1)} %copy-done.42), channel_id=1, replica_groups=mesh['row'=4,'ctx'=8] {'row','ctx'}, use_global_device_ids=true, to_apply=%region_10.11 | all-reduce | flops 2048 | bytes 16384 | tf_op jit(solution)/shard_map/psum | solution.py:256
  2314.1 27.5 %reduce-scatter.43.cloned.1.call-done = bf16[704,128]{1,0:T(8,128)(2,1)} async-done(((bf16[2816,128]{1,0:T(8,128)(2,1)}), bf16[704,128]{1,0:T(8,128)(2,1)}) %reduce-scatter.43.cloned.1.call-update) | async-done | bytes 180240
  2343.5 27.0 %reduce-scatter.41.cloned.1.call-done = bf16[704,128]{1,0:T(8,128)(2,1)} async-done(((bf16[2816,128]{1,0:T(8,128)(2,1)}), bf16[704,128]{1,0:T(8,128)(2,1)}) %reduce-scatter.41.cloned.1.call-update) | async-done | bytes 180240
  2372.4 26.5 %reduce-scatter.35.cloned.1.call-done = bf16[352,256]{1,0:T(8,128)(2,1)} async-done(((bf16[352,1024]{1,0:T(8,128)(2,1)}), bf16[352,256]{1,0:T(8,128)(2,1)}) %reduce-scatter.35.cloned.1.call-update) | async-done | bytes 180240 | tf_op jit(solution)/shard_map/reduce_scatter | solution.py:277
  (243 shorter events, 167.5 us)
Async XLA Ops:
  7.2 110.7 %copy-start = (bf16[1024,1024]{1,0:T(8,128)(2,1)S(1)}, bf16[1024,1024]{1,0:T(8,128)(2,1)}, u32[]{:S(2)}) copy-start(bf16[1024,1024]{1,0:T(8,128)(2,1)} %param.14) | copy-start | bytes 6291460
  7.2 528.3 %reduce-scatter.37.cloned.1.call-start = ((), (), s32[]{:S(2)}) async-start(), calls=%async_computation.19 | async-start | bytes 37748736
  11.1 69.9 %copy-start.32 = (f32[128,32]{1,0:T(8,128)}, f32[128,32]{1,0:T(8,128)S(1)}, u32[]{:S(2)}) copy-start(f32[128,32]{1,0:T(8,128)S(1)} %copy.135) | copy-start | bytes 49156
  11.2 69.7 %copy-start.34 = (f32[128,32]{1,0:T(8,128)}, f32[128,32]{1,0:T(8,128)S(1)}, u32[]{:S(2)}) copy-start(f32[128,32]{1,0:T(8,128)S(1)} %copy.137) | copy-start | bytes 49156
  75.4 57.1 %copy-start.45 = (bf16[128]{0:T(256)(128)(2,1)}, bf16[128]{0:T(256)(128)(2,1)S(1)}, u32[]{:S(2)}) copy-start(bf16[128]{0:T(256)(128)(2,1)S(1)} %compare_convert_fusion) | copy-start | bytes 772
  118.4 14.0 copy-start.7
  210.9 1594.8 %reduce-scatter.39.cloned.1.call-start = ((), (), s32[]{:S(2)}) async-start(), calls=%async_computation.20 | async-start | bytes 150994944
  362.4 1493.9 %reduce-scatter.25.cloned.1.call-start = ((), (), s32[]{:S(2)}) async-start(), calls=%async_computation.13 | async-start | bytes 4718592 | tf_op jit(solution)/shard_map/reduce_scatter | solution.py:259
  366.2 1531.9 %reduce-scatter.23.cloned.1.call-start = ((), (), s32[]{:S(2)}) async-start(), calls=%async_computation.12 | async-start | bytes 3686400 | tf_op jit(solution)/shard_map/reduce_scatter | solution.py:258
  538.6 1276.0 %copy-start.37 = (f32[128,32]{0,1:T(8,128)S(1)}, f32[128,32]{0,1:T(8,128)}, u32[]{:S(2)}) copy-start(f32[128,32]{0,1:T(8,128)} %copy-done.36) | copy-start | bytes 49156
  538.6 1276.0 %copy-start.39 = (f32[128,32]{0,1:T(8,128)S(1)}, f32[128,32]{0,1:T(8,128)}, u32[]{:S(2)}) copy-start(f32[128,32]{0,1:T(8,128)} %copy-done.38) | copy-start | bytes 49156
  538.6 1276.1 %copy-start.12 = (bf16[1,128,1024]{2,1,0:T(8,128)(2,1)S(1)}, bf16[1,128,1024]{2,1,0:T(8,128)(2,1)}, u32[]{:S(2)}) copy-start(bf16[1,128,1024]{2,1,0:T(8,128)(2,1)} %param.10) | copy-start | bytes 786436
  538.6 1276.1 %copy-start.40 = (f32[1024]{0:T(1024)S(1)}, f32[1024]{0:T(1024)}, u32[]{:S(2)}) copy-start(f32[1024]{0:T(1024)} %param.12) | copy-start | bytes 12292
  538.6 1276.1 %copy-start.44 = (f32[128]{0:T(128)S(1)}, f32[128]{0:T(128)}, u32[]{:S(2)}) copy-start(f32[128]{0:T(128)} %copy-done.43) | copy-start | bytes 1540
  1817.1 201.4 %reduce-scatter.31.cloned.1.call-start = ((), (), s32[]{:S(2)}) async-start(), calls=%async_computation.16 | async-start | bytes 12976128 | tf_op jit(solution)/shard_map/reduce_scatter | solution.py:261
  1823.1 315.3 %reduce-scatter.29.cloned.1.call-start = ((), (), s32[]{:S(2)}) async-start(), calls=%async_computation.15 | async-start | bytes 12976128 | tf_op jit(solution)/shard_map/reduce_scatter | solution.py:260
  1830.1 428.4 %reduce-scatter.33.cloned.1.call-start = ((), (), s32[]{:S(2)}) async-start(), calls=%async_computation.17 | async-start | bytes 12976128 | tf_op jit(solution)/shard_map/reduce_scatter | solution.py:262
  1837.3 472.9 %reduce-scatter.27.cloned.1.call-start = ((), (), s32[]{:S(2)}) async-start(), calls=%async_computation.14 | async-start | bytes 327680 | tf_op jit(solution)/shard_map/reduce_scatter | solution.py:268
  1858.1 454.5 %reduce-scatter.45.cloned.1.call-start = ((), (), s32[]{:S(2)}) async-start(), calls=%async_computation.23 | async-start | bytes 256000
  1899.8 441.8 %reduce-scatter.43.cloned.1.call-start = ((), (), s32[]{:S(2)}) async-start(), calls=%async_computation.22 | async-start | bytes 901120
  2021.1 239.9 %copy-start.8 = (f32[128,1024]{1,0:T(8,128)S(1)}, f32[128,1024]{1,0:T(8,128)}, u32[]{:S(2)}) copy-start(f32[128,1024]{1,0:T(8,128)} %copy-done.7) | copy-start | bytes 1572868
  2021.1 349.3 %reduce-scatter.41.cloned.1.call-start = ((), (), s32[]{:S(2)}) async-start(), calls=%async_computation.21 | async-start | bytes 901120
  2141.0 257.9 %reduce-scatter.35.cloned.1.call-start = ((), (), s32[]{:S(2)}) async-start(), calls=%async_computation.18 | async-start | bytes 901120 | tf_op jit(solution)/shard_map/reduce_scatter | solution.py:277
  2261.0 139.6 %copy-start.1 = (bf16[1024,1024]{1,0:T(8,128)(2,1)S(1)}, bf16[1024,1024]{1,0:T(8,128)(2,1)}, u32[]{:S(2)}) copy-start(bf16[1024,1024]{1,0:T(8,128)(2,1)} %param.14) | copy-start | bytes 6291460
  (43 other events, 183.1 us)
Sparse Core Ops, SparseCore 0:
  211.0 324.4 reduce-scatter.36
  537.9 1267.6 reduce-scatter.38
  1808.0 48.2 reduce-scatter.24
  1858.5 39.5 reduce-scatter.22
  1900.3 118.1 reduce-scatter.30
  2020.8 117.6 reduce-scatter.28
  2140.8 117.6 reduce-scatter.32
  2262.1 24.0 reduce-scatter.26
  2289.6 22.9 reduce-scatter.44
  2315.4 26.1 reduce-scatter.42
  2344.7 25.6 reduce-scatter.40
  2373.2 25.6 reduce-scatter.34
where the time goes:
time: 2410 us
  waiting for transfers between devices  1920 us (80%)
  local copies, waits for them, and re-layouts  232 us (10%)
  matrix products  129 us (5%)
  blocking collectives  72.8 us (3%)
  other arithmetic  39.4 us (2%)
    unnamed x17, waiting for transfers between devices  1480 us
    broadcast_in_dim x2, local copies, waits for them, and re-layouts, body(): lax.map(attend_backward, (queries, grad_mixed, log_total, back_a, back_b,...  157 us
    reduce_scatter x1, waiting for transfers between devices, body(): lax.psum_scatter(grad_w_up, 'ctx', scatter_dimension=0, tiled=True)  119 us
    reduce_scatter x1, waiting for transfers between devices, body(): lax.psum_scatter(grad_w_down, 'ctx', scatter_dimension=0, tiled=True)  117 us
    reduce_scatter x1, waiting for transfers between devices, body(): lax.psum_scatter(grad_w_gate, 'ctx', scatter_dimension=0, tiled=True)  117 us
  transfers between devices with their start and end apart: 12, of which 11 were waited for; matrix products, arithmetic and copies ran while one was open for 9% of the time, Pallas kernels for 0%

commit v1 on v0

v1 whole, which is shorter than its diff:
```python
import functools

import jax
import jax.numpy as jnp
from jax import lax
from jax.experimental import pallas as pl
from jax.experimental.pallas import tpu as pltpu
from jax.sharding import PartitionSpec as P

H = 16
DH = 64
RQ = 6
RK = 2
EPS = 1e-06
QA = RQ * H
QF = RQ * (H + DH)
KA = 2 * RK * H
KB = 2 * RK * DH
KF = KA + KB
SCALE = DH ** (-0.5)
F32 = jnp.float32
BF16 = jnp.bfloat16
VMEM_BYTES = 56 * 1024 * 1024

NN = (((1,), (0,)), ((), ()))
NT = (((1,), (1,)), ((), ()))


def mm(a, b, dims=NN):
    return lax.dot_general(a, b, dims, preferred_element_type=F32)


def vmem():
    return pl.BlockSpec(memory_space=pltpu.VMEM)


def smem():
    return pl.BlockSpec(memory_space=pltpu.SMEM)


def hbm():
    return pl.BlockSpec(memory_space=pl.ANY)


def call(kernel, outs, ins, args, scratch=(), flops=0, moved=0, name=None):
    return pl.pallas_call(
        kernel,
        out_shape=[jax.ShapeDtypeStruct(s, d) for s, d in outs],
        in_specs=ins,
        out_specs=[vmem() for _ in outs],
        scratch_shapes=list(scratch),
        compiler_params=pltpu.CompilerParams(vmem_limit_bytes=VMEM_BYTES),
        cost_estimate=pl.CostEstimate(flops=flops, transcendentals=0, bytes_accessed=moved),
        name=name,
    )(*args)


def slot_position(index, block_len, slots_all):
    block_id = index // (2 * block_len)
    within = index % (2 * block_len)
    return jnp.where(
        within < block_len,
        block_id * block_len + within,
        (slots_all // block_len - 1 - block_id) * block_len + within - block_len,
    )


def rope_angles(positions):
    frequency = jnp.exp(
        -jnp.log(10000.0) * (2.0 * jnp.arange(DH // 2, dtype=F32)) / DH
    )
    angles = frequency[:, None] * positions.astype(F32)[None, :]
    return jnp.cos(angles), jnp.sin(angles)


def turn(rows, cosine, sine):
    half = DH // 2
    upper, lower = rows[:half], rows[half:]
    return jnp.concatenate([upper * cosine - lower * sine, lower * cosine + upper * sine], axis=0)


def turn_back(rows, cosine, sine):
    half = DH // 2
    upper, lower = rows[:half], rows[half:]
    return jnp.concatenate([upper * cosine + lower * sine, lower * cosine - upper * sine], axis=0)


def swap(value, axis, k):
    size = lax.axis_size(axis)
    return lax.ppermute(value, axis, [(j, j ^ k) for j in range(size)])


def tree_sum(parts):
    parts = list(parts)
    while len(parts) > 1:
        parts = [parts[i] + parts[i + 1] for i in range(0, len(parts), 2)]
    return parts[0]


def factor_kernel(
    x_ref, cot_ref, valid_ref, gain_ref, wf_ref, cos_ref, sin_ref,
    hg_ref, s1_ref, q_ref, qt_ref, qf_ref, kv_ref, ft,
):
    width = x_ref.shape[1]
    x = x_ref[...].astype(F32)
    s1 = lax.rsqrt(jnp.mean(x * x, axis=1, keepdims=True) + EPS)
    s1_ref[...] = s1
    h1 = (x * s1 * gain_ref[...]).astype(BF16)
    hg_ref[:, :width] = h1
    hg_ref[:, width:] = (cot_ref[...].astype(F32) * valid_ref[...]).astype(BF16)
    ft[:wf_ref.shape[1], :] = mm(h1, wf_ref[...]).T
    cosine, sine = cos_ref[...], sin_ref[...]
    kv_ref[:KA, :] = ft[QF:QF + KA, :].astype(BF16)
    for r in range(2 * RK):
        rows = ft[QF + KA + r * DH:QF + KA + (r + 1) * DH, :]
        if r < RK:
            rows = turn(rows, cosine, sine)
        kv_ref[KA + r * DH:KA + (r + 1) * DH, :] = rows.astype(BF16)
    qf_ref[:QA, :] = ft[:QA, :]
    for r in range(RQ):
        qf_ref[QA + r * DH:QA + (r + 1) * DH, :] = turn(ft[QA + r * DH:QA + (r + 1) * DH, :], cosine, sine)
    for h in range(H):
        total = None
        for r in range(RQ):
            term = qf_ref[r * H + h:r * H + h + 1, :] * qf_ref[QA + r * DH:QA + (r + 1) * DH, :]
            total = term if total is None else total + term
        ft[h * DH:(h + 1) * DH, :] = total / RQ
    qt = ft[:H * DH, :]
    qt_ref[...] = qt.astype(BF16)
    q_ref[...] = qt.T.astype(BF16)


def project(x, cot, valid, gain, w_fact, cosine, sine):
    tokens, width = x.shape
    nf = w_fact.shape[1]
    return call(
        factor_kernel,
        [((tokens, 2 * width), BF16), ((tokens, 1), F32), ((tokens, H * DH), BF16), ((H * DH, tokens), BF16),
         ((QF, tokens), F32), ((KF, tokens), BF16)],
        [vmem()] * 7,
        (x, cot, valid, gain, w_fact, cosine, sine),
        [pltpu.VMEM((max(nf, H * DH), tokens), F32)],
        2 * tokens * width * nf, 2 * width * nf, "factors",
    )


def load_factors(pieces, a_rows, b_rows):
    at = 0
    for piece in pieces:
        n = piece.shape[1]
        a_rows[:, at:at + n] = piece[:KA, :].astype(F32)
        b_rows[:, at:at + n] = piece[KA:, :].astype(F32)
        at += n


def expand_pair(pair, side, a_rows, b_rows):
    halves = []
    for sub in range(2):
        total = None
        for r in range(RK):
            a = a_rows[pl.ds((side * RK + r) * H + 2 * pair + sub, 1), :]
            term = a * b_rows[(side * RK + r) * DH:(side * RK + r + 1) * DH, :]
            total = term if total is None else total + term
        halves.append((total * (1.0 / RK)).astype(BF16))
    return jnp.concatenate(halves, axis=0)


def stack_pair(rows):
    lane = lax.broadcasted_iota(jnp.int32, rows.shape, 1)
    zero = jnp.zeros_like(rows)
    return jnp.concatenate([jnp.where(lane < DH, rows, zero), jnp.where(lane < DH, zero, rows)], axis=0)


def pair_lanes(pair):
    return pl.ds(pl.multiple_of(pair * 2 * DH, 2 * DH), 2 * DH)


def attend_kernel(n_pieces, *refs):
    q_ref, bias_ref, wo_ref, x_ref, gain_ref = refs[:5]
    pieces = refs[5:5 + n_pieces]
    mh_ref, resid_ref, lse_ref, a_rows, b_rows, mixed = refs[5 + n_pieces:]
    tokens, width = x_ref.shape
    load_factors(pieces, a_rows, b_rows)
    bias = bias_ref[...]
    bias = jnp.concatenate([bias, bias], axis=0)

    def step(pair, carry):
        keys = expand_pair(pair, 0, a_rows, b_rows)
        values = expand_pair(pair, 1, a_rows, b_rows)
        q = stack_pair(q_ref[:, pair_lanes(pair)])
        scores = mm(q, keys) * SCALE + bias
        top = jnp.max(scores, axis=1, keepdims=True)
        exponent = jnp.exp(scores - top)
        total = jnp.sum(exponent, axis=1, keepdims=True)
        probs = (exponent * (1.0 / total)).astype(BF16)
        lse_ref[pair] = top + jnp.log(total)
        out = mm(probs, values, NT)
        lane = lax.broadcasted_iota(jnp.int32, (tokens, 2 * DH), 1)
        mixed[:, pair_lanes(pair)] = jnp.where(lane < DH, out[:tokens], out[tokens:]).astype(BF16)
        return carry

    lax.fori_loop(0, H // 2, step, 0)
    mh_ref[:, :width] = mixed[...]
    resid = x_ref[...].astype(F32) + mm(mixed[...], wo_ref[...])
    resid_ref[...] = resid
    s2 = lax.rsqrt(jnp.mean(resid * resid, axis=1, keepdims=True) + EPS)
    mh_ref[:, width:] = (resid * s2 * gain_ref[...]).astype(BF16)


def attend(q, bias, w_out, x, gain, pieces):
    tokens, width = x.shape
    slots = sum(p.shape[1] for p in pieces)
    return call(
        functools.partial(attend_kernel, len(pieces)),
        [((tokens, 2 * width), BF16), ((tokens, width), F32), ((H // 2, 2 * tokens, 1), F32)],
        [vmem()] * (5 + len(pieces)),
        (q, bias, w_out, x, gain, *pieces),
        [pltpu.VMEM((KA, slots), F32), pltpu.VMEM((KB, slots), F32), pltpu.VMEM((tokens, H * DH), BF16)],
        4 * tokens * slots * H * DH, 2 * width * width, "attend",
    )


def attend_back_kernel(n_pieces, *refs):
    q_ref, qt_ref, gm_ref, gmt_ref, lse_ref, bias_ref, qf_ref, cos_ref, sin_ref = refs[:9]
    pieces = refs[9:9 + n_pieces]
    gq_ref, gkv_ref, a_rows, b_rows, ga_rows, gb_rows, gqb_rows = refs[9 + n_pieces:]
    tokens = q_ref.shape[0]
    load_factors(pieces, a_rows, b_rows)
    gb_rows[...] = jnp.zeros_like(gb_rows)
    gqb_rows[...] = jnp.zeros_like(gqb_rows)

    def spread(rows):
        top = lax.broadcasted_iota(jnp.int32, rows.shape, 0) < DH
        zero = jnp.zeros_like(rows)
        return jnp.concatenate([jnp.where(top, rows, zero), jnp.where(top, zero, rows)], axis=1)

    def step(pair, carry):
        keys = expand_pair(pair, 0, a_rows, b_rows)
        values = expand_pair(pair, 1, a_rows, b_rows)
        rows = pl.ds(pl.multiple_of(pair * 2 * DH, 2 * DH), 2 * DH)
        both = (
            stack_pair(q_ref[:, pair_lanes(pair)]), stack_pair(gm_ref[:, pair_lanes(pair)]),
            spread(qt_ref[rows, :]), spread(gmt_ref[rows, :]), lse_ref[pair],
        )
        takes = [slice(0, 2 * tokens)] if keys.shape[1] <= 2048 else [slice(0, tokens), slice(tokens, 2 * tokens)]
        grad_q, grad_k, grad_v = [], None, None
        for take in takes:
            q, g, qt, gt, lse = both[0][take], both[1][take], both[2][:, take], both[3][:, take], both[4][take]
            heads = q.shape[0] // tokens
            scores = mm(q, keys) * SCALE + jnp.concatenate([bias_ref[...]] * heads, axis=0)
            probs = jnp.exp(scores - lse)
            grad_probs = mm(g, values)
            inner = jnp.sum(probs * grad_probs, axis=1, keepdims=True)
            grad_scores = (probs * (grad_probs - inner)).astype(BF16)
            grad_q.append(mm(keys, grad_scores, NT) * SCALE)
            gk, gv = mm(qt, grad_scores) * SCALE, mm(gt, probs.astype(BF16))
            grad_k, grad_v = (gk, gv) if grad_k is None else (grad_k + gk, grad_v + gv)
        grad_q = jnp.concatenate(grad_q, axis=1)
        for sub in range(2):
            head = 2 * pair + sub
            part = slice(sub * DH, (sub + 1) * DH)
            for side, grad in ((0, grad_k[part]), (1, grad_v[part])):
                for r in range(RK):
                    s = side * RK + r
                    row = pl.ds(s * H + head, 1)
                    seg = slice(s * DH, (s + 1) * DH)
                    ga_rows[row, :] = jnp.sum(grad * b_rows[seg, :], axis=0, keepdims=True) * (1.0 / RK)
                    gb_rows[seg, :] += grad * (a_rows[row, :] * (1.0 / RK))
            dq = grad_q[part, sub * tokens:(sub + 1) * tokens]
            for r in range(RQ):
                row = pl.ds(r * H + head, 1)
                seg = slice(QA + r * DH, QA + (r + 1) * DH)
                gq_ref[row, :] = jnp.sum(dq * qf_ref[seg, :], axis=0, keepdims=True) * (1.0 / RQ)
                gqb_rows[r * DH:(r + 1) * DH, :] += dq * (qf_ref[row, :] * (1.0 / RQ))
        return carry

    lax.fori_loop(0, H // 2, step, 0)
    cosine, sine = cos_ref[...], sin_ref[...]
    for r in range(RQ):
        gq_ref[QA + r * DH:QA + (r + 1) * DH, :] = turn_back(gqb_rows[r * DH:(r + 1) * DH, :], cosine, sine)
    at = 0
    for j in range(n_pieces):
        n = pieces[j].shape[1]
        m, k = j % 2, j // 2
        gkv_ref[m, k, :KA, :] = ga_rows[:, at:at + n].astype(BF16)
        gkv_ref[m, k, KA:, :] = gb_rows[:, at:at + n].astype(BF16)
        at += n


def attend_back(q, qt, gm, gmt, lse, bias, qf, cosine, sine, pieces):
    tokens = q.shape[0]
    slots = sum(p.shape[1] for p in pieces)
    n = len(pieces)
    return call(
        functools.partial(attend_back_kernel, n),
        [((QF, tokens), F32), ((2, n // 2, KF, slots // n), BF16)],
        [vmem()] * (9 + n),
        (q, qt, gm, gmt, lse, bias, qf, cosine, sine, *pieces),
        [pltpu.VMEM((KA, slots), F32), pltpu.VMEM((KB, slots), F32), pltpu.VMEM((KA, slots), F32),
         pltpu.VMEM((KB, slots), F32), pltpu.VMEM((RQ * DH, tokens), F32)],
        10 * tokens * slots * H * DH, 4 * tokens * slots, "attend_back",
    )


def ffn_kernel(
    place_ref, h2_ref, go_ref, wg_ref, wu_ref, wd_ref, resid_ref, gain_ref, wo_ref,
    out_ref, gain_grad_ref, gres_ref, gm_ref, gmt_ref, gbx_ref, branch, grad_h2, gb_rows,
):
    step = pl.program_id(0)

    @pl.when(step == 0)
    def _():
        branch[...] = jnp.zeros_like(branch)
        grad_h2[...] = jnp.zeros_like(grad_h2)

    h2, go = h2_ref[...], go_ref[...]
    gate, up = mm(h2, wg_ref[...]), mm(h2, wu_ref[...])
    grad_hidden = mm(go, wd_ref[...], NT)
    sig = jax.nn.sigmoid(gate)
    silu = gate * sig
    hidden = (silu * up).astype(BF16)
    grad_gate = (grad_hidden * up * sig * (1.0 + gate * (1.0 - sig))).astype(BF16)
    grad_up = (grad_hidden * silu).astype(BF16)
    branch[...] += mm(hidden, wd_ref[...])
    grad_h2[...] += mm(grad_gate, wg_ref[...], NT) + mm(grad_up, wu_ref[...], NT)

    @pl.when(step == pl.num_programs(0) - 1)
    def _():
        resid = resid_ref[...]
        out_ref[...] = (resid + branch[...]).astype(BF16)
        s2 = lax.rsqrt(jnp.mean(resid * resid, axis=1, keepdims=True) + EPS)
        n2 = resid * s2
        gh = grad_h2[...]
        gain_grad_ref[...] = jnp.sum(gh * n2, axis=0, keepdims=True)
        g2 = gh * gain_ref[...]
        gres = go_ref[...].astype(F32) + s2 * (g2 - n2 * jnp.mean(g2 * n2, axis=1, keepdims=True))
        gres_ref[...] = gres
        gb = gres.astype(BF16)
        gm = mm(gb, wo_ref[...], NT)
        gm_ref[...] = gm.astype(BF16)
        gmt_ref[...] = gm.T.astype(BF16)
        gb_rows[...] = gres.T.astype(BF16)
        n_rows, _, part, _ = gbx_ref.shape
        for k in range(n_rows):
            for m in range(2):
                block = (place_ref[0] ^ k) * 2 + (place_ref[1] ^ m)
                gbx_ref[k, m] = gb_rows[pl.ds(pl.multiple_of(block * part, part), part), :]


def feed_forward(place, mh, hg, w_gate, w_up, w_down, resid, gain, w_out, n_rows, chunk):
    tokens, width = resid.shape
    ff = w_gate.shape[1]
    part = width // (2 * n_rows)
    one = lambda j, p: (0, 0)
    second = lambda j, p: (0, 1)
    return pl.pallas_call(
        ffn_kernel,
        grid_spec=pltpu.PrefetchScalarGridSpec(
            num_scalar_prefetch=1,
            grid=(ff // chunk,),
            in_specs=[
                pl.BlockSpec((tokens, width), second),
                pl.BlockSpec((tokens, width), second),
                pl.BlockSpec((width, chunk), lambda j, p: (0, j)),
                pl.BlockSpec((width, chunk), lambda j, p: (0, j)),
                pl.BlockSpec((chunk, width), lambda j, p: (j, 0)),
                pl.BlockSpec((tokens, width), one),
                pl.BlockSpec((1, width), one),
                pl.BlockSpec((width, width), one),
            ],
            out_specs=[
                pl.BlockSpec((tokens, width), one),
                pl.BlockSpec((1, width), one),
                pl.BlockSpec((tokens, width), one),
                pl.BlockSpec((tokens, width), one),
                pl.BlockSpec((width, tokens), one),
                pl.BlockSpec((n_rows, 2, part, tokens), lambda j, p: (0, 0, 0, 0)),
            ],
            scratch_shapes=[
                pltpu.VMEM((tokens, width), F32),
                pltpu.VMEM((tokens, width), F32),
                pltpu.VMEM((width, tokens), BF16),
            ],
        ),
        out_shape=[
            jax.ShapeDtypeStruct((tokens, width), BF16),
            jax.ShapeDtypeStruct((1, width), F32),
            jax.ShapeDtypeStruct((tokens, width), F32),
            jax.ShapeDtypeStruct((tokens, width), BF16),
            jax.ShapeDtypeStruct((width, tokens), BF16),
            jax.ShapeDtypeStruct((n_rows, 2, part, tokens), BF16),
        ],
        compiler_params=pltpu.CompilerParams(vmem_limit_bytes=VMEM_BYTES),
        cost_estimate=pl.CostEstimate(
            flops=12 * tokens * width * ff, transcendentals=tokens * ff, bytes_accessed=6 * width * ff
        ),
        name="feed_forward",
    )(place, mh, hg, w_gate, w_up, w_down, resid, gain, w_out)


def weight_kernel(n_pieces, ordered, *refs):
    place_ref, wg_ref, wu_ref, wd_ref = refs[:4]
    mh_pieces = refs[4:4 + n_pieces]
    hg_pieces = refs[4 + n_pieces:4 + 2 * n_pieces]
    gb_pieces = refs[4 + 2 * n_pieces:4 + 2 * n_pieces + 2]
    up_ref, down_ref, h2s, gos, mixs, gbs, sems = refs[4 + 2 * n_pieces + 2:]
    tokens, width = mh_pieces[0].shape[0], h2s.shape[1]
    ff = wd_ref.shape[0]
    groups = []
    for s, (slab, pieces, col) in enumerate(((h2s, mh_pieces, 1), (gos, hg_pieces, 1), (mixs, mh_pieces, 0))):
        copies = []
        for j, piece in enumerate(pieces):
            copies.append(pltpu.make_async_copy(
                piece.at[:, pl.ds(col * width, width)], slab.at[pl.ds(j * tokens, tokens), :], sems.at[s, j]))
        groups.append(copies)
    for copies in groups:
        for copy in copies:
            copy.start()
    wgt = wg_ref[...].T
    wut = wu_ref[...].T
    for j in range(n_pieces):
        half = n_pieces // 2
        gbs[:, j * tokens:(j + 1) * tokens] = gb_pieces[j // half][j % half]
    for copy in groups[0]:
        copy.wait()
    gate = mm(wgt, h2s[...], NT)
    up = mm(wut, h2s[...], NT)
    for copy in groups[1]:
        copy.wait()
    grad_hidden = mm(wd_ref[...], gos[...], NT)
    sig = jax.nn.sigmoid(gate)
    silu = gate * sig
    hidden = (silu * up).astype(BF16)
    grad_gate = (grad_hidden * up * sig * (1.0 + gate * (1.0 - sig))).astype(BF16)
    grad_up = (grad_hidden * silu).astype(BF16)
    for copy in groups[2]:
        copy.wait()
    n_z = up_ref.shape[0]
    cols = width // n_z
    half = cols // 2
    for slot, k in enumerate(halving_order(n_z)):
        if ordered:
            z = place_ref[2] ^ k
            core = place_ref[1]
            first = pl.ds(pl.multiple_of(z * cols + core * half, half), half)
            other = pl.ds(pl.multiple_of(z * cols + (1 - core) * half, half), half)
            straight = pl.ds(pl.multiple_of(z * cols, cols), cols)
            pick = lambda slab: jnp.concatenate([slab[:, first], slab[:, other]], axis=1)
        else:
            straight = slice(slot * cols, (slot + 1) * cols)
            pick = lambda slab: slab[:, straight]
        h2c = pick(h2s)
        up_ref[slot, :ff, :] = mm(grad_gate, h2c).astype(BF16)
        up_ref[slot, ff:, :] = mm(grad_up, h2c).astype(BF16)
        down_ref[slot, :ff, :] = mm(hidden, gos[:, straight]).astype(BF16)
        down_ref[slot, ff:, :] = mm(gbs[...], pick(mixs)).astype(BF16)


def halving_order(n):
    order = [0]
    k = n // 2
    while k >= 1:
        order = order + [o | k for o in order]
        k //= 2
    return order


def halve(value, axis, unit, n):
    k = 1
    total = value.astype(F32)
    while n > 1:
        n //= 2
        got = swap(total[n:].astype(BF16), axis, unit * k)
        total = total[:n] + got.astype(F32)
        k *= 2
    return total[0]


def weight_grads(place, wg, wu, wd, mh_pieces, hg_pieces, gb_pieces, n_z, ordered):
    n = len(mh_pieces)
    tokens = mh_pieces[0].shape[0]
    width, ff = wg.shape
    part = gb_pieces[0].shape[1]
    cols = width // n_z
    total = n * tokens
    return call(
        functools.partial(weight_kernel, n, ordered),
        [((n_z, 2 * ff, cols), BF16), ((n_z, ff + part, cols), BF16)],
        [smem(), vmem(), vmem(), vmem()] + [hbm()] * (2 * n) + [vmem()] * 2,
        (place, wg, wu, wd, *mh_pieces, *hg_pieces, *gb_pieces),
        [pltpu.VMEM((total, width), BF16), pltpu.VMEM((total, width), BF16), pltpu.VMEM((total, width), BF16),
         pltpu.VMEM((part, total), BF16), pltpu.SemaphoreType.DMA((3, n))],
        12 * total * width * ff, 6 * width * ff + 6 * total * width, "weight_grads",
    )


def input_kernel(
    place_ref, gq_ref, own_ref, got_ref, wf_ref, x_ref, s1_ref, gain_ref, gres_ref, cos_ref, sin_ref,
    gfx_ref, gin_ref, gain_grad_ref, gf,
):
    cosine, sine = cos_ref[...], sin_ref[...]
    n_got = got_ref.shape[0]
    kv = own_ref[...].astype(F32)
    for k in range(n_got):
        kv = kv + got_ref[k].astype(F32)
    gf[:QF, :] = gq_ref[...]
    gf[QF:QF + KA, :] = kv[:KA]
    for r in range(2 * RK):
        rows = kv[KA + r * DH:KA + (r + 1) * DH]
        if r < RK:
            rows = turn_back(rows, cosine, sine)
        gf[QF + KA + r * DH:QF + KA + (r + 1) * DH, :] = rows
    n_rows, part, _ = gfx_ref.shape
    for k in range(n_rows):
        block = place_ref[0] ^ k
        gfx_ref[k] = gf[pl.ds(pl.multiple_of(block * part, 8), part), :].astype(BF16)
    grad = gf[...].T.astype(BF16)
    grad_h1 = mm(grad, wf_ref[...], NT)
    s1 = s1_ref[...]
    n1 = x_ref[...].astype(F32) * s1
    gain_grad_ref[...] = jnp.sum(grad_h1 * n1, axis=0, keepdims=True)
    g1 = grad_h1 * gain_ref[...]
    gin_ref[...] = gres_ref[...] + s1 * (g1 - n1 * jnp.mean(g1 * n1, axis=1, keepdims=True))


def input_grads(place, gq, own, got, w_fact, x, s1, gain, gres, cosine, sine, n_rows):
    tokens, width = x.shape
    nf = w_fact.shape[1]
    return call(
        input_kernel,
        [((n_rows, nf // n_rows, tokens), BF16), ((tokens, width), F32), ((1, width), F32)],
        [smem()] + [vmem()] * 10,
        (place, gq, own, got, w_fact, x, s1, gain, gres, cosine, sine),
        [pltpu.VMEM((nf, tokens), F32)],
        2 * tokens * width * nf, 2 * width * nf, "input_grads",
    )


def fact_kernel(n_pieces, ordered, *refs):
    place_ref = refs[0]
    hg_pieces = refs[1:1 + n_pieces]
    gf_pieces = refs[1 + n_pieces:1 + 2 * n_pieces]
    out_ref, h1s, gfs = refs[1 + 2 * n_pieces:]
    tokens = gf_pieces[0].shape[1]
    n_z, _, cols = out_ref.shape
    for j in range(n_pieces):
        gfs[:, j * tokens:(j + 1) * tokens] = gf_pieces[j][...]
        for k in range(n_z):
            if ordered:
                block = (place_ref[2] ^ k) * 2 + place_ref[1]
                where = pl.ds(pl.multiple_of(block * cols, cols), cols)
                h1s[j * tokens:(j + 1) * tokens, k * cols:(k + 1) * cols] = hg_pieces[j][:, where]
            else:
                h1s[j * tokens:(j + 1) * tokens, k * cols:(k + 1) * cols] = hg_pieces[j][:, k * cols:(k + 1) * cols]
    full = mm(gfs[...], h1s[...]).astype(BF16)
    for k in range(n_z):
        out_ref[k] = full[:, k * cols:(k + 1) * cols]


def fact_grads(place, hg_pieces, gf_pieces, n_z, cols, ordered):
    n = len(hg_pieces)
    part, tokens = gf_pieces[0].shape
    return call(
        functools.partial(fact_kernel, n, ordered),
        [((n_z, part, cols), BF16)],
        [smem()] + [vmem()] * (2 * n),
        (place, *hg_pieces, *gf_pieces),
        [pltpu.VMEM((n * tokens, n_z * cols), BF16), pltpu.VMEM((part, n * tokens), BF16)],
        2 * n * tokens * part * n_z * cols, 0, "fact_grads",
    )[0]


def body(inputs, lengths, gain_attn, w_fact, w_out, gain_ffn, w_gate, w_up, w_down, cotangent):
    seqs, local_len, width = inputs.shape
    tokens = seqs * local_len
    n_rows, n_ctx = lax.axis_size("row"), lax.axis_size("ctx")
    n_z = n_ctx // 2
    row, ctx = lax.axis_index("row"), lax.axis_index("ctx")
    z, core = ctx // 2, ctx % 2
    slots_all = local_len * n_ctx
    block_len = local_len // 2
    ff = w_gate.shape[1]
    ff_part = ff // (2 * n_rows)
    place = jnp.stack([row, core, z]).astype(jnp.int32)

    within = jnp.arange(local_len, dtype=jnp.int32)
    local_pos = jnp.tile(slot_position(ctx * local_len + within, block_len, slots_all), seqs)
    local_seq = jnp.repeat(jnp.arange(seqs, dtype=jnp.int32), local_len)
    cosine, sine = rope_angles(local_pos)
    valid = (local_pos < jnp.repeat(lengths, local_len)).astype(F32)[:, None]
    piece_of = jnp.arange(n_ctx, dtype=jnp.int32) ^ ctx
    key_pos = jnp.tile(
        slot_position(piece_of[:, None] * local_len + within[None, :], block_len, slots_all)[:, None, :], (1, seqs, 1)
    ).reshape(-1)
    key_seq = jnp.tile(local_seq, n_ctx)
    key_len = jnp.tile(jnp.repeat(lengths, local_len), n_ctx)
    allowed = (
        (key_pos[None, :] <= local_pos[:, None])
        & (key_pos < key_len)[None, :]
        & (key_seq[None, :] == local_seq[:, None])
    )
    bias = jnp.where(allowed, 0.0, -1e30).astype(F32)

    x = inputs.reshape(tokens, width)
    cot = cotangent.reshape(tokens, width)
    gain_one, gain_two = gain_attn[None, :], gain_ffn[None, :]

    hg, s1, q, qt, qf, kv = project(x, cot, valid, gain_one, w_fact, cosine, sine)

    z_kv = [kv] + [swap(kv, "ctx", 2 * k) for k in range(1, n_z)]
    kv_pieces = []
    for part in z_kv:
        kv_pieces += [part, swap(part, "ctx", 1)]

    def spread(value):
        same = [value] + [swap(value, "row", k) for k in range(1, n_rows)]
        return same + [swap(part, "ctx", 1) for part in same]

    hg_pieces = spread(hg)
    mh, resid, lse = attend(q, bias, w_out, x, gain_two, kv_pieces)
    mh_pieces = spread(mh)
    block_out, gain_two_part, gres, gm, gmt, gbx = feed_forward(
        place, mh, hg, w_gate, w_up, w_down, resid, gain_two, w_out, n_rows, 256
    )
    gb_same = [gbx[0]] + [swap(gbx[k], "row", k) for k in range(1, n_rows)]
    gb_own = jnp.stack([part[0] for part in gb_same])
    gb_other = swap(jnp.stack([part[1] for part in gb_same]), "ctx", 1)

    at = (row * 2 + core) * ff_part
    wg_part = lax.dynamic_slice(w_gate, (0, at), (width, ff_part))
    wu_part = lax.dynamic_slice(w_up, (0, at), (width, ff_part))
    wd_part = lax.dynamic_slice(w_down, (at, 0), (ff_part, width))
    per = n_ctx // (2 * n_rows)
    ordered = (width // n_ctx) % 128 == 0 and per == 1
    up_parts, down_parts = weight_grads(
        place, wg_part, wu_part, wd_part, mh_pieces, hg_pieces, (gb_own, gb_other), n_z, ordered
    )
    if not ordered:
        turns = jnp.asarray(halving_order(n_z), jnp.int32) ^ z
        cores = jnp.arange(2, dtype=jnp.int32) ^ core

        def own_first(parts):
            blocks = parts.reshape(n_z, parts.shape[1], 2, width // n_ctx)
            return jnp.take(blocks, cores, axis=2).reshape(parts.shape)

        up_parts = own_first(jnp.take(up_parts, turns, axis=0))
        out_parts = own_first(jnp.take(down_parts[:, ff_part:], turns, axis=0))
        down_parts = down_parts[:, :ff_part].transpose(1, 0, 2).reshape(per, ff_part // per, n_rows, width // n_rows)
        down_parts = jnp.take(down_parts.transpose(0, 2, 1, 3).reshape(n_z, ff_part // per, -1), turns, axis=0)

    gq, gkv = attend_back(q, qt, gm, gmt, lse, bias, qf, cosine, sine, kv_pieces)
    gkv_z = (gkv[0].astype(F32) + swap(gkv[1], "ctx", 1).astype(F32)).astype(BF16)
    got = jnp.stack([swap(gkv_z[k], "ctx", 2 * k) for k in range(1, n_z)])
    gfx, grad_inputs, gain_one_part = input_grads(
        place, gq, gkv_z[0], got, w_fact, x, s1, gain_one, gres, cosine, sine, n_rows
    )

    gains = jnp.concatenate([gain_one_part, gain_two_part], axis=0)
    gf_same = [gfx[0]] + [swap(gfx[k], "row", k) for k in range(1, n_rows)]
    gains = tree_sum([gains] + [swap(gains, "row", k) for k in range(1, n_rows)])
    gf_pieces = gf_same + [swap(part, "ctx", 1) for part in gf_same]
    gains = gains + swap(gains, "ctx", 1)
    fact_cols = width // n_ctx
    fact_parts = fact_grads(place, hg_pieces, gf_pieces, n_z if ordered else n_ctx, fact_cols, ordered)
    if not ordered:
        fact_parts = jnp.take(fact_parts, (jnp.arange(n_z, dtype=jnp.int32) ^ z) * 2 + core, axis=0)
    grad_fact = tree_sum(
        [fact_parts[0].astype(F32)] + [swap(fact_parts[k], "ctx", 2 * k).astype(F32) for k in range(1, n_z)]
    ).T
    gains = tree_sum([gains] + [swap(gains, "ctx", 2 * k) for k in range(1, n_z)])

    up_total = halve(up_parts, "ctx", 2, n_z)
    down_total = halve(down_parts, "ctx", 2, n_z)
    if ordered:
        down_total, out_total = down_total[:ff_part], down_total[ff_part:]
    else:
        out_total = halve(out_parts, "ctx", 2, n_z)
    half = width // n_ctx
    mine = jnp.concatenate([up_total[:, :half], out_total[:, :half]], axis=0)
    other = jnp.concatenate([up_total[:, half:], out_total[:, half:]], axis=0)
    other = swap(other.astype(BF16), "ctx", 1).astype(F32)
    first = jnp.where(core == 0, mine, other)
    second = jnp.where(core == 0, other, mine)

    def columns(lo, hi):
        return jnp.concatenate([first[lo:hi], second[lo:hi]], axis=0).T

    grad_gate = columns(0, ff_part)
    grad_up = columns(ff_part, 2 * ff_part)
    grad_out = columns(2 * ff_part, first.shape[0])

    moves = []
    for r in range(n_rows):
        for c in range(2):
            for p in range(n_z):
                b, s = p // n_rows, p % n_rows
                moves.append((r * n_ctx + 2 * p + c, s * n_ctx + (r * 2 + c) * per + b))
    grad_down = lax.ppermute(down_total.astype(BF16), ("row", "ctx"), moves).astype(F32)

    return (
        block_out.reshape(inputs.shape),
        grad_inputs.reshape(inputs.shape),
        gains[0],
        grad_fact,
        grad_out,
        gains[1],
        grad_gate,
        grad_up,
        grad_down,
    )


def solution(mesh):
    placed = (P("row", "ctx", None), P("row"), P(), P(), P(), P(), P(), P(), P(), P("row", "ctx", None))
    return jax.shard_map(
        body,
        mesh=mesh,
        in_specs=placed,
        out_specs=(
            P("row", "ctx", None), P("row", "ctx", None), P(), P("ctx", "row"), P("ctx", "row"), P(),
            P("ctx", "row"), P("ctx", "row"), P("ctx", "row"),
        ),
        check_vma=False,
    )
```

time: 2410 us -> 229 us (0.10)
  waiting for transfers between devices: 1920 us -> 62.8 us
  local copies, waits for them, and re-layouts: 232 us -> 17.8 us
  matrix products: 129 us -> 0 us
  blocking collectives: 72.8 us -> 0 us
  Pallas kernels: 0 us -> 65.9 us
  starting transfers between devices: 1.04 us -> 66.4 us
  other arithmetic: 39.4 us -> 11.3 us
    unnamed x17 -> x0, waiting for transfers between devices: 1480 us -> none
    reduce_scatter x7 -> x0, waiting for transfers between devices: 439 us -> none  [the longest x1 119 us: body(): lax.psum_scatter(grad_w_up, 'ctx', scatter_dimension=0, tiled=True)]
    broadcast_in_dim x2 -> x0, local copies, waits for them, and re-layouts: 157 us -> none  [body(): lax.map(attend_backward, (queries, grad_mixed, log_total, back_a, back_b,...]
    dot_general x30 -> x0, matrix products: 129 us -> none  [the longest x1 9.76 us: attend_backward(): jnp.einsum('thd,tsd->tsh', grad_keys, wide_b[:, :RK], precision=highest)]
    ppermute x0 -> x52, starting transfers between devices: none -> 66.4 us  [the longest x51 61.4 us: swap(): return lax.ppermute(value, axis, [(j, j ^ k) for j in range(size)])]
    pallas_call x0 -> x7, Pallas kernels: none -> 65.9 us  [the longest x6 46.9 us: call(): pl.pallas_call(kernel, out_shape=[jax.ShapeDtypeStruct(s, d) for s, d in...]
    ppermute x0 -> x52, waiting for transfers between devices: none -> 62.8 us  [the longest x51 62.8 us: swap(): return lax.ppermute(value, axis, [(j, j ^ k) for j in range(size)])]
    psum x1 -> x0, blocking collectives: 39.7 us -> none  [body(): gain_sums = lax.psum((grad_gain_attn, grad_gain_ffn), ('row', 'ctx'))]
  transfers between devices with their start and end apart: 12 -> 52, of which waited for: 11 -> 12; matrix products, arithmetic and copies ran while one was open for 9% -> 9% of each run, Pallas kernels for 0% -> 28%
where the time goes in v1:
time: 229 us; the launch traced here: 226 us
  starting transfers between devices  66.4 us (29%)
  Pallas kernels  65.9 us (29%)
  waiting for transfers between devices  62.8 us (27%)
  local copies, waits for them, and re-layouts  17.8 us (8%)
  other arithmetic  11.3 us (5%)
    ppermute x51, waiting for transfers between devices, swap(): return lax.ppermute(value, axis, [(j, j ^ k) for j in range(size)])  62.8 us
    ppermute x51, starting transfers between devices, swap(): return lax.ppermute(value, axis, [(j, j ^ k) for j in range(size)])  61.4 us
    pallas_call x6, Pallas kernels, call(): pl.pallas_call(kernel, out_shape=[jax.ShapeDtypeStruct(s, d) for s, d in...  46.9 us
    pallas_call x1, Pallas kernels, feed_forward(): pl.pallas_call(ffn_kernel, grid_spec=pltpu.PrefetchScalarGridSpec(num_sca...  19 us
    unnamed x58, local copies, waits for them, and re-layouts  6.36 us
    ppermute x1, starting transfers between devices, body(): lax.ppermute(down_total.astype(BF16), ('row', 'ctx'), moves).astype(F32)  5.03 us
  transfers between devices with their start and end apart: 52, of which 12 were waited for; matrix products, arithmetic and copies ran while one was open for 9% of the time, Pallas kernels for 28%

profile of v1, /device:TPU:3, one launch (start us, length us, event | category | flops | bytes accessed | tf_op | source)
XLA Modules:
  0.0 226.0 jit_solution(691368637024789565)
XLA Ops:
  2.1 3.7 %copy.19.wf_ref = bf16[1024,800]{1,0:T(8,128)(2,1)} copy(bf16[1024,800]{0,1:T(8,128)(2,1)} %param.13) | data formatting | bytes 3276800 | tf_op args[3]
  6.5 3.5 %factors.1 = (bf16[128,2048]{1,0:T(8,128)(2,1)}, f32[128,1]{1,0:T(8,128)}, bf16[128,1024]{1,0:T(8,128)(2,1)}, bf16[1024,128]{1,0:T(8,128)(2,1)}, f32[480,128]{1,0:T(8,128)}, /*index=5*/bf16[320,128]{1,0:T(8,128)(2,1)}) custom-call(bf16[128,1024]{1,0:T(8,128)(2,1)} %bitcast.110, bf16[128,1024]{1,0:T(8,128)(2,1)} %bitcast.113, f32[128,1]{1,0:T(8,128)} %fusion.10.valid_ref, ...), custom_call_target="tpu_custom_call" | custom-call | flops 209715200 | bytes 1638400 | tf_op jit(solution)/shard_map/factors/pallas_call | solution.py:46
  12.0 2.3 %collective-permute-start.3 = (bf16[320,128]{1,0:T(8,128)(2,1)}, bf16[320,128]{1,0:T(8,128)(2,1)S(1)}, u32[]{:S(2)}, u32[]{:S(2)}) collective-permute-start(bf16[320,128]{1,0:T(8,128)(2,1)} %get-tuple-element.32.refs_5_.refs_9_), channel_id=1, source_target_pairs={{0,4},{1,5},{2,6},{3,7},{4,0},{5,1},{6,2},{7,3},{8,12},{9,13},{10,... | collective-permute-start | bytes 245768 | tf_op jit(solution)/shard_map/ppermute | solution.py:90
  16.9 5.2 %collective-permute-start.4 = (bf16[320,128]{1,0:T(8,128)(2,1)S(1)}, bf16[320,128]{1,0:T(8,128)(2,1)S(1)}, u32[]{:S(2)}, u32[]{:S(2)}) collective-permute-start(bf16[320,128]{1,0:T(8,128)(2,1)S(1)} %collective-permute-done.3.refs_9_.refs_13_), channel_id=1, source_target_pairs={{0,1},{1,0},{2,3},{3,2},{4,5},{5,4},{6,7},{7,6},{8,9},{9,8},{10,11... | collective-permute-start | bytes 245768 | tf_op jit(solution)/shard_map/ppermute | solution.py:90
  24.8 11.8 %attend.1 = (bf16[128,2048]{1,0:T(8,128)(2,1)}, f32[128,1024]{1,0:T(8,128)}, f32[8,256,1]{2,1,0:T(8,128)}) custom-call(bf16[128,1024]{1,0:T(8,128)(2,1)} %get-tuple-element.31.refs_0_, f32[128,1024]{1,0:T(8,128)} %and_select_fusion.refs_1_.refs_5_, bf16[1024,1024]{1,0:T(8,128)(2,1)} %wo_ref.1, bf16[128,1024]{1,0:T(8,128)(2,1)} %bitcast.111, ...), custom_call_target="tpu_custom_call" | custom-call | flops 536870912 | bytes 2097152 | tf_op jit(solution)/shard_map/attend/pallas_call | solution.py:46
  36.6 19.0 %feed_forward.1 = (bf16[128,1024]{1,0:T(8,128)(2,1)}, f32[1,1024]{1,0:T(1,128)}, f32[128,1024]{1,0:T(8,128)}, bf16[128,1024]{1,0:T(8,128)(2,1)}, bf16[1024,128]{...) custom-call(s32[3]{0:T(128)} %pad_add_fusion.place_ref.refs_0_, bf16[128,2048]{1,0:T(8,128)(2,1)} %get-tuple-element.33.h2_ref.refs_4_, ...), custom_call_target="tpu_custom_call" | custom-call | flops 4429185024 | bytes 17301504 | tf_op jit(solution)/shard_map/feed_forward/pallas_call | solution.py:356
  55.6 13.7 %attend_back.1 = (f32[480,128]{1,0:T(8,128)}, bf16[2,4,320,128]{3,2,1,0:T(8,128)(2,1)}) custom-call(bf16[128,1024]{1,0:T(8,128)(2,1)} %get-tuple-element.31.refs_0_, bf16[1024,128]{1,0:T(8,128)(2,1)} %get-tuple-element.37.refs_1_, bf16[128,1024]{1,0:T(8,128)(2,1)} %get-tuple-element.38.refs_2_, bf16[1024,128]{1,0:T(8,128)(2,1)} %get-tuple-element.39.refs_3_, ...), custom_call_target="tpu_custom_call" | custom-call | flops 1342177280 | bytes 524288 | tf_op jit(solution)/shard_map/attend_back/pallas_call | solution.py:46
  74.0 2.4 %collective-permute-start.10 = (bf16[320,128]{1,0:T(8,128)(2,1)S(1)}, bf16[320,128]{1,0:T(8,128)(2,1)S(1)}, u32[]{:S(2)}, u32[]{:S(2)}) collective-permute-start(bf16[320,128]{1,0:T(8,128)(2,1)S(1)} %get-tuple-element.71), channel_id=1, source_target_pairs={{0,6},{1,7},{2,4},{3,5},{4,2},{5,3},{6,0},{7,1},{8,14},{9,15},{10,... | collective-permute-start | bytes 245768 | tf_op jit(solution)/shard_map/ppermute | solution.py:90
  80.8 3.1 %collective-permute-done.9 = bf16[320,128]{1,0:T(8,128)(2,1)S(1)} collective-permute-done((bf16[320,128]{1,0:T(8,128)(2,1)S(1)}, bf16[320,128]{1,0:T(8,128)(2,1)S(1)}, u32[]{:S(2)}, u32[]{:S(2)}) %collective-permute-start.9) | collective-permute-done | bytes 81952 | tf_op jit(solution)/shard_map/ppermute | solution.py:90
  86.1 3.7 %input_grads.1 = (bf16[4,200,128]{2,1,0:T(8,128)(2,1)}, f32[128,1024]{1,0:T(8,128)}, f32[1,1024]{1,0:T(1,128)}) custom-call(s32[3]{0:T(128)} %pad_add_fusion.place_ref.refs_0_, f32[480,128]{1,0:T(8,128)} %get-tuple-element.42.gq_ref, bf16[320,128]{1,0:T(8,128)(2,1)} %get-tuple-element.73.own_ref, bf16[3,320,128]{2,1,0:T(8,128)(2,1)} %pad_maximum_fusion.1.got_ref, ...), custom_call_target="tpu_custom_call" | custom-call | flops 209715200 | bytes 1638400 | tf_op jit(solution)/shard_map/input_grads/pallas_call | solution.py:46
  90.5 5.1 %collective-permute-done.43 = bf16[2,128,128]{2,1,0:T(8,128)(2,1)S(1)} collective-permute-done((bf16[2,128,128]{2,1,0:T(8,128)(2,1)S(1)}, bf16[2,128,128]{2,1,0:T(8,128)(2,1)S(1)}, u32[]{:S(2)}, u32[]{:S(2)}) %collective-permute-start.43) | collective-permute-done | bytes 65568 | tf_op jit(solution)/shard_map/ppermute | solution.py:90
  99.5 2.1 collective-permute-done.13
  101.8 2.2 collective-permute-done.11
  104.1 3.9 %collective-permute-start.45 = (bf16[4,128,128]{2,1,0:T(8,128)(2,1)S(1)}, bf16[4,128,128]{2,1,0:T(8,128)(2,1)S(1)}, u32[]{:S(2)}, u32[]{:S(2)}) collective-permute-start(bf16[4,128,128]{2,1,0:T(8,128)(2,1)S(1)} %pad_maximum_fusion.4), channel_id=1, source_target_pairs={{0,1},{1,0},{2,3},{3,2},{4,5},{5,4},{6,7},{7,6},{8,9},{9,8},{10,11... | collective-permute-start | bytes 393224 | tf_op jit(solution)/shard_map/ppermute | solution.py:90
  113.2 9.7 %collective-permute-done.35.refs_5_ = bf16[128,2048]{1,0:T(8,128)(2,1)} collective-permute-done((bf16[128,2048]{1,0:T(8,128)(2,1)S(1)}, bf16[128,2048]{1,0:T(8,128)(2,1)}, u32[]{:S(2)}, u32[]{:S(2)}) %collective-permute-start.35) | collective-permute-done | bytes 524320 | tf_op jit(solution)/shard_map/ppermute | solution.py:90
  124.4 10.9 %collective-permute-start.24 = (bf16[128,2048]{1,0:T(8,128)(2,1)S(1)}, bf16[128,2048]{1,0:T(8,128)(2,1)}, u32[]{:S(2)}, u32[]{:S(2)}) collective-permute-start(bf16[128,2048]{1,0:T(8,128)(2,1)S(1)} %collective-permute-done.20.refs_4_.refs_15_), channel_id=1, source_target_pairs={{0,1},{1,0},{2,3},{3,2},{4,5},{5,4},{6,7},{7,6},{8,9},{9,8},{10,11... | collective-permute-start | bytes 1572872 | tf_op jit(solution)/shard_map/ppermute | solution.py:90
  136.0 2.2 constant_dynamic-slice_fusion.refs_3_
  138.1 3.5 %constant_dynamic-slice_fusion.1 = (bf16[1024,352]{1,0:T(8,128)(2,1)}, bf16[1024,352]{1,0:T(8,128)(2,1)}) fusion(bf16[1024,2816]{1,0:T(8,128)(2,1)} %wu_ref.1, s32[]{:T(128)S(6)} %select_n.145, bf16[1024,2816]{1,0:T(8,128)(2,1)} %wg_ref.1), kind=kLoop, calls=%fused_computation.87 | loop fusion | bytes 2883588 | tf_op jit(solution)/shard_map/dynamic_slice | solution.py:631
  144.2 2.4 %collective-permute-start.17 = (f32[2,1024]{1,0:T(2,128)S(1)}, f32[2,1024]{1,0:T(2,128)S(1)}, u32[]{:S(2)}, u32[]{:S(2)}) collective-permute-start(f32[2,1024]{1,0:T(2,128)S(1)} %add.272), channel_id=1, source_target_pairs={{0,6},{1,7},{2,4},{3,5},{4,2},{5,3},{6,0},{7,1},{8,14},{9,15},{10,... | collective-permute-start | bytes 24584 | tf_op jit(solution)/shard_map/ppermute | solution.py:90
  146.9 10.6 %weight_grads.1 = (bf16[4,704,256]{2,1,0:T(8,128)(2,1)}, bf16[4,480,256]{2,1,0:T(8,128)(2,1)}) custom-call(s32[3]{0:T(128)} %pad_add_fusion.place_ref.refs_0_, bf16[1024,352]{1,0:T(8,128)(2,1)} %get-tuple-element.97.refs_1_, bf16[1024,352]{1,0:T(8,128)(2,1)} %get-tuple-element.96.refs_2_, bf16[352,1024]{1,0:T(8,128)(2,1)} %constant_dynamic-slice_fusion.refs_3_, ...), custom_call_target="tpu_custom_call" | custom-call | flops 4429185024 | bytes 8454144 | tf_op jit(solution)/shard_map/weight_grads/pallas_call | solution.py:46
  169.4 3.6 %fact_grads.1 = bf16[4,200,128]{2,1,0:T(8,128)(2,1)} custom-call(s32[3]{0:T(128)} %pad_add_fusion.place_ref.refs_0_, bf16[128,2048]{1,0:T(8,128)(2,1)} %get-tuple-element.34.go_ref.refs_1_.refs_12_, bf16[128,2048]{1,0:T(8,128)(2,1)} %copy-done.3, bf16[128,2048]{1,0:T(8,128)(2,1)} %copy-done.4, bf16[128,2048]{1,0:T(8,128)(2,1)} %copy-done.5, ...), custom_call_target="tpu_custom_call" | custom-call | flops 209715200 | tf_op jit(solution)/shard_map/fact_grads/pallas_call | solution.py:46
  178.6 18.7 %collective-permute-done.46 = bf16[2,704,256]{2,1,0:T(8,128)(2,1)S(1)} collective-permute-done((bf16[2,704,256]{2,1,0:T(8,128)(2,1)S(1)}, bf16[2,704,256]{2,1,0:T(8,128)(2,1)S(1)}, u32[]{:S(2)}, u32[]{:S(2)}) %collective-permute-start.46) | collective-permute-done | bytes 720928 | tf_op jit(solution)/shard_map/ppermute | solution.py:90
  198.2 5.0 %collective-permute-start.51 = (bf16[352,256]{1,0:T(8,128)(2,1)S(1)}, bf16[352,256]{1,0:T(8,128)(2,1)S(1)}, u32[]{:S(2)}, u32[]{:S(2)}) collective-permute-start(bf16[352,256]{1,0:T(8,128)(2,1)S(1)} %fusion.2), channel_id=1, source_target_pairs={{0,0},{2,8},{4,16},{6,24},{1,1},{3,9},{5,17},{7,25},{8,2},{10,10},... | collective-permute-start | bytes 540680 | tf_op jit(solution)/shard_map/ppermute | solution.py:698
  203.2 17.0 %collective-permute-done.47 = bf16[1,704,256]{2,1,0:T(8,128)(2,1)S(1)} collective-permute-done((bf16[1,704,256]{2,1,0:T(8,128)(2,1)S(1)}, bf16[1,704,256]{2,1,0:T(8,128)(2,1)S(1)}, u32[]{:S(2)}, u32[]{:S(2)}) %collective-permute-start.47) | collective-permute-done | bytes 360480 | tf_op jit(solution)/shard_map/ppermute | solution.py:90
  (199 shorter events, 58.7 us)
Async XLA Ops:
  14.3 95.0 %collective-permute-start.18 = (bf16[128,2048]{1,0:T(8,128)(2,1)}, bf16[128,2048]{1,0:T(8,128)(2,1)S(1)}, u32[]{:S(2)}, u32[]{:S(2)}) collective-permute-start(bf16[128,2048]{1,0:T(8,128)(2,1)} %get-tuple-element.34.go_ref.refs_1_.refs_12_), channel_id=1, source_target_pairs={{0,8},{8,0},{16,24},{24,16},{1,9},{9,1},{17,25},{25,17},{2,10},{10... | collective-permute-start | bytes 1572872 | tf_op jit(solution)/shard_map/ppermute | solution.py:90
  22.8 86.8 %collective-permute-start.19 = (bf16[128,2048]{1,0:T(8,128)(2,1)}, bf16[128,2048]{1,0:T(8,128)(2,1)S(1)}, u32[]{:S(2)}, u32[]{:S(2)}) collective-permute-start(bf16[128,2048]{1,0:T(8,128)(2,1)} %get-tuple-element.34.go_ref.refs_1_.refs_12_), channel_id=1, source_target_pairs={{0,16},{8,24},{16,0},{24,8},{1,17},{9,25},{17,1},{25,9},{2,18},{10... | collective-permute-start | bytes 1572872 | tf_op jit(solution)/shard_map/ppermute | solution.py:90
  79.5 31.5 %collective-permute-start.20 = (bf16[128,2048]{1,0:T(8,128)(2,1)S(1)}, bf16[128,2048]{1,0:T(8,128)(2,1)S(1)}, u32[]{:S(2)}, u32[]{:S(2)}) collective-permute-start(bf16[128,2048]{1,0:T(8,128)(2,1)S(1)} %copy-done), channel_id=1, source_target_pairs={{0,24},{8,16},{16,8},{24,0},{1,25},{9,17},{17,9},{25,1},{2,26},{10... | collective-permute-start | bytes 1572872 | tf_op jit(solution)/shard_map/ppermute | solution.py:90
  96.0 16.0 %collective-permute-start.21 = (bf16[128,2048]{1,0:T(8,128)(2,1)S(1)}, bf16[128,2048]{1,0:T(8,128)(2,1)S(1)}, u32[]{:S(2)}, u32[]{:S(2)}) collective-permute-start(bf16[128,2048]{1,0:T(8,128)(2,1)S(1)} %copy-done), channel_id=1, source_target_pairs={{0,1},{1,0},{2,3},{3,2},{4,5},{5,4},{6,7},{7,6},{8,9},{9,8},{10,11... | collective-permute-start | bytes 1572872 | tf_op jit(solution)/shard_map/ppermute | solution.py:90
  109.4 13.5 %collective-permute-start.35 = (bf16[128,2048]{1,0:T(8,128)(2,1)S(1)}, bf16[128,2048]{1,0:T(8,128)(2,1)}, u32[]{:S(2)}, u32[]{:S(2)}) collective-permute-start(bf16[128,2048]{1,0:T(8,128)(2,1)S(1)} %copy-done.6), channel_id=1, source_target_pairs={{0,8},{8,0},{16,24},{24,16},{1,9},{9,1},{17,25},{25,17},{2,10},{10... | collective-permute-start | bytes 1572872 | tf_op jit(solution)/shard_map/ppermute | solution.py:90
  109.7 14.8 %collective-permute-start.36 = (bf16[128,2048]{1,0:T(8,128)(2,1)S(1)}, bf16[128,2048]{1,0:T(8,128)(2,1)}, u32[]{:S(2)}, u32[]{:S(2)}) collective-permute-start(bf16[128,2048]{1,0:T(8,128)(2,1)S(1)} %copy-done.6), channel_id=1, source_target_pairs={{0,16},{8,24},{16,0},{24,8},{1,17},{9,25},{17,1},{25,9},{2,18},{10... | collective-permute-start | bytes 1572872 | tf_op jit(solution)/shard_map/ppermute | solution.py:90
  111.0 24.3 %collective-permute-start.37 = (bf16[128,2048]{1,0:T(8,128)(2,1)S(1)}, bf16[128,2048]{1,0:T(8,128)(2,1)}, u32[]{:S(2)}, u32[]{:S(2)}) collective-permute-start(bf16[128,2048]{1,0:T(8,128)(2,1)S(1)} %copy-done.6), channel_id=1, source_target_pairs={{0,24},{8,16},{16,8},{24,0},{1,25},{9,17},{17,9},{25,1},{2,26},{10... | collective-permute-start | bytes 1572872 | tf_op jit(solution)/shard_map/ppermute | solution.py:90
  112.1 23.3 %collective-permute-start.38 = (bf16[128,2048]{1,0:T(8,128)(2,1)S(1)}, bf16[128,2048]{1,0:T(8,128)(2,1)}, u32[]{:S(2)}, u32[]{:S(2)}) collective-permute-start(bf16[128,2048]{1,0:T(8,128)(2,1)S(1)} %copy-done.6), channel_id=1, source_target_pairs={{0,1},{1,0},{2,3},{3,2},{4,5},{5,4},{6,7},{7,6},{8,9},{9,8},{10,11... | collective-permute-start | bytes 1572872 | tf_op jit(solution)/shard_map/ppermute | solution.py:90
  113.1 22.8 %collective-permute-start.22 = (bf16[128,2048]{1,0:T(8,128)(2,1)S(1)}, bf16[128,2048]{1,0:T(8,128)(2,1)S(1)}, u32[]{:S(2)}, u32[]{:S(2)}) collective-permute-start(bf16[128,2048]{1,0:T(8,128)(2,1)S(1)} %collective-permute-done.18.refs_2_.refs_13_), channel_id=1, source_target_pairs={{0,1},{1,0},{2,3},{3,2},{4,5},{5,4},{6,7},{7,6},{8,9},{9,8},{10,11... | collective-permute-start | bytes 1572872 | tf_op jit(solution)/shard_map/ppermute | solution.py:90
  122.9 19.5 %collective-permute-start.23 = (bf16[128,2048]{1,0:T(8,128)(2,1)S(1)}, bf16[128,2048]{1,0:T(8,128)(2,1)}, u32[]{:S(2)}, u32[]{:S(2)}) collective-permute-start(bf16[128,2048]{1,0:T(8,128)(2,1)S(1)} %collective-permute-done.19.refs_3_.refs_14_), channel_id=1, source_target_pairs={{0,1},{1,0},{2,3},{3,2},{4,5},{5,4},{6,7},{7,6},{8,9},{9,8},{10,11... | collective-permute-start | bytes 1572872 | tf_op jit(solution)/shard_map/ppermute | solution.py:90
  124.4 19.3 %collective-permute-start.24 = (bf16[128,2048]{1,0:T(8,128)(2,1)S(1)}, bf16[128,2048]{1,0:T(8,128)(2,1)}, u32[]{:S(2)}, u32[]{:S(2)}) collective-permute-start(bf16[128,2048]{1,0:T(8,128)(2,1)S(1)} %collective-permute-done.20.refs_4_.refs_15_), channel_id=1, source_target_pairs={{0,1},{1,0},{2,3},{3,2},{4,5},{5,4},{6,7},{7,6},{8,9},{9,8},{10,11... | collective-permute-start | bytes 1572872 | tf_op jit(solution)/shard_map/ppermute | solution.py:90
  142.4 20.3 %collective-permute-start.25 = (bf16[200,128]{1,0:T(8,128)(2,1)S(1)}, bf16[200,128]{1,0:T(8,128)(2,1)S(1)}, u32[]{:S(2)}, u32[]{:S(2)}) collective-permute-start(bf16[200,128]{1,0:T(8,128)(2,1)S(1)} %get-tuple-element.84), channel_id=1, source_target_pairs={{0,8},{8,0},{16,24},{24,16},{1,9},{9,1},{17,25},{25,17},{2,10},{10... | collective-permute-start | bytes 153608 | tf_op jit(solution)/shard_map/ppermute | solution.py:90
  143.7 19.4 %collective-permute-start.26 = (bf16[200,128]{1,0:T(8,128)(2,1)S(1)}, bf16[200,128]{1,0:T(8,128)(2,1)S(1)}, u32[]{:S(2)}, u32[]{:S(2)}) collective-permute-start(bf16[200,128]{1,0:T(8,128)(2,1)S(1)} %get-tuple-element.83), channel_id=1, source_target_pairs={{0,16},{8,24},{16,0},{24,8},{1,17},{9,25},{17,1},{25,9},{2,18},{10... | collective-permute-start | bytes 153608 | tf_op jit(solution)/shard_map/ppermute | solution.py:90
  144.1 14.5 %collective-permute-start.16 = (f32[2,1024]{1,0:T(2,128)S(1)}, f32[2,1024]{1,0:T(2,128)S(1)}, u32[]{:S(2)}, u32[]{:S(2)}) collective-permute-start(f32[2,1024]{1,0:T(2,128)S(1)} %add.272), channel_id=1, source_target_pairs={{0,4},{1,5},{2,6},{3,7},{4,0},{5,1},{6,2},{7,3},{8,12},{9,13},{10,... | collective-permute-start | bytes 24584 | tf_op jit(solution)/shard_map/ppermute | solution.py:90
  144.2 15.5 %collective-permute-start.17 = (f32[2,1024]{1,0:T(2,128)S(1)}, f32[2,1024]{1,0:T(2,128)S(1)}, u32[]{:S(2)}, u32[]{:S(2)}) collective-permute-start(f32[2,1024]{1,0:T(2,128)S(1)} %add.272), channel_id=1, source_target_pairs={{0,6},{1,7},{2,4},{3,5},{4,2},{5,3},{6,0},{7,1},{8,14},{9,15},{10,... | collective-permute-start | bytes 24584 | tf_op jit(solution)/shard_map/ppermute | solution.py:90
  146.6 15.0 %collective-permute-start.15 = (f32[2,1024]{1,0:T(2,128)S(1)}, f32[2,1024]{1,0:T(2,128)S(1)}, u32[]{:S(2)}, u32[]{:S(2)}) collective-permute-start(f32[2,1024]{1,0:T(2,128)S(1)} %add.272), channel_id=1, source_target_pairs={{0,2},{1,3},{2,0},{3,1},{4,6},{5,7},{6,4},{7,5},{8,10},{9,11},{10,... | collective-permute-start | bytes 24584 | tf_op jit(solution)/shard_map/ppermute | solution.py:90
  161.6 16.0 %collective-permute-start.48 = (bf16[2,480,256]{2,1,0:T(8,128)(2,1)S(1)}, bf16[2,480,256]{2,1,0:T(8,128)(2,1)S(1)}, u32[]{:S(2)}, u32[]{:S(2)}) collective-permute-start(bf16[2,480,256]{2,1,0:T(8,128)(2,1)S(1)} %slice.203), channel_id=1, source_target_pairs={{0,2},{1,3},{2,0},{3,1},{4,6},{5,7},{6,4},{7,5},{8,10},{9,11},{10,... | collective-permute-start | bytes 1474568 | tf_op jit(solution)/shard_map/ppermute | solution.py:90
  166.4 30.9 %collective-permute-start.46 = (bf16[2,704,256]{2,1,0:T(8,128)(2,1)S(1)}, bf16[2,704,256]{2,1,0:T(8,128)(2,1)S(1)}, u32[]{:S(2)}, u32[]{:S(2)}) collective-permute-start(bf16[2,704,256]{2,1,0:T(8,128)(2,1)S(1)} %slice.197), channel_id=1, source_target_pairs={{0,2},{1,3},{2,0},{3,1},{4,6},{5,7},{6,4},{7,5},{8,10},{9,11},{10,... | collective-permute-start | bytes 2162696 | tf_op jit(solution)/shard_map/ppermute | solution.py:90
  174.0 47.3 %collective-permute-start.34 = (bf16[200,128]{1,0:T(8,128)(2,1)S(1)}, bf16[200,128]{1,0:T(8,128)(2,1)S(1)}, u32[]{:S(2)}, u32[]{:S(2)}) collective-permute-start(bf16[200,128]{1,0:T(8,128)(2,1)S(1)} %get-tuple-element.80), channel_id=1, source_target_pairs={{0,6},{1,7},{2,4},{3,5},{4,2},{5,3},{6,0},{7,1},{8,14},{9,15},{10,... | collective-permute-start | bytes 153608 | tf_op jit(solution)/shard_map/ppermute | solution.py:90
  175.5 45.8 %collective-permute-start.33 = (bf16[200,128]{1,0:T(8,128)(2,1)S(1)}, bf16[200,128]{1,0:T(8,128)(2,1)S(1)}, u32[]{:S(2)}, u32[]{:S(2)}) collective-permute-start(bf16[200,128]{1,0:T(8,128)(2,1)S(1)} %get-tuple-element.81), channel_id=1, source_target_pairs={{0,4},{1,5},{2,6},{3,7},{4,0},{5,1},{6,2},{7,3},{8,12},{9,13},{10,... | collective-permute-start | bytes 153608 | tf_op jit(solution)/shard_map/ppermute | solution.py:90
  175.8 45.5 %collective-permute-start.32 = (bf16[200,128]{1,0:T(8,128)(2,1)S(1)}, bf16[200,128]{1,0:T(8,128)(2,1)S(1)}, u32[]{:S(2)}, u32[]{:S(2)}) collective-permute-start(bf16[200,128]{1,0:T(8,128)(2,1)S(1)} %get-tuple-element.79), channel_id=1, source_target_pairs={{0,2},{1,3},{2,0},{3,1},{4,6},{5,7},{6,4},{7,5},{8,10},{9,11},{10,... | collective-permute-start | bytes 153608 | tf_op jit(solution)/shard_map/ppermute | solution.py:90
  177.8 20.3 %collective-permute-start.49 = (bf16[1,480,256]{2,1,0:T(8,128)(2,1)S(1)}, bf16[1,480,256]{2,1,0:T(8,128)(2,1)S(1)}, u32[]{:S(2)}, u32[]{:S(2)}) collective-permute-start(bf16[1,480,256]{2,1,0:T(8,128)(2,1)S(1)} %slice.289), channel_id=1, source_target_pairs={{0,4},{1,5},{2,6},{3,7},{4,0},{5,1},{6,2},{7,3},{8,12},{9,13},{10,... | collective-permute-start | bytes 737288 | tf_op jit(solution)/shard_map/ppermute | solution.py:90
  197.5 22.8 %collective-permute-start.47 = (bf16[1,704,256]{2,1,0:T(8,128)(2,1)S(1)}, bf16[1,704,256]{2,1,0:T(8,128)(2,1)S(1)}, u32[]{:S(2)}, u32[]{:S(2)}) collective-permute-start(bf16[1,704,256]{2,1,0:T(8,128)(2,1)S(1)} %slice.288), channel_id=1, source_target_pairs={{0,4},{1,5},{2,6},{3,7},{4,0},{5,1},{6,2},{7,3},{8,12},{9,13},{10,... | collective-permute-start | bytes 1081352 | tf_op jit(solution)/shard_map/ppermute | solution.py:90
  198.2 24.5 %collective-permute-start.51 = (bf16[352,256]{1,0:T(8,128)(2,1)S(1)}, bf16[352,256]{1,0:T(8,128)(2,1)S(1)}, u32[]{:S(2)}, u32[]{:S(2)}) collective-permute-start(bf16[352,256]{1,0:T(8,128)(2,1)S(1)} %fusion.2), channel_id=1, source_target_pairs={{0,0},{2,8},{4,16},{6,24},{1,1},{3,9},{5,17},{7,25},{8,2},{10,10},... | collective-permute-start | bytes 540680 | tf_op jit(solution)/shard_map/ppermute | solution.py:698
  (56 other events, 487.2 us)

commit v2 on v1

v2 whole, which is shorter than its diff:
```python
import functools

import jax
import jax.numpy as jnp
from jax import lax
from jax.experimental import pallas as pl
from jax.experimental.pallas import tpu as pltpu
from jax.sharding import Mesh
from jax.sharding import PartitionSpec as P

H = 16
DH = 64
RQ = 6
RK = 2
EPS = 1e-06
QA = RQ * H
QF = RQ * (H + DH)
KA = 2 * RK * H
KB = 2 * RK * DH
KF = KA + KB
SCALE = DH ** (-0.5)
F32 = jnp.float32
BF16 = jnp.bfloat16
VMEM_BYTES = 56 * 1024 * 1024

NN = (((1,), (0,)), ((), ()))
NT = (((1,), (1,)), ((), ()))


def mm(a, b, dims=NN):
    return lax.dot_general(a, b, dims, preferred_element_type=F32)


def vmem():
    return pl.BlockSpec(memory_space=pltpu.VMEM)


def smem():
    return pl.BlockSpec(memory_space=pltpu.SMEM)


def hbm():
    return pl.BlockSpec(memory_space=pltpu.HBM)


def call(kernel, outs, ins, args, scratch=(), flops=0, moved=0, name=None):
    return pl.pallas_call(
        kernel,
        out_shape=[jax.ShapeDtypeStruct(s, d) for s, d in outs],
        in_specs=ins,
        out_specs=[vmem() for _ in outs],
        scratch_shapes=list(scratch),
        compiler_params=pltpu.CompilerParams(vmem_limit_bytes=VMEM_BYTES),
        cost_estimate=pl.CostEstimate(flops=flops, transcendentals=0, bytes_accessed=moved),
        name=name,
    )(*args)


def slot_position(index, block_len, slots_all):
    block_id = index // (2 * block_len)
    within = index % (2 * block_len)
    return jnp.where(
        within < block_len,
        block_id * block_len + within,
        (slots_all // block_len - 1 - block_id) * block_len + within - block_len,
    )


def turn(rows, cosine, sine):
    half = DH // 2
    upper, lower = rows[:half], rows[half:]
    return jnp.concatenate([upper * cosine - lower * sine, lower * cosine + upper * sine], axis=0)


def turn_back(rows, cosine, sine):
    half = DH // 2
    upper, lower = rows[:half], rows[half:]
    return jnp.concatenate([upper * cosine + lower * sine, lower * cosine - upper * sine], axis=0)


ROW = ("r1", "r0")
CTX = ("z", "core")
GROUP = ("r1", "r0", "core")


def swap(value, axis, k):
    size = lax.axis_size(axis)
    return lax.ppermute(value, axis, [(j, j ^ k) for j in range(size)])


def tree_sum(parts):
    parts = list(parts)
    while len(parts) > 1:
        parts = [parts[i] + parts[i + 1] for i in range(0, len(parts), 2)]
    return parts[0]


def factor_kernel(
    x_ref, cot_ref, valid_ref, gain_ref, wft_ref, pos_ref,
    hg_ref, s1_ref, q_ref, qt_ref, qf_ref, kv_ref, cos_ref, sin_ref, ft,
):
    x = x_ref[...].astype(F32)
    s1 = lax.rsqrt(jnp.mean(x * x, axis=1, keepdims=True) + EPS)
    s1_ref[...] = s1
    h1 = (x * s1 * gain_ref[...]).astype(BF16)
    hg_ref[:, :x.shape[1]] = h1
    hg_ref[:, x.shape[1]:] = (cot_ref[...].astype(F32) * valid_ref[...]).astype(BF16)
    half = lax.broadcasted_iota(jnp.int32, cos_ref.shape, 0).astype(F32)
    angles = pos_ref[...] * jnp.exp(-jnp.log(10000.0) * (2.0 * half) / DH)
    cosine, sine = jnp.cos(angles), jnp.sin(angles)
    cos_ref[...] = cosine
    sin_ref[...] = sine
    ft[:wft_ref.shape[0], :] = mm(wft_ref[...], h1, NT)
    kv_ref[:KA, :] = ft[QF:QF + KA, :].astype(BF16)
    for r in range(2 * RK):
        rows = ft[QF + KA + r * DH:QF + KA + (r + 1) * DH, :]
        if r < RK:
            rows = turn(rows, cosine, sine)
        kv_ref[KA + r * DH:KA + (r + 1) * DH, :] = rows.astype(BF16)
    qf_ref[:QA, :] = ft[:QA, :]
    for r in range(RQ):
        qf_ref[QA + r * DH:QA + (r + 1) * DH, :] = turn(ft[QA + r * DH:QA + (r + 1) * DH, :], cosine, sine)
    for h in range(H):
        total = None
        for r in range(RQ):
            term = qf_ref[r * H + h:r * H + h + 1, :] * qf_ref[QA + r * DH:QA + (r + 1) * DH, :]
            total = term if total is None else total + term
        ft[h * DH:(h + 1) * DH, :] = total / RQ
    qt = ft[:H * DH, :]
    qt_ref[...] = qt.astype(BF16)
    q_ref[...] = qt.T.astype(BF16)


def project(x, cot, valid, gain, w_fact_t, pos):
    tokens, width = x.shape
    nf = w_fact_t.shape[0]
    angles = ((DH // 2, tokens), F32)
    return call(
        factor_kernel,
        [((tokens, 2 * width), BF16), ((tokens, 1), F32), ((tokens, H * DH), BF16),
         ((H * DH, tokens), BF16), ((QF, tokens), F32), ((KF, tokens), BF16), angles, angles],
        [vmem()] * 6,
        (x, cot, valid, gain, w_fact_t, pos),
        [pltpu.VMEM((max(nf, H * DH), tokens), F32)],
        2 * tokens * width * nf, 2 * width * nf, "factors",
    )


def load_factors(pieces, a_rows, b_rows):
    at = 0
    for piece in pieces:
        n = piece.shape[1]
        a_rows[:, at:at + n] = piece[:KA, :].astype(F32)
        b_rows[:, at:at + n] = piece[KA:, :].astype(F32)
        at += n


def expand_pair(pair, side, a_rows, b_rows):
    halves = []
    for sub in range(2):
        total = None
        for r in range(RK):
            a = a_rows[pl.ds((side * RK + r) * H + 2 * pair + sub, 1), :]
            term = a * b_rows[(side * RK + r) * DH:(side * RK + r + 1) * DH, :]
            total = term if total is None else total + term
        halves.append((total * (1.0 / RK)).astype(BF16))
    return jnp.concatenate(halves, axis=0)


def stack_pair(rows):
    lane = lax.broadcasted_iota(jnp.int32, rows.shape, 1)
    zero = jnp.zeros_like(rows)
    return jnp.concatenate([jnp.where(lane < DH, rows, zero), jnp.where(lane < DH, zero, rows)], axis=0)


def pair_lanes(pair):
    return pl.ds(pl.multiple_of(pair * 2 * DH, 2 * DH), 2 * DH)


def attend_kernel(n_pieces, *refs):
    q_ref, bias_ref, wo_ref, x_ref, gain_ref = refs[:5]
    pieces = refs[5:5 + n_pieces]
    h2_ref, mixed, resid_ref, lse_ref, a_rows, b_rows = refs[5 + n_pieces:]
    tokens, width = x_ref.shape
    load_factors(pieces, a_rows, b_rows)
    bias = bias_ref[...]
    bias = jnp.concatenate([bias, bias], axis=0)

    def step(pair, carry):
        keys = expand_pair(pair, 0, a_rows, b_rows)
        values = expand_pair(pair, 1, a_rows, b_rows)
        q = stack_pair(q_ref[:, pair_lanes(pair)])
        scores = mm(q, keys) * SCALE + bias
        top = jnp.max(scores, axis=1, keepdims=True)
        exponent = jnp.exp(scores - top)
        total = jnp.sum(exponent, axis=1, keepdims=True)
        probs = (exponent * (1.0 / total)).astype(BF16)
        lse_ref[pair] = top + jnp.log(total)
        out = mm(probs, values, NT)
        lane = lax.broadcasted_iota(jnp.int32, (tokens, 2 * DH), 1)
        mixed[:, pair_lanes(pair)] = jnp.where(lane < DH, out[:tokens], out[tokens:]).astype(BF16)
        return carry

    lax.fori_loop(0, H // 2, step, 0)
    resid = x_ref[...].astype(F32) + mm(mixed[...], wo_ref[...])
    resid_ref[...] = resid
    s2 = lax.rsqrt(jnp.mean(resid * resid, axis=1, keepdims=True) + EPS)
    h2_ref[...] = (resid * s2 * gain_ref[...]).astype(BF16)


def attend(q, bias, w_out, x, gain, pieces):
    tokens, width = x.shape
    slots = sum(p.shape[1] for p in pieces)
    return call(
        functools.partial(attend_kernel, len(pieces)),
        [((tokens, width), BF16), ((tokens, H * DH), BF16), ((tokens, width), F32), ((H // 2, 2 * tokens, 1), F32)],
        [vmem()] * (5 + len(pieces)),
        (q, bias, w_out, x, gain, *pieces),
        [pltpu.VMEM((KA, slots), F32), pltpu.VMEM((KB, slots), F32)],
        4 * tokens * slots * H * DH, 2 * width * width, "attend",
    )


def attend_back_kernel(n_pieces, *refs):
    q_ref, qt_ref, gm_ref, gmt_ref, lse_ref, bias_ref, qf_ref, cos_ref, sin_ref = refs[:9]
    pieces = refs[9:9 + n_pieces]
    gq_ref, own_ref, send_ref, a_rows, b_rows, ga_rows, gb_rows, gqb_rows = refs[9 + n_pieces:]
    tokens = q_ref.shape[0]
    load_factors(pieces, a_rows, b_rows)
    gb_rows[...] = jnp.zeros_like(gb_rows)
    gqb_rows[...] = jnp.zeros_like(gqb_rows)

    def spread(rows):
        top = lax.broadcasted_iota(jnp.int32, rows.shape, 0) < DH
        zero = jnp.zeros_like(rows)
        return jnp.concatenate([jnp.where(top, rows, zero), jnp.where(top, zero, rows)], axis=1)

    def step(pair, carry):
        keys = expand_pair(pair, 0, a_rows, b_rows)
        values = expand_pair(pair, 1, a_rows, b_rows)
        rows = pl.ds(pl.multiple_of(pair * 2 * DH, 2 * DH), 2 * DH)
        both = (
            stack_pair(q_ref[:, pair_lanes(pair)]), stack_pair(gm_ref[:, pair_lanes(pair)]),
            spread(qt_ref[rows, :]), spread(gmt_ref[rows, :]), lse_ref[pair],
        )
        takes = [slice(0, 2 * tokens)] if keys.shape[1] <= 2048 else [slice(0, tokens), slice(tokens, 2 * tokens)]
        grad_q, grad_k, grad_v = [], None, None
        for take in takes:
            q, g, qt, gt, lse = both[0][take], both[1][take], both[2][:, take], both[3][:, take], both[4][take]
            heads = q.shape[0] // tokens
            scores = mm(q, keys) * SCALE + jnp.concatenate([bias_ref[...]] * heads, axis=0)
            probs = jnp.exp(scores - lse)
            grad_probs = mm(g, values)
            inner = jnp.sum(probs * grad_probs, axis=1, keepdims=True)
            grad_scores = (probs * (grad_probs - inner)).astype(BF16)
            grad_q.append(mm(keys, grad_scores, NT) * SCALE)
            gk, gv = mm(qt, grad_scores) * SCALE, mm(gt, probs.astype(BF16))
            grad_k, grad_v = (gk, gv) if grad_k is None else (grad_k + gk, grad_v + gv)
        grad_q = jnp.concatenate(grad_q, axis=1)
        for sub in range(2):
            head = 2 * pair + sub
            part = slice(sub * DH, (sub + 1) * DH)
            for side, grad in ((0, grad_k[part]), (1, grad_v[part])):
                for r in range(RK):
                    s = side * RK + r
                    row = pl.ds(s * H + head, 1)
                    seg = slice(s * DH, (s + 1) * DH)
                    ga_rows[row, :] = jnp.sum(grad * b_rows[seg, :], axis=0, keepdims=True) * (1.0 / RK)
                    gb_rows[seg, :] += grad * (a_rows[row, :] * (1.0 / RK))
            dq = grad_q[part, sub * tokens:(sub + 1) * tokens]
            for r in range(RQ):
                row = pl.ds(r * H + head, 1)
                seg = slice(QA + r * DH, QA + (r + 1) * DH)
                gq_ref[row, :] = jnp.sum(dq * qf_ref[seg, :], axis=0, keepdims=True) * (1.0 / RQ)
                gqb_rows[r * DH:(r + 1) * DH, :] += dq * (qf_ref[row, :] * (1.0 / RQ))
        return carry

    lax.fori_loop(0, H // 2, step, 0)
    cosine, sine = cos_ref[...], sin_ref[...]
    for r in range(RQ):
        gq_ref[QA + r * DH:QA + (r + 1) * DH, :] = turn_back(gqb_rows[r * DH:(r + 1) * DH, :], cosine, sine)
    at = 0
    for j in range(n_pieces):
        n = pieces[j].shape[1]
        out_ref = send_ref if j % 2 else own_ref
        out_ref[j // 2, :KA, :] = ga_rows[:, at:at + n].astype(BF16)
        out_ref[j // 2, KA:, :] = gb_rows[:, at:at + n].astype(BF16)
        at += n


def attend_back(q, qt, gm, gmt, lse, bias, qf, cosine, sine, pieces):
    tokens = q.shape[0]
    slots = sum(p.shape[1] for p in pieces)
    n = len(pieces)
    return call(
        functools.partial(attend_back_kernel, n),
        [((QF, tokens), F32)] + [((n // 2, KF, slots // n), BF16)] * 2,
        [vmem()] * (9 + n),
        (q, qt, gm, gmt, lse, bias, qf, cosine, sine, *pieces),
        [pltpu.VMEM((KA, slots), F32), pltpu.VMEM((KB, slots), F32), pltpu.VMEM((KA, slots), F32),
         pltpu.VMEM((KB, slots), F32), pltpu.VMEM((RQ * DH, tokens), F32)],
        10 * tokens * slots * H * DH, 4 * tokens * slots, "attend_back",
    )


def hidden_kernel(go_ref, wd_ref, out_ref):
    out_ref[...] = mm(go_ref[...], wd_ref[...], NT)


def hidden_grads(hg, w_down):
    tokens, width = hg.shape[0], hg.shape[1] // 2
    ff = w_down.shape[0]
    chunk = max(c for c in range(128, ff + 1, 128) if ff % c == 0 and c <= ff // 2)
    return pl.pallas_call(
        hidden_kernel,
        grid=(ff // chunk,),
        in_specs=[pl.BlockSpec((tokens, width), lambda j: (0, 1)), pl.BlockSpec((chunk, width), lambda j: (j, 0))],
        out_specs=pl.BlockSpec((tokens, chunk), lambda j: (0, j)),
        out_shape=jax.ShapeDtypeStruct((tokens, ff), F32),
        compiler_params=pltpu.CompilerParams(vmem_limit_bytes=VMEM_BYTES),
        cost_estimate=pl.CostEstimate(
            flops=2 * tokens * width * ff, transcendentals=0, bytes_accessed=2 * width * ff + 4 * tokens * ff
        ),
        name="hidden_grads",
    )(hg, w_down)


def column_kernel(place_ref, wg_ref, wu_ref, wgt_ref, wut_ref, window, turned, sems):
    span = window.shape[2]
    part, width = wgt_ref.shape
    at = (place_ref[0] * 2 + place_ref[1]) * part
    start = jnp.minimum(at // 128 * 128, wg_ref.shape[1] - span)
    cols = pl.ds(pl.multiple_of(start, 128), span)
    copies = [
        pltpu.make_async_copy(ref.at[:, cols], window.at[i], sems.at[i]) for i, ref in enumerate((wg_ref, wu_ref))
    ]
    for copy in copies:
        copy.start()
    for i, out_ref in enumerate((wgt_ref, wut_ref)):
        copies[i].wait()
        turned[...] = window[i].T
        out_ref[...] = turned[pl.ds(pl.multiple_of(at - start, 32), part), :]


def own_columns(place, w_gate, w_up, part):
    width, ff = w_gate.shape
    span = min(ff, -(-part // 128) * 128 + 128)
    return call(
        column_kernel,
        [((part, width), BF16)] * 2,
        [smem(), hbm(), hbm()],
        (place, w_gate, w_up),
        [pltpu.VMEM((2, width, span), BF16), pltpu.VMEM((span, width), BF16), pltpu.SemaphoreType.DMA((2,))],
        0, 4 * width * span, "own_columns",
    )


def ffn_kernel(
    place_ref, h2_ref, hg_ref, gh_ref, resid_ref, gain_ref, mixed_ref, wg_hbm, wu_hbm, wd_hbm, wo_hbm, *refs,
):
    out_ref, gain_grad_ref, gres_ref, gm_ref, gmt_ref = refs[:5]
    mgx_refs, (branch, grad_h2, gb_cols, wg, wu, wd, wo, sems) = refs[5:-8], refs[-8:]
    width, ff = wg.shape
    n_chunks = sems.shape[1]
    chunk = ff // n_chunks
    copies = []
    for j in range(n_chunks):
        part = pl.ds(j * chunk, chunk)
        copies.append([
            pltpu.make_async_copy(wg_hbm.at[:, part], wg.at[:, part], sems.at[0, j]),
            pltpu.make_async_copy(wu_hbm.at[:, part], wu.at[:, part], sems.at[1, j]),
            pltpu.make_async_copy(wd_hbm.at[part, :], wd.at[part, :], sems.at[2, j]),
        ])
    wo_copy = pltpu.make_async_copy(wo_hbm, wo, sems.at[3, 0])
    for group in copies:
        for copy in group:
            copy.start()
    wo_copy.start()
    h2 = h2_ref[...]
    for j in range(n_chunks):
        for copy in copies[j]:
            copy.wait()
        part = slice(j * chunk, (j + 1) * chunk)
        gate, up = mm(h2, wg[:, part]), mm(h2, wu[:, part])
        grad_hidden = gh_ref[:, part]
        sig = jax.nn.sigmoid(gate)
        silu = gate * sig
        hidden = (silu * up).astype(BF16)
        grad_gate = (grad_hidden * up * sig * (1.0 + gate * (1.0 - sig))).astype(BF16)
        grad_up = (grad_hidden * silu).astype(BF16)
        more_branch = mm(hidden, wd[part, :])
        more_grad = mm(grad_gate, wg[:, part], NT) + mm(grad_up, wu[:, part], NT)
        if j == 0:
            branch[...] = more_branch
            grad_h2[...] = more_grad
        else:
            branch[...] += more_branch
            grad_h2[...] += more_grad
    resid = resid_ref[...]
    out_ref[...] = (resid + branch[...]).astype(BF16)
    s2 = lax.rsqrt(jnp.mean(resid * resid, axis=1, keepdims=True) + EPS)
    n2 = resid * s2
    gh = grad_h2[...]
    gain_grad_ref[...] = jnp.sum(gh * n2, axis=0, keepdims=True)
    g2 = gh * gain_ref[...]
    gres = hg_ref[:, width:].astype(F32) + s2 * (g2 - n2 * jnp.mean(g2 * n2, axis=1, keepdims=True))
    gres_ref[...] = gres
    gb = gres.astype(BF16)
    gb_cols[...] = gb
    wo_copy.wait()
    gm = mm(gb, wo[...], NT)
    gm_ref[...] = gm.astype(BF16)
    gmt_ref[...] = gm.T.astype(BF16)
    for k, mgx_ref in enumerate(mgx_refs):
        cols = mgx_ref.shape[1] - width
        mgx_ref[:, :width] = mixed_ref[...]
        mgx_ref[:, width:] = gb_cols[:, pl.ds(pl.multiple_of((place_ref[0] ^ k) * cols, cols), cols)]


def feed_forward(place, h2, hg, gh, w_gate, w_up, w_down, resid, gain, w_out, mixed, n_rows):
    tokens, width = resid.shape
    ff = w_gate.shape[1]
    chunk = 256 if ff % 256 == 0 else 128
    return call(
        ffn_kernel,
        [((tokens, width), BF16), ((1, width), F32), ((tokens, width), F32), ((tokens, width), BF16),
         ((width, tokens), BF16)] + [((tokens, width + width // n_rows), BF16)] * n_rows,
        [smem()] + [vmem()] * 6 + [hbm()] * 4,
        (place, h2, hg, gh, resid, gain, mixed, w_gate, w_up, w_down, w_out),
        [pltpu.VMEM((tokens, width), F32), pltpu.VMEM((tokens, width), F32), pltpu.VMEM((tokens, width), BF16),
         pltpu.VMEM((width, ff), BF16), pltpu.VMEM((width, ff), BF16), pltpu.VMEM((ff, width), BF16),
         pltpu.VMEM((width, width), BF16), pltpu.SemaphoreType.DMA((4, ff // chunk))],
        10 * tokens * width * ff, 6 * width * ff, "feed_forward",
    )


def weight_kernel(n_pieces, ordered, place_ref, wgt_ref, wut_ref, wd_ref, *refs):
    h2_pieces, hg_pieces = refs[:n_pieces], refs[n_pieces:2 * n_pieces]
    up_keep, up_send, down_keep, down_send, h2s, gos, wds, sems = refs[2 * n_pieces:]
    tokens, width = h2_pieces[0].shape
    ff = wgt_ref.shape[0]
    groups = [[], []]
    for j in range(n_pieces):
        rows = pl.ds(j * tokens, tokens)
        groups[0].append(pltpu.make_async_copy(h2_pieces[j], h2s.at[rows, :], sems.at[0, j]))
        groups[1].append(pltpu.make_async_copy(
            hg_pieces[j].at[:, pl.ds(width, width)], gos.at[rows, :], sems.at[1, j]))
    at = pl.multiple_of((place_ref[0] * 2 + place_ref[1]) * ff, 32)
    groups[1].append(pltpu.make_async_copy(wd_ref.at[pl.ds(at, ff), :], wds, sems.at[1, n_pieces]))
    for group in groups:
        for copy in group:
            copy.start()
    for copy in groups[0]:
        copy.wait()
    gate = mm(wgt_ref[...], h2s[...], NT)
    up = mm(wut_ref[...], h2s[...], NT)
    for copy in groups[1]:
        copy.wait()
    grad_hidden = mm(wds[...], gos[...], NT)
    sig = jax.nn.sigmoid(gate)
    silu = gate * sig
    hidden = (silu * up).astype(BF16)
    grad_gate = (grad_hidden * up * sig * (1.0 + gate * (1.0 - sig))).astype(BF16)
    grad_up = (grad_hidden * silu).astype(BF16)
    kept = up_keep.shape[0]
    n_z = 2 * kept
    cols = width // n_z
    half = cols // 2
    for slot, k in enumerate(halving_order(n_z)):
        up_ref, down_ref, i = (up_keep, down_keep, slot) if slot < kept else (up_send, down_send, slot - kept)
        if ordered:
            z, core = place_ref[2] ^ k, place_ref[1]
            first = pl.ds(pl.multiple_of(z * cols + core * half, half), half)
            other = pl.ds(pl.multiple_of(z * cols + (1 - core) * half, half), half)
            straight = pl.ds(pl.multiple_of(z * cols, cols), cols)
            h2c = jnp.concatenate([h2s[:, first], h2s[:, other]], axis=1)
        else:
            straight = slice(slot * cols, (slot + 1) * cols)
            h2c = h2s[:, straight]
        up_ref[i, :ff, :] = mm(grad_gate, h2c).astype(BF16)
        up_ref[i, ff:, :] = mm(grad_up, h2c).astype(BF16)
        down_ref[i] = mm(hidden, gos[:, straight]).astype(BF16)


def halving_order(n):
    order = [0]
    k = n // 2
    while k >= 1:
        order = order + [o | k for o in order]
        k //= 2
    return order


def halve(keep, got, axis, k):
    while True:
        total = keep.astype(F32) + got.astype(F32)
        n = total.shape[0]
        if n == 1:
            return total[0]
        k *= 2
        keep, got = total[:n // 2], swap(total[n // 2:].astype(BF16), axis, k)


def weight_grads(place, wgt, wut, w_down, h2_pieces, hg_pieces, n_z, ordered):
    n = len(h2_pieces)
    tokens = h2_pieces[0].shape[0]
    ff, width = wgt.shape
    total = n * tokens
    up, down = ((n_z // 2, 2 * ff, width // n_z), BF16), ((n_z // 2, ff, width // n_z), BF16)
    return call(
        functools.partial(weight_kernel, n, ordered),
        [up, up, down, down],
        [smem(), vmem(), vmem(), hbm()] + [hbm()] * (2 * n),
        (place, wgt, wut, w_down, *h2_pieces, *hg_pieces),
        [pltpu.VMEM((total, width), BF16), pltpu.VMEM((total, width), BF16), pltpu.VMEM((ff, width), BF16),
         pltpu.SemaphoreType.DMA((2, n + 1))],
        12 * total * width * ff, 6 * width * ff + 4 * total * width, "weight_grads",
    )


def own_cut(ordered, place_ref, k, cols):
    if not ordered:
        return slice(k * cols, (k + 1) * cols)
    return pl.ds(pl.multiple_of(((place_ref[2] ^ k) * 2 + place_ref[1]) * cols, cols), cols)


def out_kernel(n_pieces, n_out, ordered, place_ref, mine_ref, other_ref, *refs):
    hg_pieces = refs[:n_pieces]
    out_refs, (h1_ref, wide, thin, sems) = refs[n_pieces:-4], refs[-4:]
    cols = out_refs[0].shape[1]
    n_rows, tokens, both = mine_ref.shape
    part = thin.shape[1]
    copies = []
    for j, piece in enumerate(hg_pieces):
        for k in range(n_out):
            copies.append(pltpu.make_async_copy(
                piece.at[:, own_cut(ordered, place_ref, k, cols)],
                h1_ref.at[pl.ds(j * tokens, tokens), pl.ds(k * cols, cols)], sems.at[j, k]))
    if ordered:
        for copy in copies:
            copy.start()
    for i, ref in enumerate((mine_ref, other_ref)):
        for j in range(n_rows):
            rows = slice((i * n_rows + j) * tokens, (i * n_rows + j + 1) * tokens)
            thin[rows, :] = ref[j, :, both - part:]
            for k in range(n_out):
                wide[rows, k * cols:(k + 1) * cols] = ref[j, :, own_cut(ordered, place_ref, k, cols)]
    full = mm(thin[...].T, wide[...]).astype(BF16)
    for k in range(n_out):
        out_refs[k][...] = full[:, k * cols:(k + 1) * cols]
    if ordered:
        for copy in copies:
            copy.wait()


def out_grads(place, mine, other, hg_pieces, width, n_out, cols, ordered):
    n = len(hg_pieces)
    n_rows, tokens, both = mine.shape
    part = both - width
    total = 2 * n_rows * tokens
    *parts, h1_slab = call(
        functools.partial(out_kernel, n, n_out, ordered),
        [((part, cols), BF16)] * n_out + [((total, n_out * cols), BF16)],
        [smem(), vmem(), vmem()] + [hbm()] * n,
        (place, mine, other, *hg_pieces),
        [pltpu.VMEM((total, n_out * cols), BF16), pltpu.VMEM((total, part), BF16), pltpu.SemaphoreType.DMA((n, n_out))],
        2 * total * part * n_out * cols, 4 * total * n_out * cols, "out_grads",
    )
    if not ordered:
        h1_slab = jnp.concatenate([piece[:, :width] for piece in hg_pieces], axis=0)
    return parts, h1_slab


def fact_kernel(n_out, head, ordered, h1_ref, mine_ref, other_ref, *refs):
    carried, out_refs, thin = refs[:n_out], refs[n_out:-1], refs[-1]
    cols = out_refs[0].shape[1]
    tokens = mine_ref.shape[2]
    rows = mine_ref.shape[1]
    parts = [ref[j] for ref in (mine_ref, other_ref) for j in range(ref.shape[0])]
    for j, part in enumerate(parts):
        thin[:, j * tokens:(j + 1) * tokens] = part[head:, :]
    full = mm(thin[...], h1_ref[...]).astype(BF16)
    for k in range(n_out):
        out_refs[k][head:rows, :] = full[:, k * cols:(k + 1) * cols]
        out_refs[k][rows:, :] = carried[k][...]
    if ordered:
        half = head // 2
        gains = tree_sum([p[:half].astype(F32) + p[half:head].astype(F32) for p in parts])
        high = gains.astype(BF16)
        low = (gains - high.astype(F32)).astype(BF16)
        for k in range(n_out):
            out_refs[k][:half, :] = high
            out_refs[k][half:head, :] = low


def fact_grads(h1_slab, mine, other, carried, head, ordered):
    n_rows, rows, tokens = mine.shape
    n_out = len(carried)
    part, cols = carried[0].shape
    total = 2 * n_rows * tokens
    return call(
        functools.partial(fact_kernel, n_out, head, ordered),
        [((rows + part, cols), BF16)] * n_out,
        [vmem()] * (3 + n_out),
        (h1_slab, mine, other, *carried),
        [pltpu.VMEM((rows - head, total), BF16)],
        2 * total * rows * n_out * cols, 2 * total * n_out * cols, "fact_grads",
    )


def input_kernel(
    n_parts, place_ref, gq_ref, *refs,
):
    parts = refs[:n_parts]
    wft_ref, x_ref, s1_ref, gain_ref, gres_ref, gain_two_ref, cos_ref, sin_ref = refs[n_parts:n_parts + 8]
    gin_ref, *gfx_refs = refs[n_parts + 8:-2]
    gf, gains = refs[-2:]
    cosine, sine = cos_ref[...], sin_ref[...]
    kv = tree_sum([part[...].astype(F32) for part in parts])
    gf[:QF, :] = gq_ref[...]
    gf[QF:QF + KA, :] = kv[:KA]
    for r in range(2 * RK):
        rows = kv[KA + r * DH:KA + (r + 1) * DH]
        if r < RK:
            rows = turn_back(rows, cosine, sine)
        gf[QF + KA + r * DH:QF + KA + (r + 1) * DH, :] = rows
    grad = gf[...].T.astype(BF16)
    grad_h1 = mm(grad, wft_ref[...])
    s1 = s1_ref[...]
    n1 = x_ref[...].astype(F32) * s1
    gain_one = jnp.sum(grad_h1 * n1, axis=0, keepdims=True)
    gain_two = gain_two_ref[...]
    g1 = grad_h1 * gain_ref[...]
    gin_ref[...] = gres_ref[...] + s1 * (g1 - n1 * jnp.mean(g1 * n1, axis=1, keepdims=True))
    tokens, width = x_ref.shape
    half = gains.shape[0]
    for i in range(half // 2):
        gains[i:i + 1, :] = gain_one[:, i * tokens:(i + 1) * tokens]
        gains[half // 2 + i:half // 2 + i + 1, :] = gain_two[:, i * tokens:(i + 1) * tokens]
    high = gains[...].astype(BF16)
    low = (gains[...] - high.astype(F32)).astype(BF16)
    for k, gfx_ref in enumerate(gfx_refs):
        part = gfx_ref.shape[0] - 2 * half
        gfx_ref[:half, :] = high
        gfx_ref[half:2 * half, :] = low
        gfx_ref[2 * half:, :] = gf[pl.ds(pl.multiple_of((place_ref[0] ^ k) * part, 8), part), :].astype(BF16)


def input_grads(place, gq, parts, w_fact_t, x, s1, gain, gres, gain_two, cosine, sine, n_rows):
    tokens, width = x.shape
    nf = w_fact_t.shape[0]
    half = 2 * width // tokens
    return call(
        functools.partial(input_kernel, len(parts)),
        [((tokens, width), F32)] + [((2 * half + nf // n_rows, tokens), BF16)] * n_rows,
        [smem()] + [vmem()] * (9 + len(parts)),
        (place, gq, *parts, w_fact_t, x, s1, gain, gres, gain_two, cosine, sine),
        [pltpu.VMEM((nf, tokens), F32), pltpu.VMEM((half, tokens), F32)],
        2 * tokens * width * nf, 2 * width * nf, "input_grads",
    )


def after(values, *others):
    flat, tree = jax.tree.flatten((values, others))
    return jax.tree.unflatten(tree, lax.optimization_barrier(flat))[0]


def body(inputs, lengths, gain_attn, w_fact, w_out, gain_ffn, w_gate, w_up, w_down, cotangent):
    seqs, local_len, width = inputs.shape
    tokens = seqs * local_len
    n_rows, n_ctx = lax.axis_size(ROW), lax.axis_size(CTX)
    n_z = n_ctx // 2
    row, ctx = lax.axis_index(ROW), lax.axis_index(CTX)
    z, core = ctx // 2, ctx % 2
    slots_all = local_len * n_ctx
    block_len = local_len // 2
    ff = w_gate.shape[1]
    ff_part = ff // (2 * n_rows)
    own_cols = width // n_ctx
    per = n_ctx // (2 * n_rows)
    ordered = own_cols % 128 == 0 and per == 1 and tokens == 128
    n_out = n_z if ordered else n_ctx
    place = jnp.stack([row, core, z]).astype(jnp.int32)

    within = jnp.arange(local_len, dtype=jnp.int32)
    local_pos = jnp.tile(slot_position(ctx * local_len + within, block_len, slots_all), seqs)
    local_seq = jnp.repeat(jnp.arange(seqs, dtype=jnp.int32), local_len)
    valid = (local_pos < jnp.repeat(lengths, local_len)).astype(F32)[:, None]
    piece_of = jnp.arange(n_ctx, dtype=jnp.int32) ^ ctx
    key_pos = jnp.tile(
        slot_position(piece_of[:, None] * local_len + within[None, :], block_len, slots_all)[:, None, :], (1, seqs, 1)
    ).reshape(-1)
    key_seq = jnp.tile(local_seq, n_ctx)
    key_len = jnp.tile(jnp.repeat(lengths, local_len), n_ctx)
    allowed = (
        (key_pos[None, :] <= local_pos[:, None])
        & (key_pos < key_len)[None, :]
        & (key_seq[None, :] == local_seq[:, None])
    )
    bias = jnp.where(allowed, 0.0, -1e30).astype(F32)

    x = inputs.reshape(tokens, width)
    gain_one, gain_two = gain_attn[None, :], gain_ffn[None, :]
    w_fact_t = w_fact.T

    def others(values, axis, n):
        return [swap(values[k], axis, k) for k in range(1, n)]

    def along_core(values):
        return list(values) + [swap(value, "core", 1) for value in values]

    def both_cores(values):
        mine = jnp.stack(values)
        return [mine, swap(mine, "core", 1)]

    hg, s1, q, qt, qf, kv, cosine, sine = project(
        x, cotangent.reshape(tokens, width), valid, gain_one, w_fact_t, local_pos.astype(F32)[None, :]
    )
    kv_z = [kv] + others([kv] * n_z, "z", n_z)
    gh = hidden_grads(hg, w_down)
    kv_z = after(kv_z, gh)
    kv_pieces = []
    for part in kv_z:
        kv_pieces += [part, swap(part, "core", 1)]
    wgt, wut = own_columns(place, w_gate, w_up, ff_part)
    hg_same = [hg] + others([hg] * n_rows, ROW, n_rows)
    h2, mixed, resid, lse = attend(after(q, wgt), bias, w_out, x, gain_two, kv_pieces)
    h2_same = [h2] + others([h2] * n_rows, ROW, n_rows)
    hg_pieces = along_core(after(hg_same, h2))
    block_out, gain_two_part, gres, gm, gmt, *mgx = feed_forward(
        place, h2, after(hg, hg_same), gh, w_gate, w_up, w_down, resid, gain_two, w_out, mixed, n_rows
    )
    h2_pieces = along_core(after(h2_same, gm))
    up_keep, up_send, down_keep, down_send = weight_grads(
        place, wgt, wut, w_down, h2_pieces, hg_pieces, n_z, ordered
    )
    if not ordered:
        turns = jnp.asarray(halving_order(n_z), jnp.int32) ^ z
        cores = jnp.arange(2, dtype=jnp.int32) ^ core
        up = jnp.take(jnp.concatenate([up_keep, up_send]), turns, axis=0)
        up = jnp.take(up.reshape(n_z, 2 * ff_part, 2, own_cols), cores, axis=2).reshape(up.shape)
        down = jnp.concatenate([down_keep, down_send]).transpose(1, 0, 2)
        down = down.reshape(per, ff_part // per, n_rows, width // n_rows).transpose(0, 2, 1, 3)
        down = jnp.take(down.reshape(n_z, ff_part // per, width // n_rows), turns, axis=0)
        up_keep, up_send, down_keep, down_send = up[:n_z // 2], up[n_z // 2:], down[:n_z // 2], down[n_z // 2:]

    up_got, down_got = swap(up_send, "z", 1), swap(down_send, "z", 1)
    mg_same = [mgx[0]] + others(after(mgx, up_send), ROW, n_rows)
    gq, gkv_own, gkv_send = attend_back(q, qt, after(gm, up_send), gmt, lse, bias, qf, cosine, sine, kv_pieces)
    gkv_send, mg_same, up_got, down_got = lax.optimization_barrier((gkv_send, mg_same, up_got, down_got))
    gkv_got = swap(gkv_send, "core", 1)
    gkv_z = [(gkv_own[k].astype(F32) + gkv_got[k].astype(F32)).astype(BF16) for k in range(n_z)]
    kv_parts = [gkv_z[0]] + others(gkv_z, "z", n_z)

    def own_blocks(parts):
        if ordered:
            return parts
        parts = jnp.take(jnp.stack(parts), (jnp.arange(n_z, dtype=jnp.int32) ^ z) * 2 + core, axis=0)
        return [parts[k] for k in range(n_z)]

    out_parts, h1_slab = out_grads(place, *both_cores(mg_same), hg_pieces, width, n_out, own_cols, ordered)
    gq = after(gq, out_parts)
    up_keep, down_keep = after((up_keep, down_keep), gkv_z)
    grad_inputs, *gfx = input_grads(
        place, gq, kv_parts, w_fact_t, x, s1, gain_one, gres, gain_two_part, cosine, sine, n_rows
    )
    up_total = halve(up_keep, up_got, "z", 1)
    down_total = halve(down_keep, down_got, "z", 1)
    head = gfx[0].shape[0] - w_fact.shape[1] // n_rows
    gf_all = both_cores([gfx[0]] + others(gfx, ROW, n_rows))
    tail_parts = own_blocks(fact_grads(h1_slab, *gf_all, out_parts, head, ordered))
    tail_got = others(tail_parts, "z", n_z)

    up_total, down_total = after((up_total, down_total), tail_parts)
    mine, other = up_total[:, :own_cols], swap(up_total[:, own_cols:].astype(BF16), "core", 1).astype(F32)
    first = jnp.where(core == 0, mine, other)
    second = jnp.where(core == 0, other, mine)
    grad_gate = jnp.concatenate([first[:ff_part], second[:ff_part]], axis=0).T
    grad_up = jnp.concatenate([first[ff_part:], second[ff_part:]], axis=0).T

    moves = []
    for r in range(n_rows):
        for c in range(2):
            for p in range(n_z):
                b, s = p // n_rows, p % n_rows
                moves.append((r * n_ctx + 2 * p + c, s * n_ctx + (r * 2 + c) * per + b))
    grad_down = lax.ppermute(down_total.astype(BF16), ROW + CTX, moves).astype(F32)

    tail_got = after(tail_got, grad_gate, grad_up)
    tail = tree_sum([part.astype(F32) for part in [tail_parts[0]] + tail_got])
    rows = gfx[0].shape[0]
    grad_fact, grad_out = tail[head:rows].T, tail[rows:].T
    if ordered:
        gains = (tail[:head // 2] + tail[head // 2:head]).reshape(2, width)
    else:
        sums = gfx[0][:head // 2].astype(F32) + gfx[0][head // 2:head].astype(F32)
        gains = lax.psum(sums, ROW + CTX).reshape(2, width)

    return (
        block_out.reshape(inputs.shape),
        grad_inputs.reshape(inputs.shape),
        gains[0],
        grad_fact,
        grad_out,
        gains[1],
        grad_gate,
        grad_up,
        grad_down,
    )


def solution(mesh):
    n_rows, n_ctx = mesh.shape["row"], mesh.shape["ctx"]
    fine = Mesh(mesh.devices.reshape(n_rows // 2, 2, n_ctx // 2, 2), ROW + CTX)
    placed = (P(ROW, CTX, None), P(ROW), P(), P(), P(), P(), P(), P(), P(), P(ROW, CTX, None))
    return jax.shard_map(
        body,
        mesh=fine,
        in_specs=placed,
        out_specs=(
            P(ROW, CTX, None), P(ROW, CTX, None), P(), P(CTX, ROW), P(CTX, ROW), P(), P(CTX, ROW), P(CTX, ROW),
            P(CTX, ROW),
        ),
        check_vma=False,
    )
```

time: 229 us -> 171 us (0.75); the launches traced: 226 us -> 170 us
  starting transfers between devices: 66.4 us -> 38.9 us
  waiting for transfers between devices: 62.8 us -> 44.2 us
  local copies, waits for them, and re-layouts: 17.8 us -> 5.86 us
  Pallas kernels: 65.9 us -> 72 us
  other arithmetic: 11.3 us -> 7.49 us
    ppermute x51 -> x41, waiting for transfers between devices: 62.8 us -> 34.7 us  [swap(): return lax.ppermute(value, axis, [(j, j ^ k) for j in range(size)])]
    ppermute x51 -> x41, starting transfers between devices: 61.4 us -> 37 us  [swap(): return lax.ppermute(value, axis, [(j, j ^ k) for j in range(size)])]
    pallas_call x6 -> x9, Pallas kernels: 46.9 us -> 67.1 us  [call(): pl.pallas_call(kernel, out_shape=[jax.ShapeDtypeStruct(s, d) for s, d in...]
    pallas_call x1, Pallas kernels: 19 us -> 4.87 us  [hidden_grads(): pl.pallas_call(hidden_kernel, grid=(ff // chunk,), in_specs=[pl.BlockSpec...]
    ppermute x1, waiting for transfers between devices: 0.01 us -> 9.49 us  [body(): lax.ppermute(down_total.astype(BF16), ROW + CTX, moves).astype(F32)]
    dynamic_slice x2 -> x0, local copies, waits for them, and re-layouts: 5.69 us -> none  [the longest x1 3.53 us: body(): wu_part = lax.dynamic_slice(w_up, (0, at), (width, ff_part))]
    ppermute x1, starting transfers between devices: 5.03 us -> 1.91 us  [body(): lax.ppermute(down_total.astype(BF16), ROW + CTX, moves).astype(F32)]
    slice x18 -> x4, local copies, waits for them, and re-layouts: 3.05 us -> 0.13 us  [the longest x2 0.06 us: halve(): keep, got = (total[:n // 2], swap(total[n // 2:].astype(BF16), axis, k))]
  transfers between devices with their start and end apart: 52 -> 42, of which waited for: 12 -> 13; matrix products, arithmetic and copies ran while one was open for 9% -> 4% of each run, Pallas kernels for 28% -> 33%
where the time goes in v2:
time: 171 us; the launch traced here: 170 us
  Pallas kernels  72 us (42%)
  waiting for transfers between devices  44.2 us (26%)
  starting transfers between devices  38.9 us (23%)
  other arithmetic  7.49 us (4%)
  local copies, waits for them, and re-layouts  5.86 us (3%)
  between operations  1.85 us (1%)
    pallas_call x9, Pallas kernels, call(): pl.pallas_call(kernel, out_shape=[jax.ShapeDtypeStruct(s, d) for s, d in...  67.1 us
    ppermute x41, starting transfers between devices, swap(): return lax.ppermute(value, axis, [(j, j ^ k) for j in range(size)])  37 us
    ppermute x41, waiting for transfers between devices, swap(): return lax.ppermute(value, axis, [(j, j ^ k) for j in range(size)])  34.7 us
    ppermute x1, waiting for transfers between devices, body(): lax.ppermute(down_total.astype(BF16), ROW + CTX, moves).astype(F32)  9.49 us
    pallas_call x1, Pallas kernels, hidden_grads(): pl.pallas_call(hidden_kernel, grid=(ff // chunk,), in_specs=[pl.BlockSpec...  4.87 us
    unnamed x81, local copies, waits for them, and re-layouts  4.47 us
  transfers between devices with their start and end apart: 42, of which 13 were waited for; matrix products, arithmetic and copies ran while one was open for 4% of the time, Pallas kernels for 33%

profile of v2, /device:TPU:3, one launch (start us, length us, event | category | flops | bytes accessed | tf_op | source)
XLA Modules:
  0.0 170.3 jit_solution(225667525267668786)
XLA Ops:
  2.5 3.5 %factors.1 = (bf16[128,2048]{1,0:T(8,128)(2,1)}, f32[128,1]{1,0:T(8,128)}, bf16[128,1024]{1,0:T(8,128)(2,1)}, bf16[1024,128]{1,0:T(8,128)(2,1)}, f32[480,128]{1,...) custom-call(bf16[128,1024]{1,0:T(8,128)(2,1)} %bitcast.84, ...), custom_call_target="tpu_custom_call" | custom-call | flops 209715200 | bytes 1638400 | tf_op jit(solution)/shard_map/factors/pallas_call | solution.py:47
  6.0 3.3 %collective-permute-start.2 = (bf16[320,128]{1,0:T(8,128)(2,1)}, bf16[320,128]{1,0:T(8,128)(2,1)S(1)}, u32[]{:S(2)}, u32[]{:S(2)}) collective-permute-start(bf16[320,128]{1,0:T(8,128)(2,1)} %get-tuple-element.91.refs_5_.refs_9_), channel_id=1, source_target_pairs={{0,6},{2,4},{4,2},{6,0},{1,7},{3,5},{5,3},{7,1},{8,14},{10,12},{12... | collective-permute-start | bytes 245768 | tf_op jit(solution)/shard_map/ppermute | solution.py:88
  12.6 4.9 %hidden_grads.1.gh_ref = f32[128,2816]{1,0:T(8,128)} custom-call(bf16[128,2048]{1,0:T(8,128)(2,1)} %get-tuple-element.107.go_ref.hg_ref.refs_8_.refs_0_, bf16[2816,1024]{1,0:T(8,128)(2,1)} %wd_ref.3), custom_call_target="tpu_custom_call" | custom-call | flops 738197504 | bytes 7208960 | tf_op jit(solution)/shard_map/hidden_grads/pallas_call | solution.py:314
  17.5 2.3 %collective-permute-start.3 = (bf16[320,128]{1,0:T(8,128)(2,1)S(1)}, bf16[320,128]{1,0:T(8,128)(2,1)S(1)}, u32[]{:S(2)}, u32[]{:S(2)}) collective-permute-start(bf16[320,128]{1,0:T(8,128)(2,1)S(1)} %copy-done.21), channel_id=1, source_target_pairs={{0,1},{1,0},{2,3},{3,2},{4,5},{5,4},{6,7},{7,6},{8,9},{9,8},{10,11... | collective-permute-start | bytes 245768 | tf_op jit(solution)/shard_map/ppermute | solution.py:88
  22.1 3.6 %own_columns.1 = (bf16[352,1024]{1,0:T(8,128)(2,1)}, bf16[352,1024]{1,0:T(8,128)(2,1)}) custom-call(s32[3]{0:T(128)} %pad_add_fusion.place_ref, bf16[1024,2816]{1,0:T(8,128)(2,1)} %wg_hbm.1, bf16[1024,2816]{1,0:T(8,128)(2,1)} %wu_hbm.1), custom_call_target="tpu_custom_call" | custom-call | bytes 2097152 | tf_op jit(solution)/shard_map/own_columns/pallas_call | solution.py:47
  26.4 11.5 %attend.1 = (bf16[128,1024]{1,0:T(8,128)(2,1)}, bf16[128,1024]{1,0:T(8,128)(2,1)}, f32[128,1024]{1,0:T(8,128)}, f32[8,256,1]{2,1,0:T(8,128)}) custom-call(bf16[128,1024]{1,0:T(8,128)(2,1)} %get-tuple-element.88.refs_0_, f32[128,1024]{1,0:T(8,128)} %and_select_fusion.refs_1_.refs_5_, bf16[1024,1024]{1,0:T(8,128)(2,1)} %wo_hbm.1, bf16[128,1024]{1,0:T(8,128)(2,1)} %bitcast.85, ...), custom_call_target="tpu_custom_call" | custom-call | flops 536870912 | bytes 2097152 | tf_op jit(solution)/shard_map/attend/pallas_call | solution.py:47
  40.6 14.8 %feed_forward.1 = (bf16[128,1024]{1,0:T(8,128)(2,1)}, f32[1,1024]{1,0:T(1,128)}, f32[128,1024]{1,0:T(8,128)}, bf16[128,1024]{1,0:T(8,128)(2,1)}, bf16[1024,128]{...) custom-call(s32[3]{0:T(128)} %pad_add_fusion.place_ref, ...), custom_call_target="tpu_custom_call" | custom-call | flops 3690987520 | bytes 17301504 | tf_op jit(solution)/shard_map/feed_forward/pallas_call | solution.py:47
  59.1 3.0 %collective-permute-done.16.refs_7_ = bf16[128,1024]{1,0:T(8,128)(2,1)S(1)} collective-permute-done((bf16[128,1024]{1,0:T(8,128)(2,1)S(1)}, bf16[128,1024]{1,0:T(8,128)(2,1)S(1)}, u32[]{:S(2)}, u32[]{:S(2)}) %collective-permute-start.16) | collective-permute-done | bytes 262176 | tf_op jit(solution)/shard_map/ppermute | solution.py:88
  63.6 9.4 %weight_grads.1 = (bf16[2,704,256]{2,1,0:T(8,128)(2,1)}, bf16[2,704,256]{2,1,0:T(8,128)(2,1)}, bf16[2,352,256]{2,1,0:T(8,128)(2,1)}, bf16[2,352,256]{2,1,0:T(8,128)(2,1)}) custom-call(s32[3]{0:T(128)} %pad_add_fusion.place_ref, bf16[352,1024]{1,0:T(8,128)(2,1)} %get-tuple-element.87.wgt_ref, bf16[352,1024]{1,0:T(8,128)(2,1)} %get-tuple-element.102.wut_ref, ...), custom_call_target="tpu_custom_call" | custom-call | flops 4429185024 | bytes 6356992 | tf_op jit(solution)/shard_map/weight_grads/pallas_call | solution.py:47
  73.0 2.6 %collective-permute-start.24 = (bf16[2,704,256]{2,1,0:T(8,128)(2,1)}, bf16[2,704,256]{2,1,0:T(8,128)(2,1)S(1)}, u32[]{:S(2)}, u32[]{:S(2)}) collective-permute-start(bf16[2,704,256]{2,1,0:T(8,128)(2,1)} %get-tuple-element.111), channel_id=1, source_target_pairs={{0,2},{2,0},{4,6},{6,4},{1,3},{3,1},{5,7},{7,5},{8,10},{10,8},{12,... | collective-permute-start | bytes 2162696 | tf_op jit(solution)/shard_map/ppermute | solution.py:88
  78.3 13.7 %attend_back.1 = (f32[480,128]{1,0:T(8,128)}, bf16[4,320,128]{2,1,0:T(8,128)(2,1)}, bf16[4,320,128]{2,1,0:T(8,128)(2,1)}) custom-call(bf16[128,1024]{1,0:T(8,128)(2,1)} %get-tuple-element.88.refs_0_, bf16[1024,128]{1,0:T(8,128)(2,1)} %get-tuple-element.100.refs_1_, bf16[128,1024]{1,0:T(8,128)(2,1)} %get-tuple-element.112.refs_2_, ...), custom_call_target="tpu_custom_call" | custom-call | flops 1342177280 | bytes 524288 | tf_op jit(solution)/shard_map/attend_back/pallas_call | solution.py:47
  92.1 7.6 %collective-permute-done.25 = bf16[2,352,256]{2,1,0:T(8,128)(2,1)S(1)} collective-permute-done((bf16[2,352,256]{2,1,0:T(8,128)(2,1)}, bf16[2,352,256]{2,1,0:T(8,128)(2,1)S(1)}, u32[]{:S(2)}, u32[]{:S(2)}) %collective-permute-start.25) | collective-permute-done | bytes 360480 | tf_op jit(solution)/shard_map/ppermute | solution.py:88
  101.0 3.0 %collective-permute-done.27 = bf16[4,320,128]{2,1,0:T(8,128)(2,1)S(1)} collective-permute-done((bf16[4,320,128]{2,1,0:T(8,128)(2,1)S(1)}, bf16[4,320,128]{2,1,0:T(8,128)(2,1)S(1)}, u32[]{:S(2)}, u32[]{:S(2)}) %collective-permute-start.27) | collective-permute-done | bytes 327712 | tf_op jit(solution)/shard_map/ppermute | solution.py:88
  104.7 2.3 %collective-permute-start.30 = (bf16[320,128]{1,0:T(8,128)(2,1)S(1)}, bf16[320,128]{1,0:T(8,128)(2,1)S(1)}, u32[]{:S(2)}, u32[]{:S(2)}) collective-permute-start(bf16[320,128]{1,0:T(8,128)(2,1)S(1)} %get-tuple-element.176), channel_id=1, source_target_pairs={{0,6},{2,4},{4,2},{6,0},{1,7},{3,5},{5,3},{7,1},{8,14},{10,12},{12... | collective-permute-start | bytes 245768 | tf_op jit(solution)/shard_map/ppermute | solution.py:88
  111.4 4.6 %out_grads.1 = (bf16[256,128]{1,0:T(8,128)(2,1)}, bf16[256,128]{1,0:T(8,128)(2,1)}, bf16[256,128]{1,0:T(8,128)(2,1)}, bf16[256,128]{1,0:T(8,128)(2,1)}, bf16[1024,512]{1,0:T(8,128)(2,1)}) custom-call(s32[3]{0:T(128)} %pad_add_fusion.place_ref, bf16[4,128,1280]{2,1,0:T(8,128)(2,1)} %copy-done, bf16[4,128,1280]{2,1,0:T(8,128)(2,1)} %copy-done.2, ...), custom_call_target="tpu_custom_call" | custom-call | flops 268435456 | bytes 2097152 | tf_op jit(solution)/shard_map/out_grads/pallas_call | solution.py:47
  116.0 10.5 %collective-permute-done.29.refs_2_ = bf16[320,128]{1,0:T(8,128)(2,1)S(1)} collective-permute-done((bf16[320,128]{1,0:T(8,128)(2,1)S(1)}, bf16[320,128]{1,0:T(8,128)(2,1)S(1)}, u32[]{:S(2)}, u32[]{:S(2)}) %collective-permute-start.29) | collective-permute-done | bytes 81952 | tf_op jit(solution)/shard_map/ppermute | solution.py:88
  127.2 3.4 %input_grads.1 = (f32[128,1024]{1,0:T(8,128)}, bf16[232,128]{1,0:T(8,128)(2,1)}, bf16[232,128]{1,0:T(8,128)(2,1)}, bf16[232,128]{1,0:T(8,128)(2,1)}, bf16[232,128]{1,0:T(8,128)(2,1)}) custom-call(s32[3]{0:T(128)} %pad_add_fusion.place_ref, f32[480,128]{1,0:T(8,128)} %get-tuple-element.136.gq_ref, bf16[320,128]{1,0:T(8,128)(2,1)} %get-tuple-element.179.refs_0_, ...), custom_call_target="tpu_custom_call" | custom-call | flops 209715200 | bytes 1638400 | tf_op jit(solution)/shard_map/input_grads/pallas_call | solution.py:47
  135.3 2.5 %collective-permute-done.33 = bf16[232,128]{1,0:T(8,128)(2,1)S(1)} collective-permute-done((bf16[232,128]{1,0:T(8,128)(2,1)}, bf16[232,128]{1,0:T(8,128)(2,1)S(1)}, u32[]{:S(2)}, u32[]{:S(2)}) %collective-permute-start.33) | collective-permute-done | bytes 59424 | tf_op jit(solution)/shard_map/ppermute | solution.py:88
  138.7 2.8 %collective-permute-start.34 = (bf16[4,232,128]{2,1,0:T(8,128)(2,1)S(1)}, bf16[4,232,128]{2,1,0:T(8,128)(2,1)S(1)}, u32[]{:S(2)}, u32[]{:S(2)}) collective-permute-start(bf16[4,232,128]{2,1,0:T(8,128)(2,1)S(1)} %pad_maximum_fusion.1.mine_ref), channel_id=1, source_target_pairs={{0,1},{1,0},{2,3},{3,2},{4,5},{5,4},{6,7},{7,6},{8,9},{9,8},{10,11... | collective-permute-start | bytes 712712 | tf_op jit(solution)/shard_map/ppermute | solution.py:88
  143.3 2.6 %fact_grads.1 = (bf16[488,128]{1,0:T(8,128)(2,1)}, bf16[488,128]{1,0:T(8,128)(2,1)}, bf16[488,128]{1,0:T(8,128)(2,1)}, bf16[488,128]{1,0:T(8,128)(2,1)}) custom-call(bf16[1024,512]{1,0:T(8,128)(2,1)} %get-tuple-element.143.h1_ref, bf16[4,232,128]{2,1,0:T(8,128)(2,1)} %copy-done.3, bf16[4,232,128]{2,1,0:T(8,128)(2,1)} %copy-done.16, ...), custom_call_target="tpu_custom_call" | custom-call | flops 243269632 | bytes 1048576 | tf_op jit(solution)/shard_map/fact_grads/pallas_call | solution.py:47
  146.4 2.7 %collective-permute-start.36 = (bf16[488,128]{1,0:T(8,128)(2,1)}, bf16[488,128]{1,0:T(8,128)(2,1)S(1)}, u32[]{:S(2)}, u32[]{:S(2)}) collective-permute-start(bf16[488,128]{1,0:T(8,128)(2,1)} %get-tuple-element.150), channel_id=1, source_target_pairs={{0,4},{2,6},{4,0},{6,2},{1,5},{3,7},{5,1},{7,3},{8,12},{10,14},{12... | collective-permute-start | bytes 374792 | tf_op jit(solution)/shard_map/ppermute | solution.py:88
  149.9 1.9 %collective-permute-start.41 = (bf16[352,256]{1,0:T(8,128)(2,1)S(1)}, bf16[352,256]{1,0:T(8,128)(2,1)S(1)}, u32[]{:S(2)}, u32[]{:S(2)}) collective-permute-start(bf16[352,256]{1,0:T(8,128)(2,1)S(1)} %fusion.1), channel_id=1, source_target_pairs={{0,0},{2,8},{4,16},{6,24},{1,1},{3,9},{5,17},{7,25},{8,2},{10,10},... | collective-permute-start | bytes 540680 | tf_op jit(solution)/shard_map/ppermute | solution.py:787
  153.7 4.3 %collective-permute-done.37 = bf16[488,128]{1,0:T(8,128)(2,1)S(1)} collective-permute-done((bf16[488,128]{1,0:T(8,128)(2,1)}, bf16[488,128]{1,0:T(8,128)(2,1)S(1)}, u32[]{:S(2)}, u32[]{:S(2)}) %collective-permute-start.37) | collective-permute-done | bytes 124960 | tf_op jit(solution)/shard_map/ppermute | solution.py:88
  160.1 9.5 %collective-permute-done.41 = bf16[352,256]{1,0:T(8,128)(2,1)S(1)} collective-permute-done((bf16[352,256]{1,0:T(8,128)(2,1)S(1)}, bf16[352,256]{1,0:T(8,128)(2,1)S(1)}, u32[]{:S(2)}, u32[]{:S(2)}) %collective-permute-start.41) | collective-permute-done | bytes 180256 | tf_op jit(solution)/shard_map/ppermute | solution.py:787
  (178 shorter events, 38.1 us)
Async XLA Ops:
  9.4 8.1 %collective-permute-start.1 = (bf16[320,128]{1,0:T(8,128)(2,1)}, bf16[320,128]{1,0:T(8,128)(2,1)S(1)}, u32[]{:S(2)}, u32[]{:S(2)}) collective-permute-start(bf16[320,128]{1,0:T(8,128)(2,1)} %get-tuple-element.91.refs_5_.refs_9_), channel_id=1, source_target_pairs={{0,4},{2,6},{4,0},{6,2},{1,5},{3,7},{5,1},{7,3},{8,12},{10,14},{12... | collective-permute-start | bytes 245768 | tf_op jit(solution)/shard_map/ppermute | solution.py:88
  9.4 8.1 %collective-permute-start = (bf16[320,128]{1,0:T(8,128)(2,1)}, bf16[320,128]{1,0:T(8,128)(2,1)S(1)}, u32[]{:S(2)}, u32[]{:S(2)}) collective-permute-start(bf16[320,128]{1,0:T(8,128)(2,1)} %get-tuple-element.91.refs_5_.refs_9_), channel_id=1, source_target_pairs={{0,2},{2,0},{4,6},{6,4},{1,3},{3,1},{5,7},{7,5},{8,10},{10,8},{12,... | collective-permute-start | bytes 245768 | tf_op jit(solution)/shard_map/ppermute | solution.py:88
  9.7 30.2 %collective-permute-start.9 = (bf16[128,2048]{1,0:T(8,128)(2,1)}, bf16[128,2048]{1,0:T(8,128)(2,1)S(1)}, u32[]{:S(2)}, u32[]{:S(2)}) collective-permute-start(bf16[128,2048]{1,0:T(8,128)(2,1)} %get-tuple-element.107.go_ref.hg_ref.refs_8_.refs_0_), channel_id=1, source_target_pairs={{0,24},{8,16},{16,8},{24,0},{1,25},{9,17},{17,9},{25,1},{2,26},{10... | collective-permute-start | bytes 1572872 | tf_op jit(solution)/shard_map/ppermute | solution.py:88
  10.9 29.6 %collective-permute-start.8 = (bf16[128,2048]{1,0:T(8,128)(2,1)}, bf16[128,2048]{1,0:T(8,128)(2,1)S(1)}, u32[]{:S(2)}, u32[]{:S(2)}) collective-permute-start(bf16[128,2048]{1,0:T(8,128)(2,1)} %get-tuple-element.107.go_ref.hg_ref.refs_8_.refs_0_), channel_id=1, source_target_pairs={{0,16},{8,24},{16,0},{24,8},{1,17},{9,25},{17,1},{25,9},{2,18},{10... | collective-permute-start | bytes 1572872 | tf_op jit(solution)/shard_map/ppermute | solution.py:88
  11.5 29.1 %collective-permute-start.7 = (bf16[128,2048]{1,0:T(8,128)(2,1)}, bf16[128,2048]{1,0:T(8,128)(2,1)S(1)}, u32[]{:S(2)}, u32[]{:S(2)}) collective-permute-start(bf16[128,2048]{1,0:T(8,128)(2,1)} %get-tuple-element.107.go_ref.hg_ref.refs_8_.refs_0_), channel_id=1, source_target_pairs={{0,8},{8,0},{16,24},{24,16},{1,9},{9,1},{17,25},{25,17},{2,10},{10... | collective-permute-start | bytes 1572872 | tf_op jit(solution)/shard_map/ppermute | solution.py:88
  37.9 17.5 %collective-permute-start.12 = (bf16[128,1024]{1,0:T(8,128)(2,1)}, bf16[128,1024]{1,0:T(8,128)(2,1)S(1)}, u32[]{:S(2)}, u32[]{:S(2)}) collective-permute-start(bf16[128,1024]{1,0:T(8,128)(2,1)} %get-tuple-element.103.h2_ref.refs_0_), channel_id=1, source_target_pairs={{0,24},{8,16},{16,8},{24,0},{1,25},{9,17},{17,9},{25,1},{2,26},{10... | collective-permute-start | bytes 786440 | tf_op jit(solution)/shard_map/ppermute | solution.py:88
  39.7 15.8 %collective-permute-start.11 = (bf16[128,1024]{1,0:T(8,128)(2,1)}, bf16[128,1024]{1,0:T(8,128)(2,1)S(1)}, u32[]{:S(2)}, u32[]{:S(2)}) collective-permute-start(bf16[128,1024]{1,0:T(8,128)(2,1)} %get-tuple-element.103.h2_ref.refs_0_), channel_id=1, source_target_pairs={{0,16},{8,24},{16,0},{24,8},{1,17},{9,25},{17,1},{25,9},{2,18},{10... | collective-permute-start | bytes 786440 | tf_op jit(solution)/shard_map/ppermute | solution.py:88
  39.9 15.6 %collective-permute-start.10 = (bf16[128,1024]{1,0:T(8,128)(2,1)}, bf16[128,1024]{1,0:T(8,128)(2,1)S(1)}, u32[]{:S(2)}, u32[]{:S(2)}) collective-permute-start(bf16[128,1024]{1,0:T(8,128)(2,1)} %get-tuple-element.103.h2_ref.refs_0_), channel_id=1, source_target_pairs={{0,8},{8,0},{16,24},{24,16},{1,9},{9,1},{17,25},{25,17},{2,10},{10... | collective-permute-start | bytes 786440 | tf_op jit(solution)/shard_map/ppermute | solution.py:88
  73.0 26.7 %collective-permute-start.24 = (bf16[2,704,256]{2,1,0:T(8,128)(2,1)}, bf16[2,704,256]{2,1,0:T(8,128)(2,1)S(1)}, u32[]{:S(2)}, u32[]{:S(2)}) collective-permute-start(bf16[2,704,256]{2,1,0:T(8,128)(2,1)} %get-tuple-element.111), channel_id=1, source_target_pairs={{0,2},{2,0},{4,6},{6,4},{1,3},{3,1},{5,7},{7,5},{8,10},{10,8},{12,... | collective-permute-start | bytes 2162696 | tf_op jit(solution)/shard_map/ppermute | solution.py:88
  75.6 24.1 %collective-permute-start.25 = (bf16[2,352,256]{2,1,0:T(8,128)(2,1)}, bf16[2,352,256]{2,1,0:T(8,128)(2,1)S(1)}, u32[]{:S(2)}, u32[]{:S(2)}) collective-permute-start(bf16[2,352,256]{2,1,0:T(8,128)(2,1)} %get-tuple-element.127), channel_id=1, source_target_pairs={{0,2},{2,0},{4,6},{6,4},{1,3},{3,1},{5,7},{7,5},{8,10},{10,8},{12,... | collective-permute-start | bytes 1081352 | tf_op jit(solution)/shard_map/ppermute | solution.py:88
  75.7 16.4 %collective-permute-start.21 = (bf16[128,1280]{1,0:T(8,128)(2,1)S(1)}, bf16[128,1280]{1,0:T(8,128)(2,1)S(1)}, u32[]{:S(2)}, u32[]{:S(2)}) collective-permute-start(bf16[128,1280]{1,0:T(8,128)(2,1)S(1)} %copy-done.31), channel_id=1, source_target_pairs={{0,8},{8,0},{16,24},{24,16},{1,9},{9,1},{17,25},{25,17},{2,10},{10... | collective-permute-start | bytes 983048 | tf_op jit(solution)/shard_map/ppermute | solution.py:88
  76.7 15.4 %collective-permute-start.22 = (bf16[128,1280]{1,0:T(8,128)(2,1)S(1)}, bf16[128,1280]{1,0:T(8,128)(2,1)S(1)}, u32[]{:S(2)}, u32[]{:S(2)}) collective-permute-start(bf16[128,1280]{1,0:T(8,128)(2,1)S(1)} %copy-done.30), channel_id=1, source_target_pairs={{0,16},{8,24},{16,0},{24,8},{1,17},{9,25},{17,1},{25,9},{2,18},{10... | collective-permute-start | bytes 983048 | tf_op jit(solution)/shard_map/ppermute | solution.py:88
  78.0 14.2 %collective-permute-start.23 = (bf16[128,1280]{1,0:T(8,128)(2,1)S(1)}, bf16[128,1280]{1,0:T(8,128)(2,1)S(1)}, u32[]{:S(2)}, u32[]{:S(2)}) collective-permute-start(bf16[128,1280]{1,0:T(8,128)(2,1)S(1)} %copy-done.29), channel_id=1, source_target_pairs={{0,24},{8,16},{16,8},{24,0},{1,25},{9,17},{17,9},{25,1},{2,26},{10... | collective-permute-start | bytes 983048 | tf_op jit(solution)/shard_map/ppermute | solution.py:88
  99.9 10.4 %collective-permute-start.26 = (bf16[4,128,1280]{2,1,0:T(8,128)(2,1)S(1)}, bf16[4,128,1280]{2,1,0:T(8,128)(2,1)S(1)}, u32[]{:S(2)}, u32[]{:S(2)}) collective-permute-start(bf16[4,128,1280]{2,1,0:T(8,128)(2,1)S(1)} %pad_maximum_fusion.mine_ref), channel_id=1, source_target_pairs={{0,1},{1,0},{2,3},{3,2},{4,5},{5,4},{6,7},{7,6},{8,9},{9,8},{10,11... | collective-permute-start | bytes 3932168 | tf_op jit(solution)/shard_map/ppermute | solution.py:88
  104.7 11.3 %collective-permute-start.30 = (bf16[320,128]{1,0:T(8,128)(2,1)S(1)}, bf16[320,128]{1,0:T(8,128)(2,1)S(1)}, u32[]{:S(2)}, u32[]{:S(2)}) collective-permute-start(bf16[320,128]{1,0:T(8,128)(2,1)S(1)} %get-tuple-element.176), channel_id=1, source_target_pairs={{0,6},{2,4},{4,2},{6,0},{1,7},{3,5},{5,3},{7,1},{8,14},{10,12},{12... | collective-permute-start | bytes 245768 | tf_op jit(solution)/shard_map/ppermute | solution.py:88
  107.0 19.5 %collective-permute-start.29 = (bf16[320,128]{1,0:T(8,128)(2,1)S(1)}, bf16[320,128]{1,0:T(8,128)(2,1)S(1)}, u32[]{:S(2)}, u32[]{:S(2)}) collective-permute-start(bf16[320,128]{1,0:T(8,128)(2,1)S(1)} %get-tuple-element.177), channel_id=1, source_target_pairs={{0,4},{2,6},{4,0},{6,2},{1,5},{3,7},{5,1},{7,3},{8,12},{10,14},{12... | collective-permute-start | bytes 245768 | tf_op jit(solution)/shard_map/ppermute | solution.py:88
  107.4 19.2 %collective-permute-start.28 = (bf16[320,128]{1,0:T(8,128)(2,1)S(1)}, bf16[320,128]{1,0:T(8,128)(2,1)S(1)}, u32[]{:S(2)}, u32[]{:S(2)}) collective-permute-start(bf16[320,128]{1,0:T(8,128)(2,1)S(1)} %get-tuple-element.178), channel_id=1, source_target_pairs={{0,2},{2,0},{4,6},{6,4},{1,3},{3,1},{5,7},{7,5},{8,10},{10,8},{12,... | collective-permute-start | bytes 245768 | tf_op jit(solution)/shard_map/ppermute | solution.py:88
  108.4 24.8 %collective-permute-start.39 = (bf16[1,352,256]{2,1,0:T(8,128)(2,1)S(1)}, bf16[1,352,256]{2,1,0:T(8,128)(2,1)S(1)}, u32[]{:S(2)}, u32[]{:S(2)}) collective-permute-start(bf16[1,352,256]{2,1,0:T(8,128)(2,1)S(1)} %slice.147), channel_id=1, source_target_pairs={{0,4},{2,6},{4,0},{6,2},{1,5},{3,7},{5,1},{7,3},{8,12},{10,14},{12... | collective-permute-start | bytes 540680 | tf_op jit(solution)/shard_map/ppermute | solution.py:88
  110.3 31.1 %collective-permute-start.38 = (bf16[1,704,256]{2,1,0:T(8,128)(2,1)S(1)}, bf16[1,704,256]{2,1,0:T(8,128)(2,1)S(1)}, u32[]{:S(2)}, u32[]{:S(2)}) collective-permute-start(bf16[1,704,256]{2,1,0:T(8,128)(2,1)S(1)} %slice.145), channel_id=1, source_target_pairs={{0,4},{2,6},{4,0},{6,2},{1,5},{3,7},{5,1},{7,3},{8,12},{10,14},{12... | collective-permute-start | bytes 1081352 | tf_op jit(solution)/shard_map/ppermute | solution.py:88
  145.9 5.9 %collective-permute-start.40 = (bf16[704,128]{1,0:T(8,128)(2,1)S(1)}, bf16[704,128]{1,0:T(8,128)(2,1)S(1)}, u32[]{:S(2)}, u32[]{:S(2)}) collective-permute-start(bf16[704,128]{1,0:T(8,128)(2,1)S(1)} %slice.146), channel_id=1, source_target_pairs={{0,1},{1,0},{2,3},{3,2},{4,5},{5,4},{6,7},{7,6},{8,9},{9,8},{10,11... | collective-permute-start | bytes 540680 | tf_op jit(solution)/shard_map/ppermute | solution.py:88
  146.3 7.3 %collective-permute-start.35 = (bf16[488,128]{1,0:T(8,128)(2,1)}, bf16[488,128]{1,0:T(8,128)(2,1)S(1)}, u32[]{:S(2)}, u32[]{:S(2)}) collective-permute-start(bf16[488,128]{1,0:T(8,128)(2,1)} %get-tuple-element.149), channel_id=1, source_target_pairs={{0,2},{2,0},{4,6},{6,4},{1,3},{3,1},{5,7},{7,5},{8,10},{10,8},{12,... | collective-permute-start | bytes 374792 | tf_op jit(solution)/shard_map/ppermute | solution.py:88
  146.4 7.3 %collective-permute-start.36 = (bf16[488,128]{1,0:T(8,128)(2,1)}, bf16[488,128]{1,0:T(8,128)(2,1)S(1)}, u32[]{:S(2)}, u32[]{:S(2)}) collective-permute-start(bf16[488,128]{1,0:T(8,128)(2,1)} %get-tuple-element.150), channel_id=1, source_target_pairs={{0,4},{2,6},{4,0},{6,2},{1,5},{3,7},{5,1},{7,3},{8,12},{10,14},{12... | collective-permute-start | bytes 374792 | tf_op jit(solution)/shard_map/ppermute | solution.py:88
  149.1 8.9 %collective-permute-start.37 = (bf16[488,128]{1,0:T(8,128)(2,1)}, bf16[488,128]{1,0:T(8,128)(2,1)S(1)}, u32[]{:S(2)}, u32[]{:S(2)}) collective-permute-start(bf16[488,128]{1,0:T(8,128)(2,1)} %get-tuple-element.151), channel_id=1, source_target_pairs={{0,6},{2,4},{4,2},{6,0},{1,7},{3,5},{5,3},{7,1},{8,14},{10,12},{12... | collective-permute-start | bytes 374792 | tf_op jit(solution)/shard_map/ppermute | solution.py:88
  149.9 19.7 %collective-permute-start.41 = (bf16[352,256]{1,0:T(8,128)(2,1)S(1)}, bf16[352,256]{1,0:T(8,128)(2,1)S(1)}, u32[]{:S(2)}, u32[]{:S(2)}) collective-permute-start(bf16[352,256]{1,0:T(8,128)(2,1)S(1)} %fusion.1), channel_id=1, source_target_pairs={{0,0},{2,8},{4,16},{6,24},{1,1},{3,9},{5,17},{7,25},{8,2},{10,10},... | collective-permute-start | bytes 540680 | tf_op jit(solution)/shard_map/ppermute | solution.py:787
  (58 other events, 363.2 us)

commit v3 on v2

--- a/solution.py
+++ b/solution.py
@@ -323,36 +323,6 @@
         ),
         name="hidden_grads",
     )(hg, w_down)
-
-
-def column_kernel(place_ref, wg_ref, wu_ref, wgt_ref, wut_ref, window, turned, sems):
-    span = window.shape[2]
-    part, width = wgt_ref.shape
-    at = (place_ref[0] * 2 + place_ref[1]) * part
-    start = jnp.minimum(at // 128 * 128, wg_ref.shape[1] - span)
-    cols = pl.ds(pl.multiple_of(start, 128), span)
-    copies = [
-        pltpu.make_async_copy(ref.at[:, cols], window.at[i], sems.at[i]) for i, ref in enumerate((wg_ref, wu_ref))
-    ]
-    for copy in copies:
-        copy.start()
-    for i, out_ref in enumerate((wgt_ref, wut_ref)):
-        copies[i].wait()
-        turned[...] = window[i].T
-        out_ref[...] = turned[pl.ds(pl.multiple_of(at - start, 32), part), :]
-
-
-def own_columns(place, w_gate, w_up, part):
-    width, ff = w_gate.shape
-    span = min(ff, -(-part // 128) * 128 + 128)
-    return call(
-        column_kernel,
-        [((part, width), BF16)] * 2,
-        [smem(), hbm(), hbm()],
-        (place, w_gate, w_up),
-        [pltpu.VMEM((2, width, span), BF16), pltpu.VMEM((span, width), BF16), pltpu.SemaphoreType.DMA((2,))],
-        0, 4 * width * span, "own_columns",
-    )
 
 
 def ffn_kernel(
@@ -411,10 +381,12 @@
     gm = mm(gb, wo[...], NT)
     gm_ref[...] = gm.astype(BF16)
     gmt_ref[...] = gm.T.astype(BF16)
+    tokens = gb.shape[0]
     for k, mgx_ref in enumerate(mgx_refs):
-        cols = mgx_ref.shape[1] - width
-        mgx_ref[:, :width] = mixed_ref[...]
-        mgx_ref[:, width:] = gb_cols[:, pl.ds(pl.multiple_of((place_ref[0] ^ k) * cols, cols), cols)]
+        cols = mgx_ref.shape[1]
+        for i in range(width // cols):
+            mgx_ref[i * tokens:(i + 1) * tokens, :] = mixed_ref[:, i * cols:(i + 1) * cols]
+        mgx_ref[width // cols * tokens:, :] = gb_cols[:, pl.ds(pl.multiple_of((place_ref[0] ^ k) * cols, cols), cols)]
 
 
 def feed_forward(place, h2, hg, gh, w_gate, w_up, w_down, resid, gain, w_out, mixed, n_rows):
@@ -424,7 +396,7 @@
     return call(
         ffn_kernel,
         [((tokens, width), BF16), ((1, width), F32), ((tokens, width), F32), ((tokens, width), BF16),
-         ((width, tokens), BF16)] + [((tokens, width + width // n_rows), BF16)] * n_rows,
+         ((width, tokens), BF16)] + [((tokens * (n_rows + 1), width // n_rows), BF16)] * n_rows,
         [smem()] + [vmem()] * 6 + [hbm()] * 4,
         (place, h2, hg, gh, resid, gain, mixed, w_gate, w_up, w_down, w_out),
         [pltpu.VMEM((tokens, width), F32), pltpu.VMEM((tokens, width), F32), pltpu.VMEM((tokens, width), BF16),
@@ -434,27 +406,41 @@
     )
 
 
-def weight_kernel(n_pieces, ordered, place_ref, wgt_ref, wut_ref, wd_ref, *refs):
-    h2_pieces, hg_pieces = refs[:n_pieces], refs[n_pieces:2 * n_pieces]
-    up_keep, up_send, down_keep, down_send, h2s, gos, wds, sems = refs[2 * n_pieces:]
+def weight_kernel(n_pieces, ordered, place_ref, wg_ref, wu_ref, wd_ref, go_other, *refs):
+    n_rows = n_pieces // 2
+    h2_pieces, hg_same, mgx = refs[:n_pieces], refs[n_pieces:n_pieces + n_rows], refs[n_pieces + n_rows:2 * n_pieces]
+    up_keep, up_send, *row_refs = refs[2 * n_pieces:-6]
+    h2s, gos, wds, window, turned, sems = refs[-6:]
     tokens, width = h2_pieces[0].shape
-    ff = wgt_ref.shape[0]
-    groups = [[], []]
+    ff, span = wds.shape[0], window.shape[2]
+    at = (place_ref[0] * 2 + place_ref[1]) * ff
+    start = jnp.minimum(at // 128 * 128, wg_ref.shape[1] - span)
+    cut = pl.ds(pl.multiple_of(start, 128), span)
+    groups = [[pltpu.make_async_copy(ref.at[:, cut], window.at[i], sems.at[2, i])] for i, ref in enumerate((wg_ref, wu_ref))]
+    groups += [[], []]
     for j in range(n_pieces):
         rows = pl.ds(j * tokens, tokens)
-        groups[0].append(pltpu.make_async_copy(h2_pieces[j], h2s.at[rows, :], sems.at[0, j]))
-        groups[1].append(pltpu.make_async_copy(
-            hg_pieces[j].at[:, pl.ds(width, width)], gos.at[rows, :], sems.at[1, j]))
-    at = pl.multiple_of((place_ref[0] * 2 + place_ref[1]) * ff, 32)
-    groups[1].append(pltpu.make_async_copy(wd_ref.at[pl.ds(at, ff), :], wds, sems.at[1, n_pieces]))
+        groups[2].append(pltpu.make_async_copy(h2_pieces[j], h2s.at[rows, :], sems.at[0, j]))
+        half = n_pieces // 2
+        go = hg_same[j].at[:, pl.ds(width, width)] if j < half else go_other.at[j - half]
+        groups[3].append(pltpu.make_async_copy(go, gos.at[rows, :], sems.at[1, j]))
+    groups[3].append(pltpu.make_async_copy(
+        wd_ref.at[pl.ds(pl.multiple_of(at, 32), ff), :], wds, sems.at[1, n_pieces]))
+    groups.append([
+        pltpu.make_async_copy(mgx[k], row_refs[k].at[pl.ds(ff, mgx[k].shape[0]), :], sems.at[3, k]) for k in range(n_rows)
+    ])
     for group in groups:
         for copy in group:
             copy.start()
-    for copy in groups[0]:
+    own = pl.ds(pl.multiple_of(at - start, 32), ff)
+    for i in range(2):
+        groups[i][0].wait()
+        turned[i] = window[i].T
+    for copy in groups[2]:
         copy.wait()
-    gate = mm(wgt_ref[...], h2s[...], NT)
-    up = mm(wut_ref[...], h2s[...], NT)
-    for copy in groups[1]:
+    gate = mm(turned[0, own, :], h2s[...], NT)
+    up = mm(turned[1, own, :], h2s[...], NT)
+    for copy in groups[3]:
         copy.wait()
     grad_hidden = mm(wds[...], gos[...], NT)
     sig = jax.nn.sigmoid(gate)
@@ -467,19 +453,21 @@
     cols = width // n_z
     half = cols // 2
     for slot, k in enumerate(halving_order(n_z)):
-        up_ref, down_ref, i = (up_keep, down_keep, slot) if slot < kept else (up_send, down_send, slot - kept)
+        up_ref, i = (up_keep, slot) if slot < kept else (up_send, slot - kept)
         if ordered:
             z, core = place_ref[2] ^ k, place_ref[1]
             first = pl.ds(pl.multiple_of(z * cols + core * half, half), half)
             other = pl.ds(pl.multiple_of(z * cols + (1 - core) * half, half), half)
-            straight = pl.ds(pl.multiple_of(z * cols, cols), cols)
             h2c = jnp.concatenate([h2s[:, first], h2s[:, other]], axis=1)
         else:
-            straight = slice(slot * cols, (slot + 1) * cols)
-            h2c = h2s[:, straight]
+            h2c = h2s[:, slot * cols:(slot + 1) * cols]
         up_ref[i, :ff, :] = mm(grad_gate, h2c).astype(BF16)
         up_ref[i, ff:, :] = mm(grad_up, h2c).astype(BF16)
-        down_ref[i] = mm(hidden, gos[:, straight]).astype(BF16)
+    for k, row_ref in enumerate(row_refs):
+        cols = row_ref.shape[1]
+        row_ref[:ff, :] = mm(hidden, gos[:, pl.ds(pl.multiple_of((place_ref[0] ^ k) * cols, cols), cols)]).astype(BF16)
+    for copy in groups[4]:
+        copy.wait()
 
 
 def halving_order(n):
@@ -491,29 +479,19 @@
     return order
 
 
-def halve(keep, got, axis, k):
-    while True:
-        total = keep.astype(F32) + got.astype(F32)
-        n = total.shape[0]
-        if n == 1:
-            return total[0]
-        k *= 2
-        keep, got = total[:n // 2], swap(total[n // 2:].astype(BF16), axis, k)
-
-
-def weight_grads(place, wgt, wut, w_down, h2_pieces, hg_pieces, n_z, ordered):
+def weight_grads(place, w_gate, w_up, w_down, h2_pieces, hg_same, go_other, mgx, n_z, ordered):
     n = len(h2_pieces)
-    tokens = h2_pieces[0].shape[0]
-    ff, width = wgt.shape
+    tokens, width = h2_pieces[0].shape
+    ff = w_gate.shape[1] // n
+    span = min(w_gate.shape[1], -(-ff // 128) * 128 + 128)
     total = n * tokens
-    up, down = ((n_z // 2, 2 * ff, width // n_z), BF16), ((n_z // 2, ff, width // n_z), BF16)
     return call(
         functools.partial(weight_kernel, n, ordered),
-        [up, up, down, down],
-        [smem(), vmem(), vmem(), hbm()] + [hbm()] * (2 * n),
-        (place, wgt, wut, w_down, *h2_pieces, *hg_pieces),
+        [((n_z // 2, 2 * ff, width // n_z), BF16)] * 2 + [((ff + p.shape[0], p.shape[1]), BF16) for p in mgx],
+        [smem()] + [hbm()] * (4 + 2 * n),
+        (place, w_gate, w_up, w_down, go_other, *h2_pieces, *hg_same, *mgx),
         [pltpu.VMEM((total, width), BF16), pltpu.VMEM((total, width), BF16), pltpu.VMEM((ff, width), BF16),
-         pltpu.SemaphoreType.DMA((2, n + 1))],
+         pltpu.VMEM((2, width, span), BF16), pltpu.VMEM((2, span, width), BF16), pltpu.SemaphoreType.DMA((4, n + 1))],
         12 * total * width * ff, 6 * width * ff + 4 * total * width, "weight_grads",
     )
 
@@ -524,85 +502,104 @@
     return pl.ds(pl.multiple_of(((place_ref[2] ^ k) * 2 + place_ref[1]) * cols, cols), cols)
 
 
-def out_kernel(n_pieces, n_out, ordered, place_ref, mine_ref, other_ref, *refs):
-    hg_pieces = refs[:n_pieces]
-    out_refs, (h1_ref, wide, thin, sems) = refs[n_pieces:-4], refs[-4:]
-    cols = out_refs[0].shape[1]
-    n_rows, tokens, both = mine_ref.shape
-    part = thin.shape[1]
+def slab_kernel(n_out, ordered, place_ref, h1_other, *refs):
+    *hg_same, h1_ref, sems = refs
+    n_same = len(hg_same)
+    tokens = h1_other.shape[1]
+    cols = h1_ref.shape[1] // n_out
     copies = []
-    for j, piece in enumerate(hg_pieces):
+    for j in range(2 * n_same):
+        piece = hg_same[j] if j < n_same else h1_other.at[j - n_same]
         for k in range(n_out):
             copies.append(pltpu.make_async_copy(
                 piece.at[:, own_cut(ordered, place_ref, k, cols)],
                 h1_ref.at[pl.ds(j * tokens, tokens), pl.ds(k * cols, cols)], sems.at[j, k]))
-    if ordered:
-        for copy in copies:
-            copy.start()
+    for copy in copies:
+        copy.start()
+    for copy in copies:
+        copy.wait()
+
+
+def own_slab(place, hg_same, h1_other, n_out, cols, ordered):
+    n, tokens, width = h1_other.shape
+    if not ordered:
+        return jnp.concatenate([piece[:, :width] for piece in hg_same] + [h1_other.reshape(-1, width)], axis=0)
+    return call(
+        functools.partial(slab_kernel, n_out, ordered),
+        [((2 * n * tokens, n_out * cols), BF16)],
+        [smem()] + [hbm()] * (1 + n),
+        (place, h1_other, *hg_same),
+        [pltpu.SemaphoreType.DMA((2 * n, n_out))],
+        0, 4 * n * tokens * n_out * cols, "own_slab",
+    )[0]
+
+
+def out_kernel(n_out, ordered, place_ref, mine_ref, other_ref, keep_ref, send_ref, wide, thin):
+    kept, _, cols = keep_ref.shape
+    offsets = halving_order(n_out) if ordered else list(range(n_out))
+    n_rows, _, part = mine_ref.shape
+    tokens = wide.shape[0] // (2 * n_rows)
+    per_block = part // cols
     for i, ref in enumerate((mine_ref, other_ref)):
         for j in range(n_rows):
             rows = slice((i * n_rows + j) * tokens, (i * n_rows + j + 1) * tokens)
-            thin[rows, :] = ref[j, :, both - part:]
-            for k in range(n_out):
-                wide[rows, k * cols:(k + 1) * cols] = ref[j, :, own_cut(ordered, place_ref, k, cols)]
+            thin[rows, :] = ref[j, n_rows * tokens:, :]
+            for i_out, k in enumerate(offsets):
+                if ordered:
+                    where = pl.ds(pl.multiple_of((place_ref[2] ^ k) * tokens, tokens), tokens)
+                    cut = pl.ds(pl.multiple_of(place_ref[1] * cols, cols), cols)
+                else:
+                    where = slice(k // per_block * tokens, (k // per_block + 1) * tokens)
+                    cut = slice(k % per_block * cols, (k % per_block + 1) * cols)
+                wide[rows, i_out * cols:(i_out + 1) * cols] = ref[j, where, cut]
     full = mm(thin[...].T, wide[...]).astype(BF16)
-    for k in range(n_out):
-        out_refs[k][...] = full[:, k * cols:(k + 1) * cols]
-    if ordered:
-        for copy in copies:
-            copy.wait()
-
-
-def out_grads(place, mine, other, hg_pieces, width, n_out, cols, ordered):
-    n = len(hg_pieces)
-    n_rows, tokens, both = mine.shape
-    part = both - width
+    for k in range(kept):
+        keep_ref[k] = full[:, k * cols:(k + 1) * cols]
+        send_ref[k] = full[:, (kept + k) * cols:(kept + k + 1) * cols]
+
+
+def out_grads(place, mine, other, tokens, n_out, cols, ordered):
+    n_rows, both, part = mine.shape
     total = 2 * n_rows * tokens
-    *parts, h1_slab = call(
-        functools.partial(out_kernel, n, n_out, ordered),
-        [((part, cols), BF16)] * n_out + [((total, n_out * cols), BF16)],
-        [smem(), vmem(), vmem()] + [hbm()] * n,
-        (place, mine, other, *hg_pieces),
-        [pltpu.VMEM((total, n_out * cols), BF16), pltpu.VMEM((total, part), BF16), pltpu.SemaphoreType.DMA((n, n_out))],
-        2 * total * part * n_out * cols, 4 * total * n_out * cols, "out_grads",
-    )
-    if not ordered:
-        h1_slab = jnp.concatenate([piece[:, :width] for piece in hg_pieces], axis=0)
-    return parts, h1_slab
-
-
-def fact_kernel(n_out, head, ordered, h1_ref, mine_ref, other_ref, *refs):
-    carried, out_refs, thin = refs[:n_out], refs[n_out:-1], refs[-1]
+    return call(
+        functools.partial(out_kernel, n_out, ordered),
+        [((n_out // 2, part, cols), BF16)] * 2,
+        [smem(), vmem(), vmem()],
+        (place, mine, other),
+        [pltpu.VMEM((total, n_out * cols), BF16), pltpu.VMEM((total, part), BF16)],
+        2 * total * part * n_out * cols, 4 * n_rows * both * part, "out_grads",
+    )
+
+
+def fact_kernel(head, ordered, h1_ref, mine_ref, other_ref, *refs):
+    out_refs, thin = refs[:-1], refs[-1]
     cols = out_refs[0].shape[1]
     tokens = mine_ref.shape[2]
-    rows = mine_ref.shape[1]
     parts = [ref[j] for ref in (mine_ref, other_ref) for j in range(ref.shape[0])]
     for j, part in enumerate(parts):
         thin[:, j * tokens:(j + 1) * tokens] = part[head:, :]
     full = mm(thin[...], h1_ref[...]).astype(BF16)
-    for k in range(n_out):
-        out_refs[k][head:rows, :] = full[:, k * cols:(k + 1) * cols]
-        out_refs[k][rows:, :] = carried[k][...]
+    for k, out_ref in enumerate(out_refs):
+        out_ref[head:, :] = full[:, k * cols:(k + 1) * cols]
     if ordered:
         half = head // 2
         gains = tree_sum([p[:half].astype(F32) + p[half:head].astype(F32) for p in parts])
         high = gains.astype(BF16)
         low = (gains - high.astype(F32)).astype(BF16)
-        for k in range(n_out):
-            out_refs[k][:half, :] = high
-            out_refs[k][half:head, :] = low
-
-
-def fact_grads(h1_slab, mine, other, carried, head, ordered):
+        for out_ref in out_refs:
+            out_ref[:half, :] = high
+            out_ref[half:head, :] = low
+
+
+def fact_grads(h1_slab, mine, other, head, n_out, ordered):
     n_rows, rows, tokens = mine.shape
-    n_out = len(carried)
-    part, cols = carried[0].shape
     total = 2 * n_rows * tokens
+    cols = h1_slab.shape[1] // n_out
     return call(
-        functools.partial(fact_kernel, n_out, head, ordered),
-        [((rows + part, cols), BF16)] * n_out,
-        [vmem()] * (3 + n_out),
-        (h1_slab, mine, other, *carried),
+        functools.partial(fact_kernel, head, ordered),
+        [((rows, cols), BF16)] * n_out,
+        [vmem()] * 3,
+        (h1_slab, mine, other),
         [pltpu.VMEM((rows - head, total), BF16)],
         2 * total * rows * n_out * cols, 2 * total * n_out * cols, "fact_grads",
     )
@@ -722,74 +719,107 @@
     kv_pieces = []
     for part in kv_z:
         kv_pieces += [part, swap(part, "core", 1)]
-    wgt, wut = own_columns(place, w_gate, w_up, ff_part)
     hg_same = [hg] + others([hg] * n_rows, ROW, n_rows)
-    h2, mixed, resid, lse = attend(after(q, wgt), bias, w_out, x, gain_two, kv_pieces)
+    h2, mixed, resid, lse = attend(q, bias, w_out, x, gain_two, kv_pieces)
     h2_same = [h2] + others([h2] * n_rows, ROW, n_rows)
-    hg_pieces = along_core(after(hg_same, h2))
+    hg_same = after(hg_same, h2)
+    go_other = swap(jnp.stack([part[:, width:] for part in hg_same]), "core", 1)
     block_out, gain_two_part, gres, gm, gmt, *mgx = feed_forward(
         place, h2, after(hg, hg_same), gh, w_gate, w_up, w_down, resid, gain_two, w_out, mixed, n_rows
     )
-    h2_pieces = along_core(after(h2_same, gm))
-    up_keep, up_send, down_keep, down_send = weight_grads(
-        place, wgt, wut, w_down, h2_pieces, hg_pieces, n_z, ordered
+    h2_pieces = along_core(after(h2_same, gm, go_other))
+    up_keep, up_send, *row_out = weight_grads(
+        place, w_gate, w_up, w_down, h2_pieces, hg_same, go_other, mgx, n_z, ordered
     )
     if not ordered:
         turns = jnp.asarray(halving_order(n_z), jnp.int32) ^ z
         cores = jnp.arange(2, dtype=jnp.int32) ^ core
         up = jnp.take(jnp.concatenate([up_keep, up_send]), turns, axis=0)
         up = jnp.take(up.reshape(n_z, 2 * ff_part, 2, own_cols), cores, axis=2).reshape(up.shape)
-        down = jnp.concatenate([down_keep, down_send]).transpose(1, 0, 2)
-        down = down.reshape(per, ff_part // per, n_rows, width // n_rows).transpose(0, 2, 1, 3)
-        down = jnp.take(down.reshape(n_z, ff_part // per, width // n_rows), turns, axis=0)
-        up_keep, up_send, down_keep, down_send = up[:n_z // 2], up[n_z // 2:], down[:n_z // 2], down[n_z // 2:]
-
-    up_got, down_got = swap(up_send, "z", 1), swap(down_send, "z", 1)
-    mg_same = [mgx[0]] + others(after(mgx, up_send), ROW, n_rows)
-    gq, gkv_own, gkv_send = attend_back(q, qt, after(gm, up_send), gmt, lse, bias, qf, cosine, sine, kv_pieces)
-    gkv_send, mg_same, up_got, down_got = lax.optimization_barrier((gkv_send, mg_same, up_got, down_got))
+        up_keep, up_send = up[:n_z // 2], up[n_z // 2:]
+
+    up_got = swap(up_send, "z", 1)
+    row_same = [row_out[0]] + others(row_out, ROW, n_rows)
+    gm_in, hg_same = after((gm, hg_same), up_send)
+    h1_other = swap(jnp.stack([part[:, :width] for part in hg_same]), "core", 1)
+    gq, gkv_own, gkv_send = attend_back(q, qt, gm_in, gmt, lse, bias, qf, cosine, sine, kv_pieces)
+    gkv_send, h1_other, up_got = lax.optimization_barrier((gkv_send, h1_other, up_got))
     gkv_got = swap(gkv_send, "core", 1)
+    row_same = after(row_same, gkv_got)
     gkv_z = [(gkv_own[k].astype(F32) + gkv_got[k].astype(F32)).astype(BF16) for k in range(n_z)]
     kv_parts = [gkv_z[0]] + others(gkv_z, "z", n_z)
-
-    def own_blocks(parts):
-        if ordered:
-            return parts
-        parts = jnp.take(jnp.stack(parts), (jnp.arange(n_z, dtype=jnp.int32) ^ z) * 2 + core, axis=0)
+    mg_mine, mg_other = both_cores([part[ff_part:] for part in row_same])
+    if ordered:
+        down = jnp.stack([part[:ff_part] for part in row_same])
+        down = jnp.take(down, jnp.asarray(halving_order(n_z), jnp.int32) ^ z ^ row, axis=0)
+        down_keep, down_send = down[:n_z // 2], down[n_z // 2:]
+        down_got = swap(down_send, "z", 1)
+    if ordered:
+        kv_parts, down_got = lax.optimization_barrier((kv_parts, down_got))
+
+    def own_blocks(parts, offsets):
+        parts = jnp.take(parts, (jnp.asarray(offsets, jnp.int32) ^ z) * 2 + core, axis=0)
         return [parts[k] for k in range(n_z)]
 
-    out_parts, h1_slab = out_grads(place, *both_cores(mg_same), hg_pieces, width, n_out, own_cols, ordered)
-    gq = after(gq, out_parts)
-    up_keep, down_keep = after((up_keep, down_keep), gkv_z)
+    out_keep, out_send = out_grads(place, mg_mine, mg_other, tokens, n_out, own_cols, ordered)
+    if not ordered:
+        out_parts = own_blocks(jnp.concatenate([out_keep, out_send]), halving_order(n_z))
+        out_keep, out_send = jnp.stack(out_parts[:n_z // 2]), jnp.stack(out_parts[n_z // 2:])
+    out_got = swap(out_send, "z", 1)
+    gq, out_got = after((gq, out_got), kv_parts)
+
+    def add_up(keep, got, hold, step=1):
+        total = keep.astype(F32) + got.astype(F32)
+        n = total.shape[0]
+        while n > 1:
+            n //= 2
+            step *= 2
+            kept, got = total[:n], swap(total[n:].astype(BF16), "z", step)
+            total = (after(kept, *hold) if n == 1 else kept) + got.astype(F32)
+        return total[0]
+
+    side = (out_keep.shape[0], -1, 2 * own_cols)
+    ffn_keep = [up_keep, down_keep, out_keep.reshape(side)] if ordered else [up_keep, out_keep.reshape(side)]
+    ffn_got = [up_got, down_got, out_got.reshape(side)] if ordered else [up_got, out_got.reshape(side)]
+    ffn_keep, ffn_got = jnp.concatenate(ffn_keep, axis=1), jnp.concatenate(ffn_got, axis=1)
     grad_inputs, *gfx = input_grads(
         place, gq, kv_parts, w_fact_t, x, s1, gain_one, gres, gain_two_part, cosine, sine, n_rows
     )
-    up_total = halve(up_keep, up_got, "z", 1)
-    down_total = halve(down_keep, down_got, "z", 1)
     head = gfx[0].shape[0] - w_fact.shape[1] // n_rows
-    gf_all = both_cores([gfx[0]] + others(gfx, ROW, n_rows))
-    tail_parts = own_blocks(fact_grads(h1_slab, *gf_all, out_parts, head, ordered))
+    gf_same = [gfx[0]] + others(gfx, ROW, n_rows)
+    h1_slab = own_slab(place, hg_same, after(h1_other, gfx[0]), n_out, own_cols, ordered)
+    gf_all = both_cores(after(gf_same, h1_slab))
+    tail_parts = fact_grads(h1_slab, *gf_all, head, n_out, ordered)
+    if not ordered:
+        tail_parts = own_blocks(jnp.stack(tail_parts), list(range(n_z)))
+    total = add_up(ffn_keep, ffn_got, tail_parts)
     tail_got = others(tail_parts, "z", n_z)
-
-    up_total, down_total = after((up_total, down_total), tail_parts)
+    up_total = total[:2 * ff_part]
+    grad_out = total[-own_cols * out_keep.shape[1] // (2 * own_cols):].reshape(out_keep.shape[1:]).T
     mine, other = up_total[:, :own_cols], swap(up_total[:, own_cols:].astype(BF16), "core", 1).astype(F32)
     first = jnp.where(core == 0, mine, other)
     second = jnp.where(core == 0, other, mine)
     grad_gate = jnp.concatenate([first[:ff_part], second[:ff_part]], axis=0).T
     grad_up = jnp.concatenate([first[ff_part:], second[ff_part:]], axis=0).T
 
-    moves = []
-    for r in range(n_rows):
-        for c in range(2):
-            for p in range(n_z):
-                b, s = p // n_rows, p % n_rows
-                moves.append((r * n_ctx + 2 * p + c, s * n_ctx + (r * 2 + c) * per + b))
-    grad_down = lax.ppermute(down_total.astype(BF16), ROW + CTX, moves).astype(F32)
-
-    tail_got = after(tail_got, grad_gate, grad_up)
+    if ordered:
+        grad_down = total[2 * ff_part:3 * ff_part]
+    else:
+        down = jnp.stack([part[:ff_part] for part in row_out])
+        down = jnp.take(down, jnp.arange(n_rows, dtype=jnp.int32) ^ row, axis=0)
+        down = down.reshape(n_rows, per, ff_part // per, width // n_rows).transpose(1, 0, 2, 3)
+        down = lax.psum_scatter(down.reshape(n_z, ff_part // per, -1), "z", scatter_dimension=0)
+        moves = []
+        for r in range(n_rows):
+            for c in range(2):
+                for p in range(n_z):
+                    b, s = p // n_rows, p % n_rows
+                    moves.append((r * n_ctx + 2 * p + c, s * n_ctx + (r * 2 + c) * per + b))
+        grad_down = lax.ppermute(down, ROW + CTX, moves).astype(F32)
+
+    tail_parts = after(tail_parts, grad_gate, grad_up, grad_out)
     tail = tree_sum([part.astype(F32) for part in [tail_parts[0]] + tail_got])
-    rows = gfx[0].shape[0]
-    grad_fact, grad_out = tail[head:rows].T, tail[rows:].T
+    grad_fact = tail[head:].T
     if ordered:
         gains = (tail[:head // 2] + tail[head // 2:head]).reshape(2, width)
     else:

time: 171 us -> 164 us (0.959)
  waiting for transfers between devices: 44.2 us -> 31.7 us
  local copies, waits for them, and re-layouts: 5.86 us -> 10.9 us
  starting transfers between devices: 38.9 us -> 36.6 us
  other arithmetic: 7.49 us -> 9.73 us
    ppermute x1 -> x0, waiting for transfers between devices: 9.49 us -> none  [body(): lax.ppermute(down_total.astype(BF16), ROW + CTX, moves).astype(F32)]
    reshape x0 -> x4, local copies, waits for them, and re-layouts: none -> 3.22 us  [the longest x1 1.75 us: body(): out_keep.reshape(side)]
    ppermute x41 -> x39, waiting for transfers between devices: 34.7 us -> 31.7 us  [swap(): return lax.ppermute(value, axis, [(j, j ^ k) for j in range(size)])]
    add x2, other arithmetic: 0.21 us -> 2.79 us  [the longest x1 1.6 us: add_up(): total = keep.astype(F32) + got.astype(F32)]
    ppermute x1 -> x0, starting transfers between devices: 1.91 us -> none  [body(): lax.ppermute(down_total.astype(BF16), ROW + CTX, moves).astype(F32)]
    ppermute x41 -> x39, starting transfers between devices: 37 us -> 36.6 us  [swap(): return lax.ppermute(value, axis, [(j, j ^ k) for j in range(size)])]
    unnamed x81 -> x94, local copies, waits for them, and re-layouts: 4.47 us -> 4.5 us
  transfers between devices with their start and end apart: 42 -> 39, of which waited for: 13 -> 14; matrix products, arithmetic and copies ran while one was open for 4% -> 6% of each run, Pallas kernels for 33% -> 35%
where the time goes in v3:
time: 164 us; the launch traced here: 162 us
  Pallas kernels  70.8 us (43%)
  starting transfers between devices  36.6 us (22%)
  waiting for transfers between devices  31.7 us (19%)
  local copies, waits for them, and re-layouts  10.9 us (7%)
  other arithmetic  9.73 us (6%)
  between operations  1.98 us (1%)
    pallas_call x9, Pallas kernels, call(): pl.pallas_call(kernel, out_shape=[jax.ShapeDtypeStruct(s, d) for s, d in...  66 us
    ppermute x39, starting transfers between devices, swap(): return lax.ppermute(value, axis, [(j, j ^ k) for j in range(size)])  36.6 us
    ppermute x39, waiting for transfers between devices, swap(): return lax.ppermute(value, axis, [(j, j ^ k) for j in range(size)])  31.7 us
    pallas_call x1, Pallas kernels, hidden_grads(): pl.pallas_call(hidden_kernel, grid=(ff // chunk,), in_specs=[pl.BlockSpec...  4.88 us
    unnamed x94, local copies, waits for them, and re-layouts  4.5 us
  transfers between devices with their start and end apart: 39, of which 14 were waited for; matrix products, arithmetic and copies ran while one was open for 6% of the time, Pallas kernels for 35%

profile of v3, /device:TPU:3, one launch (start us, length us, event | category | flops | bytes accessed | tf_op | source)
XLA Modules:
  0.0 161.7 jit_solution(122521414267313092)
XLA Ops:
  2.5 3.5 %factors.1 = (bf16[128,2048]{1,0:T(8,128)(2,1)}, f32[128,1]{1,0:T(8,128)}, bf16[128,1024]{1,0:T(8,128)(2,1)}, bf16[1024,128]{1,0:T(8,128)(2,1)}, f32[480,128]{1,...) custom-call(bf16[128,1024]{1,0:T(8,128)(2,1)} %bitcast.111, ...), custom_call_target="tpu_custom_call" | custom-call | flops 209715200 | bytes 1638400 | tf_op jit(solution)/shard_map/factors/pallas_call | solution.py:47
  7.4 2.3 %collective-permute-start.1 = (bf16[320,128]{1,0:T(8,128)(2,1)}, bf16[320,128]{1,0:T(8,128)(2,1)S(1)}, u32[]{:S(2)}, u32[]{:S(2)}) collective-permute-start(bf16[320,128]{1,0:T(8,128)(2,1)} %get-tuple-element.92.refs_5_.refs_9_), channel_id=1, source_target_pairs={{0,4},{2,6},{4,0},{6,2},{1,5},{3,7},{5,1},{7,3},{8,12},{10,14},{12... | collective-permute-start | bytes 245768 | tf_op jit(solution)/shard_map/ppermute | solution.py:88
  12.5 4.9 %hidden_grads.1.gh_ref = f32[128,2816]{1,0:T(8,128)} custom-call(bf16[128,2048]{1,0:T(8,128)(2,1)} %get-tuple-element.128.go_ref.hg_ref.refs_8_.refs_0_, bf16[2816,1024]{1,0:T(8,128)(2,1)} %wd_ref.3), custom_call_target="tpu_custom_call" | custom-call | flops 738197504 | bytes 7208960 | tf_op jit(solution)/shard_map/hidden_grads/pallas_call | solution.py:314
  17.4 2.4 %collective-permute-start.3 = (bf16[320,128]{1,0:T(8,128)(2,1)S(1)}, bf16[320,128]{1,0:T(8,128)(2,1)S(1)}, u32[]{:S(2)}, u32[]{:S(2)}) collective-permute-start(bf16[320,128]{1,0:T(8,128)(2,1)S(1)} %copy-done.33), channel_id=1, source_target_pairs={{0,1},{1,0},{2,3},{3,2},{4,5},{5,4},{6,7},{7,6},{8,9},{9,8},{10,11... | collective-permute-start | bytes 245768 | tf_op jit(solution)/shard_map/ppermute | solution.py:88
  23.0 11.5 %attend.1 = (bf16[128,1024]{1,0:T(8,128)(2,1)}, bf16[128,1024]{1,0:T(8,128)(2,1)}, f32[128,1024]{1,0:T(8,128)}, f32[8,256,1]{2,1,0:T(8,128)}) custom-call(bf16[128,1024]{1,0:T(8,128)(2,1)} %get-tuple-element.89.refs_0_, f32[128,1024]{1,0:T(8,128)} %and_select_fusion.refs_1_.refs_5_, bf16[1024,1024]{1,0:T(8,128)(2,1)} %wo_hbm.1, bf16[128,1024]{1,0:T(8,128)(2,1)} %bitcast.112, ...), custom_call_target="tpu_custom_call" | custom-call | flops 536870912 | bytes 2097152 | tf_op jit(solution)/shard_map/attend/pallas_call | solution.py:47
  36.0 1.7 %collective-permute-start.10 = (bf16[4,128,1024]{2,1,0:T(8,128)(2,1)}, bf16[4,128,1024]{2,1,0:T(8,128)(2,1)S(1)}, u32[]{:S(2)}, u32[]{:S(2)}) collective-permute-start(bf16[4,128,1024]{2,1,0:T(8,128)(2,1)} %pad_maximum_fusion.1), channel_id=1, source_target_pairs={{0,1},{1,0},{2,3},{3,2},{4,5},{5,4},{6,7},{7,6},{8,9},{9,8},{10,11... | collective-permute-start | bytes 3145736 | tf_op jit(solution)/shard_map/ppermute | solution.py:88
  41.0 14.5 %feed_forward.1 = (bf16[128,1024]{1,0:T(8,128)(2,1)}, f32[1,1024]{1,0:T(1,128)}, f32[128,1024]{1,0:T(8,128)}, bf16[128,1024]{1,0:T(8,128)(2,1)}, bf16[1024,128]{...) custom-call(s32[3]{0:T(128)} %pad_add_fusion.place_ref, ...), custom_call_target="tpu_custom_call" | custom-call | flops 3690987520 | bytes 17301504 | tf_op jit(solution)/shard_map/feed_forward/pallas_call | solution.py:47
  59.5 10.1 %weight_grads.1 = (bf16[2,704,256]{2,1,0:T(8,128)(2,1)}, bf16[2,704,256]{2,1,0:T(8,128)(2,1)}, bf16[992,256]{1,0:T(8,128)(2,1)}, bf16[992,256]{1,0:T(8,128)(2,1)...) custom-call(s32[3]{0:T(128)} %pad_add_fusion.place_ref, bf16[1024,2816]{1,0:T(8,128)(2,1)} %wg_ref.1, ...), custom_call_target="tpu_custom_call" | custom-call | flops 4429185024 | bytes 6356992 | tf_op jit(solution)/shard_map/weight_grads/pallas_call | solution.py:47
  74.8 13.5 %attend_back.1 = (f32[480,128]{1,0:T(8,128)}, bf16[4,320,128]{2,1,0:T(8,128)(2,1)}, bf16[4,320,128]{2,1,0:T(8,128)(2,1)}) custom-call(bf16[128,1024]{1,0:T(8,128)(2,1)} %get-tuple-element.89.refs_0_, bf16[1024,128]{1,0:T(8,128)(2,1)} %get-tuple-element.105.refs_1_, bf16[128,1024]{1,0:T(8,128)(2,1)} %get-tuple-element.116.refs_2_, ...), custom_call_target="tpu_custom_call" | custom-call | flops 1342177280 | bytes 524288 | tf_op jit(solution)/shard_map/attend_back/pallas_call | solution.py:47
  90.5 5.5 %collective-permute-done.20 = bf16[992,256]{1,0:T(8,128)(2,1)S(1)} collective-permute-done((bf16[992,256]{1,0:T(8,128)(2,1)S(1)}, bf16[992,256]{1,0:T(8,128)(2,1)S(1)}, u32[]{:S(2)}, u32[]{:S(2)}) %collective-permute-start.20) | collective-permute-done | bytes 507936 | tf_op jit(solution)/shard_map/ppermute | solution.py:88
  97.1 1.6 %collective-permute-start.24 = (bf16[4,640,256]{2,1,0:T(8,128)(2,1)S(1)}, bf16[4,640,256]{2,1,0:T(8,128)(2,1)}, u32[]{:S(2)}, u32[]{:S(2)}) collective-permute-start(bf16[4,640,256]{2,1,0:T(8,128)(2,1)S(1)} %pad_maximum_fusion.mine_ref), channel_id=1, source_target_pairs={{0,1},{1,0},{2,3},{3,2},{4,5},{5,4},{6,7},{7,6},{8,9},{9,8},{10,11... | collective-permute-start | bytes 3932168 | tf_op jit(solution)/shard_map/ppermute | solution.py:88
  101.5 3.0 %out_grads.1 = (bf16[2,256,128]{2,1,0:T(8,128)(2,1)}, bf16[2,256,128]{2,1,0:T(8,128)(2,1)}) custom-call(s32[3]{0:T(128)} %pad_add_fusion.place_ref, bf16[4,640,256]{2,1,0:T(8,128)(2,1)} %copy-done.3, bf16[4,640,256]{2,1,0:T(8,128)(2,1)} %collective-permute-done.24.other_ref), custom_call_target="tpu_custom_call" | custom-call | flops 268435456 | bytes 2621440 | tf_op jit(solution)/shard_map/out_grads/pallas_call | solution.py:47
  106.7 3.2 %collective-permute-start.27 = (bf16[320,128]{1,0:T(8,128)(2,1)S(1)}, bf16[320,128]{1,0:T(8,128)(2,1)S(1)}, u32[]{:S(2)}, u32[]{:S(2)}) collective-permute-start(bf16[320,128]{1,0:T(8,128)(2,1)S(1)} %get-tuple-element.178), channel_id=1, source_target_pairs={{0,4},{2,6},{4,0},{6,2},{1,5},{3,7},{5,1},{7,3},{8,12},{10,14},{12... | collective-permute-start | bytes 245768 | tf_op jit(solution)/shard_map/ppermute | solution.py:88
  109.9 5.9 %collective-permute-done.26.refs_1_ = bf16[320,128]{1,0:T(8,128)(2,1)S(1)} collective-permute-done((bf16[320,128]{1,0:T(8,128)(2,1)S(1)}, bf16[320,128]{1,0:T(8,128)(2,1)S(1)}, u32[]{:S(2)}, u32[]{:S(2)}) %collective-permute-start.26) | collective-permute-done | bytes 81952 | tf_op jit(solution)/shard_map/ppermute | solution.py:88
  115.8 4.7 %collective-permute-done.28.refs_3_ = bf16[320,128]{1,0:T(8,128)(2,1)S(1)} collective-permute-done((bf16[320,128]{1,0:T(8,128)(2,1)S(1)}, bf16[320,128]{1,0:T(8,128)(2,1)S(1)}, u32[]{:S(2)}, u32[]{:S(2)}) %collective-permute-start.28) | collective-permute-done | bytes 81952 | tf_op jit(solution)/shard_map/ppermute | solution.py:88
  120.5 1.7 %reshape.342 = bf16[2,128,256]{2,1,0:T(8,128)(2,1)} reshape(bf16[2,256,128]{2,1,0:T(8,128)(2,1)} %get-tuple-element.163) | data formatting | bytes 262144 | tf_op jit(solution)/shard_map/reshape | solution.py:782
  123.0 1.6 convert_add_fusion
  124.8 4.1 %input_grads.1 = (f32[128,1024]{1,0:T(8,128)}, bf16[232,128]{1,0:T(8,128)(2,1)}, bf16[232,128]{1,0:T(8,128)(2,1)}, bf16[232,128]{1,0:T(8,128)(2,1)}, bf16[232,128]{1,0:T(8,128)(2,1)}) custom-call(s32[3]{0:T(128)} %pad_add_fusion.place_ref, f32[480,128]{1,0:T(8,128)} %get-tuple-element.143.gq_ref, bf16[320,128]{1,0:T(8,128)(2,1)} %get-tuple-element.139.refs_0_, ...), custom_call_target="tpu_custom_call" | custom-call | flops 209715200 | bytes 1638400 | tf_op jit(solution)/shard_map/input_grads/pallas_call | solution.py:47
  131.5 3.3 %own_slab.1.h1_ref = bf16[1024,512]{1,0:T(8,128)(2,1)} custom-call(s32[3]{0:T(128)} %pad_add_fusion.place_ref, bf16[4,128,1024]{2,1,0:T(8,128)(2,1)} %copy-done.12, bf16[128,2048]{1,0:T(8,128)(2,1)} %get-tuple-element.128.go_ref.hg_ref.refs_8_.refs_0_, bf16[128,2048]{1,0:T(8,128)(2,1)} %copy-done.4, bf16[128,2048]{1,0:T(8,128)(2,1)} %copy-done.6, ...), custom_call_target="tpu_custom_call" | custom-call | bytes 1048576 | tf_op jit(solution)/shard_map/own_slab/pallas_call | solution.py:47
  135.1 2.4 %collective-permute-start.33 = (bf16[4,232,128]{2,1,0:T(8,128)(2,1)S(1)}, bf16[4,232,128]{2,1,0:T(8,128)(2,1)S(1)}, u32[]{:S(2)}, u32[]{:S(2)}) collective-permute-start(bf16[4,232,128]{2,1,0:T(8,128)(2,1)S(1)} %pad_maximum_fusion.4.mine_ref), channel_id=1, source_target_pairs={{0,1},{1,0},{2,3},{3,2},{4,5},{5,4},{6,7},{7,6},{8,9},{9,8},{10,11... | collective-permute-start | bytes 712712 | tf_op jit(solution)/shard_map/ppermute | solution.py:88
  139.3 2.5 %fact_grads.1 = (bf16[232,128]{1,0:T(8,128)(2,1)}, bf16[232,128]{1,0:T(8,128)(2,1)}, bf16[232,128]{1,0:T(8,128)(2,1)}, bf16[232,128]{1,0:T(8,128)(2,1)}) custom-call(bf16[1024,512]{1,0:T(8,128)(2,1)} %own_slab.1.h1_ref, bf16[4,232,128]{2,1,0:T(8,128)(2,1)} %copy-done.14, bf16[4,232,128]{2,1,0:T(8,128)(2,1)} %copy-done.29), custom_call_target="tpu_custom_call" | custom-call | flops 243269632 | bytes 1048576 | tf_op jit(solution)/shard_map/fact_grads/pallas_call | solution.py:47
  141.7 1.9 %collective-permute-start.37 = (bf16[232,128]{1,0:T(8,128)(2,1)}, bf16[232,128]{1,0:T(8,128)(2,1)S(1)}, u32[]{:S(2)}, u32[]{:S(2)}) collective-permute-start(bf16[232,128]{1,0:T(8,128)(2,1)} %get-tuple-element.160), channel_id=1, source_target_pairs={{0,4},{2,6},{4,0},{6,2},{1,5},{3,7},{5,1},{7,3},{8,12},{10,14},{12... | collective-permute-start | bytes 178184 | tf_op jit(solution)/shard_map/ppermute | solution.py:88
  143.6 1.6 collective-permute-start.38
  145.3 10.0 %collective-permute-done.34 = bf16[1,1184,256]{2,1,0:T(8,128)(2,1)} collective-permute-done((bf16[1,1184,256]{2,1,0:T(8,128)(2,1)S(1)}, bf16[1,1184,256]{2,1,0:T(8,128)(2,1)}, u32[]{:S(2)}, u32[]{:S(2)}) %collective-permute-start.34) | collective-permute-done | bytes 606240 | tf_op jit(solution)/shard_map/ppermute | solution.py:88
  (212 shorter events, 42.3 us)
Async XLA Ops:
  7.4 10.0 %collective-permute-start.1 = (bf16[320,128]{1,0:T(8,128)(2,1)}, bf16[320,128]{1,0:T(8,128)(2,1)S(1)}, u32[]{:S(2)}, u32[]{:S(2)}) collective-permute-start(bf16[320,128]{1,0:T(8,128)(2,1)} %get-tuple-element.92.refs_5_.refs_9_), channel_id=1, source_target_pairs={{0,4},{2,6},{4,0},{6,2},{1,5},{3,7},{5,1},{7,3},{8,12},{10,14},{12... | collective-permute-start | bytes 245768 | tf_op jit(solution)/shard_map/ppermute | solution.py:88
  9.7 7.7 %collective-permute-start.2 = (bf16[320,128]{1,0:T(8,128)(2,1)}, bf16[320,128]{1,0:T(8,128)(2,1)S(1)}, u32[]{:S(2)}, u32[]{:S(2)}) collective-permute-start(bf16[320,128]{1,0:T(8,128)(2,1)} %get-tuple-element.92.refs_5_.refs_9_), channel_id=1, source_target_pairs={{0,6},{2,4},{4,2},{6,0},{1,7},{3,5},{5,3},{7,1},{8,14},{10,12},{12... | collective-permute-start | bytes 245768 | tf_op jit(solution)/shard_map/ppermute | solution.py:88
  9.7 24.8 %collective-permute-start.7 = (bf16[128,2048]{1,0:T(8,128)(2,1)}, bf16[128,2048]{1,0:T(8,128)(2,1)S(1)}, u32[]{:S(2)}, u32[]{:S(2)}) collective-permute-start(bf16[128,2048]{1,0:T(8,128)(2,1)} %get-tuple-element.128.go_ref.hg_ref.refs_8_.refs_0_), channel_id=1, source_target_pairs={{0,8},{8,0},{16,24},{24,16},{1,9},{9,1},{17,25},{25,17},{2,10},{10... | collective-permute-start | bytes 1572872 | tf_op jit(solution)/shard_map/ppermute | solution.py:88
  9.9 24.6 %collective-permute-start.8 = (bf16[128,2048]{1,0:T(8,128)(2,1)}, bf16[128,2048]{1,0:T(8,128)(2,1)S(1)}, u32[]{:S(2)}, u32[]{:S(2)}) collective-permute-start(bf16[128,2048]{1,0:T(8,128)(2,1)} %get-tuple-element.128.go_ref.hg_ref.refs_8_.refs_0_), channel_id=1, source_target_pairs={{0,16},{8,24},{16,0},{24,8},{1,17},{9,25},{17,1},{25,9},{2,18},{10... | collective-permute-start | bytes 1572872 | tf_op jit(solution)/shard_map/ppermute | solution.py:88
  11.2 23.4 %collective-permute-start.9 = (bf16[128,2048]{1,0:T(8,128)(2,1)}, bf16[128,2048]{1,0:T(8,128)(2,1)S(1)}, u32[]{:S(2)}, u32[]{:S(2)}) collective-permute-start(bf16[128,2048]{1,0:T(8,128)(2,1)} %get-tuple-element.128.go_ref.hg_ref.refs_8_.refs_0_), channel_id=1, source_target_pairs={{0,24},{8,16},{16,8},{24,0},{1,25},{9,17},{17,9},{25,1},{2,26},{10... | collective-permute-start | bytes 1572872 | tf_op jit(solution)/shard_map/ppermute | solution.py:88
  36.0 19.6 %collective-permute-start.10 = (bf16[4,128,1024]{2,1,0:T(8,128)(2,1)}, bf16[4,128,1024]{2,1,0:T(8,128)(2,1)S(1)}, u32[]{:S(2)}, u32[]{:S(2)}) collective-permute-start(bf16[4,128,1024]{2,1,0:T(8,128)(2,1)} %pad_maximum_fusion.1), channel_id=1, source_target_pairs={{0,1},{1,0},{2,3},{3,2},{4,5},{5,4},{6,7},{7,6},{8,9},{9,8},{10,11... | collective-permute-start | bytes 3145736 | tf_op jit(solution)/shard_map/ppermute | solution.py:88
  38.3 17.2 %collective-permute-start.11 = (bf16[128,1024]{1,0:T(8,128)(2,1)S(1)}, bf16[128,1024]{1,0:T(8,128)(2,1)S(1)}, u32[]{:S(2)}, u32[]{:S(2)}) collective-permute-start(bf16[128,1024]{1,0:T(8,128)(2,1)S(1)} %copy-done.10), channel_id=1, source_target_pairs={{0,8},{8,0},{16,24},{24,16},{1,9},{9,1},{17,25},{25,17},{2,10},{10... | collective-permute-start | bytes 786440 | tf_op jit(solution)/shard_map/ppermute | solution.py:88
  38.9 16.7 %collective-permute-start.12 = (bf16[128,1024]{1,0:T(8,128)(2,1)S(1)}, bf16[128,1024]{1,0:T(8,128)(2,1)S(1)}, u32[]{:S(2)}, u32[]{:S(2)}) collective-permute-start(bf16[128,1024]{1,0:T(8,128)(2,1)S(1)} %copy-done.10), channel_id=1, source_target_pairs={{0,16},{8,24},{16,0},{24,8},{1,17},{9,25},{17,1},{25,9},{2,18},{10... | collective-permute-start | bytes 786440 | tf_op jit(solution)/shard_map/ppermute | solution.py:88
  40.1 15.4 %collective-permute-start.13 = (bf16[128,1024]{1,0:T(8,128)(2,1)S(1)}, bf16[128,1024]{1,0:T(8,128)(2,1)S(1)}, u32[]{:S(2)}, u32[]{:S(2)}) collective-permute-start(bf16[128,1024]{1,0:T(8,128)(2,1)S(1)} %copy-done.10), channel_id=1, source_target_pairs={{0,24},{8,16},{16,8},{24,0},{1,25},{9,17},{17,9},{25,1},{2,26},{10... | collective-permute-start | bytes 786440 | tf_op jit(solution)/shard_map/ppermute | solution.py:88
  70.9 18.3 %collective-permute-start.21 = (bf16[4,128,1024]{2,1,0:T(8,128)(2,1)S(1)}, bf16[4,128,1024]{2,1,0:T(8,128)(2,1)S(1)}, u32[]{:S(2)}, u32[]{:S(2)}) collective-permute-start(bf16[4,128,1024]{2,1,0:T(8,128)(2,1)S(1)} %pad_maximum_fusion.2), channel_id=1, source_target_pairs={{0,1},{1,0},{2,3},{3,2},{4,5},{5,4},{6,7},{7,6},{8,9},{9,8},{10,11... | collective-permute-start | bytes 3145736 | tf_op jit(solution)/shard_map/ppermute | solution.py:88
  71.8 17.4 %collective-permute-start.22 = (bf16[2,704,256]{2,1,0:T(8,128)(2,1)S(1)}, bf16[2,704,256]{2,1,0:T(8,128)(2,1)S(1)}, u32[]{:S(2)}, u32[]{:S(2)}) collective-permute-start(bf16[2,704,256]{2,1,0:T(8,128)(2,1)S(1)} %copy-done.44), channel_id=1, source_target_pairs={{0,2},{2,0},{4,6},{6,4},{1,3},{3,1},{5,7},{7,5},{8,10},{10,8},{12,... | collective-permute-start | bytes 2162696 | tf_op jit(solution)/shard_map/ppermute | solution.py:88
  72.2 18.3 %collective-permute-start.18 = (bf16[992,256]{1,0:T(8,128)(2,1)}, bf16[992,256]{1,0:T(8,128)(2,1)S(1)}, u32[]{:S(2)}, u32[]{:S(2)}) collective-permute-start(bf16[992,256]{1,0:T(8,128)(2,1)} %get-tuple-element.124), channel_id=1, source_target_pairs={{0,8},{8,0},{16,24},{24,16},{1,9},{9,1},{17,25},{25,17},{2,10},{10... | collective-permute-start | bytes 1523720 | tf_op jit(solution)/shard_map/ppermute | solution.py:88
  72.7 17.8 %collective-permute-start.19 = (bf16[992,256]{1,0:T(8,128)(2,1)S(1)}, bf16[992,256]{1,0:T(8,128)(2,1)S(1)}, u32[]{:S(2)}, u32[]{:S(2)}) collective-permute-start(bf16[992,256]{1,0:T(8,128)(2,1)S(1)} %copy-done.46), channel_id=1, source_target_pairs={{0,16},{8,24},{16,0},{24,8},{1,17},{9,25},{17,1},{25,9},{2,18},{10... | collective-permute-start | bytes 1523720 | tf_op jit(solution)/shard_map/ppermute | solution.py:88
  74.0 22.1 %collective-permute-start.20 = (bf16[992,256]{1,0:T(8,128)(2,1)S(1)}, bf16[992,256]{1,0:T(8,128)(2,1)S(1)}, u32[]{:S(2)}, u32[]{:S(2)}) collective-permute-start(bf16[992,256]{1,0:T(8,128)(2,1)S(1)} %copy-done.45), channel_id=1, source_target_pairs={{0,24},{8,16},{16,8},{24,0},{1,25},{9,17},{17,9},{25,1},{2,26},{10... | collective-permute-start | bytes 1523720 | tf_op jit(solution)/shard_map/ppermute | solution.py:88
  89.2 6.8 %collective-permute-start.23 = (bf16[4,320,128]{2,1,0:T(8,128)(2,1)}, bf16[4,320,128]{2,1,0:T(8,128)(2,1)S(1)}, u32[]{:S(2)}, u32[]{:S(2)}) collective-permute-start(bf16[4,320,128]{2,1,0:T(8,128)(2,1)} %get-tuple-element.132), channel_id=1, source_target_pairs={{0,1},{1,0},{2,3},{3,2},{4,5},{5,4},{6,7},{7,6},{8,9},{9,8},{10,11... | collective-permute-start | bytes 983048 | tf_op jit(solution)/shard_map/ppermute | solution.py:88
  99.7 20.8 %collective-permute-start.29 = (bf16[2,352,256]{2,1,0:T(8,128)(2,1)S(1)}, bf16[2,352,256]{2,1,0:T(8,128)(2,1)S(1)}, u32[]{:S(2)}, u32[]{:S(2)}) collective-permute-start(bf16[2,352,256]{2,1,0:T(8,128)(2,1)S(1)} %get-tuple-element.176), channel_id=1, source_target_pairs={{0,2},{2,0},{4,6},{6,4},{1,3},{3,1},{5,7},{7,5},{8,10},{10,8},{12,... | collective-permute-start | bytes 1081352 | tf_op jit(solution)/shard_map/ppermute | solution.py:88
  104.5 17.8 %collective-permute-start.25 = (bf16[2,256,128]{2,1,0:T(8,128)(2,1)}, bf16[2,256,128]{2,1,0:T(8,128)(2,1)S(1)}, u32[]{:S(2)}, u32[]{:S(2)}) collective-permute-start(bf16[2,256,128]{2,1,0:T(8,128)(2,1)} %get-tuple-element.137), channel_id=1, source_target_pairs={{0,2},{2,0},{4,6},{6,4},{1,3},{3,1},{5,7},{7,5},{8,10},{10,8},{12,... | collective-permute-start | bytes 393224 | tf_op jit(solution)/shard_map/ppermute | solution.py:88
  106.3 9.5 %collective-permute-start.26 = (bf16[320,128]{1,0:T(8,128)(2,1)S(1)}, bf16[320,128]{1,0:T(8,128)(2,1)S(1)}, u32[]{:S(2)}, u32[]{:S(2)}) collective-permute-start(bf16[320,128]{1,0:T(8,128)(2,1)S(1)} %get-tuple-element.179), channel_id=1, source_target_pairs={{0,2},{2,0},{4,6},{6,4},{1,3},{3,1},{5,7},{7,5},{8,10},{10,8},{12,... | collective-permute-start | bytes 245768 | tf_op jit(solution)/shard_map/ppermute | solution.py:88
  106.7 9.2 %collective-permute-start.27 = (bf16[320,128]{1,0:T(8,128)(2,1)S(1)}, bf16[320,128]{1,0:T(8,128)(2,1)S(1)}, u32[]{:S(2)}, u32[]{:S(2)}) collective-permute-start(bf16[320,128]{1,0:T(8,128)(2,1)S(1)} %get-tuple-element.178), channel_id=1, source_target_pairs={{0,4},{2,6},{4,0},{6,2},{1,5},{3,7},{5,1},{7,3},{8,12},{10,14},{12... | collective-permute-start | bytes 245768 | tf_op jit(solution)/shard_map/ppermute | solution.py:88
  109.9 10.6 %collective-permute-start.28 = (bf16[320,128]{1,0:T(8,128)(2,1)S(1)}, bf16[320,128]{1,0:T(8,128)(2,1)S(1)}, u32[]{:S(2)}, u32[]{:S(2)}) collective-permute-start(bf16[320,128]{1,0:T(8,128)(2,1)S(1)} %get-tuple-element.177), channel_id=1, source_target_pairs={{0,6},{2,4},{4,2},{6,0},{1,7},{3,5},{5,3},{7,1},{8,14},{10,12},{12... | collective-permute-start | bytes 245768 | tf_op jit(solution)/shard_map/ppermute | solution.py:88
  124.7 30.5 %collective-permute-start.34 = (bf16[1,1184,256]{2,1,0:T(8,128)(2,1)S(1)}, bf16[1,1184,256]{2,1,0:T(8,128)(2,1)}, u32[]{:S(2)}, u32[]{:S(2)}) collective-permute-start(bf16[1,1184,256]{2,1,0:T(8,128)(2,1)S(1)} %slice.240), channel_id=1, source_target_pairs={{0,4},{2,6},{4,0},{6,2},{1,5},{3,7},{5,1},{7,3},{8,12},{10,14},{12... | collective-permute-start | bytes 1818632 | tf_op jit(solution)/shard_map/ppermute | solution.py:88
  141.7 18.7 %collective-permute-start.36 = (bf16[232,128]{1,0:T(8,128)(2,1)}, bf16[232,128]{1,0:T(8,128)(2,1)S(1)}, u32[]{:S(2)}, u32[]{:S(2)}) collective-permute-start(bf16[232,128]{1,0:T(8,128)(2,1)} %get-tuple-element.159), channel_id=1, source_target_pairs={{0,2},{2,0},{4,6},{6,4},{1,3},{3,1},{5,7},{7,5},{8,10},{10,8},{12,... | collective-permute-start | bytes 178184 | tf_op jit(solution)/shard_map/ppermute | solution.py:88
  141.7 18.7 %collective-permute-start.37 = (bf16[232,128]{1,0:T(8,128)(2,1)}, bf16[232,128]{1,0:T(8,128)(2,1)S(1)}, u32[]{:S(2)}, u32[]{:S(2)}) collective-permute-start(bf16[232,128]{1,0:T(8,128)(2,1)} %get-tuple-element.160), channel_id=1, source_target_pairs={{0,4},{2,6},{4,0},{6,2},{1,5},{3,7},{5,1},{7,3},{8,12},{10,14},{12... | collective-permute-start | bytes 178184 | tf_op jit(solution)/shard_map/ppermute | solution.py:88
  143.6 16.7 %collective-permute-start.38 = (bf16[232,128]{1,0:T(8,128)(2,1)}, bf16[232,128]{1,0:T(8,128)(2,1)S(1)}, u32[]{:S(2)}, u32[]{:S(2)}) collective-permute-start(bf16[232,128]{1,0:T(8,128)(2,1)} %get-tuple-element.161), channel_id=1, source_target_pairs={{0,6},{2,4},{4,2},{6,0},{1,7},{3,5},{5,3},{7,1},{8,14},{10,12},{12... | collective-permute-start | bytes 178184 | tf_op jit(solution)/shard_map/ppermute | solution.py:88
  (63 other events, 293.4 us)

commit v4 on v3

--- a/solution.py
+++ b/solution.py
@@ -381,12 +381,10 @@
     gm = mm(gb, wo[...], NT)
     gm_ref[...] = gm.astype(BF16)
     gmt_ref[...] = gm.T.astype(BF16)
-    tokens = gb.shape[0]
     for k, mgx_ref in enumerate(mgx_refs):
-        cols = mgx_ref.shape[1]
-        for i in range(width // cols):
-            mgx_ref[i * tokens:(i + 1) * tokens, :] = mixed_ref[:, i * cols:(i + 1) * cols]
-        mgx_ref[width // cols * tokens:, :] = gb_cols[:, pl.ds(pl.multiple_of((place_ref[0] ^ k) * cols, cols), cols)]
+        cols = mgx_ref.shape[1] - width
+        mgx_ref[:, :width] = mixed_ref[...]
+        mgx_ref[:, width:] = gb_cols[:, pl.ds(pl.multiple_of((place_ref[0] ^ k) * cols, cols), cols)]
 
 
 def feed_forward(place, h2, hg, gh, w_gate, w_up, w_down, resid, gain, w_out, mixed, n_rows):
@@ -396,7 +394,7 @@
     return call(
         ffn_kernel,
         [((tokens, width), BF16), ((1, width), F32), ((tokens, width), F32), ((tokens, width), BF16),
-         ((width, tokens), BF16)] + [((tokens * (n_rows + 1), width // n_rows), BF16)] * n_rows,
+         ((width, tokens), BF16)] + [((tokens, width + width // n_rows), BF16)] * n_rows,
         [smem()] + [vmem()] * 6 + [hbm()] * 4,
         (place, h2, hg, gh, resid, gain, mixed, w_gate, w_up, w_down, w_out),
         [pltpu.VMEM((tokens, width), F32), pltpu.VMEM((tokens, width), F32), pltpu.VMEM((tokens, width), BF16),
@@ -407,10 +405,8 @@
 
 
 def weight_kernel(n_pieces, ordered, place_ref, wg_ref, wu_ref, wd_ref, go_other, *refs):
-    n_rows = n_pieces // 2
-    h2_pieces, hg_same, mgx = refs[:n_pieces], refs[n_pieces:n_pieces + n_rows], refs[n_pieces + n_rows:2 * n_pieces]
-    up_keep, up_send, *row_refs = refs[2 * n_pieces:-6]
-    h2s, gos, wds, window, turned, sems = refs[-6:]
+    h2_pieces, hg_same = refs[:n_pieces], refs[n_pieces:n_pieces + n_pieces // 2]
+    up_keep, up_send, down_keep, down_send, h2s, gos, wds, window, turned, sems = refs[n_pieces + n_pieces // 2:]
     tokens, width = h2_pieces[0].shape
     ff, span = wds.shape[0], window.shape[2]
     at = (place_ref[0] * 2 + place_ref[1]) * ff
@@ -426,9 +422,6 @@
         groups[3].append(pltpu.make_async_copy(go, gos.at[rows, :], sems.at[1, j]))
     groups[3].append(pltpu.make_async_copy(
         wd_ref.at[pl.ds(pl.multiple_of(at, 32), ff), :], wds, sems.at[1, n_pieces]))
-    groups.append([
-        pltpu.make_async_copy(mgx[k], row_refs[k].at[pl.ds(ff, mgx[k].shape[0]), :], sems.at[3, k]) for k in range(n_rows)
-    ])
     for group in groups:
         for copy in group:
             copy.start()
@@ -453,21 +446,19 @@
     cols = width // n_z
     half = cols // 2
     for slot, k in enumerate(halving_order(n_z)):
-        up_ref, i = (up_keep, slot) if slot < kept else (up_send, slot - kept)
+        up_ref, down_ref, i = (up_keep, down_keep, slot) if slot < kept else (up_send, down_send, slot - kept)
         if ordered:
             z, core = place_ref[2] ^ k, place_ref[1]
             first = pl.ds(pl.multiple_of(z * cols + core * half, half), half)
             other = pl.ds(pl.multiple_of(z * cols + (1 - core) * half, half), half)
+            straight = pl.ds(pl.multiple_of((z ^ place_ref[0]) * cols, cols), cols)
             h2c = jnp.concatenate([h2s[:, first], h2s[:, other]], axis=1)
         else:
-            h2c = h2s[:, slot * cols:(slot + 1) * cols]
+            straight = slice(slot * cols, (slot + 1) * cols)
+            h2c = h2s[:, straight]
         up_ref[i, :ff, :] = mm(grad_gate, h2c).astype(BF16)
         up_ref[i, ff:, :] = mm(grad_up, h2c).astype(BF16)
-    for k, row_ref in enumerate(row_refs):
-        cols = row_ref.shape[1]
-        row_ref[:ff, :] = mm(hidden, gos[:, pl.ds(pl.multiple_of((place_ref[0] ^ k) * cols, cols), cols)]).astype(BF16)
-    for copy in groups[4]:
-        copy.wait()
+        down_ref[i] = mm(hidden, gos[:, straight]).astype(BF16)
 
 
 def halving_order(n):
@@ -479,7 +470,7 @@
     return order
 
 
-def weight_grads(place, w_gate, w_up, w_down, h2_pieces, hg_same, go_other, mgx, n_z, ordered):
+def weight_grads(place, w_gate, w_up, w_down, h2_pieces, hg_same, go_other, n_z, ordered):
     n = len(h2_pieces)
     tokens, width = h2_pieces[0].shape
     ff = w_gate.shape[1] // n
@@ -487,11 +478,11 @@
     total = n * tokens
     return call(
         functools.partial(weight_kernel, n, ordered),
-        [((n_z // 2, 2 * ff, width // n_z), BF16)] * 2 + [((ff + p.shape[0], p.shape[1]), BF16) for p in mgx],
-        [smem()] + [hbm()] * (4 + 2 * n),
-        (place, w_gate, w_up, w_down, go_other, *h2_pieces, *hg_same, *mgx),
+        [((n_z // 2, 2 * ff, width // n_z), BF16)] * 2 + [((n_z // 2, ff, width // n_z), BF16)] * 2,
+        [smem()] + [hbm()] * (4 + n + n // 2),
+        (place, w_gate, w_up, w_down, go_other, *h2_pieces, *hg_same),
         [pltpu.VMEM((total, width), BF16), pltpu.VMEM((total, width), BF16), pltpu.VMEM((ff, width), BF16),
-         pltpu.VMEM((2, width, span), BF16), pltpu.VMEM((2, span, width), BF16), pltpu.SemaphoreType.DMA((4, n + 1))],
+         pltpu.VMEM((2, width, span), BF16), pltpu.VMEM((2, span, width), BF16), pltpu.SemaphoreType.DMA((3, n + 1))],
         12 * total * width * ff, 6 * width * ff + 4 * total * width, "weight_grads",
     )
 
@@ -534,53 +525,46 @@
     )[0]
 
 
-def out_kernel(n_out, ordered, place_ref, mine_ref, other_ref, keep_ref, send_ref, wide, thin):
-    kept, _, cols = keep_ref.shape
-    offsets = halving_order(n_out) if ordered else list(range(n_out))
-    n_rows, _, part = mine_ref.shape
-    tokens = wide.shape[0] // (2 * n_rows)
-    per_block = part // cols
+def out_kernel(n_out, ordered, place_ref, mine_ref, other_ref, *refs):
+    out_refs, (wide, thin) = refs[:-2], refs[-2:]
+    n_rows, tokens, both = mine_ref.shape
+    part, cols = thin.shape[1], out_refs[0].shape[1]
     for i, ref in enumerate((mine_ref, other_ref)):
         for j in range(n_rows):
             rows = slice((i * n_rows + j) * tokens, (i * n_rows + j + 1) * tokens)
-            thin[rows, :] = ref[j, n_rows * tokens:, :]
-            for i_out, k in enumerate(offsets):
-                if ordered:
-                    where = pl.ds(pl.multiple_of((place_ref[2] ^ k) * tokens, tokens), tokens)
-                    cut = pl.ds(pl.multiple_of(place_ref[1] * cols, cols), cols)
-                else:
-                    where = slice(k // per_block * tokens, (k // per_block + 1) * tokens)
-                    cut = slice(k % per_block * cols, (k % per_block + 1) * cols)
-                wide[rows, i_out * cols:(i_out + 1) * cols] = ref[j, where, cut]
+            thin[rows, :] = ref[j, :, both - part:]
+            for k in range(n_out):
+                wide[rows, k * cols:(k + 1) * cols] = ref[j, :, own_cut(ordered, place_ref, k, cols)]
     full = mm(thin[...].T, wide[...]).astype(BF16)
-    for k in range(kept):
-        keep_ref[k] = full[:, k * cols:(k + 1) * cols]
-        send_ref[k] = full[:, (kept + k) * cols:(kept + k + 1) * cols]
-
-
-def out_grads(place, mine, other, tokens, n_out, cols, ordered):
-    n_rows, both, part = mine.shape
+    for k, out_ref in enumerate(out_refs):
+        out_ref[...] = full[:, k * cols:(k + 1) * cols]
+
+
+def out_grads(place, mine, other, width, n_out, cols, ordered):
+    n_rows, tokens, both = mine.shape
+    part = both - width
     total = 2 * n_rows * tokens
     return call(
         functools.partial(out_kernel, n_out, ordered),
-        [((n_out // 2, part, cols), BF16)] * 2,
+        [((part, cols), BF16)] * n_out,
         [smem(), vmem(), vmem()],
         (place, mine, other),
         [pltpu.VMEM((total, n_out * cols), BF16), pltpu.VMEM((total, part), BF16)],
-        2 * total * part * n_out * cols, 4 * n_rows * both * part, "out_grads",
-    )
-
-
-def fact_kernel(head, ordered, h1_ref, mine_ref, other_ref, *refs):
-    out_refs, thin = refs[:-1], refs[-1]
+        2 * total * part * n_out * cols, 4 * total * both, "out_grads",
+    )
+
+
+def fact_kernel(n_out, head, ordered, h1_ref, mine_ref, other_ref, *refs):
+    carried, out_refs, thin = refs[:n_out], refs[n_out:-1], refs[-1]
     cols = out_refs[0].shape[1]
-    tokens = mine_ref.shape[2]
+    rows, tokens = mine_ref.shape[1:]
     parts = [ref[j] for ref in (mine_ref, other_ref) for j in range(ref.shape[0])]
     for j, part in enumerate(parts):
         thin[:, j * tokens:(j + 1) * tokens] = part[head:, :]
     full = mm(thin[...], h1_ref[...]).astype(BF16)
     for k, out_ref in enumerate(out_refs):
-        out_ref[head:, :] = full[:, k * cols:(k + 1) * cols]
+        out_ref[head:rows, :] = full[:, k * cols:(k + 1) * cols]
+        out_ref[rows:, :] = carried[k][...]
     if ordered:
         half = head // 2
         gains = tree_sum([p[:half].astype(F32) + p[half:head].astype(F32) for p in parts])
@@ -591,15 +575,16 @@
             out_ref[half:head, :] = low
 
 
-def fact_grads(h1_slab, mine, other, head, n_out, ordered):
+def fact_grads(h1_slab, mine, other, carried, head, ordered):
     n_rows, rows, tokens = mine.shape
     total = 2 * n_rows * tokens
-    cols = h1_slab.shape[1] // n_out
+    n_out = len(carried)
+    part, cols = carried[0].shape
     return call(
-        functools.partial(fact_kernel, head, ordered),
-        [((rows, cols), BF16)] * n_out,
-        [vmem()] * 3,
-        (h1_slab, mine, other),
+        functools.partial(fact_kernel, n_out, head, ordered),
+        [((rows + part, cols), BF16)] * n_out,
+        [vmem()] * (3 + n_out),
+        (h1_slab, mine, other, *carried),
         [pltpu.VMEM((rows - head, total), BF16)],
         2 * total * rows * n_out * cols, 2 * total * n_out * cols, "fact_grads",
     )
@@ -728,45 +713,40 @@
         place, h2, after(hg, hg_same), gh, w_gate, w_up, w_down, resid, gain_two, w_out, mixed, n_rows
     )
     h2_pieces = along_core(after(h2_same, gm, go_other))
-    up_keep, up_send, *row_out = weight_grads(
-        place, w_gate, w_up, w_down, h2_pieces, hg_same, go_other, mgx, n_z, ordered
+    up_keep, up_send, down_keep, down_send = weight_grads(
+        place, w_gate, w_up, w_down, h2_pieces, hg_same, go_other, n_z, ordered
     )
     if not ordered:
         turns = jnp.asarray(halving_order(n_z), jnp.int32) ^ z
         cores = jnp.arange(2, dtype=jnp.int32) ^ core
         up = jnp.take(jnp.concatenate([up_keep, up_send]), turns, axis=0)
         up = jnp.take(up.reshape(n_z, 2 * ff_part, 2, own_cols), cores, axis=2).reshape(up.shape)
-        up_keep, up_send = up[:n_z // 2], up[n_z // 2:]
+        down = jnp.concatenate([down_keep, down_send]).transpose(1, 0, 2)
+        down = down.reshape(per, ff_part // per, n_rows, width // n_rows).transpose(0, 2, 1, 3)
+        down = jnp.take(down.reshape(n_z, ff_part, 2 * own_cols), turns, axis=0)
+        up_keep, up_send, down_keep, down_send = up[:n_z // 2], up[n_z // 2:], down[:n_z // 2], down[n_z // 2:]
 
     up_got = swap(up_send, "z", 1)
-    row_same = [row_out[0]] + others(row_out, ROW, n_rows)
+    mg_same = [mgx[0]] + others(mgx, ROW, n_rows)
     gm_in, hg_same = after((gm, hg_same), up_send)
     h1_other = swap(jnp.stack([part[:, :width] for part in hg_same]), "core", 1)
     gq, gkv_own, gkv_send = attend_back(q, qt, gm_in, gmt, lse, bias, qf, cosine, sine, kv_pieces)
-    gkv_send, h1_other, up_got = lax.optimization_barrier((gkv_send, h1_other, up_got))
+    gkv_send, mg_same, h1_other, up_got = lax.optimization_barrier((gkv_send, mg_same, h1_other, up_got))
+    down_got = swap(after(down_send, up_got), "z", 1)
     gkv_got = swap(gkv_send, "core", 1)
-    row_same = after(row_same, gkv_got)
+    mg_mine, mg_other = both_cores(mg_same)
     gkv_z = [(gkv_own[k].astype(F32) + gkv_got[k].astype(F32)).astype(BF16) for k in range(n_z)]
     kv_parts = [gkv_z[0]] + others(gkv_z, "z", n_z)
-    mg_mine, mg_other = both_cores([part[ff_part:] for part in row_same])
-    if ordered:
-        down = jnp.stack([part[:ff_part] for part in row_same])
-        down = jnp.take(down, jnp.asarray(halving_order(n_z), jnp.int32) ^ z ^ row, axis=0)
-        down_keep, down_send = down[:n_z // 2], down[n_z // 2:]
-        down_got = swap(down_send, "z", 1)
-    if ordered:
-        kv_parts, down_got = lax.optimization_barrier((kv_parts, down_got))
-
-    def own_blocks(parts, offsets):
-        parts = jnp.take(parts, (jnp.asarray(offsets, jnp.int32) ^ z) * 2 + core, axis=0)
+    kv_parts, down_got = lax.optimization_barrier((kv_parts, down_got))
+
+    def own_blocks(parts):
+        if ordered:
+            return parts
+        parts = jnp.take(jnp.stack(parts), (jnp.arange(n_z, dtype=jnp.int32) ^ z) * 2 + core, axis=0)
         return [parts[k] for k in range(n_z)]
 
-    out_keep, out_send = out_grads(place, mg_mine, mg_other, tokens, n_out, own_cols, ordered)
-    if not ordered:
-        out_parts = own_blocks(jnp.concatenate([out_keep, out_send]), halving_order(n_z))
-        out_keep, out_send = jnp.stack(out_parts[:n_z // 2]), jnp.stack(out_parts[n_z // 2:])
-    out_got = swap(out_send, "z", 1)
-    gq, out_got = after((gq, out_got), kv_parts)
+    out_parts = out_grads(place, mg_mine, mg_other, width, n_out, own_cols, ordered)
+    gq = after(gq, out_parts)
 
     def add_up(keep, got, hold, step=1):
         total = keep.astype(F32) + got.astype(F32)
@@ -778,10 +758,8 @@
             total = (after(kept, *hold) if n == 1 else kept) + got.astype(F32)
         return total[0]
 
-    side = (out_keep.shape[0], -1, 2 * own_cols)
-    ffn_keep = [up_keep, down_keep, out_keep.reshape(side)] if ordered else [up_keep, out_keep.reshape(side)]
-    ffn_got = [up_got, down_got, out_got.reshape(side)] if ordered else [up_got, out_got.reshape(side)]
-    ffn_keep, ffn_got = jnp.concatenate(ffn_keep, axis=1), jnp.concatenate(ffn_got, axis=1)
+    ffn_keep = jnp.concatenate([up_keep, down_keep], axis=1)
+    ffn_got = jnp.concatenate([after(up_got, kv_parts), down_got], axis=1)
     grad_inputs, *gfx = input_grads(
         place, gq, kv_parts, w_fact_t, x, s1, gain_one, gres, gain_two_part, cosine, sine, n_rows
     )
@@ -789,37 +767,28 @@
     gf_same = [gfx[0]] + others(gfx, ROW, n_rows)
     h1_slab = own_slab(place, hg_same, after(h1_other, gfx[0]), n_out, own_cols, ordered)
     gf_all = both_cores(after(gf_same, h1_slab))
-    tail_parts = fact_grads(h1_slab, *gf_all, head, n_out, ordered)
-    if not ordered:
-        tail_parts = own_blocks(jnp.stack(tail_parts), list(range(n_z)))
+    tail_parts = own_blocks(fact_grads(h1_slab, *gf_all, out_parts, head, ordered))
     total = add_up(ffn_keep, ffn_got, tail_parts)
     tail_got = others(tail_parts, "z", n_z)
-    up_total = total[:2 * ff_part]
-    grad_out = total[-own_cols * out_keep.shape[1] // (2 * own_cols):].reshape(out_keep.shape[1:]).T
+    up_total, down_total = total[:2 * ff_part], total[2 * ff_part:].reshape(ff // n_ctx, width // n_rows)
     mine, other = up_total[:, :own_cols], swap(up_total[:, own_cols:].astype(BF16), "core", 1).astype(F32)
     first = jnp.where(core == 0, mine, other)
     second = jnp.where(core == 0, other, mine)
     grad_gate = jnp.concatenate([first[:ff_part], second[:ff_part]], axis=0).T
     grad_up = jnp.concatenate([first[ff_part:], second[ff_part:]], axis=0).T
 
-    if ordered:
-        grad_down = total[2 * ff_part:3 * ff_part]
-    else:
-        down = jnp.stack([part[:ff_part] for part in row_out])
-        down = jnp.take(down, jnp.arange(n_rows, dtype=jnp.int32) ^ row, axis=0)
-        down = down.reshape(n_rows, per, ff_part // per, width // n_rows).transpose(1, 0, 2, 3)
-        down = lax.psum_scatter(down.reshape(n_z, ff_part // per, -1), "z", scatter_dimension=0)
-        moves = []
-        for r in range(n_rows):
-            for c in range(2):
-                for p in range(n_z):
-                    b, s = p // n_rows, p % n_rows
-                    moves.append((r * n_ctx + 2 * p + c, s * n_ctx + (r * 2 + c) * per + b))
-        grad_down = lax.ppermute(down, ROW + CTX, moves).astype(F32)
-
-    tail_parts = after(tail_parts, grad_gate, grad_up, grad_out)
+    moves = []
+    for r in range(n_rows):
+        for c in range(2):
+            for p in range(n_z):
+                b, s = p // n_rows, (p % n_rows) ^ (r if ordered else 0)
+                moves.append((r * n_ctx + 2 * p + c, s * n_ctx + (r * 2 + c) * per + b))
+    grad_down = lax.ppermute(down_total.astype(BF16), ROW + CTX, moves).astype(F32)
+
+    tail_parts = after(tail_parts, grad_gate, grad_up)
     tail = tree_sum([part.astype(F32) for part in [tail_parts[0]] + tail_got])
-    grad_fact = tail[head:].T
+    rows = gfx[0].shape[0]
+    grad_fact, grad_out = tail[head:rows].T, tail[rows:].T
     if ordered:
         gains = (tail[:head // 2] + tail[head // 2:head]).reshape(2, width)
     else:

time: 164 us -> 156 us (0.951); the launches traced: 162 us -> 156 us
  local copies, waits for them, and re-layouts: 10.9 us -> 7.89 us
  other arithmetic: 9.73 us -> 7.82 us
    ppermute x0 -> x1, waiting for transfers between devices: none -> 10.9 us  [body(): lax.ppermute(down_total.astype(BF16), ROW + CTX, moves).astype(F32)]
    ppermute x39 -> x38, waiting for transfers between devices: 31.7 us -> 20.8 us  [swap(): return lax.ppermute(value, axis, [(j, j ^ k) for j in range(size)])]
    reshape x4 -> x0, local copies, waits for them, and re-layouts: 3.22 us -> none  [the longest x1 1.75 us: body(): out_keep.reshape(side)]
    ppermute x0 -> x1, starting transfers between devices: none -> 1.92 us  [body(): lax.ppermute(down_total.astype(BF16), ROW + CTX, moves).astype(F32)]
    unnamed x94 -> x93, local copies, waits for them, and re-layouts: 4.5 us -> 6.28 us
    ppermute x39 -> x38, starting transfers between devices: 36.6 us -> 35.3 us  [swap(): return lax.ppermute(value, axis, [(j, j ^ k) for j in range(size)])]
  transfers between devices with their start and end apart: 39 -> 39, of which waited for: 14 -> 18; matrix products, arithmetic and copies ran while one was open for 6% -> 4% of each run, Pallas kernels for 35% -> 36%
where the time goes in v4:
time: 156 us
  Pallas kernels  69.4 us (44%)
  starting transfers between devices  37.2 us (24%)
  waiting for transfers between devices  31.7 us (20%)
  local copies, waits for them, and re-layouts  7.89 us (5%)
  other arithmetic  7.82 us (5%)
  between operations  1.88 us (1%)
    pallas_call x9, Pallas kernels, call(): pl.pallas_call(kernel, out_shape=[jax.ShapeDtypeStruct(s, d) for s, d in...  64.6 us
    ppermute x38, starting transfers between devices, swap(): return lax.ppermute(value, axis, [(j, j ^ k) for j in range(size)])  35.3 us
    ppermute x38, waiting for transfers between devices, swap(): return lax.ppermute(value, axis, [(j, j ^ k) for j in range(size)])  20.8 us
    ppermute x1, waiting for transfers between devices, body(): lax.ppermute(down_total.astype(BF16), ROW + CTX, moves).astype(F32)  10.9 us
    unnamed x93, local copies, waits for them, and re-layouts  6.28 us
    pallas_call x1, Pallas kernels, hidden_grads(): pl.pallas_call(hidden_kernel, grid=(ff // chunk,), in_specs=[pl.BlockSpec...  4.83 us
  transfers between devices with their start and end apart: 39, of which 18 were waited for; matrix products, arithmetic and copies ran while one was open for 4% of the time, Pallas kernels for 36%

profile of v4, /device:TPU:3, one launch (start us, length us, event | category | flops | bytes accessed | tf_op | source)
XLA Modules:
  0.0 155.9 jit_solution(559545386362769211)
XLA Ops:
  2.5 3.5 %factors.1 = (bf16[128,2048]{1,0:T(8,128)(2,1)}, f32[128,1]{1,0:T(8,128)}, bf16[128,1024]{1,0:T(8,128)(2,1)}, bf16[1024,128]{1,0:T(8,128)(2,1)}, f32[480,128]{1,...) custom-call(bf16[128,1024]{1,0:T(8,128)(2,1)} %bitcast.100, ...), custom_call_target="tpu_custom_call" | custom-call | flops 209715200 | bytes 1638400 | tf_op jit(solution)/shard_map/factors/pallas_call | solution.py:47
  6.1 3.3 %collective-permute-start.2 = (bf16[320,128]{1,0:T(8,128)(2,1)}, bf16[320,128]{1,0:T(8,128)(2,1)S(1)}, u32[]{:S(2)}, u32[]{:S(2)}) collective-permute-start(bf16[320,128]{1,0:T(8,128)(2,1)} %get-tuple-element.93.refs_5_.refs_9_), channel_id=1, source_target_pairs={{0,6},{2,4},{4,2},{6,0},{1,7},{3,5},{5,3},{7,1},{8,14},{10,12},{12... | collective-permute-start | bytes 245768 | tf_op jit(solution)/shard_map/ppermute | solution.py:88
  12.6 4.8 %hidden_grads.1.gh_ref = f32[128,2816]{1,0:T(8,128)} custom-call(bf16[128,2048]{1,0:T(8,128)(2,1)} %get-tuple-element.125.go_ref.hg_ref.refs_8_.refs_0_, bf16[2816,1024]{1,0:T(8,128)(2,1)} %wd_ref.3), custom_call_target="tpu_custom_call" | custom-call | flops 738197504 | bytes 7208960 | tf_op jit(solution)/shard_map/hidden_grads/pallas_call | solution.py:314
  17.4 2.3 %collective-permute-start.3 = (bf16[320,128]{1,0:T(8,128)(2,1)S(1)}, bf16[320,128]{1,0:T(8,128)(2,1)S(1)}, u32[]{:S(2)}, u32[]{:S(2)}) collective-permute-start(bf16[320,128]{1,0:T(8,128)(2,1)S(1)} %copy-done.31), channel_id=1, source_target_pairs={{0,1},{1,0},{2,3},{3,2},{4,5},{5,4},{6,7},{7,6},{8,9},{9,8},{10,11... | collective-permute-start | bytes 245768 | tf_op jit(solution)/shard_map/ppermute | solution.py:88
  23.0 11.5 %attend.1 = (bf16[128,1024]{1,0:T(8,128)(2,1)}, bf16[128,1024]{1,0:T(8,128)(2,1)}, f32[128,1024]{1,0:T(8,128)}, f32[8,256,1]{2,1,0:T(8,128)}) custom-call(bf16[128,1024]{1,0:T(8,128)(2,1)} %get-tuple-element.90.refs_0_, f32[128,1024]{1,0:T(8,128)} %and_select_fusion.refs_1_.refs_5_, bf16[1024,1024]{1,0:T(8,128)(2,1)} %wo_hbm.1, bf16[128,1024]{1,0:T(8,128)(2,1)} %bitcast.101, ...), custom_call_target="tpu_custom_call" | custom-call | flops 536870912 | bytes 2097152 | tf_op jit(solution)/shard_map/attend/pallas_call | solution.py:47
  41.0 14.4 %feed_forward.1 = (bf16[128,1024]{1,0:T(8,128)(2,1)}, f32[1,1024]{1,0:T(1,128)}, f32[128,1024]{1,0:T(8,128)}, bf16[128,1024]{1,0:T(8,128)(2,1)}, bf16[1024,128]{...) custom-call(s32[3]{0:T(128)} %pad_add_fusion.place_ref, ...), custom_call_target="tpu_custom_call" | custom-call | flops 3690987520 | bytes 17301504 | tf_op jit(solution)/shard_map/feed_forward/pallas_call | solution.py:47
  59.9 9.4 %weight_grads.1 = (bf16[2,704,256]{2,1,0:T(8,128)(2,1)}, bf16[2,704,256]{2,1,0:T(8,128)(2,1)}, bf16[2,352,256]{2,1,0:T(8,128)(2,1)}, bf16[2,352,256]{2,1,0:T(8,128)(2,1)}) custom-call(s32[3]{0:T(128)} %pad_add_fusion.place_ref, bf16[1024,2816]{1,0:T(8,128)(2,1)} %wg_ref.1, bf16[1024,2816]{1,0:T(8,128)(2,1)} %wu_ref.1, bf16[2816,1024]{1,0:T(8,128)(2,1)} %wd_ref.3, ...), custom_call_target="tpu_custom_call" | custom-call | flops 4429185024 | bytes 6356992 | tf_op jit(solution)/shard_map/weight_grads/pallas_call | solution.py:47
  75.3 13.5 %attend_back.1 = (f32[480,128]{1,0:T(8,128)}, bf16[4,320,128]{2,1,0:T(8,128)(2,1)}, bf16[4,320,128]{2,1,0:T(8,128)(2,1)}) custom-call(bf16[128,1024]{1,0:T(8,128)(2,1)} %get-tuple-element.90.refs_0_, bf16[1024,128]{1,0:T(8,128)(2,1)} %get-tuple-element.106.refs_1_, bf16[128,1024]{1,0:T(8,128)(2,1)} %get-tuple-element.113.refs_2_, ...), custom_call_target="tpu_custom_call" | custom-call | flops 1342177280 | bytes 524288 | tf_op jit(solution)/shard_map/attend_back/pallas_call | solution.py:47
  90.2 1.8 %collective-permute-start.23 = (bf16[4,128,1280]{2,1,0:T(8,128)(2,1)S(1)}, bf16[4,128,1280]{2,1,0:T(8,128)(2,1)S(1)}, u32[]{:S(2)}, u32[]{:S(2)}) collective-permute-start(bf16[4,128,1280]{2,1,0:T(8,128)(2,1)S(1)} %pad_maximum_fusion.mine_ref), channel_id=1, source_target_pairs={{0,1},{1,0},{2,3},{3,2},{4,5},{5,4},{6,7},{7,6},{8,9},{9,8},{10,11... | collective-permute-start | bytes 3932168 | tf_op jit(solution)/shard_map/ppermute | solution.py:88
  92.4 2.7 %collective-permute-done.24 = bf16[4,320,128]{2,1,0:T(8,128)(2,1)S(1)} collective-permute-done((bf16[4,320,128]{2,1,0:T(8,128)(2,1)S(1)}, bf16[4,320,128]{2,1,0:T(8,128)(2,1)S(1)}, u32[]{:S(2)}, u32[]{:S(2)}) %collective-permute-start.24) | collective-permute-done | bytes 327712 | tf_op jit(solution)/shard_map/ppermute | solution.py:88
  95.8 2.4 %collective-permute-start.27 = (bf16[320,128]{1,0:T(8,128)(2,1)S(1)}, bf16[320,128]{1,0:T(8,128)(2,1)S(1)}, u32[]{:S(2)}, u32[]{:S(2)}) collective-permute-start(bf16[320,128]{1,0:T(8,128)(2,1)S(1)} %get-tuple-element.184), channel_id=1, source_target_pairs={{0,6},{2,4},{4,2},{6,0},{1,7},{3,5},{5,3},{7,1},{8,14},{10,12},{12... | collective-permute-start | bytes 245768 | tf_op jit(solution)/shard_map/ppermute | solution.py:88
  99.4 2.5 %collective-permute-done.28 = bf16[2,352,256]{2,1,0:T(8,128)(2,1)S(1)} collective-permute-done((bf16[2,352,256]{2,1,0:T(8,128)(2,1)S(1)}, bf16[2,352,256]{2,1,0:T(8,128)(2,1)S(1)}, u32[]{:S(2)}, u32[]{:S(2)}) %collective-permute-start.28) | collective-permute-done | bytes 360480 | tf_op jit(solution)/shard_map/ppermute | solution.py:88
  101.9 3.2 %collective-permute-done.27.refs_3_ = bf16[320,128]{1,0:T(8,128)(2,1)S(1)} collective-permute-done((bf16[320,128]{1,0:T(8,128)(2,1)S(1)}, bf16[320,128]{1,0:T(8,128)(2,1)S(1)}, u32[]{:S(2)}, u32[]{:S(2)}) %collective-permute-start.27) | collective-permute-done | bytes 81952 | tf_op jit(solution)/shard_map/ppermute | solution.py:88
  105.1 2.1 %collective-permute-done.25.refs_1_ = bf16[320,128]{1,0:T(8,128)(2,1)S(1)} collective-permute-done((bf16[320,128]{1,0:T(8,128)(2,1)S(1)}, bf16[320,128]{1,0:T(8,128)(2,1)S(1)}, u32[]{:S(2)}, u32[]{:S(2)}) %collective-permute-start.25) | collective-permute-done | bytes 81952 | tf_op jit(solution)/shard_map/ppermute | solution.py:88
  107.9 1.8 %collective-permute-start.33 = (bf16[1,1056,256]{2,1,0:T(8,128)(2,1)S(1)}, bf16[1,1056,256]{2,1,0:T(8,128)(2,1)S(1)}, u32[]{:S(2)}, u32[]{:S(2)}) collective-permute-start(bf16[1,1056,256]{2,1,0:T(8,128)(2,1)S(1)} %slice.188), channel_id=1, source_target_pairs={{0,4},{2,6},{4,0},{6,2},{1,5},{3,7},{5,1},{7,3},{8,12},{10,14},{12... | collective-permute-start | bytes 1622024 | tf_op jit(solution)/shard_map/ppermute | solution.py:88
  110.7 3.0 %out_grads.1 = (bf16[256,128]{1,0:T(8,128)(2,1)}, bf16[256,128]{1,0:T(8,128)(2,1)}, bf16[256,128]{1,0:T(8,128)(2,1)}, bf16[256,128]{1,0:T(8,128)(2,1)}) custom-call(s32[3]{0:T(128)} %pad_add_fusion.place_ref, bf16[4,128,1280]{2,1,0:T(8,128)(2,1)} %copy-done.3, bf16[4,128,1280]{2,1,0:T(8,128)(2,1)} %copy-done.10), custom_call_target="tpu_custom_call" | custom-call | flops 268435456 | bytes 5242880 | tf_op jit(solution)/shard_map/out_grads/pallas_call | solution.py:47
  113.7 3.3 %input_grads.1 = (f32[128,1024]{1,0:T(8,128)}, bf16[232,128]{1,0:T(8,128)(2,1)}, bf16[232,128]{1,0:T(8,128)(2,1)}, bf16[232,128]{1,0:T(8,128)(2,1)}, bf16[232,128]{1,0:T(8,128)(2,1)}) custom-call(s32[3]{0:T(128)} %pad_add_fusion.place_ref, f32[480,128]{1,0:T(8,128)} %get-tuple-element.137.gq_ref, bf16[320,128]{1,0:T(8,128)(2,1)} %get-tuple-element.143.refs_0_, ...), custom_call_target="tpu_custom_call" | custom-call | flops 209715200 | bytes 1638400 | tf_op jit(solution)/shard_map/input_grads/pallas_call | solution.py:47
  119.7 3.2 %own_slab.1.h1_ref = bf16[1024,512]{1,0:T(8,128)(2,1)} custom-call(s32[3]{0:T(128)} %pad_add_fusion.place_ref, bf16[4,128,1024]{2,1,0:T(8,128)(2,1)} %copy-done.13, bf16[128,2048]{1,0:T(8,128)(2,1)} %get-tuple-element.125.go_ref.hg_ref.refs_8_.refs_0_, bf16[128,2048]{1,0:T(8,128)(2,1)} %copy-done.8, bf16[128,2048]{1,0:T(8,128)(2,1)} %copy-done.6, ...), custom_call_target="tpu_custom_call" | custom-call | bytes 1048576 | tf_op jit(solution)/shard_map/own_slab/pallas_call | solution.py:47
  123.8 2.7 %collective-permute-start.32 = (bf16[4,232,128]{2,1,0:T(8,128)(2,1)S(1)}, bf16[4,232,128]{2,1,0:T(8,128)(2,1)}, u32[]{:S(2)}, u32[]{:S(2)}) collective-permute-start(bf16[4,232,128]{2,1,0:T(8,128)(2,1)S(1)} %pad_maximum_fusion.3.mine_ref), channel_id=1, source_target_pairs={{0,1},{1,0},{2,3},{3,2},{4,5},{5,4},{6,7},{7,6},{8,9},{9,8},{10,11... | collective-permute-start | bytes 712712 | tf_op jit(solution)/shard_map/ppermute | solution.py:88
  127.8 2.6 %fact_grads.1 = (bf16[488,128]{1,0:T(8,128)(2,1)}, bf16[488,128]{1,0:T(8,128)(2,1)}, bf16[488,128]{1,0:T(8,128)(2,1)}, bf16[488,128]{1,0:T(8,128)(2,1)}) custom-call(bf16[1024,512]{1,0:T(8,128)(2,1)} %own_slab.1.h1_ref, bf16[4,232,128]{2,1,0:T(8,128)(2,1)} %copy-done.15, bf16[4,232,128]{2,1,0:T(8,128)(2,1)} %collective-permute-done.32.other_ref, ...), custom_call_target="tpu_custom_call" | custom-call | flops 243269632 | bytes 1048576 | tf_op jit(solution)/shard_map/fact_grads/pallas_call | solution.py:47
  131.8 2.1 %collective-permute-start.37 = (bf16[488,128]{1,0:T(8,128)(2,1)}, bf16[488,128]{1,0:T(8,128)(2,1)S(1)}, u32[]{:S(2)}, u32[]{:S(2)}) collective-permute-start(bf16[488,128]{1,0:T(8,128)(2,1)} %get-tuple-element.164), channel_id=1, source_target_pairs={{0,6},{2,4},{4,2},{6,0},{1,7},{3,5},{5,3},{7,1},{8,14},{10,12},{12... | collective-permute-start | bytes 374792 | tf_op jit(solution)/shard_map/ppermute | solution.py:88
  135.6 1.9 %collective-permute-start.38 = (bf16[352,256]{1,0:T(8,128)(2,1)S(1)}, bf16[352,256]{1,0:T(8,128)(2,1)S(1)}, u32[]{:S(2)}, u32[]{:S(2)}) collective-permute-start(bf16[352,256]{1,0:T(8,128)(2,1)S(1)} %fusion), channel_id=1, source_target_pairs={{0,0},{2,8},{4,16},{6,24},{1,1},{3,9},{5,17},{7,25},{8,10},{10,2},... | collective-permute-start | bytes 540680 | tf_op jit(solution)/shard_map/ppermute | solution.py:786
  139.2 2.9 %collective-permute-done.36 = bf16[488,128]{1,0:T(8,128)(2,1)S(1)} collective-permute-done((bf16[488,128]{1,0:T(8,128)(2,1)}, bf16[488,128]{1,0:T(8,128)(2,1)S(1)}, u32[]{:S(2)}, u32[]{:S(2)}) %collective-permute-start.36) | collective-permute-done | bytes 124960 | tf_op jit(solution)/shard_map/ppermute | solution.py:88
  144.2 10.9 %collective-permute-done.38 = bf16[352,256]{1,0:T(8,128)(2,1)S(1)} collective-permute-done((bf16[352,256]{1,0:T(8,128)(2,1)S(1)}, bf16[352,256]{1,0:T(8,128)(2,1)S(1)}, u32[]{:S(2)}, u32[]{:S(2)}) %collective-permute-start.38) | collective-permute-done | bytes 180256 | tf_op jit(solution)/shard_map/ppermute | solution.py:786
  (194 shorter events, 42.0 us)
Async XLA Ops:
  9.4 8.0 %collective-permute-start.1 = (bf16[320,128]{1,0:T(8,128)(2,1)}, bf16[320,128]{1,0:T(8,128)(2,1)S(1)}, u32[]{:S(2)}, u32[]{:S(2)}) collective-permute-start(bf16[320,128]{1,0:T(8,128)(2,1)} %get-tuple-element.93.refs_5_.refs_9_), channel_id=1, source_target_pairs={{0,4},{2,6},{4,0},{6,2},{1,5},{3,7},{5,1},{7,3},{8,12},{10,14},{12... | collective-permute-start | bytes 245768 | tf_op jit(solution)/shard_map/ppermute | solution.py:88
  9.4 8.0 %collective-permute-start = (bf16[320,128]{1,0:T(8,128)(2,1)}, bf16[320,128]{1,0:T(8,128)(2,1)S(1)}, u32[]{:S(2)}, u32[]{:S(2)}) collective-permute-start(bf16[320,128]{1,0:T(8,128)(2,1)} %get-tuple-element.93.refs_5_.refs_9_), channel_id=1, source_target_pairs={{0,2},{2,0},{4,6},{6,4},{1,3},{3,1},{5,7},{7,5},{8,10},{10,8},{12,... | collective-permute-start | bytes 245768 | tf_op jit(solution)/shard_map/ppermute | solution.py:88
  9.7 24.8 %collective-permute-start.9 = (bf16[128,2048]{1,0:T(8,128)(2,1)}, bf16[128,2048]{1,0:T(8,128)(2,1)S(1)}, u32[]{:S(2)}, u32[]{:S(2)}) collective-permute-start(bf16[128,2048]{1,0:T(8,128)(2,1)} %get-tuple-element.125.go_ref.hg_ref.refs_8_.refs_0_), channel_id=1, source_target_pairs={{0,24},{8,16},{16,8},{24,0},{1,25},{9,17},{17,9},{25,1},{2,26},{10... | collective-permute-start | bytes 1572872 | tf_op jit(solution)/shard_map/ppermute | solution.py:88
  11.0 25.0 %collective-permute-start.8 = (bf16[128,2048]{1,0:T(8,128)(2,1)}, bf16[128,2048]{1,0:T(8,128)(2,1)S(1)}, u32[]{:S(2)}, u32[]{:S(2)}) collective-permute-start(bf16[128,2048]{1,0:T(8,128)(2,1)} %get-tuple-element.125.go_ref.hg_ref.refs_8_.refs_0_), channel_id=1, source_target_pairs={{0,16},{8,24},{16,0},{24,8},{1,17},{9,25},{17,1},{25,9},{2,18},{10... | collective-permute-start | bytes 1572872 | tf_op jit(solution)/shard_map/ppermute | solution.py:88
  11.5 24.4 %collective-permute-start.7 = (bf16[128,2048]{1,0:T(8,128)(2,1)}, bf16[128,2048]{1,0:T(8,128)(2,1)S(1)}, u32[]{:S(2)}, u32[]{:S(2)}) collective-permute-start(bf16[128,2048]{1,0:T(8,128)(2,1)} %get-tuple-element.125.go_ref.hg_ref.refs_8_.refs_0_), channel_id=1, source_target_pairs={{0,8},{8,0},{16,24},{24,16},{1,9},{9,1},{17,25},{25,17},{2,10},{10... | collective-permute-start | bytes 1572872 | tf_op jit(solution)/shard_map/ppermute | solution.py:88
  37.3 18.3 %collective-permute-start.10 = (bf16[4,128,1024]{2,1,0:T(8,128)(2,1)}, bf16[4,128,1024]{2,1,0:T(8,128)(2,1)S(1)}, u32[]{:S(2)}, u32[]{:S(2)}) collective-permute-start(bf16[4,128,1024]{2,1,0:T(8,128)(2,1)} %pad_maximum_fusion.1), channel_id=1, source_target_pairs={{0,1},{1,0},{2,3},{3,2},{4,5},{5,4},{6,7},{7,6},{8,9},{9,8},{10,11... | collective-permute-start | bytes 3145736 | tf_op jit(solution)/shard_map/ppermute | solution.py:88
  38.4 17.1 %collective-permute-start.13 = (bf16[128,1024]{1,0:T(8,128)(2,1)S(1)}, bf16[128,1024]{1,0:T(8,128)(2,1)S(1)}, u32[]{:S(2)}, u32[]{:S(2)}) collective-permute-start(bf16[128,1024]{1,0:T(8,128)(2,1)S(1)} %copy-done.11), channel_id=1, source_target_pairs={{0,24},{8,16},{16,8},{24,0},{1,25},{9,17},{17,9},{25,1},{2,26},{10... | collective-permute-start | bytes 786440 | tf_op jit(solution)/shard_map/ppermute | solution.py:88
  39.5 16.0 %collective-permute-start.12 = (bf16[128,1024]{1,0:T(8,128)(2,1)S(1)}, bf16[128,1024]{1,0:T(8,128)(2,1)S(1)}, u32[]{:S(2)}, u32[]{:S(2)}) collective-permute-start(bf16[128,1024]{1,0:T(8,128)(2,1)S(1)} %copy-done.11), channel_id=1, source_target_pairs={{0,16},{8,24},{16,0},{24,8},{1,17},{9,25},{17,1},{25,9},{2,18},{10... | collective-permute-start | bytes 786440 | tf_op jit(solution)/shard_map/ppermute | solution.py:88
  39.8 15.7 %collective-permute-start.11 = (bf16[128,1024]{1,0:T(8,128)(2,1)S(1)}, bf16[128,1024]{1,0:T(8,128)(2,1)S(1)}, u32[]{:S(2)}, u32[]{:S(2)}) collective-permute-start(bf16[128,1024]{1,0:T(8,128)(2,1)S(1)} %copy-done.11), channel_id=1, source_target_pairs={{0,8},{8,0},{16,24},{24,16},{1,9},{9,1},{17,25},{25,17},{2,10},{10... | collective-permute-start | bytes 786440 | tf_op jit(solution)/shard_map/ppermute | solution.py:88
  70.5 18.7 %collective-permute-start.21 = (bf16[4,128,1024]{2,1,0:T(8,128)(2,1)S(1)}, bf16[4,128,1024]{2,1,0:T(8,128)(2,1)S(1)}, u32[]{:S(2)}, u32[]{:S(2)}) collective-permute-start(bf16[4,128,1024]{2,1,0:T(8,128)(2,1)S(1)} %pad_maximum_fusion.2), channel_id=1, source_target_pairs={{0,1},{1,0},{2,3},{3,2},{4,5},{5,4},{6,7},{7,6},{8,9},{9,8},{10,11... | collective-permute-start | bytes 3145736 | tf_op jit(solution)/shard_map/ppermute | solution.py:88
  71.4 17.8 %collective-permute-start.22 = (bf16[2,704,256]{2,1,0:T(8,128)(2,1)S(1)}, bf16[2,704,256]{2,1,0:T(8,128)(2,1)S(1)}, u32[]{:S(2)}, u32[]{:S(2)}) collective-permute-start(bf16[2,704,256]{2,1,0:T(8,128)(2,1)S(1)} %copy-done.40), channel_id=1, source_target_pairs={{0,2},{2,0},{4,6},{6,4},{1,3},{3,1},{5,7},{7,5},{8,10},{10,8},{12,... | collective-permute-start | bytes 2162696 | tf_op jit(solution)/shard_map/ppermute | solution.py:88
  72.7 16.2 %collective-permute-start.18 = (bf16[128,1280]{1,0:T(8,128)(2,1)S(1)}, bf16[128,1280]{1,0:T(8,128)(2,1)S(1)}, u32[]{:S(2)}, u32[]{:S(2)}) collective-permute-start(bf16[128,1280]{1,0:T(8,128)(2,1)S(1)} %copy-done.44), channel_id=1, source_target_pairs={{0,8},{8,0},{16,24},{24,16},{1,9},{9,1},{17,25},{25,17},{2,10},{10... | collective-permute-start | bytes 983048 | tf_op jit(solution)/shard_map/ppermute | solution.py:88
  73.8 15.1 %collective-permute-start.19 = (bf16[128,1280]{1,0:T(8,128)(2,1)S(1)}, bf16[128,1280]{1,0:T(8,128)(2,1)S(1)}, u32[]{:S(2)}, u32[]{:S(2)}) collective-permute-start(bf16[128,1280]{1,0:T(8,128)(2,1)S(1)} %copy-done.43), channel_id=1, source_target_pairs={{0,16},{8,24},{16,0},{24,8},{1,17},{9,25},{17,1},{25,9},{2,18},{10... | collective-permute-start | bytes 983048 | tf_op jit(solution)/shard_map/ppermute | solution.py:88
  75.0 14.1 %collective-permute-start.20 = (bf16[128,1280]{1,0:T(8,128)(2,1)S(1)}, bf16[128,1280]{1,0:T(8,128)(2,1)S(1)}, u32[]{:S(2)}, u32[]{:S(2)}) collective-permute-start(bf16[128,1280]{1,0:T(8,128)(2,1)S(1)} %copy-done.42), channel_id=1, source_target_pairs={{0,24},{8,16},{16,8},{24,0},{1,25},{9,17},{17,9},{25,1},{2,26},{10... | collective-permute-start | bytes 983048 | tf_op jit(solution)/shard_map/ppermute | solution.py:88
  90.2 19.4 %collective-permute-start.23 = (bf16[4,128,1280]{2,1,0:T(8,128)(2,1)S(1)}, bf16[4,128,1280]{2,1,0:T(8,128)(2,1)S(1)}, u32[]{:S(2)}, u32[]{:S(2)}) collective-permute-start(bf16[4,128,1280]{2,1,0:T(8,128)(2,1)S(1)} %pad_maximum_fusion.mine_ref), channel_id=1, source_target_pairs={{0,1},{1,0},{2,3},{3,2},{4,5},{5,4},{6,7},{7,6},{8,9},{9,8},{10,11... | collective-permute-start | bytes 3932168 | tf_op jit(solution)/shard_map/ppermute | solution.py:88
  92.2 9.7 %collective-permute-start.28 = (bf16[2,352,256]{2,1,0:T(8,128)(2,1)S(1)}, bf16[2,352,256]{2,1,0:T(8,128)(2,1)S(1)}, u32[]{:S(2)}, u32[]{:S(2)}) collective-permute-start(bf16[2,352,256]{2,1,0:T(8,128)(2,1)S(1)} %copy-done.41), channel_id=1, source_target_pairs={{0,2},{2,0},{4,6},{6,4},{1,3},{3,1},{5,7},{7,5},{8,10},{10,8},{12,... | collective-permute-start | bytes 1081352 | tf_op jit(solution)/shard_map/ppermute | solution.py:88
  95.8 9.3 %collective-permute-start.27 = (bf16[320,128]{1,0:T(8,128)(2,1)S(1)}, bf16[320,128]{1,0:T(8,128)(2,1)S(1)}, u32[]{:S(2)}, u32[]{:S(2)}) collective-permute-start(bf16[320,128]{1,0:T(8,128)(2,1)S(1)} %get-tuple-element.184), channel_id=1, source_target_pairs={{0,6},{2,4},{4,2},{6,0},{1,7},{3,5},{5,3},{7,1},{8,14},{10,12},{12... | collective-permute-start | bytes 245768 | tf_op jit(solution)/shard_map/ppermute | solution.py:88
  98.2 6.9 %collective-permute-start.26 = (bf16[320,128]{1,0:T(8,128)(2,1)S(1)}, bf16[320,128]{1,0:T(8,128)(2,1)S(1)}, u32[]{:S(2)}, u32[]{:S(2)}) collective-permute-start(bf16[320,128]{1,0:T(8,128)(2,1)S(1)} %get-tuple-element.185), channel_id=1, source_target_pairs={{0,4},{2,6},{4,0},{6,2},{1,5},{3,7},{5,1},{7,3},{8,12},{10,14},{12... | collective-permute-start | bytes 245768 | tf_op jit(solution)/shard_map/ppermute | solution.py:88
  98.2 8.9 %collective-permute-start.25 = (bf16[320,128]{1,0:T(8,128)(2,1)S(1)}, bf16[320,128]{1,0:T(8,128)(2,1)S(1)}, u32[]{:S(2)}, u32[]{:S(2)}) collective-permute-start(bf16[320,128]{1,0:T(8,128)(2,1)S(1)} %get-tuple-element.186), channel_id=1, source_target_pairs={{0,2},{2,0},{4,6},{6,4},{1,3},{3,1},{5,7},{7,5},{8,10},{10,8},{12,... | collective-permute-start | bytes 245768 | tf_op jit(solution)/shard_map/ppermute | solution.py:88
  107.9 26.7 %collective-permute-start.33 = (bf16[1,1056,256]{2,1,0:T(8,128)(2,1)S(1)}, bf16[1,1056,256]{2,1,0:T(8,128)(2,1)S(1)}, u32[]{:S(2)}, u32[]{:S(2)}) collective-permute-start(bf16[1,1056,256]{2,1,0:T(8,128)(2,1)S(1)} %slice.188), channel_id=1, source_target_pairs={{0,4},{2,6},{4,0},{6,2},{1,5},{3,7},{5,1},{7,3},{8,12},{10,14},{12... | collective-permute-start | bytes 1622024 | tf_op jit(solution)/shard_map/ppermute | solution.py:88
  130.4 8.8 %collective-permute-start.35 = (bf16[488,128]{1,0:T(8,128)(2,1)}, bf16[488,128]{1,0:T(8,128)(2,1)S(1)}, u32[]{:S(2)}, u32[]{:S(2)}) collective-permute-start(bf16[488,128]{1,0:T(8,128)(2,1)} %get-tuple-element.162), channel_id=1, source_target_pairs={{0,2},{2,0},{4,6},{6,4},{1,3},{3,1},{5,7},{7,5},{8,10},{10,8},{12,... | collective-permute-start | bytes 374792 | tf_op jit(solution)/shard_map/ppermute | solution.py:88
  131.1 11.0 %collective-permute-start.36 = (bf16[488,128]{1,0:T(8,128)(2,1)}, bf16[488,128]{1,0:T(8,128)(2,1)S(1)}, u32[]{:S(2)}, u32[]{:S(2)}) collective-permute-start(bf16[488,128]{1,0:T(8,128)(2,1)} %get-tuple-element.163), channel_id=1, source_target_pairs={{0,4},{2,6},{4,0},{6,2},{1,5},{3,7},{5,1},{7,3},{8,12},{10,14},{12... | collective-permute-start | bytes 374792 | tf_op jit(solution)/shard_map/ppermute | solution.py:88
  131.8 10.3 %collective-permute-start.37 = (bf16[488,128]{1,0:T(8,128)(2,1)}, bf16[488,128]{1,0:T(8,128)(2,1)S(1)}, u32[]{:S(2)}, u32[]{:S(2)}) collective-permute-start(bf16[488,128]{1,0:T(8,128)(2,1)} %get-tuple-element.164), channel_id=1, source_target_pairs={{0,6},{2,4},{4,2},{6,0},{1,7},{3,5},{5,3},{7,1},{8,14},{10,12},{12... | collective-permute-start | bytes 374792 | tf_op jit(solution)/shard_map/ppermute | solution.py:88
  135.6 19.5 %collective-permute-start.38 = (bf16[352,256]{1,0:T(8,128)(2,1)S(1)}, bf16[352,256]{1,0:T(8,128)(2,1)S(1)}, u32[]{:S(2)}, u32[]{:S(2)}) collective-permute-start(bf16[352,256]{1,0:T(8,128)(2,1)S(1)} %fusion), channel_id=1, source_target_pairs={{0,0},{2,8},{4,16},{6,24},{1,1},{3,9},{5,17},{7,25},{8,10},{10,2},... | collective-permute-start | bytes 540680 | tf_op jit(solution)/shard_map/ppermute | solution.py:786
  (62 other events, 305.0 us)

commit v5 on v4

--- a/solution.py
+++ b/solution.py
@@ -201,7 +201,7 @@
         mixed[:, pair_lanes(pair)] = jnp.where(lane < DH, out[:tokens], out[tokens:]).astype(BF16)
         return carry
 
-    lax.fori_loop(0, H // 2, step, 0)
+    lax.fori_loop(0, H // 2, step, 0, unroll=True)
     resid = x_ref[...].astype(F32) + mm(mixed[...], wo_ref[...])
     resid_ref[...] = resid
     s2 = lax.rsqrt(jnp.mean(resid * resid, axis=1, keepdims=True) + EPS)
@@ -253,7 +253,7 @@
             grad_probs = mm(g, values)
             inner = jnp.sum(probs * grad_probs, axis=1, keepdims=True)
             grad_scores = (probs * (grad_probs - inner)).astype(BF16)
-            grad_q.append(mm(keys, grad_scores, NT) * SCALE)
+            grad_q.append(mm(grad_scores, keys, NT).T * SCALE)
             gk, gv = mm(qt, grad_scores) * SCALE, mm(gt, probs.astype(BF16))
             grad_k, grad_v = (gk, gv) if grad_k is None else (grad_k + gk, grad_v + gv)
         grad_q = jnp.concatenate(grad_q, axis=1)
@@ -347,10 +347,13 @@
             copy.start()
     wo_copy.start()
     h2 = h2_ref[...]
-    for j in range(n_chunks):
-        for copy in copies[j]:
-            copy.wait()
-        part = slice(j * chunk, (j + 1) * chunk)
+    groups = [[j] for j in range(min(3, n_chunks))]
+    groups += [list(range(j, min(j + 2, n_chunks))) for j in range(3, n_chunks, 2)]
+    for group in groups:
+        for j in group:
+            for copy in copies[j]:
+                copy.wait()
+        part = slice(group[0] * chunk, (group[-1] + 1) * chunk)
         gate, up = mm(h2, wg[:, part]), mm(h2, wu[:, part])
         grad_hidden = gh_ref[:, part]
         sig = jax.nn.sigmoid(gate)
@@ -360,7 +363,7 @@
         grad_up = (grad_hidden * silu).astype(BF16)
         more_branch = mm(hidden, wd[part, :])
         more_grad = mm(grad_gate, wg[:, part], NT) + mm(grad_up, wu[:, part], NT)
-        if j == 0:
+        if group[0] == 0:
             branch[...] = more_branch
             grad_h2[...] = more_grad
         else:
@@ -705,7 +708,7 @@
     for part in kv_z:
         kv_pieces += [part, swap(part, "core", 1)]
     hg_same = [hg] + others([hg] * n_rows, ROW, n_rows)
-    h2, mixed, resid, lse = attend(q, bias, w_out, x, gain_two, kv_pieces)
+    h2, mixed, resid, lse = attend(after(q, place), bias, w_out, x, gain_two, kv_pieces)
     h2_same = [h2] + others([h2] * n_rows, ROW, n_rows)
     hg_same = after(hg_same, h2)
     go_other = swap(jnp.stack([part[:, width:] for part in hg_same]), "core", 1)

time: 156 us -> 154 us (0.987)
  Pallas kernels: 69.4 us -> 64.5 us
    ppermute x38, waiting for transfers between devices: 20.8 us -> 26.1 us  [swap(): return lax.ppermute(value, axis, [(j, j ^ k) for j in range(size)])]
    pallas_call x9, Pallas kernels: 64.6 us -> 59.7 us  [call(): pl.pallas_call(kernel, out_shape=[jax.ShapeDtypeStruct(s, d) for s, d in...]
    ppermute x1, waiting for transfers between devices: 10.9 us -> 6.68 us  [body(): lax.ppermute(down_total.astype(BF16), ROW + CTX, moves).astype(F32)]
    unnamed x93 -> x89, local copies, waits for them, and re-layouts: 6.28 us -> 6.91 us
  transfers between devices with their start and end apart: 39 -> 39, of which waited for: 18 -> 17; matrix products, arithmetic and copies ran while one was open for 4% -> 4% of each run, Pallas kernels for 36% -> 34%
where the time goes in v5:
time: 154 us; the launch traced here: 153 us
  Pallas kernels  64.5 us (42%)
  starting transfers between devices  38.5 us (25%)
  waiting for transfers between devices  32.8 us (21%)
  local copies, waits for them, and re-layouts  8.52 us (6%)
  other arithmetic  6.93 us (4%)
  between operations  1.87 us (1%)
    pallas_call x9, Pallas kernels, call(): pl.pallas_call(kernel, out_shape=[jax.ShapeDtypeStruct(s, d) for s, d in...  59.7 us
    ppermute x38, starting transfers between devices, swap(): return lax.ppermute(value, axis, [(j, j ^ k) for j in range(size)])  36.5 us
    ppermute x38, waiting for transfers between devices, swap(): return lax.ppermute(value, axis, [(j, j ^ k) for j in range(size)])  26.1 us
    unnamed x89, local copies, waits for them, and re-layouts  6.91 us
    ppermute x1, waiting for transfers between devices, body(): lax.ppermute(down_total.astype(BF16), ROW + CTX, moves).astype(F32)  6.68 us
    pallas_call x1, Pallas kernels, hidden_grads(): pl.pallas_call(hidden_kernel, grid=(ff // chunk,), in_specs=[pl.BlockSpec...  4.84 us
  transfers between devices with their start and end apart: 39, of which 17 were waited for; matrix products, arithmetic and copies ran while one was open for 4% of the time, Pallas kernels for 34%

profile of v5, /device:TPU:3, one launch (start us, length us, event | category | flops | bytes accessed | tf_op | source)
XLA Modules:
  0.0 153.2 jit_solution(528502604537805656)
XLA Ops:
  2.5 3.5 %factors.1 = (bf16[128,2048]{1,0:T(8,128)(2,1)}, f32[128,1]{1,0:T(8,128)}, bf16[128,1024]{1,0:T(8,128)(2,1)}, bf16[1024,128]{1,0:T(8,128)(2,1)}, f32[480,128]{1,...) custom-call(bf16[128,1024]{1,0:T(8,128)(2,1)} %bitcast.100, ...), custom_call_target="tpu_custom_call" | custom-call | flops 209715200 | bytes 1638400 | tf_op jit(solution)/shard_map/factors/pallas_call | solution.py:47
  6.1 3.3 %collective-permute-start.2 = (bf16[320,128]{1,0:T(8,128)(2,1)}, bf16[320,128]{1,0:T(8,128)(2,1)S(1)}, u32[]{:S(2)}, u32[]{:S(2)}) collective-permute-start(bf16[320,128]{1,0:T(8,128)(2,1)} %get-tuple-element.95.refs_5_.refs_9_), channel_id=1, source_target_pairs={{0,6},{2,4},{4,2},{6,0},{1,7},{3,5},{5,3},{7,1},{8,14},{10,12},{12... | collective-permute-start | bytes 245768 | tf_op jit(solution)/shard_map/ppermute | solution.py:88
  12.6 4.8 %hidden_grads.1.gh_ref = f32[128,2816]{1,0:T(8,128)} custom-call(bf16[128,2048]{1,0:T(8,128)(2,1)} %get-tuple-element.127.go_ref.hg_ref.refs_8_.refs_0_, bf16[2816,1024]{1,0:T(8,128)(2,1)} %wd_ref.3), custom_call_target="tpu_custom_call" | custom-call | flops 738197504 | bytes 7208960 | tf_op jit(solution)/shard_map/hidden_grads/pallas_call | solution.py:314
  17.5 2.3 %collective-permute-start.3 = (bf16[320,128]{1,0:T(8,128)(2,1)S(1)}, bf16[320,128]{1,0:T(8,128)(2,1)S(1)}, u32[]{:S(2)}, u32[]{:S(2)}) collective-permute-start(bf16[320,128]{1,0:T(8,128)(2,1)S(1)} %copy-done.29), channel_id=1, source_target_pairs={{0,1},{1,0},{2,3},{3,2},{4,5},{5,4},{6,7},{7,6},{8,9},{9,8},{10,11... | collective-permute-start | bytes 245768 | tf_op jit(solution)/shard_map/ppermute | solution.py:88
  23.2 7.9 %attend.1 = (bf16[128,1024]{1,0:T(8,128)(2,1)}, bf16[128,1024]{1,0:T(8,128)(2,1)}, f32[128,1024]{1,0:T(8,128)}, f32[8,256,1]{2,1,0:T(8,128)}) custom-call(bf16[128,1024]{1,0:T(8,128)(2,1)} %get-tuple-element.92.refs_0_, f32[128,1024]{1,0:T(8,128)} %and_select_fusion.refs_1_.refs_5_, bf16[1024,1024]{1,0:T(8,128)(2,1)} %wo_hbm.1, bf16[128,1024]{1,0:T(8,128)(2,1)} %bitcast.101, ...), custom_call_target="tpu_custom_call" | custom-call | flops 536870912 | bytes 2097152 | tf_op jit(solution)/shard_map/attend/pallas_call | solution.py:47
  31.2 4.8 %collective-permute-done.8.refs_10_.refs_2_ = bf16[128,2048]{1,0:T(8,128)(2,1)S(1)} collective-permute-done((bf16[128,2048]{1,0:T(8,128)(2,1)}, bf16[128,2048]{1,0:T(8,128)(2,1)S(1)}, u32[]{:S(2)}, u32[]{:S(2)}) %collective-permute-start.8) | collective-permute-done | bytes 524320 | tf_op jit(solution)/shard_map/ppermute | solution.py:88
  40.1 13.5 %feed_forward.1 = (bf16[128,1024]{1,0:T(8,128)(2,1)}, f32[1,1024]{1,0:T(1,128)}, f32[128,1024]{1,0:T(8,128)}, bf16[128,1024]{1,0:T(8,128)(2,1)}, bf16[1024,128]{...) custom-call(s32[3]{0:T(128)} %pad_add_fusion.place_ref, ...), custom_call_target="tpu_custom_call" | custom-call | flops 3690987520 | bytes 17301504 | tf_op jit(solution)/shard_map/feed_forward/pallas_call | solution.py:47
  58.0 9.4 %weight_grads.1 = (bf16[2,704,256]{2,1,0:T(8,128)(2,1)}, bf16[2,704,256]{2,1,0:T(8,128)(2,1)}, bf16[2,352,256]{2,1,0:T(8,128)(2,1)}, bf16[2,352,256]{2,1,0:T(8,128)(2,1)}) custom-call(s32[3]{0:T(128)} %pad_add_fusion.place_ref, bf16[1024,2816]{1,0:T(8,128)(2,1)} %wg_ref.1, bf16[1024,2816]{1,0:T(8,128)(2,1)} %wu_ref.1, bf16[2816,1024]{1,0:T(8,128)(2,1)} %wd_ref.3, ...), custom_call_target="tpu_custom_call" | custom-call | flops 4429185024 | bytes 6356992 | tf_op jit(solution)/shard_map/weight_grads/pallas_call | solution.py:47
  73.3 13.2 %attend_back.1 = (f32[480,128]{1,0:T(8,128)}, bf16[4,320,128]{2,1,0:T(8,128)(2,1)}, bf16[4,320,128]{2,1,0:T(8,128)(2,1)}) custom-call(bf16[128,1024]{1,0:T(8,128)(2,1)} %get-tuple-element.92.refs_0_, bf16[1024,128]{1,0:T(8,128)(2,1)} %get-tuple-element.108.refs_1_, bf16[128,1024]{1,0:T(8,128)(2,1)} %get-tuple-element.115.refs_2_, ...), custom_call_target="tpu_custom_call" | custom-call | flops 1342177280 | bytes 524288 | tf_op jit(solution)/shard_map/attend_back/pallas_call | solution.py:47
  90.4 1.8 %collective-permute-done.24 = bf16[4,320,128]{2,1,0:T(8,128)(2,1)S(1)} collective-permute-done((bf16[4,320,128]{2,1,0:T(8,128)(2,1)S(1)}, bf16[4,320,128]{2,1,0:T(8,128)(2,1)S(1)}, u32[]{:S(2)}, u32[]{:S(2)}) %collective-permute-start.24) | collective-permute-done | bytes 327712 | tf_op jit(solution)/shard_map/ppermute | solution.py:88
  93.0 3.2 %collective-permute-start.27 = (bf16[320,128]{1,0:T(8,128)(2,1)S(1)}, bf16[320,128]{1,0:T(8,128)(2,1)S(1)}, u32[]{:S(2)}, u32[]{:S(2)}) collective-permute-start(bf16[320,128]{1,0:T(8,128)(2,1)S(1)} %get-tuple-element.186), channel_id=1, source_target_pairs={{0,6},{2,4},{4,2},{6,0},{1,7},{3,5},{5,3},{7,1},{8,14},{10,12},{12... | collective-permute-start | bytes 245768 | tf_op jit(solution)/shard_map/ppermute | solution.py:88
  96.5 2.4 %collective-permute-done.28 = bf16[2,352,256]{2,1,0:T(8,128)(2,1)S(1)} collective-permute-done((bf16[2,352,256]{2,1,0:T(8,128)(2,1)S(1)}, bf16[2,352,256]{2,1,0:T(8,128)(2,1)S(1)}, u32[]{:S(2)}, u32[]{:S(2)}) %collective-permute-start.28) | collective-permute-done | bytes 360480 | tf_op jit(solution)/shard_map/ppermute | solution.py:88
  98.9 3.9 %collective-permute-done.27.refs_3_ = bf16[320,128]{1,0:T(8,128)(2,1)S(1)} collective-permute-done((bf16[320,128]{1,0:T(8,128)(2,1)S(1)}, bf16[320,128]{1,0:T(8,128)(2,1)S(1)}, u32[]{:S(2)}, u32[]{:S(2)}) %collective-permute-start.27) | collective-permute-done | bytes 81952 | tf_op jit(solution)/shard_map/ppermute | solution.py:88
  104.8 2.6 %collective-permute-start.33 = (bf16[1,1056,256]{2,1,0:T(8,128)(2,1)S(1)}, bf16[1,1056,256]{2,1,0:T(8,128)(2,1)S(1)}, u32[]{:S(2)}, u32[]{:S(2)}) collective-permute-start(bf16[1,1056,256]{2,1,0:T(8,128)(2,1)S(1)} %slice.188), channel_id=1, source_target_pairs={{0,4},{2,6},{4,0},{6,2},{1,5},{3,7},{5,1},{7,3},{8,12},{10,14},{12... | collective-permute-start | bytes 1622024 | tf_op jit(solution)/shard_map/ppermute | solution.py:88
  108.4 3.0 %out_grads.1 = (bf16[256,128]{1,0:T(8,128)(2,1)}, bf16[256,128]{1,0:T(8,128)(2,1)}, bf16[256,128]{1,0:T(8,128)(2,1)}, bf16[256,128]{1,0:T(8,128)(2,1)}) custom-call(s32[3]{0:T(128)} %pad_add_fusion.place_ref, bf16[4,128,1280]{2,1,0:T(8,128)(2,1)} %copy-done.3, bf16[4,128,1280]{2,1,0:T(8,128)(2,1)} %copy-done.10), custom_call_target="tpu_custom_call" | custom-call | flops 268435456 | bytes 5242880 | tf_op jit(solution)/shard_map/out_grads/pallas_call | solution.py:47
  111.4 3.4 %input_grads.1 = (f32[128,1024]{1,0:T(8,128)}, bf16[232,128]{1,0:T(8,128)(2,1)}, bf16[232,128]{1,0:T(8,128)(2,1)}, bf16[232,128]{1,0:T(8,128)(2,1)}, bf16[232,128]{1,0:T(8,128)(2,1)}) custom-call(s32[3]{0:T(128)} %pad_add_fusion.place_ref, f32[480,128]{1,0:T(8,128)} %get-tuple-element.139.gq_ref, bf16[320,128]{1,0:T(8,128)(2,1)} %get-tuple-element.145.refs_0_, ...), custom_call_target="tpu_custom_call" | custom-call | flops 209715200 | bytes 1638400 | tf_op jit(solution)/shard_map/input_grads/pallas_call | solution.py:47
  117.4 3.2 %own_slab.1.h1_ref = bf16[1024,512]{1,0:T(8,128)(2,1)} custom-call(s32[3]{0:T(128)} %pad_add_fusion.place_ref, bf16[4,128,1024]{2,1,0:T(8,128)(2,1)} %copy-done.11, bf16[128,2048]{1,0:T(8,128)(2,1)} %get-tuple-element.127.go_ref.hg_ref.refs_8_.refs_0_, bf16[128,2048]{1,0:T(8,128)(2,1)} %copy-done.8, bf16[128,2048]{1,0:T(8,128)(2,1)} %copy-done.6, ...), custom_call_target="tpu_custom_call" | custom-call | bytes 1048576 | tf_op jit(solution)/shard_map/own_slab/pallas_call | solution.py:47
  121.5 2.4 %collective-permute-start.32 = (bf16[4,232,128]{2,1,0:T(8,128)(2,1)S(1)}, bf16[4,232,128]{2,1,0:T(8,128)(2,1)}, u32[]{:S(2)}, u32[]{:S(2)}) collective-permute-start(bf16[4,232,128]{2,1,0:T(8,128)(2,1)S(1)} %pad_maximum_fusion.3.mine_ref), channel_id=1, source_target_pairs={{0,1},{1,0},{2,3},{3,2},{4,5},{5,4},{6,7},{7,6},{8,9},{9,8},{10,11... | collective-permute-start | bytes 712712 | tf_op jit(solution)/shard_map/ppermute | solution.py:88
  125.2 2.6 %fact_grads.1 = (bf16[488,128]{1,0:T(8,128)(2,1)}, bf16[488,128]{1,0:T(8,128)(2,1)}, bf16[488,128]{1,0:T(8,128)(2,1)}, bf16[488,128]{1,0:T(8,128)(2,1)}) custom-call(bf16[1024,512]{1,0:T(8,128)(2,1)} %own_slab.1.h1_ref, bf16[4,232,128]{2,1,0:T(8,128)(2,1)} %copy-done.13, bf16[4,232,128]{2,1,0:T(8,128)(2,1)} %collective-permute-done.32.other_ref, ...), custom_call_target="tpu_custom_call" | custom-call | flops 243269632 | bytes 1048576 | tf_op jit(solution)/shard_map/fact_grads/pallas_call | solution.py:47
  129.2 2.2 %collective-permute-start.37 = (bf16[488,128]{1,0:T(8,128)(2,1)}, bf16[488,128]{1,0:T(8,128)(2,1)S(1)}, u32[]{:S(2)}, u32[]{:S(2)}) collective-permute-start(bf16[488,128]{1,0:T(8,128)(2,1)} %get-tuple-element.166), channel_id=1, source_target_pairs={{0,6},{2,4},{4,2},{6,0},{1,7},{3,5},{5,3},{7,1},{8,14},{10,12},{12... | collective-permute-start | bytes 374792 | tf_op jit(solution)/shard_map/ppermute | solution.py:88
  131.6 1.3 collective-permute-start.34
  132.9 2.1 %collective-permute-start.38 = (bf16[352,256]{1,0:T(8,128)(2,1)S(1)}, bf16[352,256]{1,0:T(8,128)(2,1)S(1)}, u32[]{:S(2)}, u32[]{:S(2)}) collective-permute-start(bf16[352,256]{1,0:T(8,128)(2,1)S(1)} %fusion), channel_id=1, source_target_pairs={{0,0},{2,8},{4,16},{6,24},{1,1},{3,9},{5,17},{7,25},{8,10},{10,2},... | collective-permute-start | bytes 540680 | tf_op jit(solution)/shard_map/ppermute | solution.py:789
  136.7 6.9 %collective-permute-done.36 = bf16[488,128]{1,0:T(8,128)(2,1)S(1)} collective-permute-done((bf16[488,128]{1,0:T(8,128)(2,1)}, bf16[488,128]{1,0:T(8,128)(2,1)S(1)}, u32[]{:S(2)}, u32[]{:S(2)}) %collective-permute-start.36) | collective-permute-done | bytes 124960 | tf_op jit(solution)/shard_map/ppermute | solution.py:88
  145.7 6.7 %collective-permute-done.38 = bf16[352,256]{1,0:T(8,128)(2,1)S(1)} collective-permute-done((bf16[352,256]{1,0:T(8,128)(2,1)S(1)}, bf16[352,256]{1,0:T(8,128)(2,1)S(1)}, u32[]{:S(2)}, u32[]{:S(2)}) %collective-permute-start.38) | collective-permute-done | bytes 180256 | tf_op jit(solution)/shard_map/ppermute | solution.py:789
  (190 shorter events, 40.8 us)
Async XLA Ops:
  9.4 8.1 %collective-permute-start.1 = (bf16[320,128]{1,0:T(8,128)(2,1)}, bf16[320,128]{1,0:T(8,128)(2,1)S(1)}, u32[]{:S(2)}, u32[]{:S(2)}) collective-permute-start(bf16[320,128]{1,0:T(8,128)(2,1)} %get-tuple-element.95.refs_5_.refs_9_), channel_id=1, source_target_pairs={{0,4},{2,6},{4,0},{6,2},{1,5},{3,7},{5,1},{7,3},{8,12},{10,14},{12... | collective-permute-start | bytes 245768 | tf_op jit(solution)/shard_map/ppermute | solution.py:88
  9.4 8.1 %collective-permute-start = (bf16[320,128]{1,0:T(8,128)(2,1)}, bf16[320,128]{1,0:T(8,128)(2,1)S(1)}, u32[]{:S(2)}, u32[]{:S(2)}) collective-permute-start(bf16[320,128]{1,0:T(8,128)(2,1)} %get-tuple-element.95.refs_5_.refs_9_), channel_id=1, source_target_pairs={{0,2},{2,0},{4,6},{6,4},{1,3},{3,1},{5,7},{7,5},{8,10},{10,8},{12,... | collective-permute-start | bytes 245768 | tf_op jit(solution)/shard_map/ppermute | solution.py:88
  9.7 21.4 %collective-permute-start.9 = (bf16[128,2048]{1,0:T(8,128)(2,1)}, bf16[128,2048]{1,0:T(8,128)(2,1)S(1)}, u32[]{:S(2)}, u32[]{:S(2)}) collective-permute-start(bf16[128,2048]{1,0:T(8,128)(2,1)} %get-tuple-element.127.go_ref.hg_ref.refs_8_.refs_0_), channel_id=1, source_target_pairs={{0,24},{8,16},{16,8},{24,0},{1,25},{9,17},{17,9},{25,1},{2,26},{10... | collective-permute-start | bytes 1572872 | tf_op jit(solution)/shard_map/ppermute | solution.py:88
  11.0 25.0 %collective-permute-start.8 = (bf16[128,2048]{1,0:T(8,128)(2,1)}, bf16[128,2048]{1,0:T(8,128)(2,1)S(1)}, u32[]{:S(2)}, u32[]{:S(2)}) collective-permute-start(bf16[128,2048]{1,0:T(8,128)(2,1)} %get-tuple-element.127.go_ref.hg_ref.refs_8_.refs_0_), channel_id=1, source_target_pairs={{0,16},{8,24},{16,0},{24,8},{1,17},{9,25},{17,1},{25,9},{2,18},{10... | collective-permute-start | bytes 1572872 | tf_op jit(solution)/shard_map/ppermute | solution.py:88
  11.5 24.4 %collective-permute-start.7 = (bf16[128,2048]{1,0:T(8,128)(2,1)}, bf16[128,2048]{1,0:T(8,128)(2,1)S(1)}, u32[]{:S(2)}, u32[]{:S(2)}) collective-permute-start(bf16[128,2048]{1,0:T(8,128)(2,1)} %get-tuple-element.127.go_ref.hg_ref.refs_8_.refs_0_), channel_id=1, source_target_pairs={{0,8},{8,0},{16,24},{24,16},{1,9},{9,1},{17,25},{25,17},{2,10},{10... | collective-permute-start | bytes 1572872 | tf_op jit(solution)/shard_map/ppermute | solution.py:88
  36.9 16.7 %collective-permute-start.10 = (bf16[4,128,1024]{2,1,0:T(8,128)(2,1)S(1)}, bf16[4,128,1024]{2,1,0:T(8,128)(2,1)S(1)}, u32[]{:S(2)}, u32[]{:S(2)}) collective-permute-start(bf16[4,128,1024]{2,1,0:T(8,128)(2,1)S(1)} %pad_maximum_fusion.1), channel_id=1, source_target_pairs={{0,1},{1,0},{2,3},{3,2},{4,5},{5,4},{6,7},{7,6},{8,9},{9,8},{10,11... | collective-permute-start | bytes 3145736 | tf_op jit(solution)/shard_map/ppermute | solution.py:88
  37.4 16.2 %collective-permute-start.13 = (bf16[128,1024]{1,0:T(8,128)(2,1)}, bf16[128,1024]{1,0:T(8,128)(2,1)S(1)}, u32[]{:S(2)}, u32[]{:S(2)}) collective-permute-start(bf16[128,1024]{1,0:T(8,128)(2,1)} %get-tuple-element.110.h2_ref.refs_0_), channel_id=1, source_target_pairs={{0,24},{8,16},{16,8},{24,0},{1,25},{9,17},{17,9},{25,1},{2,26},{10... | collective-permute-start | bytes 786440 | tf_op jit(solution)/shard_map/ppermute | solution.py:88
  38.6 15.0 %collective-permute-start.12 = (bf16[128,1024]{1,0:T(8,128)(2,1)}, bf16[128,1024]{1,0:T(8,128)(2,1)S(1)}, u32[]{:S(2)}, u32[]{:S(2)}) collective-permute-start(bf16[128,1024]{1,0:T(8,128)(2,1)} %get-tuple-element.110.h2_ref.refs_0_), channel_id=1, source_target_pairs={{0,16},{8,24},{16,0},{24,8},{1,17},{9,25},{17,1},{25,9},{2,18},{10... | collective-permute-start | bytes 786440 | tf_op jit(solution)/shard_map/ppermute | solution.py:88
  38.9 14.8 %collective-permute-start.11 = (bf16[128,1024]{1,0:T(8,128)(2,1)}, bf16[128,1024]{1,0:T(8,128)(2,1)S(1)}, u32[]{:S(2)}, u32[]{:S(2)}) collective-permute-start(bf16[128,1024]{1,0:T(8,128)(2,1)} %get-tuple-element.110.h2_ref.refs_0_), channel_id=1, source_target_pairs={{0,8},{8,0},{16,24},{24,16},{1,9},{9,1},{17,25},{25,17},{2,10},{10... | collective-permute-start | bytes 786440 | tf_op jit(solution)/shard_map/ppermute | solution.py:88
  68.6 18.3 %collective-permute-start.21 = (bf16[4,128,1024]{2,1,0:T(8,128)(2,1)S(1)}, bf16[4,128,1024]{2,1,0:T(8,128)(2,1)S(1)}, u32[]{:S(2)}, u32[]{:S(2)}) collective-permute-start(bf16[4,128,1024]{2,1,0:T(8,128)(2,1)S(1)} %pad_maximum_fusion.2), channel_id=1, source_target_pairs={{0,1},{1,0},{2,3},{3,2},{4,5},{5,4},{6,7},{7,6},{8,9},{9,8},{10,11... | collective-permute-start | bytes 3145736 | tf_op jit(solution)/shard_map/ppermute | solution.py:88
  69.5 17.4 %collective-permute-start.22 = (bf16[2,704,256]{2,1,0:T(8,128)(2,1)S(1)}, bf16[2,704,256]{2,1,0:T(8,128)(2,1)S(1)}, u32[]{:S(2)}, u32[]{:S(2)}) collective-permute-start(bf16[2,704,256]{2,1,0:T(8,128)(2,1)S(1)} %copy-done.38), channel_id=1, source_target_pairs={{0,2},{2,0},{4,6},{6,4},{1,3},{3,1},{5,7},{7,5},{8,10},{10,8},{12,... | collective-permute-start | bytes 2162696 | tf_op jit(solution)/shard_map/ppermute | solution.py:88
  70.6 15.8 %collective-permute-start.18 = (bf16[128,1280]{1,0:T(8,128)(2,1)S(1)}, bf16[128,1280]{1,0:T(8,128)(2,1)S(1)}, u32[]{:S(2)}, u32[]{:S(2)}) collective-permute-start(bf16[128,1280]{1,0:T(8,128)(2,1)S(1)} %copy-done.42), channel_id=1, source_target_pairs={{0,8},{8,0},{16,24},{24,16},{1,9},{9,1},{17,25},{25,17},{2,10},{10... | collective-permute-start | bytes 983048 | tf_op jit(solution)/shard_map/ppermute | solution.py:88
  70.9 15.6 %collective-permute-start.19 = (bf16[128,1280]{1,0:T(8,128)(2,1)S(1)}, bf16[128,1280]{1,0:T(8,128)(2,1)S(1)}, u32[]{:S(2)}, u32[]{:S(2)}) collective-permute-start(bf16[128,1280]{1,0:T(8,128)(2,1)S(1)} %copy-done.41), channel_id=1, source_target_pairs={{0,16},{8,24},{16,0},{24,8},{1,17},{9,25},{17,1},{25,9},{2,18},{10... | collective-permute-start | bytes 983048 | tf_op jit(solution)/shard_map/ppermute | solution.py:88
  72.1 14.4 %collective-permute-start.20 = (bf16[128,1280]{1,0:T(8,128)(2,1)S(1)}, bf16[128,1280]{1,0:T(8,128)(2,1)S(1)}, u32[]{:S(2)}, u32[]{:S(2)}) collective-permute-start(bf16[128,1280]{1,0:T(8,128)(2,1)S(1)} %copy-done.40), channel_id=1, source_target_pairs={{0,24},{8,16},{16,8},{24,0},{1,25},{9,17},{17,9},{25,1},{2,26},{10... | collective-permute-start | bytes 983048 | tf_op jit(solution)/shard_map/ppermute | solution.py:88
  87.9 19.5 %collective-permute-start.23 = (bf16[4,128,1280]{2,1,0:T(8,128)(2,1)S(1)}, bf16[4,128,1280]{2,1,0:T(8,128)(2,1)S(1)}, u32[]{:S(2)}, u32[]{:S(2)}) collective-permute-start(bf16[4,128,1280]{2,1,0:T(8,128)(2,1)S(1)} %pad_maximum_fusion.mine_ref), channel_id=1, source_target_pairs={{0,1},{1,0},{2,3},{3,2},{4,5},{5,4},{6,7},{7,6},{8,9},{9,8},{10,11... | collective-permute-start | bytes 3932168 | tf_op jit(solution)/shard_map/ppermute | solution.py:88
  89.3 9.7 %collective-permute-start.28 = (bf16[2,352,256]{2,1,0:T(8,128)(2,1)S(1)}, bf16[2,352,256]{2,1,0:T(8,128)(2,1)S(1)}, u32[]{:S(2)}, u32[]{:S(2)}) collective-permute-start(bf16[2,352,256]{2,1,0:T(8,128)(2,1)S(1)} %copy-done.39), channel_id=1, source_target_pairs={{0,2},{2,0},{4,6},{6,4},{1,3},{3,1},{5,7},{7,5},{8,10},{10,8},{12,... | collective-permute-start | bytes 1081352 | tf_op jit(solution)/shard_map/ppermute | solution.py:88
  93.0 9.9 %collective-permute-start.27 = (bf16[320,128]{1,0:T(8,128)(2,1)S(1)}, bf16[320,128]{1,0:T(8,128)(2,1)S(1)}, u32[]{:S(2)}, u32[]{:S(2)}) collective-permute-start(bf16[320,128]{1,0:T(8,128)(2,1)S(1)} %get-tuple-element.186), channel_id=1, source_target_pairs={{0,6},{2,4},{4,2},{6,0},{1,7},{3,5},{5,3},{7,1},{8,14},{10,12},{12... | collective-permute-start | bytes 245768 | tf_op jit(solution)/shard_map/ppermute | solution.py:88
  96.2 6.7 %collective-permute-start.26 = (bf16[320,128]{1,0:T(8,128)(2,1)S(1)}, bf16[320,128]{1,0:T(8,128)(2,1)S(1)}, u32[]{:S(2)}, u32[]{:S(2)}) collective-permute-start(bf16[320,128]{1,0:T(8,128)(2,1)S(1)} %get-tuple-element.187), channel_id=1, source_target_pairs={{0,4},{2,6},{4,0},{6,2},{1,5},{3,7},{5,1},{7,3},{8,12},{10,14},{12... | collective-permute-start | bytes 245768 | tf_op jit(solution)/shard_map/ppermute | solution.py:88
  96.2 7.9 %collective-permute-start.25 = (bf16[320,128]{1,0:T(8,128)(2,1)S(1)}, bf16[320,128]{1,0:T(8,128)(2,1)S(1)}, u32[]{:S(2)}, u32[]{:S(2)}) collective-permute-start(bf16[320,128]{1,0:T(8,128)(2,1)S(1)} %get-tuple-element.188), channel_id=1, source_target_pairs={{0,2},{2,0},{4,6},{6,4},{1,3},{3,1},{5,7},{7,5},{8,10},{10,8},{12,... | collective-permute-start | bytes 245768 | tf_op jit(solution)/shard_map/ppermute | solution.py:88
  104.8 26.6 %collective-permute-start.33 = (bf16[1,1056,256]{2,1,0:T(8,128)(2,1)S(1)}, bf16[1,1056,256]{2,1,0:T(8,128)(2,1)S(1)}, u32[]{:S(2)}, u32[]{:S(2)}) collective-permute-start(bf16[1,1056,256]{2,1,0:T(8,128)(2,1)S(1)} %slice.188), channel_id=1, source_target_pairs={{0,4},{2,6},{4,0},{6,2},{1,5},{3,7},{5,1},{7,3},{8,12},{10,14},{12... | collective-permute-start | bytes 1622024 | tf_op jit(solution)/shard_map/ppermute | solution.py:88
  127.8 8.9 %collective-permute-start.35 = (bf16[488,128]{1,0:T(8,128)(2,1)}, bf16[488,128]{1,0:T(8,128)(2,1)S(1)}, u32[]{:S(2)}, u32[]{:S(2)}) collective-permute-start(bf16[488,128]{1,0:T(8,128)(2,1)} %get-tuple-element.164), channel_id=1, source_target_pairs={{0,2},{2,0},{4,6},{6,4},{1,3},{3,1},{5,7},{7,5},{8,10},{10,8},{12,... | collective-permute-start | bytes 374792 | tf_op jit(solution)/shard_map/ppermute | solution.py:88
  128.7 15.0 %collective-permute-start.36 = (bf16[488,128]{1,0:T(8,128)(2,1)}, bf16[488,128]{1,0:T(8,128)(2,1)S(1)}, u32[]{:S(2)}, u32[]{:S(2)}) collective-permute-start(bf16[488,128]{1,0:T(8,128)(2,1)} %get-tuple-element.165), channel_id=1, source_target_pairs={{0,4},{2,6},{4,0},{6,2},{1,5},{3,7},{5,1},{7,3},{8,12},{10,14},{12... | collective-permute-start | bytes 374792 | tf_op jit(solution)/shard_map/ppermute | solution.py:88
  129.2 14.5 %collective-permute-start.37 = (bf16[488,128]{1,0:T(8,128)(2,1)}, bf16[488,128]{1,0:T(8,128)(2,1)S(1)}, u32[]{:S(2)}, u32[]{:S(2)}) collective-permute-start(bf16[488,128]{1,0:T(8,128)(2,1)} %get-tuple-element.166), channel_id=1, source_target_pairs={{0,6},{2,4},{4,2},{6,0},{1,7},{3,5},{5,3},{7,1},{8,14},{10,12},{12... | collective-permute-start | bytes 374792 | tf_op jit(solution)/shard_map/ppermute | solution.py:88
  132.9 19.5 %collective-permute-start.38 = (bf16[352,256]{1,0:T(8,128)(2,1)S(1)}, bf16[352,256]{1,0:T(8,128)(2,1)S(1)}, u32[]{:S(2)}, u32[]{:S(2)}) collective-permute-start(bf16[352,256]{1,0:T(8,128)(2,1)S(1)} %fusion), channel_id=1, source_target_pairs={{0,0},{2,8},{4,16},{6,24},{1,1},{3,9},{5,17},{7,25},{8,10},{10,2},... | collective-permute-start | bytes 540680 | tf_op jit(solution)/shard_map/ppermute | solution.py:789
  (60 other events, 285.6 us)

commit v6 on v5

--- a/solution.py
+++ b/solution.py
@@ -97,14 +97,14 @@
 
 def factor_kernel(
     x_ref, cot_ref, valid_ref, gain_ref, wft_ref, pos_ref,
-    hg_ref, s1_ref, q_ref, qt_ref, qf_ref, kv_ref, cos_ref, sin_ref, ft,
+    h1_ref, go_ref, s1_ref, q_ref, qt_ref, qf_ref, kv_ref, cos_ref, sin_ref, ft,
 ):
     x = x_ref[...].astype(F32)
     s1 = lax.rsqrt(jnp.mean(x * x, axis=1, keepdims=True) + EPS)
     s1_ref[...] = s1
     h1 = (x * s1 * gain_ref[...]).astype(BF16)
-    hg_ref[:, :x.shape[1]] = h1
-    hg_ref[:, x.shape[1]:] = (cot_ref[...].astype(F32) * valid_ref[...]).astype(BF16)
+    h1_ref[...] = h1
+    go_ref[...] = (cot_ref[...].astype(F32) * valid_ref[...]).astype(BF16)
     half = lax.broadcasted_iota(jnp.int32, cos_ref.shape, 0).astype(F32)
     angles = pos_ref[...] * jnp.exp(-jnp.log(10000.0) * (2.0 * half) / DH)
     cosine, sine = jnp.cos(angles), jnp.sin(angles)
@@ -137,7 +137,7 @@
     angles = ((DH // 2, tokens), F32)
     return call(
         factor_kernel,
-        [((tokens, 2 * width), BF16), ((tokens, 1), F32), ((tokens, H * DH), BF16),
+        [((tokens, width), BF16), ((tokens, width), BF16), ((tokens, 1), F32), ((tokens, H * DH), BF16),
          ((H * DH, tokens), BF16), ((QF, tokens), F32), ((KF, tokens), BF16), angles, angles],
         [vmem()] * 6,
         (x, cot, valid, gain, w_fact_t, pos),
@@ -303,30 +303,8 @@
     )
 
 
-def hidden_kernel(go_ref, wd_ref, out_ref):
-    out_ref[...] = mm(go_ref[...], wd_ref[...], NT)
-
-
-def hidden_grads(hg, w_down):
-    tokens, width = hg.shape[0], hg.shape[1] // 2
-    ff = w_down.shape[0]
-    chunk = max(c for c in range(128, ff + 1, 128) if ff % c == 0 and c <= ff // 2)
-    return pl.pallas_call(
-        hidden_kernel,
-        grid=(ff // chunk,),
-        in_specs=[pl.BlockSpec((tokens, width), lambda j: (0, 1)), pl.BlockSpec((chunk, width), lambda j: (j, 0))],
-        out_specs=pl.BlockSpec((tokens, chunk), lambda j: (0, j)),
-        out_shape=jax.ShapeDtypeStruct((tokens, ff), F32),
-        compiler_params=pltpu.CompilerParams(vmem_limit_bytes=VMEM_BYTES),
-        cost_estimate=pl.CostEstimate(
-            flops=2 * tokens * width * ff, transcendentals=0, bytes_accessed=2 * width * ff + 4 * tokens * ff
-        ),
-        name="hidden_grads",
-    )(hg, w_down)
-
-
 def ffn_kernel(
-    place_ref, h2_ref, hg_ref, gh_ref, resid_ref, gain_ref, mixed_ref, wg_hbm, wu_hbm, wd_hbm, wo_hbm, *refs,
+    place_ref, h2_ref, go_ref, resid_ref, gain_ref, mixed_ref, wg_hbm, wu_hbm, wd_hbm, wo_hbm, *refs,
 ):
     out_ref, gain_grad_ref, gres_ref, gm_ref, gmt_ref = refs[:5]
     mgx_refs, (branch, grad_h2, gb_cols, wg, wu, wd, wo, sems) = refs[5:-8], refs[-8:]
@@ -346,16 +324,16 @@
         for copy in group:
             copy.start()
     wo_copy.start()
-    h2 = h2_ref[...]
-    groups = [[j] for j in range(min(3, n_chunks))]
-    groups += [list(range(j, min(j + 2, n_chunks))) for j in range(3, n_chunks, 2)]
+    h2, go = h2_ref[...], go_ref[...]
+    groups = [list(range(0, min(3, n_chunks)))]
+    groups += [list(range(j, min(j + 4, n_chunks))) for j in range(3, n_chunks, 4)]
     for group in groups:
         for j in group:
             for copy in copies[j]:
                 copy.wait()
         part = slice(group[0] * chunk, (group[-1] + 1) * chunk)
         gate, up = mm(h2, wg[:, part]), mm(h2, wu[:, part])
-        grad_hidden = gh_ref[:, part]
+        grad_hidden = mm(go, wd[part, :], NT)
         sig = jax.nn.sigmoid(gate)
         silu = gate * sig
         hidden = (silu * up).astype(BF16)
@@ -376,7 +354,7 @@
     gh = grad_h2[...]
     gain_grad_ref[...] = jnp.sum(gh * n2, axis=0, keepdims=True)
     g2 = gh * gain_ref[...]
-    gres = hg_ref[:, width:].astype(F32) + s2 * (g2 - n2 * jnp.mean(g2 * n2, axis=1, keepdims=True))
+    gres = go.astype(F32) + s2 * (g2 - n2 * jnp.mean(g2 * n2, axis=1, keepdims=True))
     gres_ref[...] = gres
     gb = gres.astype(BF16)
     gb_cols[...] = gb
@@ -390,7 +368,7 @@
         mgx_ref[:, width:] = gb_cols[:, pl.ds(pl.multiple_of((place_ref[0] ^ k) * cols, cols), cols)]
 
 
-def feed_forward(place, h2, hg, gh, w_gate, w_up, w_down, resid, gain, w_out, mixed, n_rows):
+def feed_forward(place, h2, go, w_gate, w_up, w_down, resid, gain, w_out, mixed, n_rows):
     tokens, width = resid.shape
     ff = w_gate.shape[1]
     chunk = 256 if ff % 256 == 0 else 128
@@ -398,17 +376,17 @@
         ffn_kernel,
         [((tokens, width), BF16), ((1, width), F32), ((tokens, width), F32), ((tokens, width), BF16),
          ((width, tokens), BF16)] + [((tokens, width + width // n_rows), BF16)] * n_rows,
-        [smem()] + [vmem()] * 6 + [hbm()] * 4,
-        (place, h2, hg, gh, resid, gain, mixed, w_gate, w_up, w_down, w_out),
+        [smem()] + [vmem()] * 5 + [hbm()] * 4,
+        (place, h2, go, resid, gain, mixed, w_gate, w_up, w_down, w_out),
         [pltpu.VMEM((tokens, width), F32), pltpu.VMEM((tokens, width), F32), pltpu.VMEM((tokens, width), BF16),
          pltpu.VMEM((width, ff), BF16), pltpu.VMEM((width, ff), BF16), pltpu.VMEM((ff, width), BF16),
          pltpu.VMEM((width, width), BF16), pltpu.SemaphoreType.DMA((4, ff // chunk))],
-        10 * tokens * width * ff, 6 * width * ff, "feed_forward",
+        12 * tokens * width * ff, 6 * width * ff, "feed_forward",
     )
 
 
 def weight_kernel(n_pieces, ordered, place_ref, wg_ref, wu_ref, wd_ref, go_other, *refs):
-    h2_pieces, hg_same = refs[:n_pieces], refs[n_pieces:n_pieces + n_pieces // 2]
+    h2_pieces, go_same = refs[:n_pieces], refs[n_pieces:n_pieces + n_pieces // 2]
     up_keep, up_send, down_keep, down_send, h2s, gos, wds, window, turned, sems = refs[n_pieces + n_pieces // 2:]
     tokens, width = h2_pieces[0].shape
     ff, span = wds.shape[0], window.shape[2]
@@ -421,7 +399,7 @@
         rows = pl.ds(j * tokens, tokens)
         groups[2].append(pltpu.make_async_copy(h2_pieces[j], h2s.at[rows, :], sems.at[0, j]))
         half = n_pieces // 2
-        go = hg_same[j].at[:, pl.ds(width, width)] if j < half else go_other.at[j - half]
+        go = go_same[j] if j < half else go_other.at[j - half]
         groups[3].append(pltpu.make_async_copy(go, gos.at[rows, :], sems.at[1, j]))
     groups[3].append(pltpu.make_async_copy(
         wd_ref.at[pl.ds(pl.multiple_of(at, 32), ff), :], wds, sems.at[1, n_pieces]))
@@ -473,7 +451,7 @@
     return order
 
 
-def weight_grads(place, w_gate, w_up, w_down, h2_pieces, hg_same, go_other, n_z, ordered):
+def weight_grads(place, w_gate, w_up, w_down, h2_pieces, go_same, go_other, n_z, ordered):
     n = len(h2_pieces)
     tokens, width = h2_pieces[0].shape
     ff = w_gate.shape[1] // n
@@ -483,7 +461,7 @@
         functools.partial(weight_kernel, n, ordered),
         [((n_z // 2, 2 * ff, width // n_z), BF16)] * 2 + [((n_z // 2, ff, width // n_z), BF16)] * 2,
         [smem()] + [hbm()] * (4 + n + n // 2),
-        (place, w_gate, w_up, w_down, go_other, *h2_pieces, *hg_same),
+        (place, w_gate, w_up, w_down, go_other, *h2_pieces, *go_same),
         [pltpu.VMEM((total, width), BF16), pltpu.VMEM((total, width), BF16), pltpu.VMEM((ff, width), BF16),
          pltpu.VMEM((2, width, span), BF16), pltpu.VMEM((2, span, width), BF16), pltpu.SemaphoreType.DMA((3, n + 1))],
         12 * total * width * ff, 6 * width * ff + 4 * total * width, "weight_grads",
@@ -497,13 +475,13 @@
 
 
 def slab_kernel(n_out, ordered, place_ref, h1_other, *refs):
-    *hg_same, h1_ref, sems = refs
-    n_same = len(hg_same)
+    *h1_same, h1_ref, sems = refs
+    n_same = len(h1_same)
     tokens = h1_other.shape[1]
     cols = h1_ref.shape[1] // n_out
     copies = []
     for j in range(2 * n_same):
-        piece = hg_same[j] if j < n_same else h1_other.at[j - n_same]
+        piece = h1_same[j] if j < n_same else h1_other.at[j - n_same]
         for k in range(n_out):
             copies.append(pltpu.make_async_copy(
                 piece.at[:, own_cut(ordered, place_ref, k, cols)],
@@ -514,15 +492,15 @@
         copy.wait()
 
 
-def own_slab(place, hg_same, h1_other, n_out, cols, ordered):
+def own_slab(place, h1_same, h1_other, n_out, cols, ordered):
     n, tokens, width = h1_other.shape
     if not ordered:
-        return jnp.concatenate([piece[:, :width] for piece in hg_same] + [h1_other.reshape(-1, width)], axis=0)
+        return jnp.concatenate([piece[:, :width] for piece in h1_same] + [h1_other.reshape(-1, width)], axis=0)
     return call(
         functools.partial(slab_kernel, n_out, ordered),
         [((2 * n * tokens, n_out * cols), BF16)],
         [smem()] + [hbm()] * (1 + n),
-        (place, h1_other, *hg_same),
+        (place, h1_other, *h1_same),
         [pltpu.SemaphoreType.DMA((2 * n, n_out))],
         0, 4 * n * tokens * n_out * cols, "own_slab",
     )[0]
@@ -698,26 +676,25 @@
         mine = jnp.stack(values)
         return [mine, swap(mine, "core", 1)]
 
-    hg, s1, q, qt, qf, kv, cosine, sine = project(
+    h1, go, s1, q, qt, qf, kv, cosine, sine = project(
         x, cotangent.reshape(tokens, width), valid, gain_one, w_fact_t, local_pos.astype(F32)[None, :]
     )
     kv_z = [kv] + others([kv] * n_z, "z", n_z)
-    gh = hidden_grads(hg, w_down)
-    kv_z = after(kv_z, gh)
     kv_pieces = []
     for part in kv_z:
         kv_pieces += [part, swap(part, "core", 1)]
-    hg_same = [hg] + others([hg] * n_rows, ROW, n_rows)
+    go_same = [go] + others([go] * n_rows, ROW, n_rows)
     h2, mixed, resid, lse = attend(after(q, place), bias, w_out, x, gain_two, kv_pieces)
     h2_same = [h2] + others([h2] * n_rows, ROW, n_rows)
-    hg_same = after(hg_same, h2)
-    go_other = swap(jnp.stack([part[:, width:] for part in hg_same]), "core", 1)
+    go_same = after(go_same, h2)
+    go_other = swap(jnp.stack(go_same), "core", 1)
     block_out, gain_two_part, gres, gm, gmt, *mgx = feed_forward(
-        place, h2, after(hg, hg_same), gh, w_gate, w_up, w_down, resid, gain_two, w_out, mixed, n_rows
+        place, h2, after(go, go_same), w_gate, w_up, w_down, resid, gain_two, w_out, mixed, n_rows
     )
     h2_pieces = along_core(after(h2_same, gm, go_other))
+    h1_same = [h1] + others(after([h1] * n_rows, gm), ROW, n_rows)
     up_keep, up_send, down_keep, down_send = weight_grads(
-        place, w_gate, w_up, w_down, h2_pieces, hg_same, go_other, n_z, ordered
+        place, w_gate, w_up, w_down, h2_pieces, go_same, go_other, n_z, ordered
     )
     if not ordered:
         turns = jnp.asarray(halving_order(n_z), jnp.int32) ^ z
@@ -729,10 +706,11 @@
         down = jnp.take(down.reshape(n_z, ff_part, 2 * own_cols), turns, axis=0)
         up_keep, up_send, down_keep, down_send = up[:n_z // 2], up[n_z // 2:], down[:n_z // 2], down[n_z // 2:]
 
+    h1_same = after(h1_same, up_send)
     up_got = swap(up_send, "z", 1)
     mg_same = [mgx[0]] + others(mgx, ROW, n_rows)
-    gm_in, hg_same = after((gm, hg_same), up_send)
-    h1_other = swap(jnp.stack([part[:, :width] for part in hg_same]), "core", 1)
+    gm_in = after(gm, up_send)
+    h1_other = swap(jnp.stack(h1_same), "core", 1)
     gq, gkv_own, gkv_send = attend_back(q, qt, gm_in, gmt, lse, bias, qf, cosine, sine, kv_pieces)
     gkv_send, mg_same, h1_other, up_got = lax.optimization_barrier((gkv_send, mg_same, h1_other, up_got))
     down_got = swap(after(down_send, up_got), "z", 1)
@@ -768,7 +746,7 @@
     )
     head = gfx[0].shape[0] - w_fact.shape[1] // n_rows
     gf_same = [gfx[0]] + others(gfx, ROW, n_rows)
-    h1_slab = own_slab(place, hg_same, after(h1_other, gfx[0]), n_out, own_cols, ordered)
+    h1_slab = own_slab(place, h1_same, after(h1_other, gfx[0]), n_out, own_cols, ordered)
     gf_all = both_cores(after(gf_same, h1_slab))
     tail_parts = own_blocks(fact_grads(h1_slab, *gf_all, out_parts, head, ordered))
     total = add_up(ffn_keep, ffn_got, tail_parts)

time: 154 us -> 151 us (0.981); the launches traced: 153 us -> 149 us
  Pallas kernels: 64.5 us -> 61.2 us
  starting transfers between devices: 38.5 us -> 41.8 us
  waiting for transfers between devices: 32.8 us -> 29.7 us
    ppermute x38 -> x41, waiting for transfers between devices: 26.1 us -> 18.6 us  [swap(): return lax.ppermute(value, axis, [(j, j ^ k) for j in range(size)])]
    pallas_call x1 -> x0, Pallas kernels: 4.84 us -> none  [hidden_grads(): pl.pallas_call(hidden_kernel, grid=(ff // chunk,), in_specs=[pl.BlockSpec...]
    ppermute x1, waiting for transfers between devices: 6.68 us -> 11.1 us  [body(): lax.ppermute(down_total.astype(BF16), ROW + CTX, moves).astype(F32)]
    ppermute x38 -> x41, starting transfers between devices: 36.5 us -> 39.9 us  [swap(): return lax.ppermute(value, axis, [(j, j ^ k) for j in range(size)])]
    unnamed x89 -> x91, local copies, waits for them, and re-layouts: 6.91 us -> 5.52 us
  transfers between devices with their start and end apart: 39 -> 42, of which waited for: 17 -> 13; matrix products, arithmetic and copies ran while one was open for 4% -> 4% of each run, Pallas kernels for 34% -> 39%
where the time goes in v6:
time: 151 us; the launch traced here: 149 us
  Pallas kernels  61.2 us (41%)
  starting transfers between devices  41.8 us (28%)
  waiting for transfers between devices  29.7 us (20%)
  local copies, waits for them, and re-layouts  6.98 us (5%)
  other arithmetic  6.88 us (5%)
  between operations  1.93 us (1%)
    pallas_call x9, Pallas kernels, call(): pl.pallas_call(kernel, out_shape=[jax.ShapeDtypeStruct(s, d) for s, d in...  61.2 us
    ppermute x41, starting transfers between devices, swap(): return lax.ppermute(value, axis, [(j, j ^ k) for j in range(size)])  39.9 us
    ppermute x41, waiting for transfers between devices, swap(): return lax.ppermute(value, axis, [(j, j ^ k) for j in range(size)])  18.6 us
    ppermute x1, waiting for transfers between devices, body(): lax.ppermute(down_total.astype(BF16), ROW + CTX, moves).astype(F32)  11.1 us
    unnamed x91, local copies, waits for them, and re-layouts  5.52 us
  transfers between devices with their start and end apart: 42, of which 13 were waited for; matrix products, arithmetic and copies ran while one was open for 4% of the time, Pallas kernels for 39%

profile of v6, /device:TPU:3, one launch (start us, length us, event | category | flops | bytes accessed | tf_op | source)
XLA Modules:
  0.0 148.6 jit_solution(17297364826294066187)
XLA Ops:
  2.5 3.4 %factors.1 = (bf16[128,1024]{1,0:T(8,128)(2,1)}, bf16[128,1024]{1,0:T(8,128)(2,1)}, f32[128,1]{1,0:T(8,128)}, bf16[128,1024]{1,0:T(8,128)(2,1)}, bf16[1024,128]{...) custom-call(bf16[128,1024]{1,0:T(8,128)(2,1)} %bitcast.93, ...), custom_call_target="tpu_custom_call" | custom-call | flops 209715200 | bytes 1638400 | tf_op jit(solution)/shard_map/factors/pallas_call | solution.py:47
  5.9 3.3 %collective-permute-start.5 = (bf16[320,128]{1,0:T(8,128)(2,1)}, bf16[320,128]{1,0:T(8,128)(2,1)S(1)}, u32[]{:S(2)}, u32[]{:S(2)}) collective-permute-start(bf16[320,128]{1,0:T(8,128)(2,1)} %get-tuple-element.93.refs_5_.refs_9_), channel_id=1, source_target_pairs={{0,6},{2,4},{4,2},{6,0},{1,7},{3,5},{5,3},{7,1},{8,14},{10,12},{12... | collective-permute-start | bytes 245768 | tf_op jit(solution)/shard_map/ppermute | solution.py:88
  12.6 3.6 %collective-permute-done.3.refs_9_.refs_13_ = bf16[320,128]{1,0:T(8,128)(2,1)S(1)} collective-permute-done((bf16[320,128]{1,0:T(8,128)(2,1)}, bf16[320,128]{1,0:T(8,128)(2,1)S(1)}, u32[]{:S(2)}, u32[]{:S(2)}) %collective-permute-start.3) | collective-permute-done | bytes 81952 | tf_op jit(solution)/shard_map/ppermute | solution.py:88
  16.3 1.5 %collective-permute-start.6 = (bf16[320,128]{1,0:T(8,128)(2,1)S(1)}, bf16[320,128]{1,0:T(8,128)(2,1)S(1)}, u32[]{:S(2)}, u32[]{:S(2)}) collective-permute-start(bf16[320,128]{1,0:T(8,128)(2,1)S(1)} %collective-permute-done.5.refs_11_.refs_15_), channel_id=1, source_target_pairs={{0,1},{1,0},{2,3},{3,2},{4,5},{5,4},{6,7},{7,6},{8,9},{9,8},{10,11... | collective-permute-start | bytes 245768 | tf_op jit(solution)/shard_map/ppermute | solution.py:88
  20.8 7.9 %attend.1 = (bf16[128,1024]{1,0:T(8,128)(2,1)}, bf16[128,1024]{1,0:T(8,128)(2,1)}, f32[128,1024]{1,0:T(8,128)}, f32[8,256,1]{2,1,0:T(8,128)}) custom-call(bf16[128,1024]{1,0:T(8,128)(2,1)} %get-tuple-element.92.refs_0_, f32[128,1024]{1,0:T(8,128)} %and_select_fusion.refs_1_.refs_5_, bf16[1024,1024]{1,0:T(8,128)(2,1)} %wo_hbm.1, bf16[128,1024]{1,0:T(8,128)(2,1)} %bitcast.94, ...), custom_call_target="tpu_custom_call" | custom-call | flops 536870912 | bytes 2097152 | tf_op jit(solution)/shard_map/attend/pallas_call | solution.py:47
  29.9 2.2 %collective-permute-start.13 = (bf16[128,1024]{1,0:T(8,128)(2,1)S(1)}, bf16[128,1024]{1,0:T(8,128)(2,1)S(1)}, u32[]{:S(2)}, u32[]{:S(2)}) collective-permute-start(bf16[128,1024]{1,0:T(8,128)(2,1)S(1)} %copy-done.4), channel_id=1, source_target_pairs={{0,24},{8,16},{16,8},{24,0},{1,25},{9,17},{17,9},{25,1},{2,26},{10... | collective-permute-start | bytes 786440 | tf_op jit(solution)/shard_map/ppermute | solution.py:88
  32.5 14.9 %feed_forward.1 = (bf16[128,1024]{1,0:T(8,128)(2,1)}, f32[1,1024]{1,0:T(1,128)}, f32[128,1024]{1,0:T(8,128)}, bf16[128,1024]{1,0:T(8,128)(2,1)}, bf16[1024,128]{...) custom-call(s32[3]{0:T(128)} %pad_add_fusion.place_ref, ...), custom_call_target="tpu_custom_call" | custom-call | flops 4429185024 | bytes 17301504 | tf_op jit(solution)/shard_map/feed_forward/pallas_call | solution.py:47
  53.9 9.4 %weight_grads.1 = (bf16[2,704,256]{2,1,0:T(8,128)(2,1)}, bf16[2,704,256]{2,1,0:T(8,128)(2,1)}, bf16[2,352,256]{2,1,0:T(8,128)(2,1)}, bf16[2,352,256]{2,1,0:T(8,128)(2,1)}) custom-call(s32[3]{0:T(128)} %pad_add_fusion.place_ref, bf16[1024,2816]{1,0:T(8,128)(2,1)} %wg_ref.1, bf16[1024,2816]{1,0:T(8,128)(2,1)} %wu_ref.1, bf16[2816,1024]{1,0:T(8,128)(2,1)} %wd_ref.1, ...), custom_call_target="tpu_custom_call" | custom-call | flops 4429185024 | bytes 6356992 | tf_op jit(solution)/shard_map/weight_grads/pallas_call | solution.py:47
  63.6 1.6 %collective-permute-start.24 = (bf16[4,128,1024]{2,1,0:T(8,128)(2,1)S(1)}, bf16[4,128,1024]{2,1,0:T(8,128)(2,1)S(1)}, u32[]{:S(2)}, u32[]{:S(2)}) collective-permute-start(bf16[4,128,1024]{2,1,0:T(8,128)(2,1)S(1)} %pad_maximum_fusion.2), channel_id=1, source_target_pairs={{0,1},{1,0},{2,3},{3,2},{4,5},{5,4},{6,7},{7,6},{8,9},{9,8},{10,11... | collective-permute-start | bytes 3145736 | tf_op jit(solution)/shard_map/ppermute | solution.py:88
  68.5 13.4 %attend_back.1 = (f32[480,128]{1,0:T(8,128)}, bf16[4,320,128]{2,1,0:T(8,128)(2,1)}, bf16[4,320,128]{2,1,0:T(8,128)(2,1)}) custom-call(bf16[128,1024]{1,0:T(8,128)(2,1)} %get-tuple-element.92.refs_0_, bf16[1024,128]{1,0:T(8,128)(2,1)} %get-tuple-element.104.refs_1_, bf16[128,1024]{1,0:T(8,128)(2,1)} %get-tuple-element.111.refs_2_, ...), custom_call_target="tpu_custom_call" | custom-call | flops 1342177280 | bytes 524288 | tf_op jit(solution)/shard_map/attend_back/pallas_call | solution.py:47
  85.9 1.9 %collective-permute-done.27 = bf16[4,320,128]{2,1,0:T(8,128)(2,1)S(1)} collective-permute-done((bf16[4,320,128]{2,1,0:T(8,128)(2,1)S(1)}, bf16[4,320,128]{2,1,0:T(8,128)(2,1)S(1)}, u32[]{:S(2)}, u32[]{:S(2)}) %collective-permute-start.27) | collective-permute-done | bytes 327712 | tf_op jit(solution)/shard_map/ppermute | solution.py:88
  88.5 2.4 %collective-permute-start.30 = (bf16[320,128]{1,0:T(8,128)(2,1)S(1)}, bf16[320,128]{1,0:T(8,128)(2,1)S(1)}, u32[]{:S(2)}, u32[]{:S(2)}) collective-permute-start(bf16[320,128]{1,0:T(8,128)(2,1)S(1)} %get-tuple-element.186), channel_id=1, source_target_pairs={{0,6},{2,4},{4,2},{6,0},{1,7},{3,5},{5,3},{7,1},{8,14},{10,12},{12... | collective-permute-start | bytes 245768 | tf_op jit(solution)/shard_map/ppermute | solution.py:88
  92.1 2.5 %collective-permute-done.31 = bf16[2,352,256]{2,1,0:T(8,128)(2,1)S(1)} collective-permute-done((bf16[2,352,256]{2,1,0:T(8,128)(2,1)S(1)}, bf16[2,352,256]{2,1,0:T(8,128)(2,1)S(1)}, u32[]{:S(2)}, u32[]{:S(2)}) %collective-permute-start.31) | collective-permute-done | bytes 360480 | tf_op jit(solution)/shard_map/ppermute | solution.py:88
  94.6 3.8 %collective-permute-done.30.refs_3_ = bf16[320,128]{1,0:T(8,128)(2,1)S(1)} collective-permute-done((bf16[320,128]{1,0:T(8,128)(2,1)S(1)}, bf16[320,128]{1,0:T(8,128)(2,1)S(1)}, u32[]{:S(2)}, u32[]{:S(2)}) %collective-permute-start.30) | collective-permute-done | bytes 81952 | tf_op jit(solution)/shard_map/ppermute | solution.py:88
  100.5 2.4 %collective-permute-start.36 = (bf16[1,1056,256]{2,1,0:T(8,128)(2,1)S(1)}, bf16[1,1056,256]{2,1,0:T(8,128)(2,1)S(1)}, u32[]{:S(2)}, u32[]{:S(2)}) collective-permute-start(bf16[1,1056,256]{2,1,0:T(8,128)(2,1)S(1)} %slice.148), channel_id=1, source_target_pairs={{0,4},{2,6},{4,0},{6,2},{1,5},{3,7},{5,1},{7,3},{8,12},{10,14},{12... | collective-permute-start | bytes 1622024 | tf_op jit(solution)/shard_map/ppermute | solution.py:88
  104.0 3.0 %out_grads.1 = (bf16[256,128]{1,0:T(8,128)(2,1)}, bf16[256,128]{1,0:T(8,128)(2,1)}, bf16[256,128]{1,0:T(8,128)(2,1)}, bf16[256,128]{1,0:T(8,128)(2,1)}) custom-call(s32[3]{0:T(128)} %pad_add_fusion.place_ref, bf16[4,128,1280]{2,1,0:T(8,128)(2,1)} %copy-done.1, bf16[4,128,1280]{2,1,0:T(8,128)(2,1)} %copy-done.3), custom_call_target="tpu_custom_call" | custom-call | flops 268435456 | bytes 5242880 | tf_op jit(solution)/shard_map/out_grads/pallas_call | solution.py:47
  107.0 3.4 %input_grads.1 = (f32[128,1024]{1,0:T(8,128)}, bf16[232,128]{1,0:T(8,128)(2,1)}, bf16[232,128]{1,0:T(8,128)(2,1)}, bf16[232,128]{1,0:T(8,128)(2,1)}, bf16[232,128]{1,0:T(8,128)(2,1)}) custom-call(s32[3]{0:T(128)} %pad_add_fusion.place_ref, f32[480,128]{1,0:T(8,128)} %get-tuple-element.139.gq_ref, bf16[320,128]{1,0:T(8,128)(2,1)} %get-tuple-element.145.refs_0_, ...), custom_call_target="tpu_custom_call" | custom-call | flops 209715200 | bytes 1638400 | tf_op jit(solution)/shard_map/input_grads/pallas_call | solution.py:47
  113.0 3.3 %own_slab.1.h1_ref = bf16[1024,512]{1,0:T(8,128)(2,1)} custom-call(s32[3]{0:T(128)} %pad_add_fusion.place_ref, bf16[4,128,1024]{2,1,0:T(8,128)(2,1)} %copy-done.10, bf16[128,1024]{1,0:T(8,128)(2,1)} %get-tuple-element.127.refs_0_, bf16[128,1024]{1,0:T(8,128)(2,1)} %copy-done.12, bf16[128,1024]{1,0:T(8,128)(2,1)} %copy-done.13, bf16[128,1024]{1,0:T(8,128)(2,1)} %copy-done.14), custom_call_target="tpu_custom_call" | custom-call | bytes 1048576 | tf_op jit(solution)/shard_map/own_slab/pallas_call | solution.py:47
  117.0 2.7 %collective-permute-start.35 = (bf16[4,232,128]{2,1,0:T(8,128)(2,1)S(1)}, bf16[4,232,128]{2,1,0:T(8,128)(2,1)}, u32[]{:S(2)}, u32[]{:S(2)}) collective-permute-start(bf16[4,232,128]{2,1,0:T(8,128)(2,1)S(1)} %pad_maximum_fusion.3.mine_ref), channel_id=1, source_target_pairs={{0,1},{1,0},{2,3},{3,2},{4,5},{5,4},{6,7},{7,6},{8,9},{9,8},{10,11... | collective-permute-start | bytes 712712 | tf_op jit(solution)/shard_map/ppermute | solution.py:88
  120.9 2.6 %fact_grads.1 = (bf16[488,128]{1,0:T(8,128)(2,1)}, bf16[488,128]{1,0:T(8,128)(2,1)}, bf16[488,128]{1,0:T(8,128)(2,1)}, bf16[488,128]{1,0:T(8,128)(2,1)}) custom-call(bf16[1024,512]{1,0:T(8,128)(2,1)} %own_slab.1.h1_ref, bf16[4,232,128]{2,1,0:T(8,128)(2,1)} %copy-done.15, bf16[4,232,128]{2,1,0:T(8,128)(2,1)} %collective-permute-done.35.other_ref, ...), custom_call_target="tpu_custom_call" | custom-call | flops 243269632 | bytes 1048576 | tf_op jit(solution)/shard_map/fact_grads/pallas_call | solution.py:47
  124.9 2.3 %collective-permute-start.40 = (bf16[488,128]{1,0:T(8,128)(2,1)}, bf16[488,128]{1,0:T(8,128)(2,1)S(1)}, u32[]{:S(2)}, u32[]{:S(2)}) collective-permute-start(bf16[488,128]{1,0:T(8,128)(2,1)} %get-tuple-element.166), channel_id=1, source_target_pairs={{0,6},{2,4},{4,2},{6,0},{1,7},{3,5},{5,3},{7,1},{8,14},{10,12},{12... | collective-permute-start | bytes 374792 | tf_op jit(solution)/shard_map/ppermute | solution.py:88
  128.7 1.9 %collective-permute-start.41 = (bf16[352,256]{1,0:T(8,128)(2,1)S(1)}, bf16[352,256]{1,0:T(8,128)(2,1)S(1)}, u32[]{:S(2)}, u32[]{:S(2)}) collective-permute-start(bf16[352,256]{1,0:T(8,128)(2,1)S(1)} %fusion), channel_id=1, source_target_pairs={{0,0},{2,8},{4,16},{6,24},{1,1},{3,9},{5,17},{7,25},{8,10},{10,2},... | collective-permute-start | bytes 540680 | tf_op jit(solution)/shard_map/ppermute | solution.py:767
  132.3 2.3 %collective-permute-done.39 = bf16[488,128]{1,0:T(8,128)(2,1)S(1)} collective-permute-done((bf16[488,128]{1,0:T(8,128)(2,1)}, bf16[488,128]{1,0:T(8,128)(2,1)S(1)}, u32[]{:S(2)}, u32[]{:S(2)}) %collective-permute-start.39) | collective-permute-done | bytes 124960 | tf_op jit(solution)/shard_map/ppermute | solution.py:88
  136.7 11.1 %collective-permute-done.41 = bf16[352,256]{1,0:T(8,128)(2,1)S(1)} collective-permute-done((bf16[352,256]{1,0:T(8,128)(2,1)S(1)}, bf16[352,256]{1,0:T(8,128)(2,1)S(1)}, u32[]{:S(2)}, u32[]{:S(2)}) %collective-permute-start.41) | collective-permute-done | bytes 180256 | tf_op jit(solution)/shard_map/ppermute | solution.py:767
  (190 shorter events, 40.1 us)
Async XLA Ops:
  9.6 9.2 %collective-permute-start = (bf16[320,128]{1,0:T(8,128)(2,1)}, bf16[320,128]{1,0:T(8,128)(2,1)S(1)}, u32[]{:S(2)}, u32[]{:S(2)}) collective-permute-start(bf16[320,128]{1,0:T(8,128)(2,1)} %get-tuple-element.93.refs_5_.refs_9_), channel_id=1, source_target_pairs={{0,1},{1,0},{2,3},{3,2},{4,5},{5,4},{6,7},{7,6},{8,9},{9,8},{10,11... | collective-permute-start | bytes 245768 | tf_op jit(solution)/shard_map/ppermute | solution.py:88
  11.0 17.8 %collective-permute-start.9 = (bf16[128,1024]{1,0:T(8,128)(2,1)}, bf16[128,1024]{1,0:T(8,128)(2,1)S(1)}, u32[]{:S(2)}, u32[]{:S(2)}) collective-permute-start(bf16[128,1024]{1,0:T(8,128)(2,1)} %get-tuple-element.100.go_ref.refs_8_), channel_id=1, source_target_pairs={{0,24},{8,16},{16,8},{24,0},{1,25},{9,17},{17,9},{25,1},{2,26},{10... | collective-permute-start | bytes 786440 | tf_op jit(solution)/shard_map/ppermute | solution.py:88
  12.3 16.5 %collective-permute-start.8 = (bf16[128,1024]{1,0:T(8,128)(2,1)}, bf16[128,1024]{1,0:T(8,128)(2,1)S(1)}, u32[]{:S(2)}, u32[]{:S(2)}) collective-permute-start(bf16[128,1024]{1,0:T(8,128)(2,1)} %get-tuple-element.100.go_ref.refs_8_), channel_id=1, source_target_pairs={{0,16},{8,24},{16,0},{24,8},{1,17},{9,25},{17,1},{25,9},{2,18},{10... | collective-permute-start | bytes 786440 | tf_op jit(solution)/shard_map/ppermute | solution.py:88
  16.2 12.6 %collective-permute-start.7 = (bf16[128,1024]{1,0:T(8,128)(2,1)}, bf16[128,1024]{1,0:T(8,128)(2,1)S(1)}, u32[]{:S(2)}, u32[]{:S(2)}) collective-permute-start(bf16[128,1024]{1,0:T(8,128)(2,1)} %get-tuple-element.100.go_ref.refs_8_), channel_id=1, source_target_pairs={{0,8},{8,0},{16,24},{24,16},{1,9},{9,1},{17,25},{25,17},{2,10},{10... | collective-permute-start | bytes 786440 | tf_op jit(solution)/shard_map/ppermute | solution.py:88
  29.0 18.5 %collective-permute-start.10 = (bf16[4,128,1024]{2,1,0:T(8,128)(2,1)S(1)}, bf16[4,128,1024]{2,1,0:T(8,128)(2,1)S(1)}, u32[]{:S(2)}, u32[]{:S(2)}) collective-permute-start(bf16[4,128,1024]{2,1,0:T(8,128)(2,1)S(1)} %pad_maximum_fusion.1), channel_id=1, source_target_pairs={{0,1},{1,0},{2,3},{3,2},{4,5},{5,4},{6,7},{7,6},{8,9},{9,8},{10,11... | collective-permute-start | bytes 3145736 | tf_op jit(solution)/shard_map/ppermute | solution.py:88
  29.9 17.6 %collective-permute-start.13 = (bf16[128,1024]{1,0:T(8,128)(2,1)S(1)}, bf16[128,1024]{1,0:T(8,128)(2,1)S(1)}, u32[]{:S(2)}, u32[]{:S(2)}) collective-permute-start(bf16[128,1024]{1,0:T(8,128)(2,1)S(1)} %copy-done.4), channel_id=1, source_target_pairs={{0,24},{8,16},{16,8},{24,0},{1,25},{9,17},{17,9},{25,1},{2,26},{10... | collective-permute-start | bytes 786440 | tf_op jit(solution)/shard_map/ppermute | solution.py:88
  32.0 15.4 %collective-permute-start.12 = (bf16[128,1024]{1,0:T(8,128)(2,1)S(1)}, bf16[128,1024]{1,0:T(8,128)(2,1)S(1)}, u32[]{:S(2)}, u32[]{:S(2)}) collective-permute-start(bf16[128,1024]{1,0:T(8,128)(2,1)S(1)} %copy-done.4), channel_id=1, source_target_pairs={{0,16},{8,24},{16,0},{24,8},{1,17},{9,25},{17,1},{25,9},{2,18},{10... | collective-permute-start | bytes 786440 | tf_op jit(solution)/shard_map/ppermute | solution.py:88
  32.3 15.2 %collective-permute-start.11 = (bf16[128,1024]{1,0:T(8,128)(2,1)S(1)}, bf16[128,1024]{1,0:T(8,128)(2,1)S(1)}, u32[]{:S(2)}, u32[]{:S(2)}) collective-permute-start(bf16[128,1024]{1,0:T(8,128)(2,1)S(1)} %copy-done.4), channel_id=1, source_target_pairs={{0,8},{8,0},{16,24},{24,16},{1,9},{9,1},{17,25},{25,17},{2,10},{10... | collective-permute-start | bytes 786440 | tf_op jit(solution)/shard_map/ppermute | solution.py:88
  49.4 14.0 %collective-permute-start.21 = (bf16[128,1024]{1,0:T(8,128)(2,1)S(1)}, bf16[128,1024]{1,0:T(8,128)(2,1)S(1)}, u32[]{:S(2)}, u32[]{:S(2)}) collective-permute-start(bf16[128,1024]{1,0:T(8,128)(2,1)S(1)} %copy-done.11), channel_id=1, source_target_pairs={{0,8},{8,0},{16,24},{24,16},{1,9},{9,1},{17,25},{25,17},{2,10},{10... | collective-permute-start | bytes 786440 | tf_op jit(solution)/shard_map/ppermute | solution.py:88
  50.6 12.8 %collective-permute-start.22 = (bf16[128,1024]{1,0:T(8,128)(2,1)S(1)}, bf16[128,1024]{1,0:T(8,128)(2,1)S(1)}, u32[]{:S(2)}, u32[]{:S(2)}) collective-permute-start(bf16[128,1024]{1,0:T(8,128)(2,1)S(1)} %copy-done.11), channel_id=1, source_target_pairs={{0,16},{8,24},{16,0},{24,8},{1,17},{9,25},{17,1},{25,9},{2,18},{10... | collective-permute-start | bytes 786440 | tf_op jit(solution)/shard_map/ppermute | solution.py:88
  51.8 11.6 %collective-permute-start.23 = (bf16[128,1024]{1,0:T(8,128)(2,1)S(1)}, bf16[128,1024]{1,0:T(8,128)(2,1)S(1)}, u32[]{:S(2)}, u32[]{:S(2)}) collective-permute-start(bf16[128,1024]{1,0:T(8,128)(2,1)S(1)} %copy-done.11), channel_id=1, source_target_pairs={{0,24},{8,16},{16,8},{24,0},{1,25},{9,17},{17,9},{25,1},{2,26},{10... | collective-permute-start | bytes 786440 | tf_op jit(solution)/shard_map/ppermute | solution.py:88
  63.6 19.1 %collective-permute-start.24 = (bf16[4,128,1024]{2,1,0:T(8,128)(2,1)S(1)}, bf16[4,128,1024]{2,1,0:T(8,128)(2,1)S(1)}, u32[]{:S(2)}, u32[]{:S(2)}) collective-permute-start(bf16[4,128,1024]{2,1,0:T(8,128)(2,1)S(1)} %pad_maximum_fusion.2), channel_id=1, source_target_pairs={{0,1},{1,0},{2,3},{3,2},{4,5},{5,4},{6,7},{7,6},{8,9},{9,8},{10,11... | collective-permute-start | bytes 3145736 | tf_op jit(solution)/shard_map/ppermute | solution.py:88
  65.1 17.5 %collective-permute-start.25 = (bf16[2,704,256]{2,1,0:T(8,128)(2,1)S(1)}, bf16[2,704,256]{2,1,0:T(8,128)(2,1)S(1)}, u32[]{:S(2)}, u32[]{:S(2)}) collective-permute-start(bf16[2,704,256]{2,1,0:T(8,128)(2,1)S(1)} %copy-done.39), channel_id=1, source_target_pairs={{0,2},{2,0},{4,6},{6,4},{1,3},{3,1},{5,7},{7,5},{8,10},{10,8},{12,... | collective-permute-start | bytes 2162696 | tf_op jit(solution)/shard_map/ppermute | solution.py:88
  65.8 16.0 %collective-permute-start.18 = (bf16[128,1280]{1,0:T(8,128)(2,1)S(1)}, bf16[128,1280]{1,0:T(8,128)(2,1)S(1)}, u32[]{:S(2)}, u32[]{:S(2)}) collective-permute-start(bf16[128,1280]{1,0:T(8,128)(2,1)S(1)} %copy-done.43), channel_id=1, source_target_pairs={{0,8},{8,0},{16,24},{24,16},{1,9},{9,1},{17,25},{25,17},{2,10},{10... | collective-permute-start | bytes 983048 | tf_op jit(solution)/shard_map/ppermute | solution.py:88
  66.4 15.5 %collective-permute-start.19 = (bf16[128,1280]{1,0:T(8,128)(2,1)S(1)}, bf16[128,1280]{1,0:T(8,128)(2,1)S(1)}, u32[]{:S(2)}, u32[]{:S(2)}) collective-permute-start(bf16[128,1280]{1,0:T(8,128)(2,1)S(1)} %copy-done.42), channel_id=1, source_target_pairs={{0,16},{8,24},{16,0},{24,8},{1,17},{9,25},{17,1},{25,9},{2,18},{10... | collective-permute-start | bytes 983048 | tf_op jit(solution)/shard_map/ppermute | solution.py:88
  67.0 15.0 %collective-permute-start.20 = (bf16[128,1280]{1,0:T(8,128)(2,1)S(1)}, bf16[128,1280]{1,0:T(8,128)(2,1)S(1)}, u32[]{:S(2)}, u32[]{:S(2)}) collective-permute-start(bf16[128,1280]{1,0:T(8,128)(2,1)S(1)} %copy-done.41), channel_id=1, source_target_pairs={{0,24},{8,16},{16,8},{24,0},{1,25},{9,17},{17,9},{25,1},{2,26},{10... | collective-permute-start | bytes 983048 | tf_op jit(solution)/shard_map/ppermute | solution.py:88
  83.7 19.2 %collective-permute-start.26 = (bf16[4,128,1280]{2,1,0:T(8,128)(2,1)S(1)}, bf16[4,128,1280]{2,1,0:T(8,128)(2,1)S(1)}, u32[]{:S(2)}, u32[]{:S(2)}) collective-permute-start(bf16[4,128,1280]{2,1,0:T(8,128)(2,1)S(1)} %pad_maximum_fusion.mine_ref), channel_id=1, source_target_pairs={{0,1},{1,0},{2,3},{3,2},{4,5},{5,4},{6,7},{7,6},{8,9},{9,8},{10,11... | collective-permute-start | bytes 3932168 | tf_op jit(solution)/shard_map/ppermute | solution.py:88
  84.9 9.7 %collective-permute-start.31 = (bf16[2,352,256]{2,1,0:T(8,128)(2,1)S(1)}, bf16[2,352,256]{2,1,0:T(8,128)(2,1)S(1)}, u32[]{:S(2)}, u32[]{:S(2)}) collective-permute-start(bf16[2,352,256]{2,1,0:T(8,128)(2,1)S(1)} %copy-done.40), channel_id=1, source_target_pairs={{0,2},{2,0},{4,6},{6,4},{1,3},{3,1},{5,7},{7,5},{8,10},{10,8},{12,... | collective-permute-start | bytes 1081352 | tf_op jit(solution)/shard_map/ppermute | solution.py:88
  88.5 9.8 %collective-permute-start.30 = (bf16[320,128]{1,0:T(8,128)(2,1)S(1)}, bf16[320,128]{1,0:T(8,128)(2,1)S(1)}, u32[]{:S(2)}, u32[]{:S(2)}) collective-permute-start(bf16[320,128]{1,0:T(8,128)(2,1)S(1)} %get-tuple-element.186), channel_id=1, source_target_pairs={{0,6},{2,4},{4,2},{6,0},{1,7},{3,5},{5,3},{7,1},{8,14},{10,12},{12... | collective-permute-start | bytes 245768 | tf_op jit(solution)/shard_map/ppermute | solution.py:88
  90.9 8.9 %collective-permute-start.28 = (bf16[320,128]{1,0:T(8,128)(2,1)S(1)}, bf16[320,128]{1,0:T(8,128)(2,1)S(1)}, u32[]{:S(2)}, u32[]{:S(2)}) collective-permute-start(bf16[320,128]{1,0:T(8,128)(2,1)S(1)} %get-tuple-element.188), channel_id=1, source_target_pairs={{0,2},{2,0},{4,6},{6,4},{1,3},{3,1},{5,7},{7,5},{8,10},{10,8},{12,... | collective-permute-start | bytes 245768 | tf_op jit(solution)/shard_map/ppermute | solution.py:88
  100.5 26.6 %collective-permute-start.36 = (bf16[1,1056,256]{2,1,0:T(8,128)(2,1)S(1)}, bf16[1,1056,256]{2,1,0:T(8,128)(2,1)S(1)}, u32[]{:S(2)}, u32[]{:S(2)}) collective-permute-start(bf16[1,1056,256]{2,1,0:T(8,128)(2,1)S(1)} %slice.148), channel_id=1, source_target_pairs={{0,4},{2,6},{4,0},{6,2},{1,5},{3,7},{5,1},{7,3},{8,12},{10,14},{12... | collective-permute-start | bytes 1622024 | tf_op jit(solution)/shard_map/ppermute | solution.py:88
  123.8 10.8 %collective-permute-start.39 = (bf16[488,128]{1,0:T(8,128)(2,1)}, bf16[488,128]{1,0:T(8,128)(2,1)S(1)}, u32[]{:S(2)}, u32[]{:S(2)}) collective-permute-start(bf16[488,128]{1,0:T(8,128)(2,1)} %get-tuple-element.165), channel_id=1, source_target_pairs={{0,4},{2,6},{4,0},{6,2},{1,5},{3,7},{5,1},{7,3},{8,12},{10,14},{12... | collective-permute-start | bytes 374792 | tf_op jit(solution)/shard_map/ppermute | solution.py:88
  124.9 9.7 %collective-permute-start.40 = (bf16[488,128]{1,0:T(8,128)(2,1)}, bf16[488,128]{1,0:T(8,128)(2,1)S(1)}, u32[]{:S(2)}, u32[]{:S(2)}) collective-permute-start(bf16[488,128]{1,0:T(8,128)(2,1)} %get-tuple-element.166), channel_id=1, source_target_pairs={{0,6},{2,4},{4,2},{6,0},{1,7},{3,5},{5,3},{7,1},{8,14},{10,12},{12... | collective-permute-start | bytes 374792 | tf_op jit(solution)/shard_map/ppermute | solution.py:88
  128.7 19.1 %collective-permute-start.41 = (bf16[352,256]{1,0:T(8,128)(2,1)S(1)}, bf16[352,256]{1,0:T(8,128)(2,1)S(1)}, u32[]{:S(2)}, u32[]{:S(2)}) collective-permute-start(bf16[352,256]{1,0:T(8,128)(2,1)S(1)} %fusion), channel_id=1, source_target_pairs={{0,0},{2,8},{4,16},{6,24},{1,1},{3,9},{5,17},{7,25},{8,10},{10,2},... | collective-permute-start | bytes 540680 | tf_op jit(solution)/shard_map/ppermute | solution.py:767
  (64 other events, 406.8 us)

commit v7 on v6

--- a/solution.py
+++ b/solution.py
@@ -189,8 +189,8 @@
     def step(pair, carry):
         keys = expand_pair(pair, 0, a_rows, b_rows)
         values = expand_pair(pair, 1, a_rows, b_rows)
-        q = stack_pair(q_ref[:, pair_lanes(pair)])
-        scores = mm(q, keys) * SCALE + bias
+        q = stack_pair(q_ref[:, pair_lanes(pair)] * SCALE)
+        scores = mm(q, keys) + bias
         top = jnp.max(scores, axis=1, keepdims=True)
         exponent = jnp.exp(scores - top)
         total = jnp.sum(exponent, axis=1, keepdims=True)
@@ -240,21 +240,21 @@
         values = expand_pair(pair, 1, a_rows, b_rows)
         rows = pl.ds(pl.multiple_of(pair * 2 * DH, 2 * DH), 2 * DH)
         both = (
-            stack_pair(q_ref[:, pair_lanes(pair)]), stack_pair(gm_ref[:, pair_lanes(pair)]),
-            spread(qt_ref[rows, :]), spread(gmt_ref[rows, :]), lse_ref[pair],
+            stack_pair(q_ref[:, pair_lanes(pair)] * SCALE), stack_pair(gm_ref[:, pair_lanes(pair)]),
+            spread(qt_ref[rows, :] * SCALE), spread(gmt_ref[rows, :]), lse_ref[pair],
         )
         takes = [slice(0, 2 * tokens)] if keys.shape[1] <= 2048 else [slice(0, tokens), slice(tokens, 2 * tokens)]
         grad_q, grad_k, grad_v = [], None, None
         for take in takes:
             q, g, qt, gt, lse = both[0][take], both[1][take], both[2][:, take], both[3][:, take], both[4][take]
             heads = q.shape[0] // tokens
-            scores = mm(q, keys) * SCALE + jnp.concatenate([bias_ref[...]] * heads, axis=0)
+            scores = mm(q, keys) + jnp.concatenate([bias_ref[...]] * heads, axis=0)
             probs = jnp.exp(scores - lse)
             grad_probs = mm(g, values)
             inner = jnp.sum(probs * grad_probs, axis=1, keepdims=True)
             grad_scores = (probs * (grad_probs - inner)).astype(BF16)
             grad_q.append(mm(grad_scores, keys, NT).T * SCALE)
-            gk, gv = mm(qt, grad_scores) * SCALE, mm(gt, probs.astype(BF16))
+            gk, gv = mm(qt, grad_scores), mm(gt, probs.astype(BF16))
             grad_k, grad_v = (gk, gv) if grad_k is None else (grad_k + gk, grad_v + gv)
         grad_q = jnp.concatenate(grad_q, axis=1)
         for sub in range(2):

time: 151 us -> 151 us (level)
  no operation moved by 1% of the time
where the time goes in v7:
time: 151 us; the launch traced here: 148 us
  Pallas kernels  60.6 us (40%)
  starting transfers between devices  41.8 us (28%)
  waiting for transfers between devices  30.3 us (20%)
  local copies, waits for them, and re-layouts  6.98 us (5%)
  other arithmetic  6.88 us (5%)
  between operations  1.93 us (1%)
    pallas_call x9, Pallas kernels, call(): pl.pallas_call(kernel, out_shape=[jax.ShapeDtypeStruct(s, d) for s, d in...  60.6 us
    ppermute x41, starting transfers between devices, swap(): return lax.ppermute(value, axis, [(j, j ^ k) for j in range(size)])  39.7 us
    ppermute x41, waiting for transfers between devices, swap(): return lax.ppermute(value, axis, [(j, j ^ k) for j in range(size)])  19.3 us
    ppermute x1, waiting for transfers between devices, body(): lax.ppermute(down_total.astype(BF16), ROW + CTX, moves).astype(F32)  11 us
    unnamed x91, local copies, waits for them, and re-layouts  5.52 us
  transfers between devices with their start and end apart: 42, of which 13 were waited for; matrix products, arithmetic and copies ran while one was open for 4% of the time, Pallas kernels for 39%

profile of v7, /device:TPU:3, one launch (start us, length us, event | category | flops | bytes accessed | tf_op | source)
XLA Modules:
  0.0 148.5 jit_solution(17418628889088176569)
XLA Ops:
  2.5 3.4 %factors.1 = (bf16[128,1024]{1,0:T(8,128)(2,1)}, bf16[128,1024]{1,0:T(8,128)(2,1)}, f32[128,1]{1,0:T(8,128)}, bf16[128,1024]{1,0:T(8,128)(2,1)}, bf16[1024,128]{...) custom-call(bf16[128,1024]{1,0:T(8,128)(2,1)} %bitcast.93, ...), custom_call_target="tpu_custom_call" | custom-call | flops 209715200 | bytes 1638400 | tf_op jit(solution)/shard_map/factors/pallas_call | solution.py:47
  5.9 3.3 %collective-permute-start.5 = (bf16[320,128]{1,0:T(8,128)(2,1)}, bf16[320,128]{1,0:T(8,128)(2,1)S(1)}, u32[]{:S(2)}, u32[]{:S(2)}) collective-permute-start(bf16[320,128]{1,0:T(8,128)(2,1)} %get-tuple-element.93.refs_5_.refs_9_), channel_id=1, source_target_pairs={{0,6},{2,4},{4,2},{6,0},{1,7},{3,5},{5,3},{7,1},{8,14},{10,12},{12... | collective-permute-start | bytes 245768 | tf_op jit(solution)/shard_map/ppermute | solution.py:88
  12.6 3.6 %collective-permute-done.3.refs_9_.refs_13_ = bf16[320,128]{1,0:T(8,128)(2,1)S(1)} collective-permute-done((bf16[320,128]{1,0:T(8,128)(2,1)}, bf16[320,128]{1,0:T(8,128)(2,1)S(1)}, u32[]{:S(2)}, u32[]{:S(2)}) %collective-permute-start.3) | collective-permute-done | bytes 81952 | tf_op jit(solution)/shard_map/ppermute | solution.py:88
  16.3 1.5 %collective-permute-start.6 = (bf16[320,128]{1,0:T(8,128)(2,1)S(1)}, bf16[320,128]{1,0:T(8,128)(2,1)S(1)}, u32[]{:S(2)}, u32[]{:S(2)}) collective-permute-start(bf16[320,128]{1,0:T(8,128)(2,1)S(1)} %collective-permute-done.5.refs_11_.refs_15_), channel_id=1, source_target_pairs={{0,1},{1,0},{2,3},{3,2},{4,5},{5,4},{6,7},{7,6},{8,9},{9,8},{10,11... | collective-permute-start | bytes 245768 | tf_op jit(solution)/shard_map/ppermute | solution.py:88
  20.8 7.8 %attend.1 = (bf16[128,1024]{1,0:T(8,128)(2,1)}, bf16[128,1024]{1,0:T(8,128)(2,1)}, f32[128,1024]{1,0:T(8,128)}, f32[8,256,1]{2,1,0:T(8,128)}) custom-call(bf16[128,1024]{1,0:T(8,128)(2,1)} %get-tuple-element.92.refs_0_, f32[128,1024]{1,0:T(8,128)} %and_select_fusion.refs_1_.refs_5_, bf16[1024,1024]{1,0:T(8,128)(2,1)} %wo_hbm.1, bf16[128,1024]{1,0:T(8,128)(2,1)} %bitcast.94, ...), custom_call_target="tpu_custom_call" | custom-call | flops 536870912 | bytes 2097152 | tf_op jit(solution)/shard_map/attend/pallas_call | solution.py:47
  29.7 2.2 %collective-permute-start.13 = (bf16[128,1024]{1,0:T(8,128)(2,1)S(1)}, bf16[128,1024]{1,0:T(8,128)(2,1)S(1)}, u32[]{:S(2)}, u32[]{:S(2)}) collective-permute-start(bf16[128,1024]{1,0:T(8,128)(2,1)S(1)} %copy-done.4), channel_id=1, source_target_pairs={{0,24},{8,16},{16,8},{24,0},{1,25},{9,17},{17,9},{25,1},{2,26},{10... | collective-permute-start | bytes 786440 | tf_op jit(solution)/shard_map/ppermute | solution.py:88
  32.4 14.9 %feed_forward.1 = (bf16[128,1024]{1,0:T(8,128)(2,1)}, f32[1,1024]{1,0:T(1,128)}, f32[128,1024]{1,0:T(8,128)}, bf16[128,1024]{1,0:T(8,128)(2,1)}, bf16[1024,128]{...) custom-call(s32[3]{0:T(128)} %pad_add_fusion.place_ref, ...), custom_call_target="tpu_custom_call" | custom-call | flops 4429185024 | bytes 17301504 | tf_op jit(solution)/shard_map/feed_forward/pallas_call | solution.py:47
  53.8 9.4 %weight_grads.1 = (bf16[2,704,256]{2,1,0:T(8,128)(2,1)}, bf16[2,704,256]{2,1,0:T(8,128)(2,1)}, bf16[2,352,256]{2,1,0:T(8,128)(2,1)}, bf16[2,352,256]{2,1,0:T(8,128)(2,1)}) custom-call(s32[3]{0:T(128)} %pad_add_fusion.place_ref, bf16[1024,2816]{1,0:T(8,128)(2,1)} %wg_ref.1, bf16[1024,2816]{1,0:T(8,128)(2,1)} %wu_ref.1, bf16[2816,1024]{1,0:T(8,128)(2,1)} %wd_ref.1, ...), custom_call_target="tpu_custom_call" | custom-call | flops 4429185024 | bytes 6356992 | tf_op jit(solution)/shard_map/weight_grads/pallas_call | solution.py:47
  63.5 1.6 %collective-permute-start.24 = (bf16[4,128,1024]{2,1,0:T(8,128)(2,1)S(1)}, bf16[4,128,1024]{2,1,0:T(8,128)(2,1)S(1)}, u32[]{:S(2)}, u32[]{:S(2)}) collective-permute-start(bf16[4,128,1024]{2,1,0:T(8,128)(2,1)S(1)} %pad_maximum_fusion.2), channel_id=1, source_target_pairs={{0,1},{1,0},{2,3},{3,2},{4,5},{5,4},{6,7},{7,6},{8,9},{9,8},{10,11... | collective-permute-start | bytes 3145736 | tf_op jit(solution)/shard_map/ppermute | solution.py:88
  68.4 12.9 %attend_back.1 = (f32[480,128]{1,0:T(8,128)}, bf16[4,320,128]{2,1,0:T(8,128)(2,1)}, bf16[4,320,128]{2,1,0:T(8,128)(2,1)}) custom-call(bf16[128,1024]{1,0:T(8,128)(2,1)} %get-tuple-element.92.refs_0_, bf16[1024,128]{1,0:T(8,128)(2,1)} %get-tuple-element.104.refs_1_, bf16[128,1024]{1,0:T(8,128)(2,1)} %get-tuple-element.111.refs_2_, ...), custom_call_target="tpu_custom_call" | custom-call | flops 1342177280 | bytes 524288 | tf_op jit(solution)/shard_map/attend_back/pallas_call | solution.py:47
  85.8 1.9 %collective-permute-done.27 = bf16[4,320,128]{2,1,0:T(8,128)(2,1)S(1)} collective-permute-done((bf16[4,320,128]{2,1,0:T(8,128)(2,1)S(1)}, bf16[4,320,128]{2,1,0:T(8,128)(2,1)S(1)}, u32[]{:S(2)}, u32[]{:S(2)}) %collective-permute-start.27) | collective-permute-done | bytes 327712 | tf_op jit(solution)/shard_map/ppermute | solution.py:88
  88.4 2.4 %collective-permute-start.30 = (bf16[320,128]{1,0:T(8,128)(2,1)S(1)}, bf16[320,128]{1,0:T(8,128)(2,1)S(1)}, u32[]{:S(2)}, u32[]{:S(2)}) collective-permute-start(bf16[320,128]{1,0:T(8,128)(2,1)S(1)} %get-tuple-element.186), channel_id=1, source_target_pairs={{0,6},{2,4},{4,2},{6,0},{1,7},{3,5},{5,3},{7,1},{8,14},{10,12},{12... | collective-permute-start | bytes 245768 | tf_op jit(solution)/shard_map/ppermute | solution.py:88
  92.0 2.5 %collective-permute-done.31 = bf16[2,352,256]{2,1,0:T(8,128)(2,1)S(1)} collective-permute-done((bf16[2,352,256]{2,1,0:T(8,128)(2,1)S(1)}, bf16[2,352,256]{2,1,0:T(8,128)(2,1)S(1)}, u32[]{:S(2)}, u32[]{:S(2)}) %collective-permute-start.31) | collective-permute-done | bytes 360480 | tf_op jit(solution)/shard_map/ppermute | solution.py:88
  94.5 3.8 %collective-permute-done.30.refs_3_ = bf16[320,128]{1,0:T(8,128)(2,1)S(1)} collective-permute-done((bf16[320,128]{1,0:T(8,128)(2,1)S(1)}, bf16[320,128]{1,0:T(8,128)(2,1)S(1)}, u32[]{:S(2)}, u32[]{:S(2)}) %collective-permute-start.30) | collective-permute-done | bytes 81952 | tf_op jit(solution)/shard_map/ppermute | solution.py:88
  100.4 2.4 %collective-permute-start.36 = (bf16[1,1056,256]{2,1,0:T(8,128)(2,1)S(1)}, bf16[1,1056,256]{2,1,0:T(8,128)(2,1)S(1)}, u32[]{:S(2)}, u32[]{:S(2)}) collective-permute-start(bf16[1,1056,256]{2,1,0:T(8,128)(2,1)S(1)} %slice.148), channel_id=1, source_target_pairs={{0,4},{2,6},{4,0},{6,2},{1,5},{3,7},{5,1},{7,3},{8,12},{10,14},{12... | collective-permute-start | bytes 1622024 | tf_op jit(solution)/shard_map/ppermute | solution.py:88
  103.9 3.0 %out_grads.1 = (bf16[256,128]{1,0:T(8,128)(2,1)}, bf16[256,128]{1,0:T(8,128)(2,1)}, bf16[256,128]{1,0:T(8,128)(2,1)}, bf16[256,128]{1,0:T(8,128)(2,1)}) custom-call(s32[3]{0:T(128)} %pad_add_fusion.place_ref, bf16[4,128,1280]{2,1,0:T(8,128)(2,1)} %copy-done.1, bf16[4,128,1280]{2,1,0:T(8,128)(2,1)} %copy-done.3), custom_call_target="tpu_custom_call" | custom-call | flops 268435456 | bytes 5242880 | tf_op jit(solution)/shard_map/out_grads/pallas_call | solution.py:47
  106.9 3.4 %input_grads.1 = (f32[128,1024]{1,0:T(8,128)}, bf16[232,128]{1,0:T(8,128)(2,1)}, bf16[232,128]{1,0:T(8,128)(2,1)}, bf16[232,128]{1,0:T(8,128)(2,1)}, bf16[232,128]{1,0:T(8,128)(2,1)}) custom-call(s32[3]{0:T(128)} %pad_add_fusion.place_ref, f32[480,128]{1,0:T(8,128)} %get-tuple-element.139.gq_ref, bf16[320,128]{1,0:T(8,128)(2,1)} %get-tuple-element.145.refs_0_, ...), custom_call_target="tpu_custom_call" | custom-call | flops 209715200 | bytes 1638400 | tf_op jit(solution)/shard_map/input_grads/pallas_call | solution.py:47
  112.9 3.3 %own_slab.1.h1_ref = bf16[1024,512]{1,0:T(8,128)(2,1)} custom-call(s32[3]{0:T(128)} %pad_add_fusion.place_ref, bf16[4,128,1024]{2,1,0:T(8,128)(2,1)} %copy-done.10, bf16[128,1024]{1,0:T(8,128)(2,1)} %get-tuple-element.127.refs_0_, bf16[128,1024]{1,0:T(8,128)(2,1)} %copy-done.12, bf16[128,1024]{1,0:T(8,128)(2,1)} %copy-done.13, bf16[128,1024]{1,0:T(8,128)(2,1)} %copy-done.14), custom_call_target="tpu_custom_call" | custom-call | bytes 1048576 | tf_op jit(solution)/shard_map/own_slab/pallas_call | solution.py:47
  116.9 2.5 %collective-permute-start.35 = (bf16[4,232,128]{2,1,0:T(8,128)(2,1)S(1)}, bf16[4,232,128]{2,1,0:T(8,128)(2,1)}, u32[]{:S(2)}, u32[]{:S(2)}) collective-permute-start(bf16[4,232,128]{2,1,0:T(8,128)(2,1)S(1)} %pad_maximum_fusion.3.mine_ref), channel_id=1, source_target_pairs={{0,1},{1,0},{2,3},{3,2},{4,5},{5,4},{6,7},{7,6},{8,9},{9,8},{10,11... | collective-permute-start | bytes 712712 | tf_op jit(solution)/shard_map/ppermute | solution.py:88
  120.6 2.6 %fact_grads.1 = (bf16[488,128]{1,0:T(8,128)(2,1)}, bf16[488,128]{1,0:T(8,128)(2,1)}, bf16[488,128]{1,0:T(8,128)(2,1)}, bf16[488,128]{1,0:T(8,128)(2,1)}) custom-call(bf16[1024,512]{1,0:T(8,128)(2,1)} %own_slab.1.h1_ref, bf16[4,232,128]{2,1,0:T(8,128)(2,1)} %copy-done.15, bf16[4,232,128]{2,1,0:T(8,128)(2,1)} %collective-permute-done.35.other_ref, ...), custom_call_target="tpu_custom_call" | custom-call | flops 243269632 | bytes 1048576 | tf_op jit(solution)/shard_map/fact_grads/pallas_call | solution.py:47
  124.6 2.2 %collective-permute-start.40 = (bf16[488,128]{1,0:T(8,128)(2,1)}, bf16[488,128]{1,0:T(8,128)(2,1)S(1)}, u32[]{:S(2)}, u32[]{:S(2)}) collective-permute-start(bf16[488,128]{1,0:T(8,128)(2,1)} %get-tuple-element.166), channel_id=1, source_target_pairs={{0,6},{2,4},{4,2},{6,0},{1,7},{3,5},{5,3},{7,1},{8,14},{10,12},{12... | collective-permute-start | bytes 374792 | tf_op jit(solution)/shard_map/ppermute | solution.py:88
  128.4 2.0 %collective-permute-start.41 = (bf16[352,256]{1,0:T(8,128)(2,1)S(1)}, bf16[352,256]{1,0:T(8,128)(2,1)S(1)}, u32[]{:S(2)}, u32[]{:S(2)}) collective-permute-start(bf16[352,256]{1,0:T(8,128)(2,1)S(1)} %fusion), channel_id=1, source_target_pairs={{0,0},{2,8},{4,16},{6,24},{1,1},{3,9},{5,17},{7,25},{8,10},{10,2},... | collective-permute-start | bytes 540680 | tf_op jit(solution)/shard_map/ppermute | solution.py:767
  132.1 2.5 %collective-permute-done.39 = bf16[488,128]{1,0:T(8,128)(2,1)S(1)} collective-permute-done((bf16[488,128]{1,0:T(8,128)(2,1)}, bf16[488,128]{1,0:T(8,128)(2,1)S(1)}, u32[]{:S(2)}, u32[]{:S(2)}) %collective-permute-start.39) | collective-permute-done | bytes 124960 | tf_op jit(solution)/shard_map/ppermute | solution.py:88
  136.7 11.0 %collective-permute-done.41 = bf16[352,256]{1,0:T(8,128)(2,1)S(1)} collective-permute-done((bf16[352,256]{1,0:T(8,128)(2,1)S(1)}, bf16[352,256]{1,0:T(8,128)(2,1)S(1)}, u32[]{:S(2)}, u32[]{:S(2)}) %collective-permute-start.41) | collective-permute-done | bytes 180256 | tf_op jit(solution)/shard_map/ppermute | solution.py:767
  (190 shorter events, 40.7 us)
Async XLA Ops:
  9.6 9.2 %collective-permute-start = (bf16[320,128]{1,0:T(8,128)(2,1)}, bf16[320,128]{1,0:T(8,128)(2,1)S(1)}, u32[]{:S(2)}, u32[]{:S(2)}) collective-permute-start(bf16[320,128]{1,0:T(8,128)(2,1)} %get-tuple-element.93.refs_5_.refs_9_), channel_id=1, source_target_pairs={{0,1},{1,0},{2,3},{3,2},{4,5},{5,4},{6,7},{7,6},{8,9},{9,8},{10,11... | collective-permute-start | bytes 245768 | tf_op jit(solution)/shard_map/ppermute | solution.py:88
  11.0 17.7 %collective-permute-start.9 = (bf16[128,1024]{1,0:T(8,128)(2,1)}, bf16[128,1024]{1,0:T(8,128)(2,1)S(1)}, u32[]{:S(2)}, u32[]{:S(2)}) collective-permute-start(bf16[128,1024]{1,0:T(8,128)(2,1)} %get-tuple-element.100.go_ref.refs_8_), channel_id=1, source_target_pairs={{0,24},{8,16},{16,8},{24,0},{1,25},{9,17},{17,9},{25,1},{2,26},{10... | collective-permute-start | bytes 786440 | tf_op jit(solution)/shard_map/ppermute | solution.py:88
  12.3 16.4 %collective-permute-start.8 = (bf16[128,1024]{1,0:T(8,128)(2,1)}, bf16[128,1024]{1,0:T(8,128)(2,1)S(1)}, u32[]{:S(2)}, u32[]{:S(2)}) collective-permute-start(bf16[128,1024]{1,0:T(8,128)(2,1)} %get-tuple-element.100.go_ref.refs_8_), channel_id=1, source_target_pairs={{0,16},{8,24},{16,0},{24,8},{1,17},{9,25},{17,1},{25,9},{2,18},{10... | collective-permute-start | bytes 786440 | tf_op jit(solution)/shard_map/ppermute | solution.py:88
  16.2 12.5 %collective-permute-start.7 = (bf16[128,1024]{1,0:T(8,128)(2,1)}, bf16[128,1024]{1,0:T(8,128)(2,1)S(1)}, u32[]{:S(2)}, u32[]{:S(2)}) collective-permute-start(bf16[128,1024]{1,0:T(8,128)(2,1)} %get-tuple-element.100.go_ref.refs_8_), channel_id=1, source_target_pairs={{0,8},{8,0},{16,24},{24,16},{1,9},{9,1},{17,25},{25,17},{2,10},{10... | collective-permute-start | bytes 786440 | tf_op jit(solution)/shard_map/ppermute | solution.py:88
  28.9 18.5 %collective-permute-start.10 = (bf16[4,128,1024]{2,1,0:T(8,128)(2,1)S(1)}, bf16[4,128,1024]{2,1,0:T(8,128)(2,1)S(1)}, u32[]{:S(2)}, u32[]{:S(2)}) collective-permute-start(bf16[4,128,1024]{2,1,0:T(8,128)(2,1)S(1)} %pad_maximum_fusion.1), channel_id=1, source_target_pairs={{0,1},{1,0},{2,3},{3,2},{4,5},{5,4},{6,7},{7,6},{8,9},{9,8},{10,11... | collective-permute-start | bytes 3145736 | tf_op jit(solution)/shard_map/ppermute | solution.py:88
  29.7 17.6 %collective-permute-start.13 = (bf16[128,1024]{1,0:T(8,128)(2,1)S(1)}, bf16[128,1024]{1,0:T(8,128)(2,1)S(1)}, u32[]{:S(2)}, u32[]{:S(2)}) collective-permute-start(bf16[128,1024]{1,0:T(8,128)(2,1)S(1)} %copy-done.4), channel_id=1, source_target_pairs={{0,24},{8,16},{16,8},{24,0},{1,25},{9,17},{17,9},{25,1},{2,26},{10... | collective-permute-start | bytes 786440 | tf_op jit(solution)/shard_map/ppermute | solution.py:88
  31.9 15.4 %collective-permute-start.12 = (bf16[128,1024]{1,0:T(8,128)(2,1)S(1)}, bf16[128,1024]{1,0:T(8,128)(2,1)S(1)}, u32[]{:S(2)}, u32[]{:S(2)}) collective-permute-start(bf16[128,1024]{1,0:T(8,128)(2,1)S(1)} %copy-done.4), channel_id=1, source_target_pairs={{0,16},{8,24},{16,0},{24,8},{1,17},{9,25},{17,1},{25,9},{2,18},{10... | collective-permute-start | bytes 786440 | tf_op jit(solution)/shard_map/ppermute | solution.py:88
  32.1 15.2 %collective-permute-start.11 = (bf16[128,1024]{1,0:T(8,128)(2,1)S(1)}, bf16[128,1024]{1,0:T(8,128)(2,1)S(1)}, u32[]{:S(2)}, u32[]{:S(2)}) collective-permute-start(bf16[128,1024]{1,0:T(8,128)(2,1)S(1)} %copy-done.4), channel_id=1, source_target_pairs={{0,8},{8,0},{16,24},{24,16},{1,9},{9,1},{17,25},{25,17},{2,10},{10... | collective-permute-start | bytes 786440 | tf_op jit(solution)/shard_map/ppermute | solution.py:88
  49.3 14.0 %collective-permute-start.21 = (bf16[128,1024]{1,0:T(8,128)(2,1)S(1)}, bf16[128,1024]{1,0:T(8,128)(2,1)S(1)}, u32[]{:S(2)}, u32[]{:S(2)}) collective-permute-start(bf16[128,1024]{1,0:T(8,128)(2,1)S(1)} %copy-done.11), channel_id=1, source_target_pairs={{0,8},{8,0},{16,24},{24,16},{1,9},{9,1},{17,25},{25,17},{2,10},{10... | collective-permute-start | bytes 786440 | tf_op jit(solution)/shard_map/ppermute | solution.py:88
  50.5 12.8 %collective-permute-start.22 = (bf16[128,1024]{1,0:T(8,128)(2,1)S(1)}, bf16[128,1024]{1,0:T(8,128)(2,1)S(1)}, u32[]{:S(2)}, u32[]{:S(2)}) collective-permute-start(bf16[128,1024]{1,0:T(8,128)(2,1)S(1)} %copy-done.11), channel_id=1, source_target_pairs={{0,16},{8,24},{16,0},{24,8},{1,17},{9,25},{17,1},{25,9},{2,18},{10... | collective-permute-start | bytes 786440 | tf_op jit(solution)/shard_map/ppermute | solution.py:88
  51.7 11.6 %collective-permute-start.23 = (bf16[128,1024]{1,0:T(8,128)(2,1)S(1)}, bf16[128,1024]{1,0:T(8,128)(2,1)S(1)}, u32[]{:S(2)}, u32[]{:S(2)}) collective-permute-start(bf16[128,1024]{1,0:T(8,128)(2,1)S(1)} %copy-done.11), channel_id=1, source_target_pairs={{0,24},{8,16},{16,8},{24,0},{1,25},{9,17},{17,9},{25,1},{2,26},{10... | collective-permute-start | bytes 786440 | tf_op jit(solution)/shard_map/ppermute | solution.py:88
  63.5 19.1 %collective-permute-start.24 = (bf16[4,128,1024]{2,1,0:T(8,128)(2,1)S(1)}, bf16[4,128,1024]{2,1,0:T(8,128)(2,1)S(1)}, u32[]{:S(2)}, u32[]{:S(2)}) collective-permute-start(bf16[4,128,1024]{2,1,0:T(8,128)(2,1)S(1)} %pad_maximum_fusion.2), channel_id=1, source_target_pairs={{0,1},{1,0},{2,3},{3,2},{4,5},{5,4},{6,7},{7,6},{8,9},{9,8},{10,11... | collective-permute-start | bytes 3145736 | tf_op jit(solution)/shard_map/ppermute | solution.py:88
  65.0 17.5 %collective-permute-start.25 = (bf16[2,704,256]{2,1,0:T(8,128)(2,1)S(1)}, bf16[2,704,256]{2,1,0:T(8,128)(2,1)S(1)}, u32[]{:S(2)}, u32[]{:S(2)}) collective-permute-start(bf16[2,704,256]{2,1,0:T(8,128)(2,1)S(1)} %copy-done.39), channel_id=1, source_target_pairs={{0,2},{2,0},{4,6},{6,4},{1,3},{3,1},{5,7},{7,5},{8,10},{10,8},{12,... | collective-permute-start | bytes 2162696 | tf_op jit(solution)/shard_map/ppermute | solution.py:88
  65.7 15.5 %collective-permute-start.18 = (bf16[128,1280]{1,0:T(8,128)(2,1)S(1)}, bf16[128,1280]{1,0:T(8,128)(2,1)S(1)}, u32[]{:S(2)}, u32[]{:S(2)}) collective-permute-start(bf16[128,1280]{1,0:T(8,128)(2,1)S(1)} %copy-done.43), channel_id=1, source_target_pairs={{0,8},{8,0},{16,24},{24,16},{1,9},{9,1},{17,25},{25,17},{2,10},{10... | collective-permute-start | bytes 983048 | tf_op jit(solution)/shard_map/ppermute | solution.py:88
  66.3 15.0 %collective-permute-start.19 = (bf16[128,1280]{1,0:T(8,128)(2,1)S(1)}, bf16[128,1280]{1,0:T(8,128)(2,1)S(1)}, u32[]{:S(2)}, u32[]{:S(2)}) collective-permute-start(bf16[128,1280]{1,0:T(8,128)(2,1)S(1)} %copy-done.42), channel_id=1, source_target_pairs={{0,16},{8,24},{16,0},{24,8},{1,17},{9,25},{17,1},{25,9},{2,18},{10... | collective-permute-start | bytes 983048 | tf_op jit(solution)/shard_map/ppermute | solution.py:88
  66.9 15.0 %collective-permute-start.20 = (bf16[128,1280]{1,0:T(8,128)(2,1)S(1)}, bf16[128,1280]{1,0:T(8,128)(2,1)S(1)}, u32[]{:S(2)}, u32[]{:S(2)}) collective-permute-start(bf16[128,1280]{1,0:T(8,128)(2,1)S(1)} %copy-done.41), channel_id=1, source_target_pairs={{0,24},{8,16},{16,8},{24,0},{1,25},{9,17},{17,9},{25,1},{2,26},{10... | collective-permute-start | bytes 983048 | tf_op jit(solution)/shard_map/ppermute | solution.py:88
  83.6 19.2 %collective-permute-start.26 = (bf16[4,128,1280]{2,1,0:T(8,128)(2,1)S(1)}, bf16[4,128,1280]{2,1,0:T(8,128)(2,1)S(1)}, u32[]{:S(2)}, u32[]{:S(2)}) collective-permute-start(bf16[4,128,1280]{2,1,0:T(8,128)(2,1)S(1)} %pad_maximum_fusion.mine_ref), channel_id=1, source_target_pairs={{0,1},{1,0},{2,3},{3,2},{4,5},{5,4},{6,7},{7,6},{8,9},{9,8},{10,11... | collective-permute-start | bytes 3932168 | tf_op jit(solution)/shard_map/ppermute | solution.py:88
  84.8 9.7 %collective-permute-start.31 = (bf16[2,352,256]{2,1,0:T(8,128)(2,1)S(1)}, bf16[2,352,256]{2,1,0:T(8,128)(2,1)S(1)}, u32[]{:S(2)}, u32[]{:S(2)}) collective-permute-start(bf16[2,352,256]{2,1,0:T(8,128)(2,1)S(1)} %copy-done.40), channel_id=1, source_target_pairs={{0,2},{2,0},{4,6},{6,4},{1,3},{3,1},{5,7},{7,5},{8,10},{10,8},{12,... | collective-permute-start | bytes 1081352 | tf_op jit(solution)/shard_map/ppermute | solution.py:88
  88.4 9.8 %collective-permute-start.30 = (bf16[320,128]{1,0:T(8,128)(2,1)S(1)}, bf16[320,128]{1,0:T(8,128)(2,1)S(1)}, u32[]{:S(2)}, u32[]{:S(2)}) collective-permute-start(bf16[320,128]{1,0:T(8,128)(2,1)S(1)} %get-tuple-element.186), channel_id=1, source_target_pairs={{0,6},{2,4},{4,2},{6,0},{1,7},{3,5},{5,3},{7,1},{8,14},{10,12},{12... | collective-permute-start | bytes 245768 | tf_op jit(solution)/shard_map/ppermute | solution.py:88
  90.8 8.9 %collective-permute-start.28 = (bf16[320,128]{1,0:T(8,128)(2,1)S(1)}, bf16[320,128]{1,0:T(8,128)(2,1)S(1)}, u32[]{:S(2)}, u32[]{:S(2)}) collective-permute-start(bf16[320,128]{1,0:T(8,128)(2,1)S(1)} %get-tuple-element.188), channel_id=1, source_target_pairs={{0,2},{2,0},{4,6},{6,4},{1,3},{3,1},{5,7},{7,5},{8,10},{10,8},{12,... | collective-permute-start | bytes 245768 | tf_op jit(solution)/shard_map/ppermute | solution.py:88
  100.4 26.4 %collective-permute-start.36 = (bf16[1,1056,256]{2,1,0:T(8,128)(2,1)S(1)}, bf16[1,1056,256]{2,1,0:T(8,128)(2,1)S(1)}, u32[]{:S(2)}, u32[]{:S(2)}) collective-permute-start(bf16[1,1056,256]{2,1,0:T(8,128)(2,1)S(1)} %slice.148), channel_id=1, source_target_pairs={{0,4},{2,6},{4,0},{6,2},{1,5},{3,7},{5,1},{7,3},{8,12},{10,14},{12... | collective-permute-start | bytes 1622024 | tf_op jit(solution)/shard_map/ppermute | solution.py:88
  123.7 10.9 %collective-permute-start.39 = (bf16[488,128]{1,0:T(8,128)(2,1)}, bf16[488,128]{1,0:T(8,128)(2,1)S(1)}, u32[]{:S(2)}, u32[]{:S(2)}) collective-permute-start(bf16[488,128]{1,0:T(8,128)(2,1)} %get-tuple-element.165), channel_id=1, source_target_pairs={{0,4},{2,6},{4,0},{6,2},{1,5},{3,7},{5,1},{7,3},{8,12},{10,14},{12... | collective-permute-start | bytes 374792 | tf_op jit(solution)/shard_map/ppermute | solution.py:88
  124.6 10.0 %collective-permute-start.40 = (bf16[488,128]{1,0:T(8,128)(2,1)}, bf16[488,128]{1,0:T(8,128)(2,1)S(1)}, u32[]{:S(2)}, u32[]{:S(2)}) collective-permute-start(bf16[488,128]{1,0:T(8,128)(2,1)} %get-tuple-element.166), channel_id=1, source_target_pairs={{0,6},{2,4},{4,2},{6,0},{1,7},{3,5},{5,3},{7,1},{8,14},{10,12},{12... | collective-permute-start | bytes 374792 | tf_op jit(solution)/shard_map/ppermute | solution.py:88
  128.4 19.3 %collective-permute-start.41 = (bf16[352,256]{1,0:T(8,128)(2,1)S(1)}, bf16[352,256]{1,0:T(8,128)(2,1)S(1)}, u32[]{:S(2)}, u32[]{:S(2)}) collective-permute-start(bf16[352,256]{1,0:T(8,128)(2,1)S(1)} %fusion), channel_id=1, source_target_pairs={{0,0},{2,8},{4,16},{6,24},{1,1},{3,9},{5,17},{7,25},{8,10},{10,2},... | collective-permute-start | bytes 540680 | tf_op jit(solution)/shard_map/ppermute | solution.py:767
  (64 other events, 405.4 us)
